TPU v7x, 32 devices: a whole 2x2x4 slice. The times are simulated.
32 devices in a mesh: dom: 8 (over y, x, core), pert: 4 (over z).
Axes of the slice: x: 2, y: 2, z: 4, core: 2. Of those that a mesh axis runs over, the one named last changes fastest.
Arguments:
- probes: float32 [64, 1024], P('pert', 'dom'), may hold values from -6 to 6
- melt_shape: float32 [65536], P('dom'), may hold values from 0.5 to 1.5
- obs_weight: float32 [65536], P('dom'), may hold values from 0.1 to 1
- diag_inverse: bfloat16 [1024, 64, 64], P('dom'), as said below
- coupling: bfloat16 [1024, 64, 256], P('dom'), may hold values from -0.25 to 0.25
- columns: int32 [1024, 4], P('dom'), may hold values from 0 to 191, as said below
- send_list: int32 [8, 4, 16], P('dom'), may hold values from -1 to 127, as said below
- patch_of_block: int32 [1024], P('dom'), may hold values from 0 to 1023, each once
Outputs:
- tangent: float32 [64, 65536], P('pert', 'dom')
- hessian_probe: float32 [64, 1024], P('pert', 'dom')
- hessian_diagonal: float32 [1024], P('dom')
Inputs may be any that keep to these rules, and one draw needn't show every extreme that they name: send_list[d, j] lists distinct block numbers of partition d that it sends to partition d + o, o = (-2, -1, 1, 2)[j], in its first slots, and -1 in the others; a group whose target lies outside the partitions is empty, every other group fills at least half of its 16 slots, and some group fills all of them. `columns`: an entry below 128 names a block of the same partition; an entry at or above it names a filled interface slot as in the first step. `patch_of_block`: every parameter patch belongs to exactly one block row. `diag_inverse`: the inverse of the diagonal block of each block row.
All inputs are finite; a program needn't handle non-finite values.
Results may differ from a plain program's by a relative error of at most 0.0075.
Values may be sent and summed in bfloat16 or wider, within the bound.
No kernel may reach another device: no remote copies, remote signals or barrier semaphores. Data moves between devices by JAX's collectives and lax.ppermute only.
A program may use at most 64 MiB of HBM per device.

v0:
```python
import functools

import jax
import jax.numpy as jnp
from jax import lax
from jax.experimental import pallas as pl
from jax.experimental.pallas import tpu as pltpu
from jax.sharding import PartitionSpec as P

OFFSET_LIST = (-2, -1, 1, 2)
F32 = jnp.float32
BF16 = jnp.bfloat16
LANES = 128
HALF = 64
QUAD = 4

VMEM = pl.BlockSpec(memory_space=pltpu.VMEM)
SMEM = pl.BlockSpec(memory_space=pltpu.SMEM)
PARAMS = pltpu.CompilerParams(vmem_limit_bytes=48 * 1024 * 1024)


def low_half(shape):
    return lax.broadcasted_iota(jnp.int32, shape, len(shape) - 1) < HALF


def swap_halves(value):
    return pltpu.roll(value, HALF, 1)


def rotated(value, by):
    peers = lax.axis_size("dom")
    return lax.ppermute(value, "dom", [(i, (i + by) % peers) for i in range(peers)])


def melt_kernel(send_ref, melt_ref, patch_ref, diag_ref, w_ref, *msg_refs):
    quads = diag_ref.shape[0] // QUAD
    sub = lax.broadcasted_iota(jnp.int32, (16, LANES), 0)
    low = low_half((1, LANES))

    def one(quad, _):
        row_a = melt_ref[pl.ds(2 * quad, 1), :]
        row_b = melt_ref[pl.ds(2 * quad + 1, 1), :]
        value = jnp.where(
            sub < 4,
            jnp.where(sub < 2, row_a, swap_halves(row_a)),
            jnp.where(sub < 6, row_b, swap_halves(row_b)),
        )
        top = value.astype(BF16).astype(F32)
        value = jnp.where(sub % 2 == 0, top, value - top)[:, :HALF].astype(BF16)
        blocks = diag_ref[pl.ds(quad * QUAD, QUAD)].reshape(QUAD * HALF, HALF)
        out = lax.dot_general(
            value, blocks, (((1,), (1,)), ((), ())), preferred_element_type=F32
        )
        first = out[:, :LANES]
        second = out[:, LANES:]
        w_ref[pl.ds(2 * quad, 1), :] = jnp.where(
            low, first[0:1] + first[1:2], first[2:3] + first[3:4]
        )
        w_ref[pl.ds(2 * quad + 1, 1), :] = jnp.where(
            low, second[4:5] + second[5:6], second[6:7] + second[7:8]
        )
        return 0

    lax.fori_loop(0, quads, one, 0, unroll=4)
    patch_row = patch_ref[...].astype(F32)
    lane = lax.broadcasted_iota(jnp.int32, (1, LANES), 1)
    capacity = send_ref.shape[2]
    for group, msg_ref in enumerate(msg_refs):
        ids = jnp.zeros((1, LANES), jnp.int32)
        for slot in range(capacity):
            block = jnp.maximum(send_ref[0, group, slot], 0)
            row = w_ref[pl.ds(block // 2, 1), :]
            msg_ref[slot : slot + 1, :] = jnp.where(
                low == (block % 2 == 0), row, swap_halves(row)
            )
            ids = jnp.where(lane == group * capacity + slot, block, ids)
        picked = jnp.take_along_axis(
            jnp.broadcast_to(patch_row, (8, LANES)), jnp.broadcast_to(ids, (8, LANES)), axis=1
        )
        mine = (lane >= group * capacity) & (lane < (group + 1) * capacity)
        msg_ref[capacity : capacity + 8, :] = jnp.where(mine, picked, 0.0)


def product_kernel(diag_ref, coupling_ref, m_ref):
    def one(block, _):
        m_ref[block] = jnp.dot(
            diag_ref[block], coupling_ref[block], preferred_element_type=F32
        ).astype(BF16)
        return 0

    lax.fori_loop(0, diag_ref.shape[0], one, 0, unroll=8)


def gather_multiply(quad, cols_ref, ext_ref, m_ref, low):
    rows = []
    for place in range(QUAD):
        g = quad * QUAD + place
        tiles = [ext_ref[cols_ref[g, k]] for k in range(4)]
        rows.append(
            jnp.concatenate(
                [jnp.where(low, tiles[0], tiles[1]), jnp.where(low, tiles[2], tiles[3])], axis=1
            )
        )
    lhs = jnp.concatenate(rows, axis=0)
    rhs = m_ref[pl.ds(quad * QUAD, QUAD)].reshape(QUAD * HALF, 4 * HALF)
    out = lax.dot_general(lhs, rhs, (((1,), (1,)), ((), ())), preferred_element_type=F32)
    p = out.shape[0] // QUAD
    first = jnp.where(low, out[:p, :LANES], out[p : 2 * p, :LANES])
    second = jnp.where(low, out[2 * p : 3 * p, LANES:], out[3 * p :, LANES:])
    return first, second


def store_pair(ref, pair, value, low):
    value = value.astype(BF16)
    other = swap_halves(value.astype(F32)).astype(BF16)
    ref[2 * pair] = jnp.where(low, value, other)
    ref[2 * pair + 1] = jnp.where(low, other, value)


def fill_messages(send_ref, ref, msg_refs):
    for group, msg_ref in enumerate(msg_refs):
        for slot in range(msg_ref.shape[0]):
            msg_ref[slot] = ref[jnp.maximum(send_ref[0, group, slot], 0)]


def first_kernel(
    cols_ref, send_ref, patch_ref, probe_ref, w_ref, g0, g1, g2, g3, m_ref,
    one_hot_ref, t1_ref, t2_ref, o0, o1, o2, o3, ext_ref,
):
    ghosts = (g0, g1, g2, g3)
    pert = probe_ref.shape[1]
    capacity = send_ref.shape[2]
    blocks = cols_ref.shape[0]
    low = low_half((pert, LANES))
    lane = lax.broadcasted_iota(jnp.int32, (1, LANES), 1)
    ghost_ids = g0[capacity : capacity + 1, :]
    for ref in ghosts[1:]:
        ghost_ids = ghost_ids + ref[capacity : capacity + 1, :]
    ghost_ids = jnp.where(lane < 4 * capacity, ghost_ids, -1.0)
    ids = jnp.concatenate([patch_ref[...].astype(F32), ghost_ids], axis=1)
    parts = probe_ref.shape[0]
    total = jnp.zeros((3 * pert, 2 * LANES), F32)
    for part in range(parts):
        names = (
            lax.broadcasted_iota(jnp.int32, (LANES, 2 * LANES), 0) + part * LANES
        ).astype(F32)
        hot = jnp.where(names == ids, 1.0, 0.0).astype(BF16)
        one_hot_ref[part * LANES : (part + 1) * LANES, :] = hot
        value = probe_ref[part]
        top = value.astype(BF16)
        rest = value - top.astype(F32)
        mid = rest.astype(BF16)
        last = (rest - mid.astype(F32)).astype(BF16)
        total = total + jnp.dot(
            jnp.concatenate([top, mid, last], axis=0), hot, preferred_element_type=F32
        )
    picked = total[:pert] + total[pert : 2 * pert] + total[2 * pert :]
    local_picked = picked[:, :LANES]
    ghost_picked = picked[:, LANES:]
    full_low = low.astype(jnp.int32)

    def seed(pair, _):
        index = 2 * pair + 1 - full_low
        spread = jnp.take_along_axis(local_picked, index, axis=1)
        value = spread * w_ref[pl.ds(pair, 1), :]
        t1_ref[pair] = value
        store_pair(ext_ref, pair, value, low)
        return 0

    lax.fori_loop(0, blocks // 2, seed, 0, unroll=4)
    for group, ref in enumerate(ghosts):
        for slot in range(capacity):
            place = group * capacity + slot
            spread = jnp.broadcast_to(ghost_picked[:, place : place + 1], (pert, LANES))
            ext_ref[blocks + place] = (spread * ref[slot : slot + 1, :]).astype(BF16)

    def sweep(quad, _):
        first, second = gather_multiply(quad, cols_ref, ext_ref, m_ref, low)
        store_pair(t2_ref, 2 * quad, t1_ref[2 * quad] - first, low)
        store_pair(t2_ref, 2 * quad + 1, t1_ref[2 * quad + 1] - second, low)
        return 0

    lax.fori_loop(0, blocks // QUAD, sweep, 0, unroll=2)
    fill_messages(send_ref, t2_ref, (o0, o1, o2, o3))


def extend(ext_ref, local_ref, ghosts):
    blocks = local_ref.shape[0]
    capacity = ghosts[0].shape[0]
    ext_ref[:blocks] = local_ref[...]
    for group, ref in enumerate(ghosts):
        ext_ref[blocks + group * capacity : blocks + (group + 1) * capacity] = ref[...]


def sweep_kernel(
    cols_ref, send_ref, t1_ref, prev_ref, g0, g1, g2, g3, m_ref,
    next_ref, o0, o1, o2, o3, ext_ref,
):
    low = low_half(prev_ref.shape[1:])
    extend(ext_ref, prev_ref, (g0, g1, g2, g3))

    def sweep(quad, _):
        first, second = gather_multiply(quad, cols_ref, ext_ref, m_ref, low)
        store_pair(next_ref, 2 * quad, t1_ref[2 * quad] - first, low)
        store_pair(next_ref, 2 * quad + 1, t1_ref[2 * quad + 1] - second, low)
        return 0

    lax.fori_loop(0, cols_ref.shape[0] // QUAD, sweep, 0, unroll=2)
    fill_messages(send_ref, next_ref, (o0, o1, o2, o3))


def clear(acc_refs):
    def one(place, _):
        for ref in acc_refs:
            ref[place] = jnp.zeros(ref.shape[1:], F32)
        return 0

    lax.fori_loop(0, acc_refs[0].shape[0], one, 0, unroll=4)


def multiply_scatter(quad, cols_ref, pairs, m_ref, acc_refs, low):
    zero = jnp.zeros(pairs[0].shape, F32)
    rows = []
    for place in range(QUAD):
        value = pairs[place // 2]
        kept = jnp.where(low, value, zero) if place % 2 == 0 else jnp.where(low, zero, value)
        tiles = [kept, zero] if place < 2 else [zero, kept]
        rows.append(jnp.concatenate(tiles, axis=1))
    lhs = jnp.concatenate(rows, axis=0).astype(BF16)
    rhs = m_ref[pl.ds(quad * QUAD, QUAD)].reshape(QUAD * HALF, 4 * HALF)
    out = jnp.dot(lhs, rhs, preferred_element_type=F32)
    p = pairs[0].shape[0]
    for place in range(QUAD):
        g = quad * QUAD + place
        for k in range(4):
            column = cols_ref[g, k]
            piece = out[place * p : (place + 1) * p, (k // 2) * LANES : (k // 2 + 1) * LANES]
            acc_refs[k][column] = acc_refs[k][column] + piece


def half_sums(acc_refs, place, low):
    return jnp.where(
        low, acc_refs[0][place] + acc_refs[2][place], acc_refs[1][place] + acc_refs[3][place]
    )


def pair_sum(acc_refs, pair, low):
    even = half_sums(acc_refs, 2 * pair, low)
    odd = half_sums(acc_refs, 2 * pair + 1, low)
    return jnp.where(low, even, odd) + swap_halves(jnp.where(low, odd, even))


def ghost_sum(acc_refs, place, low):
    value = half_sums(acc_refs, place, low)
    return value + swap_halves(value)


def finish_round(base_ref, target_ref, acc_refs, msg_refs, blocks, low):
    def local(pair, _):
        base_ref[pair] = target_ref[pair] - pair_sum(acc_refs, pair, low)
        return 0

    lax.fori_loop(0, blocks // 2, local, 0, unroll=4)
    for group, ref in enumerate(msg_refs):
        capacity = ref.shape[0]
        for slot in range(capacity):
            ref[slot] = ghost_sum(acc_refs, blocks + group * capacity + slot, low).astype(BF16)


def turn_kernel(
    cols_ref, t1_ref, prev_ref, g0, g1, g2, g3, m_ref, weight_ref,
    tangent_ref, target_ref, base_ref, o0, o1, o2, o3, ext_ref, *acc_refs,
):
    low = low_half(prev_ref.shape[1:])
    blocks = cols_ref.shape[0]
    extend(ext_ref, prev_ref, (g0, g1, g2, g3))
    clear(acc_refs)

    def sweep(quad, _):
        coupled = gather_multiply(quad, cols_ref, ext_ref, m_ref, low)
        pairs = []
        for place in range(2):
            pair = 2 * quad + place
            value = t1_ref[pair] - coupled[place]
            start = pl.multiple_of(pair * LANES, LANES)
            tangent_ref[:, pl.ds(start, LANES)] = value
            target = value * weight_ref[pl.ds(pair, 1), :]
            target_ref[pair] = target
            pairs.append(target)
        multiply_scatter(quad, cols_ref, pairs, m_ref, acc_refs, low)
        return 0

    lax.fori_loop(0, blocks // QUAD, sweep, 0, unroll=2)
    finish_round(base_ref, target_ref, acc_refs, (o0, o1, o2, o3), blocks, low)


def take_returned(send_ref, base_ref, u_ref, ghosts, low):
    u_ref[...] = base_ref[...]
    for group, ref in enumerate(ghosts):
        for slot in range(ref.shape[0]):
            block = send_ref[0, group, slot]
            pair = jnp.maximum(block, 0) // 2
            odd = block % 2
            wanted = jnp.where(block < 0, 2, odd)
            keep = (1 - low.astype(jnp.int32)) == wanted
            u_ref[pair] = u_ref[pair] - jnp.where(keep, ref[slot].astype(F32), 0.0)


def scatter_all(cols_ref, u_ref, m_ref, acc_refs, low):
    clear(acc_refs)

    def sweep(quad, _):
        pairs = [u_ref[2 * quad], u_ref[2 * quad + 1]]
        multiply_scatter(quad, cols_ref, pairs, m_ref, acc_refs, low)
        return 0

    lax.fori_loop(0, cols_ref.shape[0] // QUAD, sweep, 0, unroll=2)


def adjoint_kernel(
    cols_ref, send_ref, base_in_ref, target_ref, g0, g1, g2, g3, m_ref,
    base_ref, o0, o1, o2, o3, u_ref, *acc_refs,
):
    low = low_half(u_ref.shape[1:])
    take_returned(send_ref, base_in_ref, u_ref, (g0, g1, g2, g3), low)
    scatter_all(cols_ref, u_ref, m_ref, acc_refs, low)
    finish_round(base_ref, target_ref, acc_refs, (o0, o1, o2, o3), cols_ref.shape[0], low)


def last_kernel(
    cols_ref, send_ref, base_in_ref, target_ref, g0, g1, g2, g3, m_ref, w_ref, w0, w1, w2, w3,
    one_hot_ref, out_ref, u_ref, *acc_refs,
):
    pert = u_ref.shape[1]
    blocks = cols_ref.shape[0]
    low = low_half(u_ref.shape[1:])
    lane = lax.broadcasted_iota(jnp.int32, (pert, LANES), 1)
    take_returned(send_ref, base_in_ref, u_ref, (g0, g1, g2, g3), low)
    scatter_all(cols_ref, u_ref, m_ref, acc_refs, low)

    def local(pair, terms):
        value = (target_ref[pair] - pair_sum(acc_refs, pair, low)) * w_ref[pl.ds(pair, 1), :]
        even = jnp.sum(jnp.where(low, value, 0.0), axis=1, keepdims=True)
        odd = jnp.sum(jnp.where(low, 0.0, value), axis=1, keepdims=True)
        return jnp.where(lane == 2 * pair, even, jnp.where(lane == 2 * pair + 1, odd, terms))

    local_terms = lax.fori_loop(
        0, blocks // 2, local, jnp.zeros((pert, LANES), F32), unroll=4
    )
    ghost_terms = jnp.zeros((pert, LANES), F32)
    for group, ref in enumerate((w0, w1, w2, w3)):
        capacity = g0.shape[0]
        for slot in range(capacity):
            place = group * capacity + slot
            value = half_sums(acc_refs, blocks + place, low) * ref[slot : slot + 1, :]
            ghost_terms = jnp.where(
                lane == place, -jnp.sum(value, axis=1, keepdims=True), ghost_terms
            )
    terms = jnp.concatenate([local_terms, ghost_terms], axis=1)
    top = terms.astype(BF16)
    rest = (terms - top.astype(F32)).astype(BF16)
    both = jnp.concatenate([top, rest], axis=0)
    for part in range(out_ref.shape[0]):
        hot = one_hot_ref[part * LANES : (part + 1) * LANES, :]
        out = lax.dot_general(both, hot, (((1,), (1,)), ((), ())), preferred_element_type=F32)
        out_ref[part] = (out[:pert] + out[pert:]).astype(BF16)


def owner_kernel(terms_ref, probe_ref, hessian_ref, curve_ref):
    total = terms_ref[0].astype(F32)
    for part in range(1, terms_ref.shape[0]):
        total = total + terms_ref[part].astype(F32)
    hessian_ref[...] = total
    curve_ref[...] = jnp.broadcast_to(
        jnp.sum(total * probe_ref[...], axis=0, keepdims=True), curve_ref.shape
    )


def call(body, outs, spaces, scratch=(), name=None, flops=0, moved=1 << 20):
    return pl.pallas_call(
        body,
        out_shape=outs,
        in_specs=[SMEM if s == "s" else VMEM for s in spaces],
        out_specs=jax.tree.map(lambda _: VMEM, outs),
        scratch_shapes=list(scratch),
        compiler_params=PARAMS,
        name=name,
        cost_estimate=pl.CostEstimate(flops=flops, transcendentals=0, bytes_accessed=moved),
    )


def shards(
    probes, melt_shape, obs_weight, diag_inverse, coupling, columns, send_list, patch_of_block
):
    pert = probes.shape[0]
    blocks = coupling.shape[0]
    capacity = send_list.shape[2]
    parts = lax.axis_size("dom")
    pairs = blocks // 2
    shape = jax.ShapeDtypeStruct
    msgs = [shape((capacity, pert, LANES), BF16)] * 4
    pair_array = shape((pairs, pert, LANES), F32)
    block_array = shape((blocks, pert, LANES), BF16)
    ext = pltpu.VMEM((blocks + 4 * capacity, pert, LANES), BF16)
    accs = [pltpu.VMEM((blocks + 4 * capacity, pert, LANES), F32)] * 4
    held = pltpu.VMEM((pairs, pert, LANES), F32)
    melt = melt_shape.reshape(pairs, LANES)
    weight = obs_weight.reshape(pairs, LANES)
    patch = patch_of_block.reshape(1, blocks)

    spread = lax.all_to_all(
        jnp.broadcast_to(probes[None], (parts,) + probes.shape), "dom", 0, 0, tiled=True
    )
    w, *w_msgs = call(
        melt_kernel,
        [shape((pairs, LANES), F32)] + [shape((capacity + 8, LANES), F32)] * 4,
        "svvv",
        name="melt",
    )(send_list, melt, patch, diag_inverse)
    w_ghosts = [rotated(m, o) for m, o in zip(w_msgs, OFFSET_LIST)]
    m = call(
        product_kernel, shape(coupling.shape, BF16), "vv", name="product", flops=1 << 28, moved=10 << 20
    )(diag_inverse, coupling)

    one_hot, t1, state, *out = call(
        first_kernel,
        [shape((parts * probes.shape[1], 2 * LANES), BF16), pair_array, block_array] + msgs,
        "ssvvvvvvvv",
        [ext],
        name="first",
    )(columns, send_list, patch, spread, w, *w_ghosts, m)
    ghosts = [rotated(v, o) for v, o in zip(out, OFFSET_LIST)]
    state, *out = call(
        sweep_kernel, [block_array] + msgs, "ssvvvvvvv", [ext], name="sweep"
    )(columns, send_list, t1, state, *ghosts, m)
    ghosts = [rotated(v, o) for v, o in zip(out, OFFSET_LIST)]
    tangent, target, base, *out = call(
        turn_kernel,
        [shape((pert, blocks * HALF), F32), pair_array, pair_array] + msgs,
        "svvvvvvvv",
        [ext] + accs,
        name="turn",
    )(columns, t1, state, *ghosts, m, weight)
    ghosts = [rotated(v, -o) for v, o in zip(out, OFFSET_LIST)]
    base, *out = call(
        adjoint_kernel, [pair_array] + msgs, "ssvvvvvvv", [held] + accs, name="adjoint"
    )(columns, send_list, base, target, *ghosts, m)
    ghosts = [rotated(v, -o) for v, o in zip(out, OFFSET_LIST)]
    terms = call(
        last_kernel,
        shape((parts, pert, LANES), BF16),
        "ssvvvvvvvvvvvvv",
        [held] + accs,
        name="last",
    )(columns, send_list, base, target, *ghosts, m, w, *w_ghosts, one_hot)
    terms = lax.all_to_all(terms, "dom", 0, 0, tiled=True)
    hessian_probe, curve = call(
        owner_kernel, [shape(probes.shape, F32), shape((8, LANES), F32)], "vv", name="owner"
    )(terms, probes)
    perts = lax.axis_size("pert")
    curvature = jnp.sum(lax.all_gather(curve[0], "pert", axis=0), axis=0)
    return tangent, hessian_probe, curvature / (pert * perts)


def solution(mesh):
    in_specs = (
        P("pert", "dom"),
        P("dom"),
        P("dom"),
        P("dom", None, None),
        P("dom", None, None),
        P("dom", None),
        P("dom", None, None),
        P("dom"),
    )
    out_specs = (P("pert", "dom"), P("pert", "dom"), P("dom"))
    return jax.shard_map(shards, mesh=mesh, in_specs=in_specs, out_specs=out_specs, check_vma=False)
```

profile of v0, /device:TPU:0, one launch (start us, length us, event | category | flops | bytes accessed | tf_op | source)
XLA Modules:
  0.0 126.8 jit_solution(11532008600147427904)
XLA Ops:
  0.6 1.3 %broadcast_in_dim.2 = f32[8,16,128]{2,1,0:T(8,128)} broadcast(f32[16,128]{1,0:T(8,128)} %probe_ref.1), dimensions={1,2} | broadcast | bytes 73728 | tf_op jit(solution)/shard_map/broadcast_in_dim | solution.py:412
  2.0 5.2 %all-to-all-start = ((f32[8,16,128]{2,1,0:T(8,128)}), f32[8,16,128]{2,1,0:T(8,128)S(1)}, u32[]{:S(2)}, u32[]{:S(2)}) async-start(f32[8,16,128]{2,1,0:T(8,128)} %broadcast_in_dim.2), calls=%async_computation | async-start | bytes 131072 | tf_op jit(solution)/shard_map/all_to_all | solution.py:411
  7.1 3.9 %copy.18.diag_ref = bf16[128,64,64]{2,1,0:T(8,128)(2,1)S(1)} copy(bf16[128,64,64]{0,2,1:T(8,128)(2,1)} %param.11) | data formatting | bytes 2097152 | tf_op args[3]
  11.1 0.0 copy-start.1
  11.1 0.7 copy-done.1
  11.8 0.8 copy-done.3
  12.5 0.7 copy-done.6
  13.2 2.7 %melt.1 = (f32[64,128]{1,0:T(8,128)S(1)}, f32[24,128]{1,0:T(8,128)S(1)}, f32[24,128]{1,0:T(8,128)S(1)}, f32[24,128]{1,0:T(8,128)S(1)}, f32[24,128]{1,0:T(8,128)S(1)}) custom-call(s32[1,4,16]{2,1,0:T(4,128)S(1)} %copy-done.1, f32[64,128]{1,0:T(8,128)S(1)} %bitcast.5, s32[1,128]{1,0:T(1,128)S(1)} %bitcast.7, bf16[128,64,64]{2,1,0:T(8,128)(2,1)S(1)} %copy.18.diag_ref), custom_call_target="tpu_custom_call" | custom-call | bytes 1048576 | tf_op jit(solution)/shard_map/melt/pallas_call | solution.py:414
  15.9 3.0 %collective-permute-start = (f32[24,128]{1,0:T(8,128)S(1)}, f32[24,128]{1,0:T(8,128)S(1)}, u32[]{:S(2)}, u32[]{:S(2)}) collective-permute-start(f32[24,128]{1,0:T(8,128)S(1)} %get-tuple-element.35), channel_id=1, source_target_pairs={{0,24},{4,28},{8,0},{12,4},{16,8},{20,12},{24,16},{28,20},{1,25},{... | collective-permute-start | bytes 36872 | tf_op jit(solution)/shard_map/ppermute | solution.py:32
  18.9 0.1 collective-permute-start.1
  18.9 0.5 collective-permute-start.2
  19.4 1.0 collective-permute-start.3
  20.4 7.5 %product.1.m_ref = bf16[128,64,256]{2,1,0:T(8,128)(2,1)} custom-call(bf16[128,64,64]{2,1,0:T(8,128)(2,1)S(1)} %copy.18.diag_ref, bf16[128,64,256]{2,1,0:T(8,128)(2,1)} %coupling_ref.1), custom_call_target="tpu_custom_call" | custom-call | flops 268435456 | bytes 10485760 | tf_op jit(solution)/shard_map/product/pallas_call | solution.py:421
  28.0 0.0 copy-done.8
  28.0 0.1 copy.22.cols_ref
  28.1 0.0 collective-permute-done.g0.w0
  28.1 0.0 collective-permute-done.1.g1.w1
  28.1 0.0 collective-permute-done.2.g2.w2
  28.1 0.0 collective-permute-done.3.g3.w3
  28.1 0.0 all-to-all-done.probe_ref
  28.1 0.0 copy-start.4
  28.2 9.9 %first.1 = (bf16[1024,256]{1,0:T(8,128)(2,1)S(1)}, f32[64,16,128]{2,1,0:T(8,128)S(1)}, bf16[128,16,128]{2,1,0:T(8,128)(2,1)S(1)}, bf16[16,16,128]{2,1,0:T(8,128)...) custom-call(s32[128,4]{1,0:T(8,128)S(1)} %copy.22.cols_ref, ...), custom_call_target="tpu_custom_call" | custom-call | bytes 1048576 | tf_op jit(solution)/shard_map/first/pallas_call | solution.py:425
  38.0 1.9 %collective-permute-start.4 = (bf16[16,16,128]{2,1,0:T(8,128)(2,1)S(1)}, bf16[16,16,128]{2,1,0:T(8,128)(2,1)S(1)}, u32[]{:S(2)}, u32[]{:S(2)}) collective-permute-start(bf16[16,16,128]{2,1,0:T(8,128)(2,1)S(1)} %get-tuple-element.41), channel_id=1, source_target_pairs={{0,24},{4,28},{8,0},{12,4},{16,8},{20,12},{24,16},{28,20},{1,25},{... | collective-permute-start | bytes 196616 | tf_op jit(solution)/shard_map/ppermute | solution.py:32
  39.9 0.7 collective-permute-start.5
  40.7 0.0 collective-permute-start.6
  40.7 1.5 %collective-permute-start.7 = (bf16[16,16,128]{2,1,0:T(8,128)(2,1)S(1)}, bf16[16,16,128]{2,1,0:T(8,128)(2,1)S(1)}, u32[]{:S(2)}, u32[]{:S(2)}) collective-permute-start(bf16[16,16,128]{2,1,0:T(8,128)(2,1)S(1)} %get-tuple-element.44), channel_id=1, source_target_pairs={{0,8},{4,12},{8,16},{12,20},{16,24},{20,28},{24,0},{28,4},{1,9},{5... | collective-permute-start | bytes 196616 | tf_op jit(solution)/shard_map/ppermute | solution.py:32
  42.2 0.2 collective-permute-done.4.g0
  42.4 0.9 collective-permute-done.5.g1
  43.3 2.1 %collective-permute-done.6.g2 = bf16[16,16,128]{2,1,0:T(8,128)(2,1)S(1)} collective-permute-done((bf16[16,16,128]{2,1,0:T(8,128)(2,1)S(1)}, bf16[16,16,128]{2,1,0:T(8,128)(2,1)S(1)}, u32[]{:S(2)}, u32[]{:S(2)}) %collective-permute-start.6) | collective-permute-done | bytes 65568 | tf_op jit(solution)/shard_map/ppermute | solution.py:32
  45.4 0.8 collective-permute-done.7.g3
  46.3 6.8 %sweep.1 = (bf16[128,16,128]{2,1,0:T(8,128)(2,1)S(1)}, bf16[16,16,128]{2,1,0:T(8,128)(2,1)S(1)}, bf16[16,16,128]{2,1,0:T(8,128)(2,1)S(1)}, bf16[16,16,128]{2,1,0:T(8,128)(2,1)S(1)}, bf16[16,16,128]{2,1,0:T(8,128)(2,1)S(1)}) custom-call(s32[128,4]{1,0:T(8,128)S(1)} %copy.22.cols_ref, s32[1,4,16]{2,1,0:T(4,128)S(1)} %copy-done.2, ...), custom_call_target="tpu_custom_call" | custom-call | bytes 1048576 | tf_op jit(solution)/shard_map/sweep/pallas_call | solution.py:433
  53.1 1.0 collective-permute-start.8
  54.1 1.6 %collective-permute-start.9 = (bf16[16,16,128]{2,1,0:T(8,128)(2,1)S(1)}, bf16[16,16,128]{2,1,0:T(8,128)(2,1)S(1)}, u32[]{:S(2)}, u32[]{:S(2)}) collective-permute-start(bf16[16,16,128]{2,1,0:T(8,128)(2,1)S(1)} %get-tuple-element.47), channel_id=1, source_target_pairs={{0,28},{4,0},{8,4},{12,8},{16,12},{20,16},{24,20},{28,24},{1,29},{... | collective-permute-start | bytes 196616 | tf_op jit(solution)/shard_map/ppermute | solution.py:32
  55.6 0.0 collective-permute-start.10
  55.6 0.1 collective-permute-start.11
  55.7 1.7 %collective-permute-done.8.g0 = bf16[16,16,128]{2,1,0:T(8,128)(2,1)S(1)} collective-permute-done((bf16[16,16,128]{2,1,0:T(8,128)(2,1)S(1)}, bf16[16,16,128]{2,1,0:T(8,128)(2,1)S(1)}, u32[]{:S(2)}, u32[]{:S(2)}) %collective-permute-start.8) | collective-permute-done | bytes 65568 | tf_op jit(solution)/shard_map/ppermute | solution.py:32
  57.4 0.1 collective-permute-done.9.g1
  57.5 2.8 %collective-permute-done.10.g2 = bf16[16,16,128]{2,1,0:T(8,128)(2,1)S(1)} collective-permute-done((bf16[16,16,128]{2,1,0:T(8,128)(2,1)S(1)}, bf16[16,16,128]{2,1,0:T(8,128)(2,1)S(1)}, u32[]{:S(2)}, u32[]{:S(2)}) %collective-permute-start.10) | collective-permute-done | bytes 65568 | tf_op jit(solution)/shard_map/ppermute | solution.py:32
  60.4 1.1 collective-permute-done.11.g3
  61.5 13.0 %turn.1 = (f32[16,8192]{1,0:T(8,128)}, f32[64,16,128]{2,1,0:T(8,128)S(1)}, f32[64,16,128]{2,1,0:T(8,128)S(1)}, bf16[16,16,128]{2,1,0:T(8,128)(2,1)S(1)}, bf16[16...) custom-call(s32[128,4]{1,0:T(8,128)S(1)} %copy.22.cols_ref, ...), custom_call_target="tpu_custom_call" | custom-call | bytes 1048576 | tf_op jit(solution)/shard_map/turn/pallas_call | solution.py:437
  74.4 0.0 collective-permute-start.12
  74.4 0.1 collective-permute-start.13
  74.6 2.6 %collective-permute-start.14 = (bf16[16,16,128]{2,1,0:T(8,128)(2,1)S(1)}, bf16[16,16,128]{2,1,0:T(8,128)(2,1)S(1)}, u32[]{:S(2)}, u32[]{:S(2)}) collective-permute-start(bf16[16,16,128]{2,1,0:T(8,128)(2,1)S(1)} %get-tuple-element.55), channel_id=1, source_target_pairs={{0,28},{4,0},{8,4},{12,8},{16,12},{20,16},{24,20},{28,24},{1,29},{... | collective-permute-start | bytes 196616 | tf_op jit(solution)/shard_map/ppermute | solution.py:32
  77.1 2.0 %collective-permute-start.15 = (bf16[16,16,128]{2,1,0:T(8,128)(2,1)S(1)}, bf16[16,16,128]{2,1,0:T(8,128)(2,1)S(1)}, u32[]{:S(2)}, u32[]{:S(2)}) collective-permute-start(bf16[16,16,128]{2,1,0:T(8,128)(2,1)S(1)} %get-tuple-element.56), channel_id=1, source_target_pairs={{0,24},{4,28},{8,0},{12,4},{16,8},{20,12},{24,16},{28,20},{1,25},{... | collective-permute-start | bytes 196616 | tf_op jit(solution)/shard_map/ppermute | solution.py:32
  79.1 1.1 collective-permute-done.12.g0
  80.2 0.0 collective-permute-done.13.g1
  80.2 0.0 collective-permute-done.14.g2
  80.2 1.2 collective-permute-done.15.g3
  81.4 7.7 %adjoint.1 = (f32[64,16,128]{2,1,0:T(8,128)S(1)}, bf16[16,16,128]{2,1,0:T(8,128)(2,1)S(1)}, bf16[16,16,128]{2,1,0:T(8,128)(2,1)S(1)}, bf16[16,16,128]{2,1,0:T(8,128)(2,1)S(1)}, bf16[16,16,128]{2,1,0:T(8,128)(2,1)S(1)}) custom-call(s32[128,4]{1,0:T(8,128)S(1)} %copy.22.cols_ref, s32[1,4,16]{2,1,0:T(4,128)S(1)} %copy-done.2, ...), custom_call_target="tpu_custom_call" | custom-call | bytes 1048576 | tf_op jit(solution)/shard_map/adjoint/pallas_call | solution.py:445
  89.1 0.0 copy-start.5
  89.1 2.0 %collective-permute-start.16 = (bf16[16,16,128]{2,1,0:T(8,128)(2,1)S(1)}, bf16[16,16,128]{2,1,0:T(8,128)(2,1)S(1)}, u32[]{:S(2)}, u32[]{:S(2)}) collective-permute-start(bf16[16,16,128]{2,1,0:T(8,128)(2,1)S(1)} %get-tuple-element.58), channel_id=1, source_target_pairs={{0,8},{4,12},{8,16},{12,20},{16,24},{20,28},{24,0},{28,4},{1,9},{5... | collective-permute-start | bytes 196616 | tf_op jit(solution)/shard_map/ppermute | solution.py:32
  91.1 0.0 collective-permute-start.17
  91.1 2.6 %collective-permute-start.18 = (bf16[16,16,128]{2,1,0:T(8,128)(2,1)S(1)}, bf16[16,16,128]{2,1,0:T(8,128)(2,1)S(1)}, u32[]{:S(2)}, u32[]{:S(2)}) collective-permute-start(bf16[16,16,128]{2,1,0:T(8,128)(2,1)S(1)} %get-tuple-element.60), channel_id=1, source_target_pairs={{0,28},{4,0},{8,4},{12,8},{16,12},{20,16},{24,20},{28,24},{1,29},{... | collective-permute-start | bytes 196616 | tf_op jit(solution)/shard_map/ppermute | solution.py:32
  93.8 0.1 collective-permute-start.19
  93.8 0.5 collective-permute-done.16.g0
  94.3 1.8 %collective-permute-done.17.g1 = bf16[16,16,128]{2,1,0:T(8,128)(2,1)S(1)} collective-permute-done((bf16[16,16,128]{2,1,0:T(8,128)(2,1)S(1)}, bf16[16,16,128]{2,1,0:T(8,128)(2,1)S(1)}, u32[]{:S(2)}, u32[]{:S(2)}) %collective-permute-start.17) | collective-permute-done | bytes 65568 | tf_op jit(solution)/shard_map/ppermute | solution.py:32
  96.1 0.0 collective-permute-done.18.g2
  96.1 1.9 %collective-permute-done.19.g3 = bf16[16,16,128]{2,1,0:T(8,128)(2,1)S(1)} collective-permute-done((bf16[16,16,128]{2,1,0:T(8,128)(2,1)S(1)}, bf16[16,16,128]{2,1,0:T(8,128)(2,1)S(1)}, u32[]{:S(2)}, u32[]{:S(2)}) %collective-permute-start.19) | collective-permute-done | bytes 65568 | tf_op jit(solution)/shard_map/ppermute | solution.py:32
  98.0 0.0 copy-done
  98.0 8.8 %last.1 = bf16[8,16,128]{2,1,0:T(8,128)(2,1)S(1)} custom-call(s32[128,4]{1,0:T(8,128)S(1)} %copy.22.cols_ref, s32[1,4,16]{2,1,0:T(4,128)S(1)} %copy-done.2, f32[64,16,128]{2,1,0:T(8,128)S(1)} %get-tuple-element.57.base_in_ref, f32[64,16,128]{2,1,0:T(8,128)S(1)} %get-tuple-element.52.target_ref, bf16[16,16,128]{2,1,0:T(8,128)(2,1)S(1)} %collective-permute-done.16.g0, ...), custom_call_target="tpu_custom_call" | custom-call | bytes 1048576 | tf_op jit(solution)/shard_map/last/pallas_call | solution.py:449
  106.8 7.7 %all_to_all.10.terms_ref = bf16[8,16,128]{2,1,0:T(8,128)(2,1)S(1)} all-to-all(bf16[8,16,128]{2,1,0:T(8,128)(2,1)S(1)} %last.1), channel_id=1, replica_groups=mesh['dom'=8,'pert'=4] {'dom'}, dimensions={0} | all-to-all | bytes 65536 | tf_op jit(solution)/shard_map/all_to_all | solution.py:456
  114.5 0.6 owner.1
  115.1 11.1 %all-gather = f32[4,1,128]{2,1,0:T(1,128)S(1)} all-gather(f32[1,1,128]{2,1,0:T(1,128)S(1)} %slice_bitcast_fusion), channel_id=1, replica_groups=mesh['dom'=8,'pert'=4] {'pert'}, dimensions={0}, use_global_device_ids=true | all-gather | bytes 2560 | tf_op jit(solution)/shard_map/all_gather | solution.py:461
  126.2 0.5 broadcast_multiply_fusion
  (12 shorter events, 0.0 us)
Async XLA Ops:
  2.0 26.2 %all-to-all-start = ((f32[8,16,128]{2,1,0:T(8,128)}), f32[8,16,128]{2,1,0:T(8,128)S(1)}, u32[]{:S(2)}, u32[]{:S(2)}) async-start(f32[8,16,128]{2,1,0:T(8,128)} %broadcast_in_dim.2), calls=%async_computation | async-start | bytes 131072 | tf_op jit(solution)/shard_map/all_to_all | solution.py:411
  11.1 0.7 copy-start.1
  11.8 0.8 copy-start.3
  12.5 0.7 copy-start.6
  15.9 12.2 %collective-permute-start = (f32[24,128]{1,0:T(8,128)S(1)}, f32[24,128]{1,0:T(8,128)S(1)}, u32[]{:S(2)}, u32[]{:S(2)}) collective-permute-start(f32[24,128]{1,0:T(8,128)S(1)} %get-tuple-element.35), channel_id=1, source_target_pairs={{0,24},{4,28},{8,0},{12,4},{16,8},{20,12},{24,16},{28,20},{1,25},{... | collective-permute-start | bytes 36872 | tf_op jit(solution)/shard_map/ppermute | solution.py:32
  18.9 9.2 %collective-permute-start.1 = (f32[24,128]{1,0:T(8,128)S(1)}, f32[24,128]{1,0:T(8,128)S(1)}, u32[]{:S(2)}, u32[]{:S(2)}) collective-permute-start(f32[24,128]{1,0:T(8,128)S(1)} %get-tuple-element.36), channel_id=1, source_target_pairs={{0,28},{4,0},{8,4},{12,8},{16,12},{20,16},{24,20},{28,24},{1,29},{... | collective-permute-start | bytes 36872 | tf_op jit(solution)/shard_map/ppermute | solution.py:32
  18.9 9.2 %collective-permute-start.2 = (f32[24,128]{1,0:T(8,128)S(1)}, f32[24,128]{1,0:T(8,128)S(1)}, u32[]{:S(2)}, u32[]{:S(2)}) collective-permute-start(f32[24,128]{1,0:T(8,128)S(1)} %get-tuple-element.37), channel_id=1, source_target_pairs={{0,4},{4,8},{8,12},{12,16},{16,20},{20,24},{24,28},{28,0},{1,5},{5... | collective-permute-start | bytes 36872 | tf_op jit(solution)/shard_map/ppermute | solution.py:32
  19.4 8.6 %copy-start.8 = (s32[128,4]{0,1:T(4,128)S(1)}, s32[128,4]{0,1:T(4,128)}, u32[]{:S(2)}) copy-start(s32[128,4]{0,1:T(4,128)} %param.13) | copy-start | bytes 6148
  19.4 8.7 %copy-start.2 = (s32[1,4,16]{2,1,0:T(4,128)S(1)}, s32[1,4,16]{2,1,0:T(4,128)}, u32[]{:S(2)}) copy-start(s32[1,4,16]{2,1,0:T(4,128)} %send_ref.9) | copy-start | bytes 772
  19.4 8.7 %copy-start.7 = (s32[128]{0:T(128)S(1)}, s32[128]{0:T(128)}, u32[]{:S(2)}) copy-start(s32[128]{0:T(128)} %param.15) | copy-start | bytes 1540
  19.4 8.7 %collective-permute-start.3 = (f32[24,128]{1,0:T(8,128)S(1)}, f32[24,128]{1,0:T(8,128)S(1)}, u32[]{:S(2)}, u32[]{:S(2)}) collective-permute-start(f32[24,128]{1,0:T(8,128)S(1)} %get-tuple-element.38), channel_id=1, source_target_pairs={{0,8},{4,12},{8,16},{12,20},{16,24},{20,28},{24,0},{28,4},{1,9},{5... | collective-permute-start | bytes 36872 | tf_op jit(solution)/shard_map/ppermute | solution.py:32
  28.1 33.3 %copy-start.4 = (f32[8192]{0:T(1024)S(1)}, f32[8192]{0:T(1024)}, u32[]{:S(2)}) copy-start(f32[8192]{0:T(1024)} %param.10) | copy-start | bytes 98308
  38.0 4.4 %collective-permute-start.4 = (bf16[16,16,128]{2,1,0:T(8,128)(2,1)S(1)}, bf16[16,16,128]{2,1,0:T(8,128)(2,1)S(1)}, u32[]{:S(2)}, u32[]{:S(2)}) collective-permute-start(bf16[16,16,128]{2,1,0:T(8,128)(2,1)S(1)} %get-tuple-element.41), channel_id=1, source_target_pairs={{0,24},{4,28},{8,0},{12,4},{16,8},{20,12},{24,16},{28,20},{1,25},{... | collective-permute-start | bytes 196616 | tf_op jit(solution)/shard_map/ppermute | solution.py:32
  39.9 3.3 %collective-permute-start.5 = (bf16[16,16,128]{2,1,0:T(8,128)(2,1)S(1)}, bf16[16,16,128]{2,1,0:T(8,128)(2,1)S(1)}, u32[]{:S(2)}, u32[]{:S(2)}) collective-permute-start(bf16[16,16,128]{2,1,0:T(8,128)(2,1)S(1)} %get-tuple-element.42), channel_id=1, source_target_pairs={{0,28},{4,0},{8,4},{12,8},{16,12},{20,16},{24,20},{28,24},{1,29},{... | collective-permute-start | bytes 196616 | tf_op jit(solution)/shard_map/ppermute | solution.py:32
  40.7 4.7 %collective-permute-start.6 = (bf16[16,16,128]{2,1,0:T(8,128)(2,1)S(1)}, bf16[16,16,128]{2,1,0:T(8,128)(2,1)S(1)}, u32[]{:S(2)}, u32[]{:S(2)}) collective-permute-start(bf16[16,16,128]{2,1,0:T(8,128)(2,1)S(1)} %get-tuple-element.43), channel_id=1, source_target_pairs={{0,4},{4,8},{8,12},{12,16},{16,20},{20,24},{24,28},{28,0},{1,5},{5... | collective-permute-start | bytes 196616 | tf_op jit(solution)/shard_map/ppermute | solution.py:32
  40.7 5.6 %collective-permute-start.7 = (bf16[16,16,128]{2,1,0:T(8,128)(2,1)S(1)}, bf16[16,16,128]{2,1,0:T(8,128)(2,1)S(1)}, u32[]{:S(2)}, u32[]{:S(2)}) collective-permute-start(bf16[16,16,128]{2,1,0:T(8,128)(2,1)S(1)} %get-tuple-element.44), channel_id=1, source_target_pairs={{0,8},{4,12},{8,16},{12,20},{16,24},{20,28},{24,0},{28,4},{1,9},{5... | collective-permute-start | bytes 196616 | tf_op jit(solution)/shard_map/ppermute | solution.py:32
  53.1 4.3 %collective-permute-start.8 = (bf16[16,16,128]{2,1,0:T(8,128)(2,1)S(1)}, bf16[16,16,128]{2,1,0:T(8,128)(2,1)S(1)}, u32[]{:S(2)}, u32[]{:S(2)}) collective-permute-start(bf16[16,16,128]{2,1,0:T(8,128)(2,1)S(1)} %get-tuple-element.46), channel_id=1, source_target_pairs={{0,24},{4,28},{8,0},{12,4},{16,8},{20,12},{24,16},{28,20},{1,25},{... | collective-permute-start | bytes 196616 | tf_op jit(solution)/shard_map/ppermute | solution.py:32
  54.1 3.5 %collective-permute-start.9 = (bf16[16,16,128]{2,1,0:T(8,128)(2,1)S(1)}, bf16[16,16,128]{2,1,0:T(8,128)(2,1)S(1)}, u32[]{:S(2)}, u32[]{:S(2)}) collective-permute-start(bf16[16,16,128]{2,1,0:T(8,128)(2,1)S(1)} %get-tuple-element.47), channel_id=1, source_target_pairs={{0,28},{4,0},{8,4},{12,8},{16,12},{20,16},{24,20},{28,24},{1,29},{... | collective-permute-start | bytes 196616 | tf_op jit(solution)/shard_map/ppermute | solution.py:32
  55.6 4.7 %collective-permute-start.10 = (bf16[16,16,128]{2,1,0:T(8,128)(2,1)S(1)}, bf16[16,16,128]{2,1,0:T(8,128)(2,1)S(1)}, u32[]{:S(2)}, u32[]{:S(2)}) collective-permute-start(bf16[16,16,128]{2,1,0:T(8,128)(2,1)S(1)} %get-tuple-element.48), channel_id=1, source_target_pairs={{0,4},{4,8},{8,12},{12,16},{16,20},{20,24},{24,28},{28,0},{1,5},{5... | collective-permute-start | bytes 196616 | tf_op jit(solution)/shard_map/ppermute | solution.py:32
  55.6 5.8 %collective-permute-start.11 = (bf16[16,16,128]{2,1,0:T(8,128)(2,1)S(1)}, bf16[16,16,128]{2,1,0:T(8,128)(2,1)S(1)}, u32[]{:S(2)}, u32[]{:S(2)}) collective-permute-start(bf16[16,16,128]{2,1,0:T(8,128)(2,1)S(1)} %get-tuple-element.49), channel_id=1, source_target_pairs={{0,8},{4,12},{8,16},{12,20},{16,24},{20,28},{24,0},{28,4},{1,9},{5... | collective-permute-start | bytes 196616 | tf_op jit(solution)/shard_map/ppermute | solution.py:32
  74.4 23.6 %copy-start = (bf16[128,64,256]{2,1,0:T(8,128)(2,1)S(1)}, bf16[128,64,256]{2,1,0:T(8,128)(2,1)}, u32[]{:S(2)}) copy-start(bf16[128,64,256]{2,1,0:T(8,128)(2,1)} %product.1.m_ref) | copy-start | bytes 12582916
  74.4 5.7 %collective-permute-start.12 = (bf16[16,16,128]{2,1,0:T(8,128)(2,1)S(1)}, bf16[16,16,128]{2,1,0:T(8,128)(2,1)S(1)}, u32[]{:S(2)}, u32[]{:S(2)}) collective-permute-start(bf16[16,16,128]{2,1,0:T(8,128)(2,1)S(1)} %get-tuple-element.53), channel_id=1, source_target_pairs={{0,8},{4,12},{8,16},{12,20},{16,24},{20,28},{24,0},{28,4},{1,9},{5... | collective-permute-start | bytes 196616 | tf_op jit(solution)/shard_map/ppermute | solution.py:32
  74.4 5.7 %collective-permute-start.13 = (bf16[16,16,128]{2,1,0:T(8,128)(2,1)S(1)}, bf16[16,16,128]{2,1,0:T(8,128)(2,1)S(1)}, u32[]{:S(2)}, u32[]{:S(2)}) collective-permute-start(bf16[16,16,128]{2,1,0:T(8,128)(2,1)S(1)} %get-tuple-element.54), channel_id=1, source_target_pairs={{0,4},{4,8},{8,12},{12,16},{16,20},{20,24},{24,28},{28,0},{1,5},{5... | collective-permute-start | bytes 196616 | tf_op jit(solution)/shard_map/ppermute | solution.py:32
  74.6 5.6 %collective-permute-start.14 = (bf16[16,16,128]{2,1,0:T(8,128)(2,1)S(1)}, bf16[16,16,128]{2,1,0:T(8,128)(2,1)S(1)}, u32[]{:S(2)}, u32[]{:S(2)}) collective-permute-start(bf16[16,16,128]{2,1,0:T(8,128)(2,1)S(1)} %get-tuple-element.55), channel_id=1, source_target_pairs={{0,28},{4,0},{8,4},{12,8},{16,12},{20,16},{24,20},{28,24},{1,29},{... | collective-permute-start | bytes 196616 | tf_op jit(solution)/shard_map/ppermute | solution.py:32
  77.1 4.3 %collective-permute-start.15 = (bf16[16,16,128]{2,1,0:T(8,128)(2,1)S(1)}, bf16[16,16,128]{2,1,0:T(8,128)(2,1)S(1)}, u32[]{:S(2)}, u32[]{:S(2)}) collective-permute-start(bf16[16,16,128]{2,1,0:T(8,128)(2,1)S(1)} %get-tuple-element.56), channel_id=1, source_target_pairs={{0,24},{4,28},{8,0},{12,4},{16,8},{20,12},{24,16},{28,20},{1,25},{... | collective-permute-start | bytes 196616 | tf_op jit(solution)/shard_map/ppermute | solution.py:32
  89.1 25.4 %copy-start.5 = (f32[16,128]{1,0:T(8,128)S(1)}, f32[16,128]{1,0:T(8,128)}, u32[]{:S(2)}) copy-start(f32[16,128]{1,0:T(8,128)} %probe_ref.1) | copy-start | bytes 24580
  89.1 5.2 %collective-permute-start.16 = (bf16[16,16,128]{2,1,0:T(8,128)(2,1)S(1)}, bf16[16,16,128]{2,1,0:T(8,128)(2,1)S(1)}, u32[]{:S(2)}, u32[]{:S(2)}) collective-permute-start(bf16[16,16,128]{2,1,0:T(8,128)(2,1)S(1)} %get-tuple-element.58), channel_id=1, source_target_pairs={{0,8},{4,12},{8,16},{12,20},{16,24},{20,28},{24,0},{28,4},{1,9},{5... | collective-permute-start | bytes 196616 | tf_op jit(solution)/shard_map/ppermute | solution.py:32
  91.1 5.0 %collective-permute-start.17 = (bf16[16,16,128]{2,1,0:T(8,128)(2,1)S(1)}, bf16[16,16,128]{2,1,0:T(8,128)(2,1)S(1)}, u32[]{:S(2)}, u32[]{:S(2)}) collective-permute-start(bf16[16,16,128]{2,1,0:T(8,128)(2,1)S(1)} %get-tuple-element.59), channel_id=1, source_target_pairs={{0,4},{4,8},{8,12},{12,16},{16,20},{20,24},{24,28},{28,0},{1,5},{5... | collective-permute-start | bytes 196616 | tf_op jit(solution)/shard_map/ppermute | solution.py:32
  91.1 5.0 %collective-permute-start.18 = (bf16[16,16,128]{2,1,0:T(8,128)(2,1)S(1)}, bf16[16,16,128]{2,1,0:T(8,128)(2,1)S(1)}, u32[]{:S(2)}, u32[]{:S(2)}) collective-permute-start(bf16[16,16,128]{2,1,0:T(8,128)(2,1)S(1)} %get-tuple-element.60), channel_id=1, source_target_pairs={{0,28},{4,0},{8,4},{12,8},{16,12},{20,16},{24,20},{28,24},{1,29},{... | collective-permute-start | bytes 196616 | tf_op jit(solution)/shard_map/ppermute | solution.py:32
  93.8 4.3 %collective-permute-start.19 = (bf16[16,16,128]{2,1,0:T(8,128)(2,1)S(1)}, bf16[16,16,128]{2,1,0:T(8,128)(2,1)S(1)}, u32[]{:S(2)}, u32[]{:S(2)}) collective-permute-start(bf16[16,16,128]{2,1,0:T(8,128)(2,1)S(1)} %get-tuple-element.61), channel_id=1, source_target_pairs={{0,24},{4,28},{8,0},{12,4},{16,8},{20,12},{24,16},{28,20},{1,25},{... | collective-permute-start | bytes 196616 | tf_op jit(solution)/shard_map/ppermute | solution.py:32
where the time goes:
time: 127 us
  Pallas kernels  57 us (45%)
  starting transfers between devices  25.8 us (20%)
  blocking collectives  18.8 us (15%)
  waiting for transfers between devices  16.3 us (13%)
  local copies, waits for them, and re-layouts  7.5 us (6%)
    ppermute x20, starting transfers between devices, rotated(): lax.ppermute(value, 'dom', [(i, (i + by) % peers) for i in range(peers)])  20.7 us
    ppermute x20, waiting for transfers between devices, rotated(): lax.ppermute(value, 'dom', [(i, (i + by) % peers) for i in range(peers)])  16.3 us
    pallas_call x1, Pallas kernels, shards(): call(turn_kernel, [shape((pert, blocks * HALF), F32), pair_array, pair_ar...  13 us
    all_gather x1, blocking collectives, shards(): curvature = jnp.sum(lax.all_gather(curve[0], 'pert', axis=0), axis=0)  11.1 us
    pallas_call x1, Pallas kernels, shards(): call(first_kernel, [shape((parts * probes.shape[1], 2 * LANES), BF16), pa...  9.85 us
    pallas_call x1, Pallas kernels, shards(): call(last_kernel, shape((parts, pert, LANES), BF16), 'ssvvvvvvvvvvvvv', [...  8.77 us
    all_to_all x1, blocking collectives, shards(): terms = lax.all_to_all(terms, 'dom', 0, 0, tiled=True)  7.71 us
    pallas_call x1, Pallas kernels, shards(): call(adjoint_kernel, [pair_array] + msgs, 'ssvvvvvvv', [held] + accs, nam...  7.7 us
  transfers between devices with their start and end apart: 21, of which 13 were waited for; matrix products, arithmetic and copies ran while one was open for 3% of the time, Pallas kernels for 8%

commit v1 on v0

v1 whole, which is shorter than its diff:
```python
import functools

import jax
import jax.numpy as jnp
from jax import lax
from jax.experimental import pallas as pl
from jax.experimental.pallas import tpu as pltpu
from jax.sharding import PartitionSpec as P

OFFSET_LIST = (-2, -1, 1, 2)
F32 = jnp.float32
BF16 = jnp.bfloat16
LANES = 128
HALF = 64
QUAD = 4

VMEM = pl.BlockSpec(memory_space=pltpu.VMEM)
SMEM = pl.BlockSpec(memory_space=pltpu.SMEM)
PARAMS = pltpu.CompilerParams(vmem_limit_bytes=16 * 1024 * 1024)


def low_half(shape):
    return lax.broadcasted_iota(jnp.int32, shape, len(shape) - 1) < HALF


def swap_halves(value):
    return pltpu.roll(value, HALF, 1)


def rotated(value, by):
    peers = lax.axis_size("dom")
    return lax.ppermute(value, "dom", [(i, (i + by) % peers) for i in range(peers)])


def neighbours(parts):
    me = lax.axis_index("dom")
    return [lax.rem(me - offset + parts, parts) for offset in OFFSET_LIST]


def melt_kernel(send_ref, melt_ref, patch_ref, probe_ref, diag_ref, w_ref, out_ref, *, parts):
    pairs = melt_ref.shape[0]
    pert = probe_ref.shape[0]
    capacity = send_ref.shape[2]
    low = low_half((1, LANES))
    lane = lax.broadcasted_iota(jnp.int32, (HALF, LANES), 1)
    turned = jnp.transpose(jnp.concatenate([melt_ref[...], jnp.zeros((LANES - pairs, LANES), F32)], axis=0))
    even = jnp.take_along_axis(turned[:HALF], lane // 2, axis=1)
    odd = jnp.take_along_axis(turned[HALF:], lane // 2, axis=1)
    melt = jnp.where(lane % 2 == 0, even, odd)
    sums = [
        jnp.sum(diag_ref[i].astype(F32) * melt, axis=0, keepdims=True)
        for i in range(diag_ref.shape[0])
    ]
    sums = jnp.concatenate(sums, axis=0)
    source = 2 * (lane % HALF)
    both = jnp.concatenate(
        [
            jnp.take_along_axis(sums, source, axis=1),
            jnp.take_along_axis(sums, source + 1, axis=1),
        ],
        axis=0,
    )
    w_ref[...] = jnp.transpose(both)[:pairs]
    patch_row = jnp.broadcast_to(patch_ref[...].astype(F32), (8, LANES))
    lane = lax.broadcasted_iota(jnp.int32, (8, LANES), 1)
    for part in range(parts):
        out_ref[part, :pert] = probe_ref[...]
    me = lax.axis_index("dom")
    for group, offset in enumerate(OFFSET_LIST):
        to = lax.rem(me + offset + parts, parts)
        ids = jnp.zeros((8, LANES), jnp.int32)
        for slot in range(capacity):
            block = jnp.maximum(send_ref[0, group, slot], 0)
            row = w_ref[pl.ds(block // 2, 1), :]
            out_ref[to, pert + slot : pert + slot + 1, :] = jnp.where(
                low == (block % 2 == 0), row, swap_halves(row)
            )
            ids = jnp.where(lane == group * capacity + slot, block, ids)
        mine = (lane >= group * capacity) & (lane < (group + 1) * capacity)
        out_ref[to, pert + capacity :, :] = jnp.where(
            mine, jnp.take_along_axis(patch_row, ids, axis=1), 0.0
        )


def product_kernel(diag_ref, coupling_ref, m_ref):
    def one(block, _):
        m_ref[block] = jnp.dot(
            diag_ref[block], coupling_ref[block], preferred_element_type=F32
        ).astype(BF16)
        return 0

    lax.fori_loop(0, diag_ref.shape[0], one, 0, unroll=32)


def gather_multiply(quad, cols_ref, ext_ref, m_ref, low):
    rows = []
    for place in range(QUAD):
        g = quad * QUAD + place
        tiles = [ext_ref[cols_ref[k, g]] for k in range(4)]
        rows.append(
            jnp.concatenate(
                [jnp.where(low, tiles[0], tiles[1]), jnp.where(low, tiles[2], tiles[3])], axis=1
            )
        )
    lhs = jnp.concatenate(rows, axis=0)
    rhs = m_ref[pl.ds(quad * QUAD, QUAD)].reshape(QUAD * HALF, 4 * HALF)
    out = lax.dot_general(lhs, rhs, (((1,), (1,)), ((), ())), preferred_element_type=F32)
    p = out.shape[0] // QUAD
    first = jnp.where(low, out[:p, :LANES], out[p : 2 * p, :LANES])
    second = jnp.where(low, out[2 * p : 3 * p, LANES:], out[3 * p :, LANES:])
    return first, second


def store_pair(ref, pair, value, low):
    value = value.astype(BF16)
    other = swap_halves(value.astype(F32)).astype(BF16)
    ref[2 * pair] = jnp.where(low, value, other)
    ref[2 * pair + 1] = jnp.where(low, other, value)


def fill_messages(send_ref, ref, msg_refs, low):
    for group, msg_ref in enumerate(msg_refs):
        for pair in range(msg_ref.shape[0]):
            even, odd = (
                ref[jnp.maximum(send_ref[0, group, 2 * pair + half], 0)] for half in range(2)
            )
            msg_ref[pair] = jnp.where(low, even, odd)


def first_kernel(
    cols_ref, send_ref, patch_ref, got_ref, w_ref, m_ref,
    one_hot_ref, t1_ref, t2_ref, o0, o1, o2, o3, ext_ref,
):
    pert = t1_ref.shape[1]
    capacity = send_ref.shape[2]
    blocks = cols_ref.shape[1]
    parts = got_ref.shape[0]
    sources = neighbours(parts)
    low = low_half((pert, LANES))
    lane = lax.broadcasted_iota(jnp.int32, (1, LANES), 1)
    ghost_ids = sum(got_ref[source, pert + capacity : pert + capacity + 1, :] for source in sources)
    ghost_ids = jnp.where(lane < 4 * capacity, ghost_ids, -1.0)
    ids = jnp.concatenate([patch_ref[...].astype(F32), ghost_ids], axis=1)
    total = jnp.zeros((3 * pert, 2 * LANES), F32)
    for part in range(parts):
        names = (
            lax.broadcasted_iota(jnp.int32, (LANES, 2 * LANES), 0) + part * LANES
        ).astype(F32)
        hot = jnp.where(names == ids, 1.0, 0.0).astype(BF16)
        one_hot_ref[part * LANES : (part + 1) * LANES, :] = hot
        value = got_ref[part, :pert]
        top = value.astype(BF16)
        rest = value - top.astype(F32)
        mid = rest.astype(BF16)
        last = (rest - mid.astype(F32)).astype(BF16)
        total = total + jnp.dot(
            jnp.concatenate([top, mid, last], axis=0), hot, preferred_element_type=F32
        )
    picked = total[:pert] + total[pert : 2 * pert] + total[2 * pert :]
    local_picked = picked[:, :LANES]
    ghost_picked = picked[:, LANES:]
    full_low = low.astype(jnp.int32)

    def seed(pair, _):
        index = 2 * pair + 1 - full_low
        spread = jnp.take_along_axis(local_picked, index, axis=1)
        value = spread * w_ref[pl.ds(pair, 1), :]
        t1_ref[pair] = value
        store_pair(ext_ref, pair, value, low)
        return 0

    lax.fori_loop(0, blocks // 2, seed, 0, unroll=16)
    for group, source in enumerate(sources):
        for slot in range(capacity):
            place = group * capacity + slot
            row = got_ref[source, pert + slot : pert + slot + 1, :]
            spread = jnp.broadcast_to(ghost_picked[:, place : place + 1], (pert, LANES))
            ext_ref[blocks + place] = (spread * row).astype(BF16)

    def sweep(quad, _):
        first, second = gather_multiply(quad, cols_ref, ext_ref, m_ref, low)
        store_pair(t2_ref, 2 * quad, t1_ref[2 * quad] - first, low)
        store_pair(t2_ref, 2 * quad + 1, t1_ref[2 * quad + 1] - second, low)
        return 0

    lax.fori_loop(0, blocks // QUAD, sweep, 0, unroll=32)
    fill_messages(send_ref, t2_ref, (o0, o1, o2, o3), low)


def extend(ext_ref, local_ref, ghosts, low):
    blocks = local_ref.shape[0]
    count = ghosts[0].shape[0]
    ext_ref[:blocks] = local_ref[...]
    for group, ref in enumerate(ghosts):
        for pair in range(count):
            store_pair(ext_ref, blocks // 2 + group * count + pair, ref[pair], low)


def sweep_kernel(
    cols_ref, send_ref, t1_ref, prev_ref, g0, g1, g2, g3, m_ref,
    next_ref, o0, o1, o2, o3, ext_ref,
):
    low = low_half(prev_ref.shape[1:])
    extend(ext_ref, prev_ref, (g0, g1, g2, g3), low)

    def sweep(quad, _):
        first, second = gather_multiply(quad, cols_ref, ext_ref, m_ref, low)
        store_pair(next_ref, 2 * quad, t1_ref[2 * quad] - first, low)
        store_pair(next_ref, 2 * quad + 1, t1_ref[2 * quad + 1] - second, low)
        return 0

    lax.fori_loop(0, cols_ref.shape[1] // QUAD, sweep, 0, unroll=32)
    fill_messages(send_ref, next_ref, (o0, o1, o2, o3), low)


def clear(acc_refs):
    def one(place, _):
        for ref in acc_refs:
            ref[place] = jnp.zeros(ref.shape[1:], F32)
        return 0

    lax.fori_loop(0, acc_refs[0].shape[0], one, 0, unroll=16)


def multiply_scatter(quad, cols_ref, pairs, m_ref, acc_refs, low):
    zero = jnp.zeros(pairs[0].shape, F32)
    rows = []
    for place in range(QUAD):
        value = pairs[place // 2]
        kept = jnp.where(low, value, zero) if place % 2 == 0 else jnp.where(low, zero, value)
        tiles = [kept, zero] if place < 2 else [zero, kept]
        rows.append(jnp.concatenate(tiles, axis=1))
    lhs = jnp.concatenate(rows, axis=0).astype(BF16)
    rhs = m_ref[pl.ds(quad * QUAD, QUAD)].reshape(QUAD * HALF, 4 * HALF)
    out = jnp.dot(lhs, rhs, preferred_element_type=F32)
    p = pairs[0].shape[0]
    for place in range(QUAD):
        g = quad * QUAD + place
        for k in range(4):
            column = cols_ref[k, g]
            piece = out[place * p : (place + 1) * p, (k // 2) * LANES : (k // 2 + 1) * LANES]
            acc_refs[k][column] = acc_refs[k][column] + piece


def half_sums(acc_refs, place, low):
    return jnp.where(
        low, acc_refs[0][place] + acc_refs[2][place], acc_refs[1][place] + acc_refs[3][place]
    )


def pair_sum(acc_refs, pair, low):
    even = half_sums(acc_refs, 2 * pair, low)
    odd = half_sums(acc_refs, 2 * pair + 1, low)
    return jnp.where(low, even, odd) + swap_halves(jnp.where(low, odd, even))


def finish_round(base_ref, target_ref, acc_refs, msg_refs, blocks, low):
    def local(pair, _):
        base_ref[pair] = target_ref[pair] - pair_sum(acc_refs, pair, low)
        return 0

    lax.fori_loop(0, blocks // 2, local, 0, unroll=16)
    for group, ref in enumerate(msg_refs):
        count = ref.shape[0]
        for pair in range(count):
            ref[pair] = pair_sum(acc_refs, blocks // 2 + group * count + pair, low).astype(BF16)


def turn_kernel(
    cols_ref, t1_ref, prev_ref, g0, g1, g2, g3, m_ref, weight_ref,
    tangent_ref, target_ref, base_ref, o0, o1, o2, o3, ext_ref, *acc_refs,
):
    low = low_half(prev_ref.shape[1:])
    blocks = cols_ref.shape[1]
    extend(ext_ref, prev_ref, (g0, g1, g2, g3), low)
    clear(acc_refs)

    def sweep(quad, _):
        coupled = gather_multiply(quad, cols_ref, ext_ref, m_ref, low)
        pairs = []
        for place in range(2):
            pair = 2 * quad + place
            value = t1_ref[pair] - coupled[place]
            start = pl.multiple_of(pair * LANES, LANES)
            tangent_ref[:, pl.ds(start, LANES)] = value
            target = value * weight_ref[pl.ds(pair, 1), :]
            target_ref[pair] = target
            pairs.append(target)
        multiply_scatter(quad, cols_ref, pairs, m_ref, acc_refs, low)
        return 0

    lax.fori_loop(0, blocks // QUAD, sweep, 0, unroll=32)
    finish_round(base_ref, target_ref, acc_refs, (o0, o1, o2, o3), blocks, low)


def take_returned(send_ref, base_ref, u_ref, ghosts, low):
    u_ref[...] = base_ref[...]
    which = 1 - low.astype(jnp.int32)
    for group, ref in enumerate(ghosts):
        for pair in range(ref.shape[0]):
            value = ref[pair].astype(F32)
            other = swap_halves(value)
            for half, both in enumerate(
                (jnp.where(low, value, other), jnp.where(low, other, value))
            ):
                block = send_ref[0, group, 2 * pair + half]
                place = jnp.maximum(block, 0) // 2
                wanted = jnp.where(block < 0, 2, block % 2)
                u_ref[place] = u_ref[place] - jnp.where(which == wanted, both, 0.0)


def scatter_all(cols_ref, u_ref, m_ref, acc_refs, low):
    clear(acc_refs)

    def sweep(quad, _):
        pairs = [u_ref[2 * quad], u_ref[2 * quad + 1]]
        multiply_scatter(quad, cols_ref, pairs, m_ref, acc_refs, low)
        return 0

    lax.fori_loop(0, cols_ref.shape[1] // QUAD, sweep, 0, unroll=32)


def adjoint_kernel(
    cols_ref, send_ref, base_in_ref, target_ref, g0, g1, g2, g3, m_ref,
    base_ref, o0, o1, o2, o3, u_ref, *acc_refs,
):
    low = low_half(u_ref.shape[1:])
    take_returned(send_ref, base_in_ref, u_ref, (g0, g1, g2, g3), low)
    scatter_all(cols_ref, u_ref, m_ref, acc_refs, low)
    finish_round(base_ref, target_ref, acc_refs, (o0, o1, o2, o3), cols_ref.shape[1], low)


def last_kernel(
    cols_ref, send_ref, base_in_ref, target_ref, g0, g1, g2, g3, m_ref, w_ref, got_ref,
    one_hot_ref, out_ref, u_ref, *acc_refs,
):
    pert = u_ref.shape[1]
    blocks = cols_ref.shape[1]
    low = low_half(u_ref.shape[1:])
    lane = lax.broadcasted_iota(jnp.int32, (pert, LANES), 1)
    take_returned(send_ref, base_in_ref, u_ref, (g0, g1, g2, g3), low)
    scatter_all(cols_ref, u_ref, m_ref, acc_refs, low)

    def local(pair, terms):
        value = (target_ref[pair] - pair_sum(acc_refs, pair, low)) * w_ref[pl.ds(pair, 1), :]
        even = jnp.sum(jnp.where(low, value, 0.0), axis=1, keepdims=True)
        odd = jnp.sum(jnp.where(low, 0.0, value), axis=1, keepdims=True)
        return jnp.where(lane == 2 * pair, even, jnp.where(lane == 2 * pair + 1, odd, terms))

    local_terms = lax.fori_loop(
        0, blocks // 2, local, jnp.zeros((pert, LANES), F32), unroll=4
    )
    ghost_terms = jnp.zeros((pert, LANES), F32)
    parts = got_ref.shape[0]
    capacity = send_ref.shape[2]
    for group, source in enumerate(neighbours(parts)):
        for slot in range(capacity):
            place = group * capacity + slot
            row = got_ref[source, pert + slot : pert + slot + 1, :]
            value = half_sums(acc_refs, blocks + place, low) * row
            ghost_terms = jnp.where(
                lane == place, -jnp.sum(value, axis=1, keepdims=True), ghost_terms
            )
    terms = jnp.concatenate([local_terms, ghost_terms], axis=1)
    top = terms.astype(BF16)
    rest = (terms - top.astype(F32)).astype(BF16)
    both = jnp.concatenate([top, rest], axis=0)
    perts = out_ref.shape[0] // parts
    sub = lax.broadcasted_iota(jnp.int32, (8, LANES), 0)
    for part in range(parts):
        hot = one_hot_ref[part * LANES : (part + 1) * LANES, :]
        out = lax.dot_general(both, hot, (((1,), (1,)), ((), ())), preferred_element_type=F32)
        value = out[:pert] + out[pert:]
        curve = jnp.sum(value * got_ref[part, :pert], axis=0, keepdims=True)
        top = curve.astype(BF16).astype(F32)
        extra = jnp.where(sub == 0, top, jnp.where(sub == 1, curve - top, 0.0))
        for place in range(perts):
            out_ref[part * perts + place, :pert] = value.astype(BF16)
            out_ref[part * perts + place, pert:] = extra.astype(BF16)


def owner_kernel(terms_ref, hessian_ref, curve_ref, *, parts, scale):
    pert = hessian_ref.shape[0]
    perts = terms_ref.shape[0] // parts
    mine = lax.axis_index("pert")
    total = jnp.zeros(hessian_ref.shape, F32)
    for part in range(parts):
        total = total + terms_ref[part * perts + mine, :pert].astype(F32)
    hessian_ref[...] = total
    curve = jnp.zeros((8, LANES), F32)
    for place in range(terms_ref.shape[0]):
        curve = curve + terms_ref[place, pert:].astype(F32)
    curve_ref[...] = (curve[0:1] + curve[1:2]) * scale


def call(body, outs, spaces, scratch=(), name=None, flops=0, moved=1 << 20):
    return pl.pallas_call(
        body,
        out_shape=outs,
        in_specs=[SMEM if s == "s" else VMEM for s in spaces],
        out_specs=jax.tree.map(lambda _: VMEM, outs),
        scratch_shapes=list(scratch),
        compiler_params=PARAMS,
        name=name,
        cost_estimate=pl.CostEstimate(flops=flops, transcendentals=0, bytes_accessed=moved),
    )


def shards(
    probes, melt_shape, obs_weight, diag_inverse, coupling, columns, send_list, patch_of_block
):
    pert = probes.shape[0]
    blocks = coupling.shape[0]
    capacity = send_list.shape[2]
    parts = lax.axis_size("dom")
    pairs = blocks // 2
    shape = jax.ShapeDtypeStruct
    msgs = [shape((capacity // 2, pert, LANES), BF16)] * 4
    pair_array = shape((pairs, pert, LANES), F32)
    block_array = shape((blocks, pert, LANES), BF16)
    ext = pltpu.VMEM((blocks + 4 * capacity, pert, LANES), BF16)
    accs = [pltpu.VMEM((blocks + 4 * capacity, pert, LANES), F32)] * 4
    held = pltpu.VMEM((pairs, pert, LANES), F32)
    melt = melt_shape.reshape(pairs, LANES)
    weight = obs_weight.reshape(pairs, LANES)
    patch = patch_of_block.reshape(1, blocks)

    perts = lax.axis_size("pert")
    columns = columns.T
    w, outgoing = call(
        functools.partial(melt_kernel, parts=parts),
        [shape((pairs, LANES), F32), shape((parts, pert + capacity + 8, LANES), F32)],
        "svvvv",
        name="melt",
    )(send_list, melt, patch, probes, jnp.transpose(diag_inverse, (1, 2, 0)))
    got = lax.all_to_all(outgoing, "dom", 0, 0, tiled=True)
    m = call(
        product_kernel, shape(coupling.shape, BF16), "vv", name="product", flops=1 << 28, moved=10 << 20
    )(diag_inverse, coupling)

    one_hot, t1, state, *out = call(
        first_kernel,
        [shape((parts * probes.shape[1], 2 * LANES), BF16), pair_array, block_array] + msgs,
        "ssvvvv",
        [ext],
        name="first",
    )(columns, send_list, patch, got, w, m)
    ghosts = [rotated(v, o) for v, o in zip(out, OFFSET_LIST)]
    state, *out = call(
        sweep_kernel, [block_array] + msgs, "ssvvvvvvv", [ext], name="sweep"
    )(columns, send_list, t1, state, *ghosts, m)
    ghosts = [rotated(v, o) for v, o in zip(out, OFFSET_LIST)]
    tangent, target, base, *out = call(
        turn_kernel,
        [shape((pert, blocks * HALF), F32), pair_array, pair_array] + msgs,
        "svvvvvvvv",
        [ext] + accs,
        name="turn",
    )(columns, t1, state, *ghosts, m, weight)
    ghosts = [rotated(v, -o) for v, o in zip(out, OFFSET_LIST)]
    base, *out = call(
        adjoint_kernel, [pair_array] + msgs, "ssvvvvvvv", [held] + accs, name="adjoint"
    )(columns, send_list, base, target, *ghosts, m)
    ghosts = [rotated(v, -o) for v, o in zip(out, OFFSET_LIST)]
    terms = call(
        last_kernel,
        shape((parts * perts, pert + 8, LANES), BF16),
        "ssvvvvvvvvvv",
        [held] + accs,
        name="last",
    )(columns, send_list, base, target, *ghosts, m, w, got, one_hot)
    terms = lax.all_to_all(terms, ("dom", "pert"), 0, 0, tiled=True)
    hessian_probe, curvature = call(
        functools.partial(owner_kernel, parts=parts, scale=1.0 / (pert * perts)),
        [shape(probes.shape, F32), shape((1, LANES), F32)],
        "v",
        name="owner",
    )(terms)
    return tangent, hessian_probe, curvature.reshape(-1)


def solution(mesh):
    in_specs = (
        P("pert", "dom"),
        P("dom"),
        P("dom"),
        P("dom", None, None),
        P("dom", None, None),
        P("dom", None),
        P("dom", None, None),
        P("dom"),
    )
    out_specs = (P("pert", "dom"), P("pert", "dom"), P("dom"))
    return jax.shard_map(shards, mesh=mesh, in_specs=in_specs, out_specs=out_specs, check_vma=False)
```

time: 127 us -> 92.6 us (0.73)
  Pallas kernels: 57 us -> 27.1 us
  local copies, waits for them, and re-layouts: 7.5 us -> 14.3 us
  blocking collectives: 18.8 us -> 13.8 us
  starting transfers between devices: 25.8 us -> 22.2 us
  waiting for transfers between devices: 16.3 us -> 14 us
    all_gather x1 -> x0, blocking collectives: 11.1 us -> none  [shards(): curvature = jnp.sum(lax.all_gather(curve[0], 'pert', axis=0), axis=0)]
    unnamed x21 -> x27, local copies, waits for them, and re-layouts: 6.16 us -> 14.3 us
    pallas_call x1, Pallas kernels: 9.85 us -> 3.65 us  [shards(): call(first_kernel, [shape((parts * probes.shape[1], 2 * LANES), BF16), pa...]
    all_to_all x1, blocking collectives: 7.71 us -> 13.8 us  [shards(): terms = lax.all_to_all(terms, ('dom', 'pert'), 0, 0, tiled=True)]
    pallas_call x1, Pallas kernels: 7.51 us -> 1.64 us  [shards(): call(product_kernel, shape(coupling.shape, BF16), 'vv', name='product', f...]
    pallas_call x1, Pallas kernels: 7.7 us -> 2.95 us  [shards(): call(adjoint_kernel, [pair_array] + msgs, 'ssvvvvvvv', [held] + accs, nam...]
    pallas_call x1, Pallas kernels: 6.84 us -> 2.2 us  [shards(): call(sweep_kernel, [block_array] + msgs, 'ssvvvvvvv', [ext], name='sweep')]
    pallas_call x1, Pallas kernels: 13 us -> 8.46 us  [shards(): call(turn_kernel, [shape((pert, blocks * HALF), F32), pair_array, pair_ar...]
  transfers between devices with their start and end apart: 21 -> 17, of which waited for: 13 -> 11; matrix products, arithmetic and copies ran while one was open for 3% -> 4% of each run, Pallas kernels for 8% -> 2%
where the time goes in v1:
time: 92.6 us; the launch traced here: 92.1 us
  Pallas kernels  27.1 us (29%)
  starting transfers between devices  22.2 us (24%)
  local copies, waits for them, and re-layouts  14.3 us (15%)
  waiting for transfers between devices  14 us (15%)
  blocking collectives  13.8 us (15%)
    ppermute x16, starting transfers between devices, rotated(): lax.ppermute(value, 'dom', [(i, (i + by) % peers) for i in range(peers)])  17 us
    unnamed x27, local copies, waits for them, and re-layouts  14.3 us
    ppermute x16, waiting for transfers between devices, rotated(): lax.ppermute(value, 'dom', [(i, (i + by) % peers) for i in range(peers)])  14 us
    all_to_all x1, blocking collectives, shards(): terms = lax.all_to_all(terms, ('dom', 'pert'), 0, 0, tiled=True)  13.8 us
    pallas_call x1, Pallas kernels, shards(): call(turn_kernel, [shape((pert, blocks * HALF), F32), pair_array, pair_ar...  8.46 us
    pallas_call x1, Pallas kernels, shards(): call(last_kernel, shape((parts * perts, pert + 8, LANES), BF16), 'ssvvvvv...  5.58 us
    all_to_all x1, starting transfers between devices, shards(): got = lax.all_to_all(outgoing, 'dom', 0, 0, tiled=True)  5.17 us
    pallas_call x1, Pallas kernels, shards(): call(first_kernel, [shape((parts * probes.shape[1], 2 * LANES), BF16), pa...  3.65 us
  transfers between devices with their start and end apart: 17, of which 11 were waited for; matrix products, arithmetic and copies ran while one was open for 4% of the time, Pallas kernels for 2%

profile of v1, /device:TPU:0, one launch (start us, length us, event | category | flops | bytes accessed | tf_op | source)
XLA Modules:
  0.0 92.1 jit_solution(13129361383207622885)
XLA Ops:
  0.6 0.0 copy-start.3
  0.6 1.2 %copy-done.3 = bf16[128,64,64]{0,2,1:T(8,128)(2,1)S(1)} copy-done((bf16[128,64,64]{0,2,1:T(8,128)(2,1)S(1)}, bf16[128,64,64]{0,2,1:T(8,128)(2,1)}, u32[]{:S(2)}) %copy-start.3) | copy-done | bytes 1048600
  1.9 0.0 copy-start.6
  1.9 0.7 copy-done.6
  2.5 0.8 copy-done.9
  3.3 0.0 copy-start.10
  3.3 0.7 copy-done.10
  4.0 0.0 copy-start.11
  4.0 0.7 copy-done.11
  4.7 2.0 %melt.1 = (f32[64,128]{1,0:T(8,128)S(1)}, f32[8,40,128]{2,1,0:T(8,128)}) custom-call(s32[1,4,16]{2,1,0:T(4,128)S(1)} %copy-done.6, f32[64,128]{1,0:T(8,128)S(1)} %bitcast.13, s32[1,128]{1,0:T(1,128)S(1)} %bitcast.14, f32[16,128]{1,0:T(8,128)S(1)} %copy-done.10, bf16[64,64,128]{2,1,0:T(8,128)(2,1)S(1)} %bitcast.6), custom_call_target="tpu_custom_call" | custom-call | bytes 1048576 | tf_op jit(solution)/shard_map/melt/pallas_call | solution.py:430
  6.6 5.2 %all-to-all-start = ((f32[8,40,128]{2,1,0:T(8,128)}), f32[8,40,128]{2,1,0:T(8,128)S(1)}, u32[]{:S(2)}, u32[]{:S(2)}) async-start(f32[8,40,128]{2,1,0:T(8,128)} %get-tuple-element.31), calls=%async_computation | async-start | bytes 327680 | tf_op jit(solution)/shard_map/all_to_all | solution.py:436
  11.8 3.9 %copy.11.diag_ref = bf16[128,64,64]{2,1,0:T(8,128)(2,1)S(1)} copy(bf16[128,64,64]{0,2,1:T(8,128)(2,1)} %param.11) | data formatting | bytes 2097152 | tf_op args[3]
  15.7 0.0 copy-start.4
  15.7 2.2 %copy-done.4 = bf16[128,64,256]{2,1,0:T(8,128)(2,1)S(1)} copy-done((bf16[128,64,256]{2,1,0:T(8,128)(2,1)S(1)}, bf16[128,64,256]{2,1,0:T(8,128)(2,1)}, u32[]{:S(2)}) %copy-start.4) | copy-done | bytes 4194328
  17.9 1.6 %product.1.m_ref = bf16[128,64,256]{2,1,0:T(8,128)(2,1)S(1)} custom-call(bf16[128,64,64]{2,1,0:T(8,128)(2,1)S(1)} %copy.11.diag_ref, bf16[128,64,256]{2,1,0:T(8,128)(2,1)S(1)} %copy-done.4), custom_call_target="tpu_custom_call" | custom-call | flops 268435456 | bytes 10485760 | tf_op jit(solution)/shard_map/product/pallas_call | solution.py:437
  19.6 0.0 copy-start
  19.6 2.0 %copy-done = bf16[128,64,256]{2,1,0:T(8,128)(2,1)} copy-done((bf16[128,64,256]{2,1,0:T(8,128)(2,1)}, bf16[128,64,256]{2,1,0:T(8,128)(2,1)S(1)}, u32[]{:S(2)}) %copy-start) | copy-done | bytes 4194328
  21.5 0.0 all-to-all-done.got_ref
  21.5 0.0 copy-done.5
  21.5 0.0 copy-done.7
  21.6 0.0 copy-done.12
  21.6 0.0 copy-start.1
  21.6 2.2 %copy-done.1 = bf16[128,64,256]{2,1,0:T(8,128)(2,1)S(1)} copy-done((bf16[128,64,256]{2,1,0:T(8,128)(2,1)S(1)}, bf16[128,64,256]{2,1,0:T(8,128)(2,1)}, u32[]{:S(2)}) %copy-start.1) | copy-done | bytes 4194328
  23.8 3.6 %first.1 = (bf16[1024,256]{1,0:T(8,128)(2,1)S(1)}, f32[64,16,128]{2,1,0:T(8,128)S(1)}, bf16[128,16,128]{2,1,0:T(8,128)(2,1)S(1)}, bf16[8,16,128]{2,1,0:T(8,128)(...) custom-call(s32[4,128]{1,0:T(4,128)S(1)} %bitcast.7, ...), custom_call_target="tpu_custom_call" | custom-call | bytes 1048576 | tf_op jit(solution)/shard_map/first/pallas_call | solution.py:441
  27.4 3.0 %collective-permute-start = (bf16[8,16,128]{2,1,0:T(8,128)(2,1)S(1)}, bf16[8,16,128]{2,1,0:T(8,128)(2,1)S(1)}, u32[]{:S(2)}, u32[]{:S(2)}) collective-permute-start(bf16[8,16,128]{2,1,0:T(8,128)(2,1)S(1)} %get-tuple-element.35), channel_id=1, source_target_pairs={{0,24},{4,28},{8,0},{12,4},{16,8},{20,12},{24,16},{28,20},{1,25},{... | collective-permute-start | bytes 98312 | tf_op jit(solution)/shard_map/ppermute | solution.py:32
  30.4 0.0 collective-permute-start.1
  30.4 0.5 collective-permute-start.2
  30.9 1.0 %collective-permute-start.3 = (bf16[8,16,128]{2,1,0:T(8,128)(2,1)S(1)}, bf16[8,16,128]{2,1,0:T(8,128)(2,1)S(1)}, u32[]{:S(2)}, u32[]{:S(2)}) collective-permute-start(bf16[8,16,128]{2,1,0:T(8,128)(2,1)S(1)} %get-tuple-element.38), channel_id=1, source_target_pairs={{0,8},{4,12},{8,16},{12,20},{16,24},{20,28},{24,0},{28,4},{1,9},{5... | collective-permute-start | bytes 98312 | tf_op jit(solution)/shard_map/ppermute | solution.py:32
  31.9 0.1 collective-permute-done.g0
  32.0 0.3 collective-permute-done.1.g1
  32.3 2.4 %collective-permute-done.2.g2 = bf16[8,16,128]{2,1,0:T(8,128)(2,1)S(1)} collective-permute-done((bf16[8,16,128]{2,1,0:T(8,128)(2,1)S(1)}, bf16[8,16,128]{2,1,0:T(8,128)(2,1)S(1)}, u32[]{:S(2)}, u32[]{:S(2)}) %collective-permute-start.2) | collective-permute-done | bytes 32800 | tf_op jit(solution)/shard_map/ppermute | solution.py:32
  34.7 1.2 %collective-permute-done.3.g3 = bf16[8,16,128]{2,1,0:T(8,128)(2,1)S(1)} collective-permute-done((bf16[8,16,128]{2,1,0:T(8,128)(2,1)S(1)}, bf16[8,16,128]{2,1,0:T(8,128)(2,1)S(1)}, u32[]{:S(2)}, u32[]{:S(2)}) %collective-permute-start.3) | collective-permute-done | bytes 32800 | tf_op jit(solution)/shard_map/ppermute | solution.py:32
  35.9 0.0 copy-done.2
  35.9 2.2 %sweep.1 = (bf16[128,16,128]{2,1,0:T(8,128)(2,1)S(1)}, bf16[8,16,128]{2,1,0:T(8,128)(2,1)S(1)}, bf16[8,16,128]{2,1,0:T(8,128)(2,1)S(1)}, bf16[8,16,128]{2,1,0:T(8,128)(2,1)S(1)}, bf16[8,16,128]{2,1,0:T(8,128)(2,1)S(1)}) custom-call(s32[4,128]{1,0:T(4,128)S(1)} %bitcast.8, s32[1,4,16]{2,1,0:T(4,128)S(1)} %copy-done.7, ...), custom_call_target="tpu_custom_call" | custom-call | bytes 1048576 | tf_op jit(solution)/shard_map/sweep/pallas_call | solution.py:449
  38.1 0.1 collective-permute-start.4
  38.2 1.5 %collective-permute-start.5 = (bf16[8,16,128]{2,1,0:T(8,128)(2,1)S(1)}, bf16[8,16,128]{2,1,0:T(8,128)(2,1)S(1)}, u32[]{:S(2)}, u32[]{:S(2)}) collective-permute-start(bf16[8,16,128]{2,1,0:T(8,128)(2,1)S(1)} %get-tuple-element.41), channel_id=1, source_target_pairs={{0,28},{4,0},{8,4},{12,8},{16,12},{20,16},{24,20},{28,24},{1,29},{... | collective-permute-start | bytes 98312 | tf_op jit(solution)/shard_map/ppermute | solution.py:32
  39.7 0.0 collective-permute-start.6
  39.7 1.1 %collective-permute-start.7 = (bf16[8,16,128]{2,1,0:T(8,128)(2,1)S(1)}, bf16[8,16,128]{2,1,0:T(8,128)(2,1)S(1)}, u32[]{:S(2)}, u32[]{:S(2)}) collective-permute-start(bf16[8,16,128]{2,1,0:T(8,128)(2,1)S(1)} %get-tuple-element.43), channel_id=1, source_target_pairs={{0,8},{4,12},{8,16},{12,20},{16,24},{20,28},{24,0},{28,4},{1,9},{5... | collective-permute-start | bytes 98312 | tf_op jit(solution)/shard_map/ppermute | solution.py:32
  40.7 1.4 %collective-permute-done.4.g0 = bf16[8,16,128]{2,1,0:T(8,128)(2,1)S(1)} collective-permute-done((bf16[8,16,128]{2,1,0:T(8,128)(2,1)S(1)}, bf16[8,16,128]{2,1,0:T(8,128)(2,1)S(1)}, u32[]{:S(2)}, u32[]{:S(2)}) %collective-permute-start.4) | collective-permute-done | bytes 32800 | tf_op jit(solution)/shard_map/ppermute | solution.py:32
  42.1 0.0 collective-permute-done.5.g1
  42.1 1.8 %collective-permute-done.6.g2 = bf16[8,16,128]{2,1,0:T(8,128)(2,1)S(1)} collective-permute-done((bf16[8,16,128]{2,1,0:T(8,128)(2,1)S(1)}, bf16[8,16,128]{2,1,0:T(8,128)(2,1)S(1)}, u32[]{:S(2)}, u32[]{:S(2)}) %collective-permute-start.6) | collective-permute-done | bytes 32800 | tf_op jit(solution)/shard_map/ppermute | solution.py:32
  43.9 0.7 collective-permute-done.7.g3
  44.6 0.0 copy-done.8
  44.6 8.5 %turn.1 = (f32[16,8192]{1,0:T(8,128)}, f32[64,16,128]{2,1,0:T(8,128)S(1)}, f32[64,16,128]{2,1,0:T(8,128)S(1)}, bf16[8,16,128]{2,1,0:T(8,128)(2,1)S(1)}, bf16[8,1...) custom-call(s32[4,128]{1,0:T(4,128)S(1)} %bitcast.9, ...), custom_call_target="tpu_custom_call" | custom-call | bytes 1048576 | tf_op jit(solution)/shard_map/turn/pallas_call | solution.py:453
  53.1 0.0 collective-permute-start.8
  53.1 0.5 collective-permute-start.9
  53.6 2.1 %collective-permute-start.10 = (bf16[8,16,128]{2,1,0:T(8,128)(2,1)S(1)}, bf16[8,16,128]{2,1,0:T(8,128)(2,1)S(1)}, u32[]{:S(2)}, u32[]{:S(2)}) collective-permute-start(bf16[8,16,128]{2,1,0:T(8,128)(2,1)S(1)} %get-tuple-element.49), channel_id=1, source_target_pairs={{0,28},{4,0},{8,4},{12,8},{16,12},{20,16},{24,20},{28,24},{1,29},{... | collective-permute-start | bytes 98312 | tf_op jit(solution)/shard_map/ppermute | solution.py:32
  55.8 2.0 %collective-permute-start.11 = (bf16[8,16,128]{2,1,0:T(8,128)(2,1)S(1)}, bf16[8,16,128]{2,1,0:T(8,128)(2,1)S(1)}, u32[]{:S(2)}, u32[]{:S(2)}) collective-permute-start(bf16[8,16,128]{2,1,0:T(8,128)(2,1)S(1)} %get-tuple-element.50), channel_id=1, source_target_pairs={{0,24},{4,28},{8,0},{12,4},{16,8},{20,12},{24,16},{28,20},{1,25},{... | collective-permute-start | bytes 98312 | tf_op jit(solution)/shard_map/ppermute | solution.py:32
  57.7 0.1 collective-permute-done.8.g0
  57.9 0.0 collective-permute-done.9.g1
  57.9 0.0 collective-permute-done.10.g2
  57.9 2.1 %collective-permute-done.11.g3 = bf16[8,16,128]{2,1,0:T(8,128)(2,1)S(1)} collective-permute-done((bf16[8,16,128]{2,1,0:T(8,128)(2,1)S(1)}, bf16[8,16,128]{2,1,0:T(8,128)(2,1)S(1)}, u32[]{:S(2)}, u32[]{:S(2)}) %collective-permute-start.11) | collective-permute-done | bytes 32800 | tf_op jit(solution)/shard_map/ppermute | solution.py:32
  60.0 3.0 %adjoint.1 = (f32[64,16,128]{2,1,0:T(8,128)S(1)}, bf16[8,16,128]{2,1,0:T(8,128)(2,1)S(1)}, bf16[8,16,128]{2,1,0:T(8,128)(2,1)S(1)}, bf16[8,16,128]{2,1,0:T(8,128)(2,1)S(1)}, bf16[8,16,128]{2,1,0:T(8,128)(2,1)S(1)}) custom-call(s32[4,128]{1,0:T(4,128)S(1)} %bitcast.10, s32[1,4,16]{2,1,0:T(4,128)S(1)} %copy-done.7, ...), custom_call_target="tpu_custom_call" | custom-call | bytes 1048576 | tf_op jit(solution)/shard_map/adjoint/pallas_call | solution.py:461
  62.9 2.6 %collective-permute-start.12 = (bf16[8,16,128]{2,1,0:T(8,128)(2,1)S(1)}, bf16[8,16,128]{2,1,0:T(8,128)(2,1)S(1)}, u32[]{:S(2)}, u32[]{:S(2)}) collective-permute-start(bf16[8,16,128]{2,1,0:T(8,128)(2,1)S(1)} %get-tuple-element.52), channel_id=1, source_target_pairs={{0,8},{4,12},{8,16},{12,20},{16,24},{20,28},{24,0},{28,4},{1,9},{5... | collective-permute-start | bytes 98312 | tf_op jit(solution)/shard_map/ppermute | solution.py:32
  65.5 0.0 collective-permute-start.13
  65.5 2.6 %collective-permute-start.14 = (bf16[8,16,128]{2,1,0:T(8,128)(2,1)S(1)}, bf16[8,16,128]{2,1,0:T(8,128)(2,1)S(1)}, u32[]{:S(2)}, u32[]{:S(2)}) collective-permute-start(bf16[8,16,128]{2,1,0:T(8,128)(2,1)S(1)} %get-tuple-element.54), channel_id=1, source_target_pairs={{0,28},{4,0},{8,4},{12,8},{16,12},{20,16},{24,20},{28,24},{1,29},{... | collective-permute-start | bytes 98312 | tf_op jit(solution)/shard_map/ppermute | solution.py:32
  68.2 0.0 collective-permute-start.15
  68.2 0.0 collective-permute-done.12.g0
  68.2 1.7 %collective-permute-done.13.g1 = bf16[8,16,128]{2,1,0:T(8,128)(2,1)S(1)} collective-permute-done((bf16[8,16,128]{2,1,0:T(8,128)(2,1)S(1)}, bf16[8,16,128]{2,1,0:T(8,128)(2,1)S(1)}, u32[]{:S(2)}, u32[]{:S(2)}) %collective-permute-start.13) | collective-permute-done | bytes 32800 | tf_op jit(solution)/shard_map/ppermute | solution.py:32
  69.9 0.0 collective-permute-done.14.g2
  69.9 2.2 %collective-permute-done.15.g3 = bf16[8,16,128]{2,1,0:T(8,128)(2,1)S(1)} collective-permute-done((bf16[8,16,128]{2,1,0:T(8,128)(2,1)S(1)}, bf16[8,16,128]{2,1,0:T(8,128)(2,1)S(1)}, u32[]{:S(2)}, u32[]{:S(2)}) %collective-permute-start.15) | collective-permute-done | bytes 32800 | tf_op jit(solution)/shard_map/ppermute | solution.py:32
  72.1 5.6 %last.1 = bf16[32,24,128]{2,1,0:T(8,128)(2,1)S(1)} custom-call(s32[4,128]{1,0:T(4,128)S(1)} %bitcast.11, s32[1,4,16]{2,1,0:T(4,128)S(1)} %copy-done.7, f32[64,16,128]{2,1,0:T(8,128)S(1)} %get-tuple-element.51.base_in_ref, f32[64,16,128]{2,1,0:T(8,128)S(1)} %get-tuple-element.46.target_ref, bf16[8,16,128]{2,1,0:T(8,128)(2,1)S(1)} %collective-permute-done.12.g0, ...), custom_call_target="tpu_custom_call" | custom-call | bytes 1048576 | tf_op jit(solution)/shard_map/last/pallas_call | solution.py:465
  77.7 13.8 %all_to_all.10.terms_ref = bf16[32,24,128]{2,1,0:T(8,128)(2,1)S(1)} all-to-all(bf16[32,24,128]{2,1,0:T(8,128)(2,1)S(1)} %last.1), channel_id=1, replica_groups=mesh['dom'=8,'pert'=4] {'dom','pert'}, dimensions={0} | all-to-all | bytes 393216 | tf_op jit(solution)/shard_map/all_to_all | solution.py:472
  91.5 0.6 owner.1
  (6 shorter events, 0.0 us)
Async XLA Ops:
  0.6 1.2 %copy-start.3 = (bf16[128,64,64]{0,2,1:T(8,128)(2,1)S(1)}, bf16[128,64,64]{0,2,1:T(8,128)(2,1)}, u32[]{:S(2)}) copy-start(bf16[128,64,64]{0,2,1:T(8,128)(2,1)} %param.11) | copy-start | bytes 3145732
  1.9 0.7 copy-start.6
  2.5 0.8 copy-start.9
  3.3 0.7 copy-start.10
  4.0 0.7 copy-start.11
  6.6 14.9 %all-to-all-start = ((f32[8,40,128]{2,1,0:T(8,128)}), f32[8,40,128]{2,1,0:T(8,128)S(1)}, u32[]{:S(2)}, u32[]{:S(2)}) async-start(f32[8,40,128]{2,1,0:T(8,128)} %get-tuple-element.31), calls=%async_computation | async-start | bytes 327680 | tf_op jit(solution)/shard_map/all_to_all | solution.py:436
  15.7 2.2 %copy-start.4 = (bf16[128,64,256]{2,1,0:T(8,128)(2,1)S(1)}, bf16[128,64,256]{2,1,0:T(8,128)(2,1)}, u32[]{:S(2)}) copy-start(bf16[128,64,256]{2,1,0:T(8,128)(2,1)} %coupling_ref.1) | copy-start | bytes 12582916
  17.9 3.6 %copy-start.5 = (s32[128,4]{0,1:T(4,128)S(1)}, s32[128,4]{0,1:T(4,128)}, u32[]{:S(2)}) copy-start(s32[128,4]{0,1:T(4,128)} %param.13) | copy-start | bytes 6148
  17.9 3.6 %copy-start.7 = (s32[1,4,16]{2,1,0:T(4,128)S(1)}, s32[1,4,16]{2,1,0:T(4,128)}, u32[]{:S(2)}) copy-start(s32[1,4,16]{2,1,0:T(4,128)} %send_ref.9) | copy-start | bytes 772
  17.9 3.6 %copy-start.12 = (s32[128]{0:T(128)S(1)}, s32[128]{0:T(128)}, u32[]{:S(2)}) copy-start(s32[128]{0:T(128)} %param.15) | copy-start | bytes 1540
  19.6 2.0 %copy-start = (bf16[128,64,256]{2,1,0:T(8,128)(2,1)}, bf16[128,64,256]{2,1,0:T(8,128)(2,1)S(1)}, u32[]{:S(2)}) copy-start(bf16[128,64,256]{2,1,0:T(8,128)(2,1)S(1)} %product.1.m_ref) | copy-start | bytes 12582916
  21.6 2.2 %copy-start.1 = (bf16[128,64,256]{2,1,0:T(8,128)(2,1)S(1)}, bf16[128,64,256]{2,1,0:T(8,128)(2,1)}, u32[]{:S(2)}) copy-start(bf16[128,64,256]{2,1,0:T(8,128)(2,1)} %copy-done) | copy-start | bytes 12582916
  23.8 12.2 %copy-start.2 = (bf16[128,64,256]{2,1,0:T(8,128)(2,1)S(1)}, bf16[128,64,256]{2,1,0:T(8,128)(2,1)}, u32[]{:S(2)}) copy-start(bf16[128,64,256]{2,1,0:T(8,128)(2,1)} %copy-done) | copy-start | bytes 12582916
  23.8 20.9 %copy-start.8 = (f32[8192]{0:T(1024)S(1)}, f32[8192]{0:T(1024)}, u32[]{:S(2)}) copy-start(f32[8192]{0:T(1024)} %param.10) | copy-start | bytes 98308
  27.4 4.6 %collective-permute-start = (bf16[8,16,128]{2,1,0:T(8,128)(2,1)S(1)}, bf16[8,16,128]{2,1,0:T(8,128)(2,1)S(1)}, u32[]{:S(2)}, u32[]{:S(2)}) collective-permute-start(bf16[8,16,128]{2,1,0:T(8,128)(2,1)S(1)} %get-tuple-element.35), channel_id=1, source_target_pairs={{0,24},{4,28},{8,0},{12,4},{16,8},{20,12},{24,16},{28,20},{1,25},{... | collective-permute-start | bytes 98312 | tf_op jit(solution)/shard_map/ppermute | solution.py:32
  30.4 1.9 %collective-permute-start.1 = (bf16[8,16,128]{2,1,0:T(8,128)(2,1)S(1)}, bf16[8,16,128]{2,1,0:T(8,128)(2,1)S(1)}, u32[]{:S(2)}, u32[]{:S(2)}) collective-permute-start(bf16[8,16,128]{2,1,0:T(8,128)(2,1)S(1)} %get-tuple-element.36), channel_id=1, source_target_pairs={{0,28},{4,0},{8,4},{12,8},{16,12},{20,16},{24,20},{28,24},{1,29},{... | collective-permute-start | bytes 98312 | tf_op jit(solution)/shard_map/ppermute | solution.py:32
  30.4 4.2 %collective-permute-start.2 = (bf16[8,16,128]{2,1,0:T(8,128)(2,1)S(1)}, bf16[8,16,128]{2,1,0:T(8,128)(2,1)S(1)}, u32[]{:S(2)}, u32[]{:S(2)}) collective-permute-start(bf16[8,16,128]{2,1,0:T(8,128)(2,1)S(1)} %get-tuple-element.37), channel_id=1, source_target_pairs={{0,4},{4,8},{8,12},{12,16},{16,20},{20,24},{24,28},{28,0},{1,5},{5... | collective-permute-start | bytes 98312 | tf_op jit(solution)/shard_map/ppermute | solution.py:32
  30.9 5.0 %collective-permute-start.3 = (bf16[8,16,128]{2,1,0:T(8,128)(2,1)S(1)}, bf16[8,16,128]{2,1,0:T(8,128)(2,1)S(1)}, u32[]{:S(2)}, u32[]{:S(2)}) collective-permute-start(bf16[8,16,128]{2,1,0:T(8,128)(2,1)S(1)} %get-tuple-element.38), channel_id=1, source_target_pairs={{0,8},{4,12},{8,16},{12,20},{16,24},{20,28},{24,0},{28,4},{1,9},{5... | collective-permute-start | bytes 98312 | tf_op jit(solution)/shard_map/ppermute | solution.py:32
  38.1 4.0 %collective-permute-start.4 = (bf16[8,16,128]{2,1,0:T(8,128)(2,1)S(1)}, bf16[8,16,128]{2,1,0:T(8,128)(2,1)S(1)}, u32[]{:S(2)}, u32[]{:S(2)}) collective-permute-start(bf16[8,16,128]{2,1,0:T(8,128)(2,1)S(1)} %get-tuple-element.40), channel_id=1, source_target_pairs={{0,24},{4,28},{8,0},{12,4},{16,8},{20,12},{24,16},{28,20},{1,25},{... | collective-permute-start | bytes 98312 | tf_op jit(solution)/shard_map/ppermute | solution.py:32
  38.2 3.9 %collective-permute-start.5 = (bf16[8,16,128]{2,1,0:T(8,128)(2,1)S(1)}, bf16[8,16,128]{2,1,0:T(8,128)(2,1)S(1)}, u32[]{:S(2)}, u32[]{:S(2)}) collective-permute-start(bf16[8,16,128]{2,1,0:T(8,128)(2,1)S(1)} %get-tuple-element.41), channel_id=1, source_target_pairs={{0,28},{4,0},{8,4},{12,8},{16,12},{20,16},{24,20},{28,24},{1,29},{... | collective-permute-start | bytes 98312 | tf_op jit(solution)/shard_map/ppermute | solution.py:32
  39.7 4.2 %collective-permute-start.6 = (bf16[8,16,128]{2,1,0:T(8,128)(2,1)S(1)}, bf16[8,16,128]{2,1,0:T(8,128)(2,1)S(1)}, u32[]{:S(2)}, u32[]{:S(2)}) collective-permute-start(bf16[8,16,128]{2,1,0:T(8,128)(2,1)S(1)} %get-tuple-element.42), channel_id=1, source_target_pairs={{0,4},{4,8},{8,12},{12,16},{16,20},{20,24},{24,28},{28,0},{1,5},{5... | collective-permute-start | bytes 98312 | tf_op jit(solution)/shard_map/ppermute | solution.py:32
  39.7 4.9 %collective-permute-start.7 = (bf16[8,16,128]{2,1,0:T(8,128)(2,1)S(1)}, bf16[8,16,128]{2,1,0:T(8,128)(2,1)S(1)}, u32[]{:S(2)}, u32[]{:S(2)}) collective-permute-start(bf16[8,16,128]{2,1,0:T(8,128)(2,1)S(1)} %get-tuple-element.43), channel_id=1, source_target_pairs={{0,8},{4,12},{8,16},{12,20},{16,24},{20,28},{24,0},{28,4},{1,9},{5... | collective-permute-start | bytes 98312 | tf_op jit(solution)/shard_map/ppermute | solution.py:32
  53.1 4.8 %collective-permute-start.8 = (bf16[8,16,128]{2,1,0:T(8,128)(2,1)S(1)}, bf16[8,16,128]{2,1,0:T(8,128)(2,1)S(1)}, u32[]{:S(2)}, u32[]{:S(2)}) collective-permute-start(bf16[8,16,128]{2,1,0:T(8,128)(2,1)S(1)} %get-tuple-element.47), channel_id=1, source_target_pairs={{0,8},{4,12},{8,16},{12,20},{16,24},{20,28},{24,0},{28,4},{1,9},{5... | collective-permute-start | bytes 98312 | tf_op jit(solution)/shard_map/ppermute | solution.py:32
  53.1 4.8 %collective-permute-start.9 = (bf16[8,16,128]{2,1,0:T(8,128)(2,1)S(1)}, bf16[8,16,128]{2,1,0:T(8,128)(2,1)S(1)}, u32[]{:S(2)}, u32[]{:S(2)}) collective-permute-start(bf16[8,16,128]{2,1,0:T(8,128)(2,1)S(1)} %get-tuple-element.48), channel_id=1, source_target_pairs={{0,4},{4,8},{8,12},{12,16},{16,20},{20,24},{24,28},{28,0},{1,5},{5... | collective-permute-start | bytes 98312 | tf_op jit(solution)/shard_map/ppermute | solution.py:32
  53.6 4.2 %collective-permute-start.10 = (bf16[8,16,128]{2,1,0:T(8,128)(2,1)S(1)}, bf16[8,16,128]{2,1,0:T(8,128)(2,1)S(1)}, u32[]{:S(2)}, u32[]{:S(2)}) collective-permute-start(bf16[8,16,128]{2,1,0:T(8,128)(2,1)S(1)} %get-tuple-element.49), channel_id=1, source_target_pairs={{0,28},{4,0},{8,4},{12,8},{16,12},{20,16},{24,20},{28,24},{1,29},{... | collective-permute-start | bytes 98312 | tf_op jit(solution)/shard_map/ppermute | solution.py:32
  55.8 4.2 %collective-permute-start.11 = (bf16[8,16,128]{2,1,0:T(8,128)(2,1)S(1)}, bf16[8,16,128]{2,1,0:T(8,128)(2,1)S(1)}, u32[]{:S(2)}, u32[]{:S(2)}) collective-permute-start(bf16[8,16,128]{2,1,0:T(8,128)(2,1)S(1)} %get-tuple-element.50), channel_id=1, source_target_pairs={{0,24},{4,28},{8,0},{12,4},{16,8},{20,12},{24,16},{28,20},{1,25},{... | collective-permute-start | bytes 98312 | tf_op jit(solution)/shard_map/ppermute | solution.py:32
  62.9 5.2 %collective-permute-start.12 = (bf16[8,16,128]{2,1,0:T(8,128)(2,1)S(1)}, bf16[8,16,128]{2,1,0:T(8,128)(2,1)S(1)}, u32[]{:S(2)}, u32[]{:S(2)}) collective-permute-start(bf16[8,16,128]{2,1,0:T(8,128)(2,1)S(1)} %get-tuple-element.52), channel_id=1, source_target_pairs={{0,8},{4,12},{8,16},{12,20},{16,24},{20,28},{24,0},{28,4},{1,9},{5... | collective-permute-start | bytes 98312 | tf_op jit(solution)/shard_map/ppermute | solution.py:32
  65.5 4.4 %collective-permute-start.13 = (bf16[8,16,128]{2,1,0:T(8,128)(2,1)S(1)}, bf16[8,16,128]{2,1,0:T(8,128)(2,1)S(1)}, u32[]{:S(2)}, u32[]{:S(2)}) collective-permute-start(bf16[8,16,128]{2,1,0:T(8,128)(2,1)S(1)} %get-tuple-element.53), channel_id=1, source_target_pairs={{0,4},{4,8},{8,12},{12,16},{16,20},{20,24},{24,28},{28,0},{1,5},{5... | collective-permute-start | bytes 98312 | tf_op jit(solution)/shard_map/ppermute | solution.py:32
  65.5 4.4 %collective-permute-start.14 = (bf16[8,16,128]{2,1,0:T(8,128)(2,1)S(1)}, bf16[8,16,128]{2,1,0:T(8,128)(2,1)S(1)}, u32[]{:S(2)}, u32[]{:S(2)}) collective-permute-start(bf16[8,16,128]{2,1,0:T(8,128)(2,1)S(1)} %get-tuple-element.54), channel_id=1, source_target_pairs={{0,28},{4,0},{8,4},{12,8},{16,12},{20,16},{24,20},{28,24},{1,29},{... | collective-permute-start | bytes 98312 | tf_op jit(solution)/shard_map/ppermute | solution.py:32
  68.2 3.9 %collective-permute-start.15 = (bf16[8,16,128]{2,1,0:T(8,128)(2,1)S(1)}, bf16[8,16,128]{2,1,0:T(8,128)(2,1)S(1)}, u32[]{:S(2)}, u32[]{:S(2)}) collective-permute-start(bf16[8,16,128]{2,1,0:T(8,128)(2,1)S(1)} %get-tuple-element.55), channel_id=1, source_target_pairs={{0,24},{4,28},{8,0},{12,4},{16,8},{20,12},{24,16},{28,20},{1,25},{... | collective-permute-start | bytes 98312 | tf_op jit(solution)/shard_map/ppermute | solution.py:32

commit v2 on v1

--- a/solution.py
+++ b/solution.py
@@ -16,7 +16,8 @@
 
 VMEM = pl.BlockSpec(memory_space=pltpu.VMEM)
 SMEM = pl.BlockSpec(memory_space=pltpu.SMEM)
-PARAMS = pltpu.CompilerParams(vmem_limit_bytes=16 * 1024 * 1024)
+HBM = pl.BlockSpec(memory_space=pltpu.HBM)
+MIB = 1024 * 1024
 
 
 def low_half(shape):
@@ -37,7 +38,26 @@
     return [lax.rem(me - offset + parts, parts) for offset in OFFSET_LIST]
 
 
-def melt_kernel(send_ref, melt_ref, patch_ref, probe_ref, diag_ref, w_ref, out_ref, *, parts):
+def melt_kernel(
+    send_hbm, melt_hbm, patch_hbm, probe_hbm, diag_hbm, w_ref, out_ref,
+    send_ref, melt_ref, patch_ref, probe_ref, diag_ref, sems, *, parts,
+):
+    copies = [
+        pltpu.make_async_copy(source, target, sems.at[number])
+        for number, (source, target) in enumerate(
+            (
+                (diag_hbm, diag_ref),
+                (melt_hbm, melt_ref),
+                (patch_hbm, patch_ref),
+                (probe_hbm, probe_ref),
+                (send_hbm, send_ref),
+            )
+        )
+    ]
+    for copy in copies:
+        copy.start()
+    for copy in copies:
+        copy.wait()
     pairs = melt_ref.shape[0]
     pert = probe_ref.shape[0]
     capacity = send_ref.shape[2]
@@ -82,16 +102,6 @@
         )
 
 
-def product_kernel(diag_ref, coupling_ref, m_ref):
-    def one(block, _):
-        m_ref[block] = jnp.dot(
-            diag_ref[block], coupling_ref[block], preferred_element_type=F32
-        ).astype(BF16)
-        return 0
-
-    lax.fori_loop(0, diag_ref.shape[0], one, 0, unroll=32)
-
-
 def gather_multiply(quad, cols_ref, ext_ref, m_ref, low):
     rows = []
     for place in range(QUAD):
@@ -128,9 +138,21 @@
 
 
 def first_kernel(
-    cols_ref, send_ref, patch_ref, got_ref, w_ref, m_ref,
-    one_hot_ref, t1_ref, t2_ref, o0, o1, o2, o3, ext_ref,
-):
+    cols_ref, send_ref, patch_ref, got_ref, w_ref, diag_ref, coupling_hbm,
+    m_ref, one_hot_ref, t1_ref, t2_ref, o0, o1, o2, o3, ext_ref, coupling_ref, sems,
+):
+    chunks = sems.shape[0]
+    size = diag_ref.shape[0] // chunks
+    copies = [
+        pltpu.make_async_copy(
+            coupling_hbm.at[chunk * size : (chunk + 1) * size],
+            coupling_ref.at[chunk * size : (chunk + 1) * size],
+            sems.at[chunk],
+        )
+        for chunk in range(chunks)
+    ]
+    for copy in copies:
+        copy.start()
     pert = t1_ref.shape[1]
     capacity = send_ref.shape[2]
     blocks = cols_ref.shape[1]
@@ -177,6 +199,13 @@
             spread = jnp.broadcast_to(ghost_picked[:, place : place + 1], (pert, LANES))
             ext_ref[blocks + place] = (spread * row).astype(BF16)
 
+    for chunk, copy in enumerate(copies):
+        copy.wait()
+        for block in range(chunk * size, (chunk + 1) * size):
+            m_ref[block] = jnp.dot(
+                diag_ref[block], coupling_ref[block], preferred_element_type=F32
+            ).astype(BF16)
+
     def sweep(quad, _):
         first, second = gather_multiply(quad, cols_ref, ext_ref, m_ref, low)
         store_pair(t2_ref, 2 * quad, t1_ref[2 * quad] - first, low)
@@ -273,23 +302,19 @@
     low = low_half(prev_ref.shape[1:])
     blocks = cols_ref.shape[1]
     extend(ext_ref, prev_ref, (g0, g1, g2, g3), low)
-    clear(acc_refs)
 
     def sweep(quad, _):
         coupled = gather_multiply(quad, cols_ref, ext_ref, m_ref, low)
-        pairs = []
         for place in range(2):
             pair = 2 * quad + place
             value = t1_ref[pair] - coupled[place]
             start = pl.multiple_of(pair * LANES, LANES)
             tangent_ref[:, pl.ds(start, LANES)] = value
-            target = value * weight_ref[pl.ds(pair, 1), :]
-            target_ref[pair] = target
-            pairs.append(target)
-        multiply_scatter(quad, cols_ref, pairs, m_ref, acc_refs, low)
+            target_ref[pair] = value * weight_ref[pl.ds(pair, 1), :]
         return 0
 
     lax.fori_loop(0, blocks // QUAD, sweep, 0, unroll=32)
+    scatter_all(cols_ref, target_ref, m_ref, acc_refs, low)
     finish_round(base_ref, target_ref, acc_refs, (o0, o1, o2, o3), blocks, low)
 
 
@@ -393,14 +418,14 @@
     curve_ref[...] = (curve[0:1] + curve[1:2]) * scale
 
 
-def call(body, outs, spaces, scratch=(), name=None, flops=0, moved=1 << 20):
+def call(body, outs, spaces, scratch=(), name=None, flops=0, moved=1 << 20, limit=12):
     return pl.pallas_call(
         body,
         out_shape=outs,
-        in_specs=[SMEM if s == "s" else VMEM for s in spaces],
+        in_specs=[{"s": SMEM, "v": VMEM, "h": HBM}[s] for s in spaces],
         out_specs=jax.tree.map(lambda _: VMEM, outs),
         scratch_shapes=list(scratch),
-        compiler_params=PARAMS,
+        compiler_params=pltpu.CompilerParams(vmem_limit_bytes=limit * MIB),
         name=name,
         cost_estimate=pl.CostEstimate(flops=flops, transcendentals=0, bytes_accessed=moved),
     )
@@ -430,21 +455,27 @@
     w, outgoing = call(
         functools.partial(melt_kernel, parts=parts),
         [shape((pairs, LANES), F32), shape((parts, pert + capacity + 8, LANES), F32)],
-        "svvvv",
+        "hhhhh",
+        [
+            pltpu.SMEM(send_list.shape, jnp.int32),
+            pltpu.VMEM((pairs, LANES), F32),
+            pltpu.VMEM((1, blocks), jnp.int32),
+            pltpu.VMEM(probes.shape, F32),
+            pltpu.VMEM((HALF, HALF, blocks), BF16),
+            pltpu.SemaphoreType.DMA((5,)),
+        ],
         name="melt",
+        limit=60,
     )(send_list, melt, patch, probes, jnp.transpose(diag_inverse, (1, 2, 0)))
     got = lax.all_to_all(outgoing, "dom", 0, 0, tiled=True)
-    m = call(
-        product_kernel, shape(coupling.shape, BF16), "vv", name="product", flops=1 << 28, moved=10 << 20
-    )(diag_inverse, coupling)
-
-    one_hot, t1, state, *out = call(
+    m, one_hot, t1, state, *out = call(
         first_kernel,
-        [shape((parts * probes.shape[1], 2 * LANES), BF16), pair_array, block_array] + msgs,
-        "ssvvvv",
-        [ext],
+        [shape(coupling.shape, BF16), shape((parts * probes.shape[1], 2 * LANES), BF16), pair_array, block_array] + msgs,
+        "ssvvvvh",
+        [ext, pltpu.VMEM(coupling.shape, BF16), pltpu.SemaphoreType.DMA((8,))],
         name="first",
-    )(columns, send_list, patch, got, w, m)
+        limit=46,
+    )(columns, send_list, patch, got, w, diag_inverse, coupling)
     ghosts = [rotated(v, o) for v, o in zip(out, OFFSET_LIST)]
     state, *out = call(
         sweep_kernel, [block_array] + msgs, "ssvvvvvvv", [ext], name="sweep"

time: 92.6 us -> 80.2 us (0.87)
  local copies, waits for them, and re-layouts: 14.3 us -> 4.7 us
  Pallas kernels: 27.1 us -> 24.4 us
  waiting for transfers between devices: 14 us -> 15.9 us
  starting transfers between devices: 22.2 us -> 20.3 us
    unnamed x27 -> x11, local copies, waits for them, and re-layouts: 14.3 us -> 4.7 us
    pallas_call x1, Pallas kernels: 8.46 us -> 4.52 us  [shards(): call(turn_kernel, [shape((pert, blocks * HALF), F32), pair_array, pair_ar...]
    all_to_all x1, waiting for transfers between devices: 0.01 us -> 1.94 us  [shards(): got = lax.all_to_all(outgoing, 'dom', 0, 0, tiled=True)]
    ppermute x16, starting transfers between devices: 17 us -> 15.1 us  [rotated(): lax.ppermute(value, 'dom', [(i, (i + by) % peers) for i in range(peers)])]
    pallas_call x2 -> x1, Pallas kernels: 5.29 us -> 5.87 us  [shards(): call(first_kernel, [shape(coupling.shape, BF16), shape((parts * probes.sh...]
  transfers between devices with their start and end apart: 17 -> 17, of which waited for: 11 -> 11; matrix products, arithmetic and copies ran while one was open for 4% -> 5% of each run, Pallas kernels for 2% -> 0%
where the time goes in v2:
time: 80.2 us; the launch traced here: 79.9 us
  Pallas kernels  24.4 us (30%)
  starting transfers between devices  20.3 us (25%)
  waiting for transfers between devices  15.9 us (20%)
  blocking collectives  13.8 us (17%)
  local copies, waits for them, and re-layouts  4.7 us (6%)
    ppermute x16, starting transfers between devices, rotated(): lax.ppermute(value, 'dom', [(i, (i + by) % peers) for i in range(peers)])  15.1 us
    ppermute x16, waiting for transfers between devices, rotated(): lax.ppermute(value, 'dom', [(i, (i + by) % peers) for i in range(peers)])  14 us
    all_to_all x1, blocking collectives, shards(): terms = lax.all_to_all(terms, ('dom', 'pert'), 0, 0, tiled=True)  13.8 us
    pallas_call x1, Pallas kernels, shards(): call(first_kernel, [shape(coupling.shape, BF16), shape((parts * probes.sh...  5.87 us
    pallas_call x1, Pallas kernels, shards(): call(last_kernel, shape((parts * perts, pert + 8, LANES), BF16), 'ssvvvvv...  5.58 us
    all_to_all x1, starting transfers between devices, shards(): got = lax.all_to_all(outgoing, 'dom', 0, 0, tiled=True)  5.18 us
    unnamed x11, local copies, waits for them, and re-layouts  4.7 us
    pallas_call x1, Pallas kernels, shards(): call(turn_kernel, [shape((pert, blocks * HALF), F32), pair_array, pair_ar...  4.52 us
  transfers between devices with their start and end apart: 17, of which 11 were waited for; matrix products, arithmetic and copies ran while one was open for 5% of the time, Pallas kernels for 0%

profile of v2, /device:TPU:0, one launch (start us, length us, event | category | flops | bytes accessed | tf_op | source)
XLA Modules:
  0.0 79.9 jit_solution(3500816263907670114)
XLA Ops:
  0.6 0.0 copy-start.2
  0.6 0.0 copy-start.4
  0.7 0.0 copy-start.1
  0.7 2.7 %melt.1 = (f32[64,128]{1,0:T(8,128)}, f32[8,40,128]{2,1,0:T(8,128)}) custom-call(s32[1,4,16]{2,1,0:T(4,128)} %send_ref.7, f32[64,128]{1,0:T(8,128)} %bitcast.15, s32[1,128]{1,0:T(1,128)} %bitcast.12, f32[16,128]{1,0:T(8,128)} %probe_hbm.1, bf16[64,64,128]{2,1,0:T(8,128)(2,1)} %bitcast.14), custom_call_target="tpu_custom_call" | custom-call | bytes 1048576 | tf_op jit(solution)/shard_map/melt/pallas_call | solution.py:455
  3.4 5.2 %all-to-all-start = ((f32[8,40,128]{2,1,0:T(8,128)}), f32[8,40,128]{2,1,0:T(8,128)S(1)}, u32[]{:S(2)}, u32[]{:S(2)}) async-start(f32[8,40,128]{2,1,0:T(8,128)} %get-tuple-element.32), calls=%async_computation | async-start | bytes 327680 | tf_op jit(solution)/shard_map/all_to_all | solution.py:470
  8.6 3.9 %copy.11.diag_ref = bf16[128,64,64]{2,1,0:T(8,128)(2,1)S(1)} copy(bf16[128,64,64]{0,2,1:T(8,128)(2,1)} %param.11) | data formatting | bytes 2097152 | tf_op args[3]
  12.5 1.9 %all-to-all-done.got_ref = f32[8,40,128]{2,1,0:T(8,128)S(1)} async-done(((f32[8,40,128]{2,1,0:T(8,128)}), f32[8,40,128]{2,1,0:T(8,128)S(1)}, u32[]{:S(2)}, u32[]{:S(2)}) %all-to-all-start) | async-done | bytes 163872 | tf_op jit(solution)/shard_map/all_to_all | solution.py:470
  14.4 0.0 copy-done.2
  14.4 0.0 copy-done.4
  14.4 0.0 copy-done.1
  14.4 0.0 copy-start
  14.5 0.7 copy-done
  15.2 5.9 %first.1 = (bf16[128,64,256]{2,1,0:T(8,128)(2,1)S(1)}, bf16[1024,256]{1,0:T(8,128)(2,1)S(1)}, f32[64,16,128]{2,1,0:T(8,128)S(1)}, bf16[128,16,128]{2,1,0:T(8,128...) custom-call(s32[4,128]{1,0:T(4,128)S(1)} %bitcast.6, ...), custom_call_target="tpu_custom_call" | custom-call | bytes 1048576 | tf_op jit(solution)/shard_map/first/pallas_call | solution.py:471
  21.1 0.0 copy-start.3
  21.1 1.1 %collective-permute-start = (bf16[8,16,128]{2,1,0:T(8,128)(2,1)S(1)}, bf16[8,16,128]{2,1,0:T(8,128)(2,1)S(1)}, u32[]{:S(2)}, u32[]{:S(2)}) collective-permute-start(bf16[8,16,128]{2,1,0:T(8,128)(2,1)S(1)} %get-tuple-element.36), channel_id=1, source_target_pairs={{0,24},{4,28},{8,0},{12,4},{16,8},{20,12},{24,16},{28,20},{1,25},{... | collective-permute-start | bytes 98312 | tf_op jit(solution)/shard_map/ppermute | solution.py:33
  22.2 0.1 collective-permute-start.1
  22.2 0.5 collective-permute-start.2
  22.7 1.0 %collective-permute-start.3 = (bf16[8,16,128]{2,1,0:T(8,128)(2,1)S(1)}, bf16[8,16,128]{2,1,0:T(8,128)(2,1)S(1)}, u32[]{:S(2)}, u32[]{:S(2)}) collective-permute-start(bf16[8,16,128]{2,1,0:T(8,128)(2,1)S(1)} %get-tuple-element.39), channel_id=1, source_target_pairs={{0,8},{4,12},{8,16},{12,20},{16,24},{20,28},{24,0},{28,4},{1,9},{5... | collective-permute-start | bytes 98312 | tf_op jit(solution)/shard_map/ppermute | solution.py:33
  23.7 1.4 %collective-permute-done.g0 = bf16[8,16,128]{2,1,0:T(8,128)(2,1)S(1)} collective-permute-done((bf16[8,16,128]{2,1,0:T(8,128)(2,1)S(1)}, bf16[8,16,128]{2,1,0:T(8,128)(2,1)S(1)}, u32[]{:S(2)}, u32[]{:S(2)}) %collective-permute-start) | collective-permute-done | bytes 32800 | tf_op jit(solution)/shard_map/ppermute | solution.py:33
  25.1 0.0 collective-permute-done.1.g1
  25.1 1.4 %collective-permute-done.2.g2 = bf16[8,16,128]{2,1,0:T(8,128)(2,1)S(1)} collective-permute-done((bf16[8,16,128]{2,1,0:T(8,128)(2,1)S(1)}, bf16[8,16,128]{2,1,0:T(8,128)(2,1)S(1)}, u32[]{:S(2)}, u32[]{:S(2)}) %collective-permute-start.2) | collective-permute-done | bytes 32800 | tf_op jit(solution)/shard_map/ppermute | solution.py:33
  26.5 1.2 %collective-permute-done.3.g3 = bf16[8,16,128]{2,1,0:T(8,128)(2,1)S(1)} collective-permute-done((bf16[8,16,128]{2,1,0:T(8,128)(2,1)S(1)}, bf16[8,16,128]{2,1,0:T(8,128)(2,1)S(1)}, u32[]{:S(2)}, u32[]{:S(2)}) %collective-permute-start.3) | collective-permute-done | bytes 32800 | tf_op jit(solution)/shard_map/ppermute | solution.py:33
  27.7 2.2 %sweep.1 = (bf16[128,16,128]{2,1,0:T(8,128)(2,1)S(1)}, bf16[8,16,128]{2,1,0:T(8,128)(2,1)S(1)}, bf16[8,16,128]{2,1,0:T(8,128)(2,1)S(1)}, bf16[8,16,128]{2,1,0:T(8,128)(2,1)S(1)}, bf16[8,16,128]{2,1,0:T(8,128)(2,1)S(1)}) custom-call(s32[4,128]{1,0:T(4,128)S(1)} %bitcast.7, s32[1,4,16]{2,1,0:T(4,128)S(1)} %copy-done.2, ...), custom_call_target="tpu_custom_call" | custom-call | bytes 1048576 | tf_op jit(solution)/shard_map/sweep/pallas_call | solution.py:480
  29.9 0.1 collective-permute-start.4
  30.0 1.5 %collective-permute-start.5 = (bf16[8,16,128]{2,1,0:T(8,128)(2,1)S(1)}, bf16[8,16,128]{2,1,0:T(8,128)(2,1)S(1)}, u32[]{:S(2)}, u32[]{:S(2)}) collective-permute-start(bf16[8,16,128]{2,1,0:T(8,128)(2,1)S(1)} %get-tuple-element.43), channel_id=1, source_target_pairs={{0,28},{4,0},{8,4},{12,8},{16,12},{20,16},{24,20},{28,24},{1,29},{... | collective-permute-start | bytes 98312 | tf_op jit(solution)/shard_map/ppermute | solution.py:33
  31.4 0.0 collective-permute-start.6
  31.4 1.1 %collective-permute-start.7 = (bf16[8,16,128]{2,1,0:T(8,128)(2,1)S(1)}, bf16[8,16,128]{2,1,0:T(8,128)(2,1)S(1)}, u32[]{:S(2)}, u32[]{:S(2)}) collective-permute-start(bf16[8,16,128]{2,1,0:T(8,128)(2,1)S(1)} %get-tuple-element.45), channel_id=1, source_target_pairs={{0,8},{4,12},{8,16},{12,20},{16,24},{20,28},{24,0},{28,4},{1,9},{5... | collective-permute-start | bytes 98312 | tf_op jit(solution)/shard_map/ppermute | solution.py:33
  32.5 1.4 %collective-permute-done.4.g0 = bf16[8,16,128]{2,1,0:T(8,128)(2,1)S(1)} collective-permute-done((bf16[8,16,128]{2,1,0:T(8,128)(2,1)S(1)}, bf16[8,16,128]{2,1,0:T(8,128)(2,1)S(1)}, u32[]{:S(2)}, u32[]{:S(2)}) %collective-permute-start.4) | collective-permute-done | bytes 32800 | tf_op jit(solution)/shard_map/ppermute | solution.py:33
  33.9 0.0 collective-permute-done.5.g1
  33.9 1.8 %collective-permute-done.6.g2 = bf16[8,16,128]{2,1,0:T(8,128)(2,1)S(1)} collective-permute-done((bf16[8,16,128]{2,1,0:T(8,128)(2,1)S(1)}, bf16[8,16,128]{2,1,0:T(8,128)(2,1)S(1)}, u32[]{:S(2)}, u32[]{:S(2)}) %collective-permute-start.6) | collective-permute-done | bytes 32800 | tf_op jit(solution)/shard_map/ppermute | solution.py:33
  35.7 0.7 collective-permute-done.7.g3
  36.4 0.0 copy-done.3
  36.4 4.5 %turn.1 = (f32[16,8192]{1,0:T(8,128)}, f32[64,16,128]{2,1,0:T(8,128)S(1)}, f32[64,16,128]{2,1,0:T(8,128)S(1)}, bf16[8,16,128]{2,1,0:T(8,128)(2,1)S(1)}, bf16[8,1...) custom-call(s32[4,128]{1,0:T(4,128)S(1)} %bitcast.8, ...), custom_call_target="tpu_custom_call" | custom-call | bytes 1048576 | tf_op jit(solution)/shard_map/turn/pallas_call | solution.py:484
  40.9 0.0 collective-permute-start.8
  40.9 0.5 collective-permute-start.9
  41.4 2.1 %collective-permute-start.10 = (bf16[8,16,128]{2,1,0:T(8,128)(2,1)S(1)}, bf16[8,16,128]{2,1,0:T(8,128)(2,1)S(1)}, u32[]{:S(2)}, u32[]{:S(2)}) collective-permute-start(bf16[8,16,128]{2,1,0:T(8,128)(2,1)S(1)} %get-tuple-element.51), channel_id=1, source_target_pairs={{0,28},{4,0},{8,4},{12,8},{16,12},{20,16},{24,20},{28,24},{1,29},{... | collective-permute-start | bytes 98312 | tf_op jit(solution)/shard_map/ppermute | solution.py:33
  43.6 2.0 %collective-permute-start.11 = (bf16[8,16,128]{2,1,0:T(8,128)(2,1)S(1)}, bf16[8,16,128]{2,1,0:T(8,128)(2,1)S(1)}, u32[]{:S(2)}, u32[]{:S(2)}) collective-permute-start(bf16[8,16,128]{2,1,0:T(8,128)(2,1)S(1)} %get-tuple-element.52), channel_id=1, source_target_pairs={{0,24},{4,28},{8,0},{12,4},{16,8},{20,12},{24,16},{28,20},{1,25},{... | collective-permute-start | bytes 98312 | tf_op jit(solution)/shard_map/ppermute | solution.py:33
  45.6 0.1 collective-permute-done.8.g0
  45.7 0.0 collective-permute-done.9.g1
  45.7 0.0 collective-permute-done.10.g2
  45.7 2.1 %collective-permute-done.11.g3 = bf16[8,16,128]{2,1,0:T(8,128)(2,1)S(1)} collective-permute-done((bf16[8,16,128]{2,1,0:T(8,128)(2,1)S(1)}, bf16[8,16,128]{2,1,0:T(8,128)(2,1)S(1)}, u32[]{:S(2)}, u32[]{:S(2)}) %collective-permute-start.11) | collective-permute-done | bytes 32800 | tf_op jit(solution)/shard_map/ppermute | solution.py:33
  47.8 2.9 %adjoint.1 = (f32[64,16,128]{2,1,0:T(8,128)S(1)}, bf16[8,16,128]{2,1,0:T(8,128)(2,1)S(1)}, bf16[8,16,128]{2,1,0:T(8,128)(2,1)S(1)}, bf16[8,16,128]{2,1,0:T(8,128)(2,1)S(1)}, bf16[8,16,128]{2,1,0:T(8,128)(2,1)S(1)}) custom-call(s32[4,128]{1,0:T(4,128)S(1)} %bitcast.9, s32[1,4,16]{2,1,0:T(4,128)S(1)} %copy-done.2, ...), custom_call_target="tpu_custom_call" | custom-call | bytes 1048576 | tf_op jit(solution)/shard_map/adjoint/pallas_call | solution.py:492
  50.7 2.6 %collective-permute-start.12 = (bf16[8,16,128]{2,1,0:T(8,128)(2,1)S(1)}, bf16[8,16,128]{2,1,0:T(8,128)(2,1)S(1)}, u32[]{:S(2)}, u32[]{:S(2)}) collective-permute-start(bf16[8,16,128]{2,1,0:T(8,128)(2,1)S(1)} %get-tuple-element.54), channel_id=1, source_target_pairs={{0,8},{4,12},{8,16},{12,20},{16,24},{20,28},{24,0},{28,4},{1,9},{5... | collective-permute-start | bytes 98312 | tf_op jit(solution)/shard_map/ppermute | solution.py:33
  53.3 0.0 collective-permute-start.13
  53.3 2.6 %collective-permute-start.14 = (bf16[8,16,128]{2,1,0:T(8,128)(2,1)S(1)}, bf16[8,16,128]{2,1,0:T(8,128)(2,1)S(1)}, u32[]{:S(2)}, u32[]{:S(2)}) collective-permute-start(bf16[8,16,128]{2,1,0:T(8,128)(2,1)S(1)} %get-tuple-element.56), channel_id=1, source_target_pairs={{0,28},{4,0},{8,4},{12,8},{16,12},{20,16},{24,20},{28,24},{1,29},{... | collective-permute-start | bytes 98312 | tf_op jit(solution)/shard_map/ppermute | solution.py:33
  56.0 0.0 collective-permute-start.15
  56.0 0.0 collective-permute-done.12.g0
  56.0 1.7 %collective-permute-done.13.g1 = bf16[8,16,128]{2,1,0:T(8,128)(2,1)S(1)} collective-permute-done((bf16[8,16,128]{2,1,0:T(8,128)(2,1)S(1)}, bf16[8,16,128]{2,1,0:T(8,128)(2,1)S(1)}, u32[]{:S(2)}, u32[]{:S(2)}) %collective-permute-start.13) | collective-permute-done | bytes 32800 | tf_op jit(solution)/shard_map/ppermute | solution.py:33
  57.7 0.0 collective-permute-done.14.g2
  57.7 2.2 %collective-permute-done.15.g3 = bf16[8,16,128]{2,1,0:T(8,128)(2,1)S(1)} collective-permute-done((bf16[8,16,128]{2,1,0:T(8,128)(2,1)S(1)}, bf16[8,16,128]{2,1,0:T(8,128)(2,1)S(1)}, u32[]{:S(2)}, u32[]{:S(2)}) %collective-permute-start.15) | collective-permute-done | bytes 32800 | tf_op jit(solution)/shard_map/ppermute | solution.py:33
  59.9 5.6 %last.1 = bf16[32,24,128]{2,1,0:T(8,128)(2,1)S(1)} custom-call(s32[4,128]{1,0:T(4,128)S(1)} %bitcast.10, s32[1,4,16]{2,1,0:T(4,128)S(1)} %copy-done.2, f32[64,16,128]{2,1,0:T(8,128)S(1)} %get-tuple-element.53.base_in_ref, f32[64,16,128]{2,1,0:T(8,128)S(1)} %get-tuple-element.48.target_ref, bf16[8,16,128]{2,1,0:T(8,128)(2,1)S(1)} %collective-permute-done.12.g0, ...), custom_call_target="tpu_custom_call" | custom-call | bytes 1048576 | tf_op jit(solution)/shard_map/last/pallas_call | solution.py:496
  65.5 13.8 %all_to_all.10.terms_ref = bf16[32,24,128]{2,1,0:T(8,128)(2,1)S(1)} all-to-all(bf16[32,24,128]{2,1,0:T(8,128)(2,1)S(1)} %last.1), channel_id=1, replica_groups=mesh['dom'=8,'pert'=4] {'dom','pert'}, dimensions={0} | all-to-all | bytes 393216 | tf_op jit(solution)/shard_map/all_to_all | solution.py:503
  79.3 0.6 owner.1
Async XLA Ops:
  0.6 13.8 %copy-start.2 = (s32[1,4,16]{2,1,0:T(4,128)S(1)}, s32[1,4,16]{2,1,0:T(4,128)}, u32[]{:S(2)}) copy-start(s32[1,4,16]{2,1,0:T(4,128)} %send_ref.7) | copy-start | bytes 772
  0.6 13.8 %copy-start.4 = (s32[128]{0:T(128)S(1)}, s32[128]{0:T(128)}, u32[]{:S(2)}) copy-start(s32[128]{0:T(128)} %param.15) | copy-start | bytes 1540
  0.7 13.8 %copy-start.1 = (s32[128,4]{0,1:T(4,128)S(1)}, s32[128,4]{0,1:T(4,128)}, u32[]{:S(2)}) copy-start(s32[128,4]{0,1:T(4,128)} %param.13) | copy-start | bytes 6148
  3.4 11.1 %all-to-all-start = ((f32[8,40,128]{2,1,0:T(8,128)}), f32[8,40,128]{2,1,0:T(8,128)S(1)}, u32[]{:S(2)}, u32[]{:S(2)}) async-start(f32[8,40,128]{2,1,0:T(8,128)} %get-tuple-element.32), calls=%async_computation | async-start | bytes 327680 | tf_op jit(solution)/shard_map/all_to_all | solution.py:470
  14.4 0.8 copy-start
  21.1 15.3 %copy-start.3 = (f32[8192]{0:T(1024)S(1)}, f32[8192]{0:T(1024)}, u32[]{:S(2)}) copy-start(f32[8192]{0:T(1024)} %param.10) | copy-start | bytes 98308
  21.1 4.0 %collective-permute-start = (bf16[8,16,128]{2,1,0:T(8,128)(2,1)S(1)}, bf16[8,16,128]{2,1,0:T(8,128)(2,1)S(1)}, u32[]{:S(2)}, u32[]{:S(2)}) collective-permute-start(bf16[8,16,128]{2,1,0:T(8,128)(2,1)S(1)} %get-tuple-element.36), channel_id=1, source_target_pairs={{0,24},{4,28},{8,0},{12,4},{16,8},{20,12},{24,16},{28,20},{1,25},{... | collective-permute-start | bytes 98312 | tf_op jit(solution)/shard_map/ppermute | solution.py:33
  22.2 2.9 %collective-permute-start.1 = (bf16[8,16,128]{2,1,0:T(8,128)(2,1)S(1)}, bf16[8,16,128]{2,1,0:T(8,128)(2,1)S(1)}, u32[]{:S(2)}, u32[]{:S(2)}) collective-permute-start(bf16[8,16,128]{2,1,0:T(8,128)(2,1)S(1)} %get-tuple-element.37), channel_id=1, source_target_pairs={{0,28},{4,0},{8,4},{12,8},{16,12},{20,16},{24,20},{28,24},{1,29},{... | collective-permute-start | bytes 98312 | tf_op jit(solution)/shard_map/ppermute | solution.py:33
  22.2 4.2 %collective-permute-start.2 = (bf16[8,16,128]{2,1,0:T(8,128)(2,1)S(1)}, bf16[8,16,128]{2,1,0:T(8,128)(2,1)S(1)}, u32[]{:S(2)}, u32[]{:S(2)}) collective-permute-start(bf16[8,16,128]{2,1,0:T(8,128)(2,1)S(1)} %get-tuple-element.38), channel_id=1, source_target_pairs={{0,4},{4,8},{8,12},{12,16},{16,20},{20,24},{24,28},{28,0},{1,5},{5... | collective-permute-start | bytes 98312 | tf_op jit(solution)/shard_map/ppermute | solution.py:33
  22.7 5.0 %collective-permute-start.3 = (bf16[8,16,128]{2,1,0:T(8,128)(2,1)S(1)}, bf16[8,16,128]{2,1,0:T(8,128)(2,1)S(1)}, u32[]{:S(2)}, u32[]{:S(2)}) collective-permute-start(bf16[8,16,128]{2,1,0:T(8,128)(2,1)S(1)} %get-tuple-element.39), channel_id=1, source_target_pairs={{0,8},{4,12},{8,16},{12,20},{16,24},{20,28},{24,0},{28,4},{1,9},{5... | collective-permute-start | bytes 98312 | tf_op jit(solution)/shard_map/ppermute | solution.py:33
  29.9 4.0 %collective-permute-start.4 = (bf16[8,16,128]{2,1,0:T(8,128)(2,1)S(1)}, bf16[8,16,128]{2,1,0:T(8,128)(2,1)S(1)}, u32[]{:S(2)}, u32[]{:S(2)}) collective-permute-start(bf16[8,16,128]{2,1,0:T(8,128)(2,1)S(1)} %get-tuple-element.42), channel_id=1, source_target_pairs={{0,24},{4,28},{8,0},{12,4},{16,8},{20,12},{24,16},{28,20},{1,25},{... | collective-permute-start | bytes 98312 | tf_op jit(solution)/shard_map/ppermute | solution.py:33
  30.0 3.9 %collective-permute-start.5 = (bf16[8,16,128]{2,1,0:T(8,128)(2,1)S(1)}, bf16[8,16,128]{2,1,0:T(8,128)(2,1)S(1)}, u32[]{:S(2)}, u32[]{:S(2)}) collective-permute-start(bf16[8,16,128]{2,1,0:T(8,128)(2,1)S(1)} %get-tuple-element.43), channel_id=1, source_target_pairs={{0,28},{4,0},{8,4},{12,8},{16,12},{20,16},{24,20},{28,24},{1,29},{... | collective-permute-start | bytes 98312 | tf_op jit(solution)/shard_map/ppermute | solution.py:33
  31.4 4.2 %collective-permute-start.6 = (bf16[8,16,128]{2,1,0:T(8,128)(2,1)S(1)}, bf16[8,16,128]{2,1,0:T(8,128)(2,1)S(1)}, u32[]{:S(2)}, u32[]{:S(2)}) collective-permute-start(bf16[8,16,128]{2,1,0:T(8,128)(2,1)S(1)} %get-tuple-element.44), channel_id=1, source_target_pairs={{0,4},{4,8},{8,12},{12,16},{16,20},{20,24},{24,28},{28,0},{1,5},{5... | collective-permute-start | bytes 98312 | tf_op jit(solution)/shard_map/ppermute | solution.py:33
  31.4 4.9 %collective-permute-start.7 = (bf16[8,16,128]{2,1,0:T(8,128)(2,1)S(1)}, bf16[8,16,128]{2,1,0:T(8,128)(2,1)S(1)}, u32[]{:S(2)}, u32[]{:S(2)}) collective-permute-start(bf16[8,16,128]{2,1,0:T(8,128)(2,1)S(1)} %get-tuple-element.45), channel_id=1, source_target_pairs={{0,8},{4,12},{8,16},{12,20},{16,24},{20,28},{24,0},{28,4},{1,9},{5... | collective-permute-start | bytes 98312 | tf_op jit(solution)/shard_map/ppermute | solution.py:33
  40.9 4.8 %collective-permute-start.8 = (bf16[8,16,128]{2,1,0:T(8,128)(2,1)S(1)}, bf16[8,16,128]{2,1,0:T(8,128)(2,1)S(1)}, u32[]{:S(2)}, u32[]{:S(2)}) collective-permute-start(bf16[8,16,128]{2,1,0:T(8,128)(2,1)S(1)} %get-tuple-element.49), channel_id=1, source_target_pairs={{0,8},{4,12},{8,16},{12,20},{16,24},{20,28},{24,0},{28,4},{1,9},{5... | collective-permute-start | bytes 98312 | tf_op jit(solution)/shard_map/ppermute | solution.py:33
  40.9 4.8 %collective-permute-start.9 = (bf16[8,16,128]{2,1,0:T(8,128)(2,1)S(1)}, bf16[8,16,128]{2,1,0:T(8,128)(2,1)S(1)}, u32[]{:S(2)}, u32[]{:S(2)}) collective-permute-start(bf16[8,16,128]{2,1,0:T(8,128)(2,1)S(1)} %get-tuple-element.50), channel_id=1, source_target_pairs={{0,4},{4,8},{8,12},{12,16},{16,20},{20,24},{24,28},{28,0},{1,5},{5... | collective-permute-start | bytes 98312 | tf_op jit(solution)/shard_map/ppermute | solution.py:33
  41.4 4.3 %collective-permute-start.10 = (bf16[8,16,128]{2,1,0:T(8,128)(2,1)S(1)}, bf16[8,16,128]{2,1,0:T(8,128)(2,1)S(1)}, u32[]{:S(2)}, u32[]{:S(2)}) collective-permute-start(bf16[8,16,128]{2,1,0:T(8,128)(2,1)S(1)} %get-tuple-element.51), channel_id=1, source_target_pairs={{0,28},{4,0},{8,4},{12,8},{16,12},{20,16},{24,20},{28,24},{1,29},{... | collective-permute-start | bytes 98312 | tf_op jit(solution)/shard_map/ppermute | solution.py:33
  43.6 4.2 %collective-permute-start.11 = (bf16[8,16,128]{2,1,0:T(8,128)(2,1)S(1)}, bf16[8,16,128]{2,1,0:T(8,128)(2,1)S(1)}, u32[]{:S(2)}, u32[]{:S(2)}) collective-permute-start(bf16[8,16,128]{2,1,0:T(8,128)(2,1)S(1)} %get-tuple-element.52), channel_id=1, source_target_pairs={{0,24},{4,28},{8,0},{12,4},{16,8},{20,12},{24,16},{28,20},{1,25},{... | collective-permute-start | bytes 98312 | tf_op jit(solution)/shard_map/ppermute | solution.py:33
  50.7 5.2 %collective-permute-start.12 = (bf16[8,16,128]{2,1,0:T(8,128)(2,1)S(1)}, bf16[8,16,128]{2,1,0:T(8,128)(2,1)S(1)}, u32[]{:S(2)}, u32[]{:S(2)}) collective-permute-start(bf16[8,16,128]{2,1,0:T(8,128)(2,1)S(1)} %get-tuple-element.54), channel_id=1, source_target_pairs={{0,8},{4,12},{8,16},{12,20},{16,24},{20,28},{24,0},{28,4},{1,9},{5... | collective-permute-start | bytes 98312 | tf_op jit(solution)/shard_map/ppermute | solution.py:33
  53.3 4.4 %collective-permute-start.13 = (bf16[8,16,128]{2,1,0:T(8,128)(2,1)S(1)}, bf16[8,16,128]{2,1,0:T(8,128)(2,1)S(1)}, u32[]{:S(2)}, u32[]{:S(2)}) collective-permute-start(bf16[8,16,128]{2,1,0:T(8,128)(2,1)S(1)} %get-tuple-element.55), channel_id=1, source_target_pairs={{0,4},{4,8},{8,12},{12,16},{16,20},{20,24},{24,28},{28,0},{1,5},{5... | collective-permute-start | bytes 98312 | tf_op jit(solution)/shard_map/ppermute | solution.py:33
  53.3 4.4 %collective-permute-start.14 = (bf16[8,16,128]{2,1,0:T(8,128)(2,1)S(1)}, bf16[8,16,128]{2,1,0:T(8,128)(2,1)S(1)}, u32[]{:S(2)}, u32[]{:S(2)}) collective-permute-start(bf16[8,16,128]{2,1,0:T(8,128)(2,1)S(1)} %get-tuple-element.56), channel_id=1, source_target_pairs={{0,28},{4,0},{8,4},{12,8},{16,12},{20,16},{24,20},{28,24},{1,29},{... | collective-permute-start | bytes 98312 | tf_op jit(solution)/shard_map/ppermute | solution.py:33
  56.0 3.9 %collective-permute-start.15 = (bf16[8,16,128]{2,1,0:T(8,128)(2,1)S(1)}, bf16[8,16,128]{2,1,0:T(8,128)(2,1)S(1)}, u32[]{:S(2)}, u32[]{:S(2)}) collective-permute-start(bf16[8,16,128]{2,1,0:T(8,128)(2,1)S(1)} %get-tuple-element.57), channel_id=1, source_target_pairs={{0,24},{4,28},{8,0},{12,4},{16,8},{20,12},{24,16},{28,20},{1,25},{... | collective-permute-start | bytes 98312 | tf_op jit(solution)/shard_map/ppermute | solution.py:33

commit v3 on v2

--- a/solution.py
+++ b/solution.py
@@ -13,6 +13,7 @@
 LANES = 128
 HALF = 64
 QUAD = 4
+RADIX = 64
 
 VMEM = pl.BlockSpec(memory_space=pltpu.VMEM)
 SMEM = pl.BlockSpec(memory_space=pltpu.SMEM)
@@ -102,7 +103,7 @@
         )
 
 
-def gather_multiply(quad, cols_ref, ext_ref, m_ref, low):
+def gather_rows(quad, cols_ref, ext_ref, low):
     rows = []
     for place in range(QUAD):
         g = quad * QUAD + place
@@ -112,13 +113,25 @@
                 [jnp.where(low, tiles[0], tiles[1]), jnp.where(low, tiles[2], tiles[3])], axis=1
             )
         )
-    lhs = jnp.concatenate(rows, axis=0)
+    return rows
+
+
+def coupled_rows(quad, rows, m_ref):
     rhs = m_ref[pl.ds(quad * QUAD, QUAD)].reshape(QUAD * HALF, 4 * HALF)
-    out = lax.dot_general(lhs, rhs, (((1,), (1,)), ((), ())), preferred_element_type=F32)
-    p = out.shape[0] // QUAD
-    first = jnp.where(low, out[:p, :LANES], out[p : 2 * p, :LANES])
-    second = jnp.where(low, out[2 * p : 3 * p, LANES:], out[3 * p :, LANES:])
+    return lax.dot_general(
+        jnp.concatenate(rows, axis=0), rhs, (((1,), (1,)), ((), ())), preferred_element_type=F32
+    )
+
+
+def own_pairs(out, size, low):
+    first = jnp.where(low, out[:size, :LANES], out[size : 2 * size, :LANES])
+    second = jnp.where(low, out[2 * size : 3 * size, LANES:], out[3 * size : 4 * size, LANES:])
     return first, second
+
+
+def gather_multiply(quad, cols_ref, ext_ref, m_ref, low):
+    out = coupled_rows(quad, gather_rows(quad, cols_ref, ext_ref, low), m_ref)
+    return own_pairs(out, out.shape[0] // QUAD, low)
 
 
 def store_pair(ref, pair, value, low):
@@ -130,17 +143,31 @@
 
 def fill_messages(send_ref, ref, msg_refs, low):
     for group, msg_ref in enumerate(msg_refs):
-        for pair in range(msg_ref.shape[0]):
+        for pair in range(send_ref.shape[2] // 2):
             even, odd = (
                 ref[jnp.maximum(send_ref[0, group, 2 * pair + half], 0)] for half in range(2)
             )
             msg_ref[pair] = jnp.where(low, even, odd)
 
 
+def patches_of_columns(columns_ref, ids):
+    columns = jnp.concatenate([columns_ref[...], columns_ref[...]], axis=0)
+    here = jnp.broadcast_to(ids[:, :LANES], columns.shape)
+    there = jnp.broadcast_to(ids[:, LANES:], columns.shape)
+    return jnp.where(
+        columns < LANES,
+        jnp.take_along_axis(here, jnp.minimum(columns, LANES - 1), axis=1),
+        jnp.take_along_axis(there, jnp.maximum(columns - LANES, 0), axis=1),
+    )
+
+
 def first_kernel(
-    cols_ref, send_ref, patch_ref, got_ref, w_ref, diag_ref, coupling_hbm,
-    m_ref, one_hot_ref, t1_ref, t2_ref, o0, o1, o2, o3, ext_ref, coupling_ref, sems,
+    cols_ref, send_ref, patch_ref, columns_ref, got_ref, w_hbm, diag_ref, coupling_hbm,
+    m_ref, v_ref, names_ref, t1_ref, t2_ref, o0, o1, o2, o3,
+    ext_ref, row_ref, w_ref, coupling_ref, w_sem, sems,
 ):
+    w_copy = pltpu.make_async_copy(w_hbm, w_ref, w_sem)
+    w_copy.start()
     chunks = sems.shape[0]
     size = diag_ref.shape[0] // chunks
     copies = [
@@ -169,7 +196,6 @@
             lax.broadcasted_iota(jnp.int32, (LANES, 2 * LANES), 0) + part * LANES
         ).astype(F32)
         hot = jnp.where(names == ids, 1.0, 0.0).astype(BF16)
-        one_hot_ref[part * LANES : (part + 1) * LANES, :] = hot
         value = got_ref[part, :pert]
         top = value.astype(BF16)
         rest = value - top.astype(F32)
@@ -182,6 +208,26 @@
     local_picked = picked[:, :LANES]
     ghost_picked = picked[:, LANES:]
     full_low = low.astype(jnp.int32)
+    column_patches = patches_of_columns(columns_ref, ids)
+    sub = lax.broadcasted_iota(jnp.int32, (8, LANES), 0)
+    lane8 = lax.broadcasted_iota(jnp.int32, (8, LANES), 1)
+    wanted = sub == lane8 % 4
+
+    def listed(blocks_of_lanes):
+        taken = jnp.take_along_axis(column_patches, blocks_of_lanes, axis=1)
+        return jnp.sum(jnp.where(wanted, taken, 0.0), axis=0, keepdims=True)
+
+    for tile in range(4 * blocks // LANES):
+        names_ref[tile : tile + 1, :] = listed(tile * (LANES // 4) + lane8 // 4)
+    w_copy.wait()
+    w = w_ref[...]
+    w_other = swap_halves(w)
+    low_w = low_half(w.shape)
+    row_ref[pl.ds(0, blocks // 2, stride=2), :] = jnp.where(low_w, w, w_other)
+    row_ref[pl.ds(1, blocks // 2, stride=2), :] = jnp.where(low_w, w_other, w)
+    for group, source in enumerate(sources):
+        start = blocks + group * capacity
+        row_ref[start : start + capacity, :] = got_ref[source, pert : pert + capacity, :]
 
     def seed(pair, _):
         index = 2 * pair + 1 - full_low
@@ -206,19 +252,63 @@
                 diag_ref[block], coupling_ref[block], preferred_element_type=F32
             ).astype(BF16)
 
+    low8 = low_half((8, LANES))
+    masks = [(sub % 4 == k) & (low8 if k % 2 == 0 else ~low8) for k in range(4)]
+    nothing = jnp.zeros((8, LANES), F32)
+
     def sweep(quad, _):
-        first, second = gather_multiply(quad, cols_ref, ext_ref, m_ref, low)
-        store_pair(t2_ref, 2 * quad, t1_ref[2 * quad] - first, low)
-        store_pair(t2_ref, 2 * quad + 1, t1_ref[2 * quad + 1] - second, low)
+        rows = gather_rows(quad, cols_ref, ext_ref, low)
+        tiles = ([], [])
+        for place in range(QUAD):
+            w_rows = [row_ref[pl.ds(cols_ref[k, quad * QUAD + place], 1), :] for k in range(4)]
+            for side in range(2):
+                tiles[side].append(
+                    jnp.where(
+                        masks[2 * side],
+                        w_rows[2 * side],
+                        jnp.where(masks[2 * side + 1], w_rows[2 * side + 1], nothing),
+                    )
+                )
+        extra = jnp.concatenate([jnp.concatenate(side, axis=0) for side in tiles], axis=1)
+        out = coupled_rows(quad, rows + [extra.astype(BF16)], m_ref)
+        for place, value in enumerate(own_pairs(out, pert, low)):
+            pair = 2 * quad + place
+            store_pair(t2_ref, pair, t1_ref[pair] - value, low)
+        for place, value in enumerate(own_pairs(out[QUAD * pert :], 8, low8)):
+            v_ref[2 * quad + place] = value
         return 0
 
     lax.fori_loop(0, blocks // QUAD, sweep, 0, unroll=32)
-    fill_messages(send_ref, t2_ref, (o0, o1, o2, o3), low)
+    msgs = (o0, o1, o2, o3)
+    fill_messages(send_ref, t2_ref, msgs, low)
+    half = capacity // 2
+    for group, ref in enumerate(msgs):
+        places = jnp.zeros((8, LANES), jnp.int32)
+        values = []
+        for slot in range(capacity):
+            block = jnp.maximum(send_ref[0, group, slot], 0)
+            value = v_ref[block // 2]
+            right = (slot - block) % 2 == 0
+            values.append(jnp.where(right, value, swap_halves(value)))
+            places = jnp.where(lane8 // 4 == slot, block, places)
+        pairs = [
+            jnp.where(low8, values[2 * pair], values[2 * pair + 1]) for pair in range(half)
+        ]
+        for tile in range(half // 2):
+            ref[half + tile] = jnp.concatenate(pairs[2 * tile : 2 * tile + 2], axis=0).astype(BF16)
+        patch = listed(places).astype(jnp.int32)
+        ref[half + half // 2] = jnp.concatenate(
+            [
+                jnp.broadcast_to(patch // RADIX, (8, LANES)),
+                jnp.broadcast_to(patch % RADIX, (8, LANES)),
+            ],
+            axis=0,
+        ).astype(F32).astype(BF16)
 
 
 def extend(ext_ref, local_ref, ghosts, low):
     blocks = local_ref.shape[0]
-    count = ghosts[0].shape[0]
+    count = (ext_ref.shape[0] - blocks) // 2 // len(ghosts)
     ext_ref[:blocks] = local_ref[...]
     for group, ref in enumerate(ghosts):
         for pair in range(count):
@@ -345,55 +435,89 @@
     lax.fori_loop(0, cols_ref.shape[1] // QUAD, sweep, 0, unroll=32)
 
 
-def adjoint_kernel(
-    cols_ref, send_ref, base_in_ref, target_ref, g0, g1, g2, g3, m_ref,
-    base_ref, o0, o1, o2, o3, u_ref, *acc_refs,
+def prepare_kernel(
+    patch_ref, names_ref, g0, g1, g2, g3, target_ref, w_ref, hot_ref, terms_ref
 ):
+    pairs, pert, _ = target_ref.shape
+    low8 = low_half((1, LANES))
+    rows = [patch_ref[...].astype(F32)] + [names_ref[tile : tile + 1] for tile in range(4)]
+    ghosts = []
+    for ref in (g0, g1, g2, g3):
+        digits = ref[ref.shape[0] - 1].astype(F32)
+        ghosts.append(digits[0:1] * RADIX + digits[8:9])
+    for tile in range(2):
+        rows.append(jnp.where(low8, ghosts[2 * tile], swap_halves(ghosts[2 * tile + 1])))
+    low = low_half((pert, LANES))
+    lane = lax.broadcasted_iota(jnp.int32, (pert, LANES), 1)
+    first = lax.broadcasted_iota(jnp.int32, (LANES, LANES), 0).astype(F32)
+
+    def one(part, _):
+        start = pl.multiple_of(part * LANES, LANES)
+        base = (part * LANES).astype(F32)
+        for tile, row in enumerate(rows):
+            hot_ref[pl.ds(start, LANES), tile * LANES : (tile + 1) * LANES] = jnp.where(
+                first == row - base, 1.0, 0.0
+            ).astype(BF16)
+        return 0
+
+    lax.fori_loop(0, hot_ref.shape[0] // LANES, one, 0, unroll=2)
+
+    def local(pair, terms):
+        value = target_ref[pair] * w_ref[pl.ds(pair, 1), :]
+        even = jnp.sum(jnp.where(low, value, 0.0), axis=1, keepdims=True)
+        odd = jnp.sum(jnp.where(low, 0.0, value), axis=1, keepdims=True)
+        return jnp.where(lane == 2 * pair, even, jnp.where(lane == 2 * pair + 1, odd, terms))
+
+    terms_ref[...] = lax.fori_loop(0, pairs, local, jnp.zeros((pert, LANES), F32), unroll=16)
+
+
+def last_kernel(
+    cols_ref, send_ref, base_in_ref, target_ref, g0, g1, g2, g3, m_ref, v_ref, v0, v1, v2, v3,
+    hot_ref, terms_ref, got_ref, out_ref, u_ref, *acc_refs,
+):
+    pert = u_ref.shape[1]
+    blocks = cols_ref.shape[1]
+    half = send_ref.shape[2] // 2
+    parts = got_ref.shape[0]
     low = low_half(u_ref.shape[1:])
     take_returned(send_ref, base_in_ref, u_ref, (g0, g1, g2, g3), low)
     scatter_all(cols_ref, u_ref, m_ref, acc_refs, low)
-    finish_round(base_ref, target_ref, acc_refs, (o0, o1, o2, o3), cols_ref.shape[1], low)
-
-
-def last_kernel(
-    cols_ref, send_ref, base_in_ref, target_ref, g0, g1, g2, g3, m_ref, w_ref, got_ref,
-    one_hot_ref, out_ref, u_ref, *acc_refs,
-):
-    pert = u_ref.shape[1]
-    blocks = cols_ref.shape[1]
-    low = low_half(u_ref.shape[1:])
-    lane = lax.broadcasted_iota(jnp.int32, (pert, LANES), 1)
-    take_returned(send_ref, base_in_ref, u_ref, (g0, g1, g2, g3), low)
-    scatter_all(cols_ref, u_ref, m_ref, acc_refs, low)
-
-    def local(pair, terms):
-        value = (target_ref[pair] - pair_sum(acc_refs, pair, low)) * w_ref[pl.ds(pair, 1), :]
-        even = jnp.sum(jnp.where(low, value, 0.0), axis=1, keepdims=True)
-        odd = jnp.sum(jnp.where(low, 0.0, value), axis=1, keepdims=True)
-        return jnp.where(lane == 2 * pair, even, jnp.where(lane == 2 * pair + 1, odd, terms))
-
-    local_terms = lax.fori_loop(
-        0, blocks // 2, local, jnp.zeros((pert, LANES), F32), unroll=4
-    )
-    ghost_terms = jnp.zeros((pert, LANES), F32)
-    parts = got_ref.shape[0]
-    capacity = send_ref.shape[2]
-    for group, source in enumerate(neighbours(parts)):
-        for slot in range(capacity):
-            place = group * capacity + slot
-            row = got_ref[source, pert + slot : pert + slot + 1, :]
-            value = half_sums(acc_refs, blocks + place, low) * row
-            ghost_terms = jnp.where(
-                lane == place, -jnp.sum(value, axis=1, keepdims=True), ghost_terms
-            )
-    terms = jnp.concatenate([local_terms, ghost_terms], axis=1)
+    sub = lax.broadcasted_iota(jnp.int32, (8, LANES), 0)
+    own = (sub < 4) == low_half((8, LANES))
+    nothing = jnp.zeros((8, LANES), F32)
+
+    def products(pair, first_v, second_v, first_z, second_z):
+        rhs = jnp.concatenate(
+            [
+                jnp.concatenate([jnp.where(own, first_v, nothing), nothing], axis=1),
+                jnp.concatenate([nothing, jnp.where(own, second_v, nothing)], axis=1),
+            ],
+            axis=0,
+        )
+        lhs = jnp.concatenate([first_z, second_z], axis=1)
+        return lax.dot_general(
+            lhs.astype(BF16), rhs.astype(BF16), (((1,), (1,)), ((), ())),
+            preferred_element_type=F32,
+        )
+
+    pieces = []
+    for pair in range(0, blocks // 2, 2):
+        z = [pair_sum(acc_refs, pair + i, low) - target_ref[pair + i] for i in range(2)]
+        pieces.append(products(pair, v_ref[pair], v_ref[pair + 1], *z))
+    for group, ref in enumerate((v0, v1, v2, v3)):
+        for tile in range(half // 2):
+            both = ref[half + tile].astype(F32)
+            pair = blocks // 2 + group * half + 2 * tile
+            z = [pair_sum(acc_refs, pair + i, low) for i in range(2)]
+            pieces.append(products(pair, both[:8], both[8:], *z))
+    terms = jnp.concatenate([terms_ref[...]] + pieces, axis=1)
     top = terms.astype(BF16)
     rest = (terms - top.astype(F32)).astype(BF16)
     both = jnp.concatenate([top, rest], axis=0)
     perts = out_ref.shape[0] // parts
     sub = lax.broadcasted_iota(jnp.int32, (8, LANES), 0)
     for part in range(parts):
-        hot = one_hot_ref[part * LANES : (part + 1) * LANES, :]
+        hot = hot_ref[part * LANES : (part + 1) * LANES, :]
         out = lax.dot_general(both, hot, (((1,), (1,)), ((), ())), preferred_element_type=F32)
         value = out[:pert] + out[pert:]
         curve = jnp.sum(value * got_ref[part, :pert], axis=0, keepdims=True)
@@ -468,18 +592,33 @@
         limit=60,
     )(send_list, melt, patch, probes, jnp.transpose(diag_inverse, (1, 2, 0)))
     got = lax.all_to_all(outgoing, "dom", 0, 0, tiled=True)
-    m, one_hot, t1, state, *out = call(
+    wide = [shape((capacity // 2 + capacity // 4 + 1, pert, LANES), BF16)] * 4
+    m, v, names, t1, state, *out = call(
         first_kernel,
-        [shape(coupling.shape, BF16), shape((parts * probes.shape[1], 2 * LANES), BF16), pair_array, block_array] + msgs,
-        "ssvvvvh",
-        [ext, pltpu.VMEM(coupling.shape, BF16), pltpu.SemaphoreType.DMA((8,))],
+        [
+            shape(coupling.shape, BF16),
+            shape((pairs, 8, LANES), F32),
+            shape((8, LANES), F32),
+            pair_array,
+            block_array,
+        ]
+        + wide,
+        "ssvvvhvh",
+        [
+            ext,
+            pltpu.VMEM((blocks + 4 * capacity, LANES), F32),
+            pltpu.VMEM((pairs, LANES), F32),
+            pltpu.VMEM(coupling.shape, BF16),
+            pltpu.SemaphoreType.DMA,
+            pltpu.SemaphoreType.DMA((8,)),
+        ],
         name="first",
         limit=46,
-    )(columns, send_list, patch, got, w, diag_inverse, coupling)
-    ghosts = [rotated(v, o) for v, o in zip(out, OFFSET_LIST)]
+    )(columns, send_list, patch, columns, got, w, diag_inverse, coupling)
+    carried = [rotated(x, o) for x, o in zip(out, OFFSET_LIST)]
     state, *out = call(
         sweep_kernel, [block_array] + msgs, "ssvvvvvvv", [ext], name="sweep"
-    )(columns, send_list, t1, state, *ghosts, m)
+    )(columns, send_list, t1, state, *carried, m)
     ghosts = [rotated(v, o) for v, o in zip(out, OFFSET_LIST)]
     tangent, target, base, *out = call(
         turn_kernel,
@@ -489,17 +628,20 @@
         name="turn",
     )(columns, t1, state, *ghosts, m, weight)
     ghosts = [rotated(v, -o) for v, o in zip(out, OFFSET_LIST)]
-    base, *out = call(
-        adjoint_kernel, [pair_array] + msgs, "ssvvvvvvv", [held] + accs, name="adjoint"
-    )(columns, send_list, base, target, *ghosts, m)
-    ghosts = [rotated(v, -o) for v, o in zip(out, OFFSET_LIST)]
+    hot, terms = call(
+        prepare_kernel,
+        [shape((parts * LANES, 7 * LANES), BF16), shape((pert, LANES), F32)],
+        "vvvvvvvv",
+        name="prepare",
+        moved=4 << 20,
+    )(patch, names, *carried, target, w)
     terms = call(
         last_kernel,
         shape((parts * perts, pert + 8, LANES), BF16),
-        "ssvvvvvvvvvv",
+        "ss" + "v" * 15,
         [held] + accs,
         name="last",
-    )(columns, send_list, base, target, *ghosts, m, w, got, one_hot)
+    )(columns, send_list, base, target, *ghosts, m, v, *carried, hot, terms, got)
     terms = lax.all_to_all(terms, ("dom", "pert"), 0, 0, tiled=True)
     hessian_probe, curvature = call(
         functools.partial(owner_kernel, parts=parts, scale=1.0 / (pert * perts)),

time: 80.2 us -> 69 us (0.86)
  starting transfers between devices: 20.3 us -> 15.1 us
  waiting for transfers between devices: 15.9 us -> 11.5 us
  Pallas kernels: 24.4 us -> 21.2 us
  blocking collectives: 13.8 us -> 15.4 us
    ppermute x16 -> x12, starting transfers between devices: 15.1 us -> 9.88 us  [rotated(): lax.ppermute(value, 'dom', [(i, (i + by) % peers) for i in range(peers)])]
    ppermute x16 -> x12, waiting for transfers between devices: 14 us -> 9.57 us  [rotated(): lax.ppermute(value, 'dom', [(i, (i + by) % peers) for i in range(peers)])]
    pallas_call x3, Pallas kernels: 14.4 us -> 11.1 us  [the longest x1 6.37 us: shards(): call(first_kernel, [shape(coupling.shape, BF16), shape((pairs, 8, LANES),...]
    all_to_all x1, blocking collectives: 13.8 us -> 15.4 us  [shards(): terms = lax.all_to_all(terms, ('dom', 'pert'), 0, 0, tiled=True)]
  transfers between devices with their start and end apart: 17 -> 13, of which waited for: 11 -> 8; matrix products, arithmetic and copies ran while one was open for 5% -> 6% of each run, Pallas kernels for 0% -> 2%
where the time goes in v3:
time: 69 us; the launch traced here: 68.6 us
  Pallas kernels  21.2 us (31%)
  blocking collectives  15.4 us (22%)
  starting transfers between devices  15.1 us (22%)
  waiting for transfers between devices  11.5 us (17%)
  local copies, waits for them, and re-layouts  4.7 us (7%)
  between operations  0.75 us (1%)
    all_to_all x1, blocking collectives, shards(): terms = lax.all_to_all(terms, ('dom', 'pert'), 0, 0, tiled=True)  15.4 us
    ppermute x12, starting transfers between devices, rotated(): lax.ppermute(value, 'dom', [(i, (i + by) % peers) for i in range(peers)])  9.88 us
    ppermute x12, waiting for transfers between devices, rotated(): lax.ppermute(value, 'dom', [(i, (i + by) % peers) for i in range(peers)])  9.57 us
    pallas_call x1, Pallas kernels, shards(): call(first_kernel, [shape(coupling.shape, BF16), shape((pairs, 8, LANES),...  6.37 us
    all_to_all x1, starting transfers between devices, shards(): got = lax.all_to_all(outgoing, 'dom', 0, 0, tiled=True)  5.18 us
    unnamed x11, local copies, waits for them, and re-layouts  4.7 us
    pallas_call x1, Pallas kernels, shards(): call(turn_kernel, [shape((pert, blocks * HALF), F32), pair_array, pair_ar...  4.53 us
    pallas_call x1, Pallas kernels, shards(): call(last_kernel, shape((parts * perts, pert + 8, LANES), BF16), 'ss' + '...  3.66 us
  transfers between devices with their start and end apart: 13, of which 8 were waited for; matrix products, arithmetic and copies ran while one was open for 6% of the time, Pallas kernels for 2%

profile of v3, /device:TPU:0, one launch (start us, length us, event | category | flops | bytes accessed | tf_op | source)
XLA Modules:
  0.0 68.6 jit_solution(131679480150632767)
XLA Ops:
  0.6 0.0 copy-start.3
  0.6 0.0 copy-start.4
  0.7 0.0 copy-start.1
  0.7 2.7 %melt.1 = (f32[64,128]{1,0:T(8,128)}, f32[8,40,128]{2,1,0:T(8,128)}) custom-call(s32[1,4,16]{2,1,0:T(4,128)} %send_ref.5, f32[64,128]{1,0:T(8,128)} %bitcast.16, s32[1,128]{1,0:T(1,128)} %bitcast.12, f32[16,128]{1,0:T(8,128)} %probe_hbm.1, bf16[64,64,128]{2,1,0:T(8,128)(2,1)} %bitcast.15), custom_call_target="tpu_custom_call" | custom-call | bytes 1048576 | tf_op jit(solution)/shard_map/melt/pallas_call | solution.py:579
  3.4 5.2 %all-to-all-start = ((f32[8,40,128]{2,1,0:T(8,128)}), f32[8,40,128]{2,1,0:T(8,128)S(1)}, u32[]{:S(2)}, u32[]{:S(2)}) async-start(f32[8,40,128]{2,1,0:T(8,128)} %get-tuple-element.30), calls=%async_computation | async-start | bytes 327680 | tf_op jit(solution)/shard_map/all_to_all | solution.py:594
  8.6 3.9 %copy.11.diag_ref = bf16[128,64,64]{2,1,0:T(8,128)(2,1)S(1)} copy(bf16[128,64,64]{0,2,1:T(8,128)(2,1)} %param.11) | data formatting | bytes 2097152 | tf_op args[3]
  12.5 1.9 %all-to-all-done.got_ref = f32[8,40,128]{2,1,0:T(8,128)S(1)} async-done(((f32[8,40,128]{2,1,0:T(8,128)}), f32[8,40,128]{2,1,0:T(8,128)S(1)}, u32[]{:S(2)}, u32[]{:S(2)}) %all-to-all-start) | async-done | bytes 163872 | tf_op jit(solution)/shard_map/all_to_all | solution.py:594
  14.4 0.0 copy-done.3
  14.4 0.0 copy-done.4
  14.4 0.0 copy-done.1
  14.4 0.0 copy-start
  14.5 0.7 %copy-done = f32[64,128]{1,0:T(8,128)S(1)} copy-done((f32[64,128]{1,0:T(8,128)S(1)}, f32[64,128]{1,0:T(8,128)}, u32[]{:S(2)}) %copy-start) | copy-done | bytes 32792
  15.2 6.4 %first.1 = (bf16[128,64,256]{2,1,0:T(8,128)(2,1)S(1)}, f32[64,8,128]{2,1,0:T(8,128)S(1)}, f32[8,128]{1,0:T(8,128)S(1)}, f32[64,16,128]{2,1,0:T(8,128)S(1)}, bf16...) custom-call(s32[4,128]{1,0:T(4,128)S(1)} %bitcast.6, ...), custom_call_target="tpu_custom_call" | custom-call | bytes 1048576 | tf_op jit(solution)/shard_map/first/pallas_call | solution.py:596
  21.6 0.0 copy-start.2
  21.6 1.1 %collective-permute-start = (bf16[13,16,128]{2,1,0:T(8,128)(2,1)S(1)}, bf16[13,16,128]{2,1,0:T(8,128)(2,1)S(1)}, u32[]{:S(2)}, u32[]{:S(2)}) collective-permute-start(bf16[13,16,128]{2,1,0:T(8,128)(2,1)S(1)} %get-tuple-element.34), channel_id=1, source_target_pairs={{0,24},{4,28},{8,0},{12,4},{16,8},{20,12},{24,16},{28,20},{1,25},{... | collective-permute-start | bytes 159752 | tf_op jit(solution)/shard_map/ppermute | solution.py:34
  22.7 0.1 collective-permute-start.1
  22.7 0.5 collective-permute-start.2
  23.2 1.0 %collective-permute-start.3 = (bf16[13,16,128]{2,1,0:T(8,128)(2,1)S(1)}, bf16[13,16,128]{2,1,0:T(8,128)(2,1)S(1)}, u32[]{:S(2)}, u32[]{:S(2)}) collective-permute-start(bf16[13,16,128]{2,1,0:T(8,128)(2,1)S(1)} %get-tuple-element.37), channel_id=1, source_target_pairs={{0,8},{4,12},{8,16},{12,20},{16,24},{20,28},{24,0},{28,4},{1,9},{5... | collective-permute-start | bytes 159752 | tf_op jit(solution)/shard_map/ppermute | solution.py:34
  24.2 1.6 %collective-permute-done.g0.v0 = bf16[13,16,128]{2,1,0:T(8,128)(2,1)S(1)} collective-permute-done((bf16[13,16,128]{2,1,0:T(8,128)(2,1)S(1)}, bf16[13,16,128]{2,1,0:T(8,128)(2,1)S(1)}, u32[]{:S(2)}, u32[]{:S(2)}) %collective-permute-start) | collective-permute-done | bytes 53280 | tf_op jit(solution)/shard_map/ppermute | solution.py:34
  25.8 0.0 collective-permute-done.1.g1.v1
  25.8 1.4 %collective-permute-done.2.g2.v2 = bf16[13,16,128]{2,1,0:T(8,128)(2,1)S(1)} collective-permute-done((bf16[13,16,128]{2,1,0:T(8,128)(2,1)S(1)}, bf16[13,16,128]{2,1,0:T(8,128)(2,1)S(1)}, u32[]{:S(2)}, u32[]{:S(2)}) %collective-permute-start.2) | collective-permute-done | bytes 53280 | tf_op jit(solution)/shard_map/ppermute | solution.py:34
  27.2 1.4 %collective-permute-done.3.g3.v3 = bf16[13,16,128]{2,1,0:T(8,128)(2,1)S(1)} collective-permute-done((bf16[13,16,128]{2,1,0:T(8,128)(2,1)S(1)}, bf16[13,16,128]{2,1,0:T(8,128)(2,1)S(1)}, u32[]{:S(2)}, u32[]{:S(2)}) %collective-permute-start.3) | collective-permute-done | bytes 53280 | tf_op jit(solution)/shard_map/ppermute | solution.py:34
  28.6 2.2 %sweep.1 = (bf16[128,16,128]{2,1,0:T(8,128)(2,1)S(1)}, bf16[8,16,128]{2,1,0:T(8,128)(2,1)S(1)}, bf16[8,16,128]{2,1,0:T(8,128)(2,1)S(1)}, bf16[8,16,128]{2,1,0:T(8,128)(2,1)S(1)}, bf16[8,16,128]{2,1,0:T(8,128)(2,1)S(1)}) custom-call(s32[4,128]{1,0:T(4,128)S(1)} %bitcast.8, s32[1,4,16]{2,1,0:T(4,128)S(1)} %copy-done.3, ...), custom_call_target="tpu_custom_call" | custom-call | bytes 1048576 | tf_op jit(solution)/shard_map/sweep/pallas_call | solution.py:619
  30.8 0.9 %collective-permute-start.4 = (bf16[8,16,128]{2,1,0:T(8,128)(2,1)S(1)}, bf16[8,16,128]{2,1,0:T(8,128)(2,1)S(1)}, u32[]{:S(2)}, u32[]{:S(2)}) collective-permute-start(bf16[8,16,128]{2,1,0:T(8,128)(2,1)S(1)} %get-tuple-element.40), channel_id=1, source_target_pairs={{0,24},{4,28},{8,0},{12,4},{16,8},{20,12},{24,16},{28,20},{1,25},{... | collective-permute-start | bytes 98312 | tf_op jit(solution)/shard_map/ppermute | solution.py:34
  31.7 1.1 %collective-permute-start.5 = (bf16[8,16,128]{2,1,0:T(8,128)(2,1)S(1)}, bf16[8,16,128]{2,1,0:T(8,128)(2,1)S(1)}, u32[]{:S(2)}, u32[]{:S(2)}) collective-permute-start(bf16[8,16,128]{2,1,0:T(8,128)(2,1)S(1)} %get-tuple-element.41), channel_id=1, source_target_pairs={{0,28},{4,0},{8,4},{12,8},{16,12},{20,16},{24,20},{28,24},{1,29},{... | collective-permute-start | bytes 98312 | tf_op jit(solution)/shard_map/ppermute | solution.py:34
  32.9 0.0 collective-permute-start.6
  32.9 0.6 collective-permute-start.7
  33.4 1.4 %collective-permute-done.4.g0 = bf16[8,16,128]{2,1,0:T(8,128)(2,1)S(1)} collective-permute-done((bf16[8,16,128]{2,1,0:T(8,128)(2,1)S(1)}, bf16[8,16,128]{2,1,0:T(8,128)(2,1)S(1)}, u32[]{:S(2)}, u32[]{:S(2)}) %collective-permute-start.4) | collective-permute-done | bytes 32800 | tf_op jit(solution)/shard_map/ppermute | solution.py:34
  34.8 0.0 collective-permute-done.5.g1
  34.8 2.3 %collective-permute-done.6.g2 = bf16[8,16,128]{2,1,0:T(8,128)(2,1)S(1)} collective-permute-done((bf16[8,16,128]{2,1,0:T(8,128)(2,1)S(1)}, bf16[8,16,128]{2,1,0:T(8,128)(2,1)S(1)}, u32[]{:S(2)}, u32[]{:S(2)}) %collective-permute-start.6) | collective-permute-done | bytes 32800 | tf_op jit(solution)/shard_map/ppermute | solution.py:34
  37.1 0.7 %collective-permute-done.7.g3 = bf16[8,16,128]{2,1,0:T(8,128)(2,1)S(1)} collective-permute-done((bf16[8,16,128]{2,1,0:T(8,128)(2,1)S(1)}, bf16[8,16,128]{2,1,0:T(8,128)(2,1)S(1)}, u32[]{:S(2)}, u32[]{:S(2)}) %collective-permute-start.7) | collective-permute-done | bytes 32800 | tf_op jit(solution)/shard_map/ppermute | solution.py:34
  37.8 0.0 copy-done.2
  37.8 4.5 %turn.1 = (f32[16,8192]{1,0:T(8,128)}, f32[64,16,128]{2,1,0:T(8,128)S(1)}, f32[64,16,128]{2,1,0:T(8,128)S(1)}, bf16[8,16,128]{2,1,0:T(8,128)(2,1)S(1)}, bf16[8,1...) custom-call(s32[4,128]{1,0:T(4,128)S(1)} %bitcast.9, ...), custom_call_target="tpu_custom_call" | custom-call | bytes 1048576 | tf_op jit(solution)/shard_map/turn/pallas_call | solution.py:623
  42.3 0.0 collective-permute-start.8
  42.3 0.1 collective-permute-start.9
  42.4 2.6 %collective-permute-start.10 = (bf16[8,16,128]{2,1,0:T(8,128)(2,1)S(1)}, bf16[8,16,128]{2,1,0:T(8,128)(2,1)S(1)}, u32[]{:S(2)}, u32[]{:S(2)}) collective-permute-start(bf16[8,16,128]{2,1,0:T(8,128)(2,1)S(1)} %get-tuple-element.49), channel_id=1, source_target_pairs={{0,28},{4,0},{8,4},{12,8},{16,12},{20,16},{24,20},{28,24},{1,29},{... | collective-permute-start | bytes 98312 | tf_op jit(solution)/shard_map/ppermute | solution.py:34
  45.0 2.0 %collective-permute-start.11 = (bf16[8,16,128]{2,1,0:T(8,128)(2,1)S(1)}, bf16[8,16,128]{2,1,0:T(8,128)(2,1)S(1)}, u32[]{:S(2)}, u32[]{:S(2)}) collective-permute-start(bf16[8,16,128]{2,1,0:T(8,128)(2,1)S(1)} %get-tuple-element.50), channel_id=1, source_target_pairs={{0,24},{4,28},{8,0},{12,4},{16,8},{20,12},{24,16},{28,20},{1,25},{... | collective-permute-start | bytes 98312 | tf_op jit(solution)/shard_map/ppermute | solution.py:34
  47.0 1.1 %prepare.1 = (bf16[1024,896]{1,0:T(8,128)(2,1)S(1)}, f32[16,128]{1,0:T(8,128)S(1)}) custom-call(s32[1,128]{1,0:T(1,128)S(1)} %bitcast.14, f32[8,128]{1,0:T(8,128)S(1)} %get-tuple-element.52.names_ref, bf16[13,16,128]{2,1,0:T(8,128)(2,1)S(1)} %collective-permute-done.g0.v0, bf16[13,16,128]{2,1,0:T(8,128)(2,1)S(1)} %collective-permute-done.1.g1.v1, ...), custom_call_target="tpu_custom_call" | custom-call | bytes 4194304 | tf_op jit(solution)/shard_map/prepare/pallas_call | solution.py:631
  48.1 0.0 collective-permute-done.8.g0
  48.1 0.0 collective-permute-done.9.g1
  48.1 0.0 collective-permute-done.10.g2
  48.1 0.8 %collective-permute-done.11.g3 = bf16[8,16,128]{2,1,0:T(8,128)(2,1)S(1)} collective-permute-done((bf16[8,16,128]{2,1,0:T(8,128)(2,1)S(1)}, bf16[8,16,128]{2,1,0:T(8,128)(2,1)S(1)}, u32[]{:S(2)}, u32[]{:S(2)}) %collective-permute-start.11) | collective-permute-done | bytes 32800 | tf_op jit(solution)/shard_map/ppermute | solution.py:34
  48.9 3.7 %last.1 = bf16[32,24,128]{2,1,0:T(8,128)(2,1)S(1)} custom-call(s32[4,128]{1,0:T(4,128)S(1)} %bitcast.10, s32[1,4,16]{2,1,0:T(4,128)S(1)} %copy-done.3, f32[64,16,128]{2,1,0:T(8,128)S(1)} %get-tuple-element.45.base_in_ref, f32[64,16,128]{2,1,0:T(8,128)S(1)} %get-tuple-element.46.target_ref, bf16[8,16,128]{2,1,0:T(8,128)(2,1)S(1)} %collective-permute-done.8.g0, ...), custom_call_target="tpu_custom_call" | custom-call | bytes 1048576 | tf_op jit(solution)/shard_map/last/pallas_call | solution.py:638
  52.6 15.4 %all_to_all.10.terms_ref = bf16[32,24,128]{2,1,0:T(8,128)(2,1)S(1)} all-to-all(bf16[32,24,128]{2,1,0:T(8,128)(2,1)S(1)} %last.1), channel_id=1, replica_groups=mesh['dom'=8,'pert'=4] {'dom','pert'}, dimensions={0} | all-to-all | bytes 393216 | tf_op jit(solution)/shard_map/all_to_all | solution.py:645
  68.0 0.6 owner.1
Async XLA Ops:
  0.6 13.8 %copy-start.3 = (s32[1,4,16]{2,1,0:T(4,128)S(1)}, s32[1,4,16]{2,1,0:T(4,128)}, u32[]{:S(2)}) copy-start(s32[1,4,16]{2,1,0:T(4,128)} %send_ref.5) | copy-start | bytes 772
  0.6 13.8 %copy-start.4 = (s32[128]{0:T(128)S(1)}, s32[128]{0:T(128)}, u32[]{:S(2)}) copy-start(s32[128]{0:T(128)} %param.15) | copy-start | bytes 1540
  0.7 13.8 %copy-start.1 = (s32[128,4]{0,1:T(4,128)S(1)}, s32[128,4]{0,1:T(4,128)}, u32[]{:S(2)}) copy-start(s32[128,4]{0,1:T(4,128)} %param.13) | copy-start | bytes 6148
  3.4 11.1 %all-to-all-start = ((f32[8,40,128]{2,1,0:T(8,128)}), f32[8,40,128]{2,1,0:T(8,128)S(1)}, u32[]{:S(2)}, u32[]{:S(2)}) async-start(f32[8,40,128]{2,1,0:T(8,128)} %get-tuple-element.30), calls=%async_computation | async-start | bytes 327680 | tf_op jit(solution)/shard_map/all_to_all | solution.py:594
  14.4 0.8 %copy-start = (f32[64,128]{1,0:T(8,128)S(1)}, f32[64,128]{1,0:T(8,128)}, u32[]{:S(2)}) copy-start(f32[64,128]{1,0:T(8,128)} %get-tuple-element.31.w_hbm.w_ref) | copy-start | bytes 98308
  21.6 16.2 %copy-start.2 = (f32[8192]{0:T(1024)S(1)}, f32[8192]{0:T(1024)}, u32[]{:S(2)}) copy-start(f32[8192]{0:T(1024)} %param.10) | copy-start | bytes 98308
  21.6 4.2 %collective-permute-start = (bf16[13,16,128]{2,1,0:T(8,128)(2,1)S(1)}, bf16[13,16,128]{2,1,0:T(8,128)(2,1)S(1)}, u32[]{:S(2)}, u32[]{:S(2)}) collective-permute-start(bf16[13,16,128]{2,1,0:T(8,128)(2,1)S(1)} %get-tuple-element.34), channel_id=1, source_target_pairs={{0,24},{4,28},{8,0},{12,4},{16,8},{20,12},{24,16},{28,20},{1,25},{... | collective-permute-start | bytes 159752 | tf_op jit(solution)/shard_map/ppermute | solution.py:34
  22.7 3.1 %collective-permute-start.1 = (bf16[13,16,128]{2,1,0:T(8,128)(2,1)S(1)}, bf16[13,16,128]{2,1,0:T(8,128)(2,1)S(1)}, u32[]{:S(2)}, u32[]{:S(2)}) collective-permute-start(bf16[13,16,128]{2,1,0:T(8,128)(2,1)S(1)} %get-tuple-element.35), channel_id=1, source_target_pairs={{0,28},{4,0},{8,4},{12,8},{16,12},{20,16},{24,20},{28,24},{1,29},{... | collective-permute-start | bytes 159752 | tf_op jit(solution)/shard_map/ppermute | solution.py:34
  22.7 4.5 %collective-permute-start.2 = (bf16[13,16,128]{2,1,0:T(8,128)(2,1)S(1)}, bf16[13,16,128]{2,1,0:T(8,128)(2,1)S(1)}, u32[]{:S(2)}, u32[]{:S(2)}) collective-permute-start(bf16[13,16,128]{2,1,0:T(8,128)(2,1)S(1)} %get-tuple-element.36), channel_id=1, source_target_pairs={{0,4},{4,8},{8,12},{12,16},{16,20},{20,24},{24,28},{28,0},{1,5},{5... | collective-permute-start | bytes 159752 | tf_op jit(solution)/shard_map/ppermute | solution.py:34
  23.2 5.4 %collective-permute-start.3 = (bf16[13,16,128]{2,1,0:T(8,128)(2,1)S(1)}, bf16[13,16,128]{2,1,0:T(8,128)(2,1)S(1)}, u32[]{:S(2)}, u32[]{:S(2)}) collective-permute-start(bf16[13,16,128]{2,1,0:T(8,128)(2,1)S(1)} %get-tuple-element.37), channel_id=1, source_target_pairs={{0,8},{4,12},{8,16},{12,20},{16,24},{20,28},{24,0},{28,4},{1,9},{5... | collective-permute-start | bytes 159752 | tf_op jit(solution)/shard_map/ppermute | solution.py:34
  30.8 4.0 %collective-permute-start.4 = (bf16[8,16,128]{2,1,0:T(8,128)(2,1)S(1)}, bf16[8,16,128]{2,1,0:T(8,128)(2,1)S(1)}, u32[]{:S(2)}, u32[]{:S(2)}) collective-permute-start(bf16[8,16,128]{2,1,0:T(8,128)(2,1)S(1)} %get-tuple-element.40), channel_id=1, source_target_pairs={{0,24},{4,28},{8,0},{12,4},{16,8},{20,12},{24,16},{28,20},{1,25},{... | collective-permute-start | bytes 98312 | tf_op jit(solution)/shard_map/ppermute | solution.py:34
  31.7 3.1 %collective-permute-start.5 = (bf16[8,16,128]{2,1,0:T(8,128)(2,1)S(1)}, bf16[8,16,128]{2,1,0:T(8,128)(2,1)S(1)}, u32[]{:S(2)}, u32[]{:S(2)}) collective-permute-start(bf16[8,16,128]{2,1,0:T(8,128)(2,1)S(1)} %get-tuple-element.41), channel_id=1, source_target_pairs={{0,28},{4,0},{8,4},{12,8},{16,12},{20,16},{24,20},{28,24},{1,29},{... | collective-permute-start | bytes 98312 | tf_op jit(solution)/shard_map/ppermute | solution.py:34
  32.9 4.2 %collective-permute-start.6 = (bf16[8,16,128]{2,1,0:T(8,128)(2,1)S(1)}, bf16[8,16,128]{2,1,0:T(8,128)(2,1)S(1)}, u32[]{:S(2)}, u32[]{:S(2)}) collective-permute-start(bf16[8,16,128]{2,1,0:T(8,128)(2,1)S(1)} %get-tuple-element.42), channel_id=1, source_target_pairs={{0,4},{4,8},{8,12},{12,16},{16,20},{20,24},{24,28},{28,0},{1,5},{5... | collective-permute-start | bytes 98312 | tf_op jit(solution)/shard_map/ppermute | solution.py:34
  32.9 4.9 %collective-permute-start.7 = (bf16[8,16,128]{2,1,0:T(8,128)(2,1)S(1)}, bf16[8,16,128]{2,1,0:T(8,128)(2,1)S(1)}, u32[]{:S(2)}, u32[]{:S(2)}) collective-permute-start(bf16[8,16,128]{2,1,0:T(8,128)(2,1)S(1)} %get-tuple-element.43), channel_id=1, source_target_pairs={{0,8},{4,12},{8,16},{12,20},{16,24},{20,28},{24,0},{28,4},{1,9},{5... | collective-permute-start | bytes 98312 | tf_op jit(solution)/shard_map/ppermute | solution.py:34
  42.3 5.8 %collective-permute-start.8 = (bf16[8,16,128]{2,1,0:T(8,128)(2,1)S(1)}, bf16[8,16,128]{2,1,0:T(8,128)(2,1)S(1)}, u32[]{:S(2)}, u32[]{:S(2)}) collective-permute-start(bf16[8,16,128]{2,1,0:T(8,128)(2,1)S(1)} %get-tuple-element.47), channel_id=1, source_target_pairs={{0,8},{4,12},{8,16},{12,20},{16,24},{20,28},{24,0},{28,4},{1,9},{5... | collective-permute-start | bytes 98312 | tf_op jit(solution)/shard_map/ppermute | solution.py:34
  42.3 5.8 %collective-permute-start.9 = (bf16[8,16,128]{2,1,0:T(8,128)(2,1)S(1)}, bf16[8,16,128]{2,1,0:T(8,128)(2,1)S(1)}, u32[]{:S(2)}, u32[]{:S(2)}) collective-permute-start(bf16[8,16,128]{2,1,0:T(8,128)(2,1)S(1)} %get-tuple-element.48), channel_id=1, source_target_pairs={{0,4},{4,8},{8,12},{12,16},{16,20},{20,24},{24,28},{28,0},{1,5},{5... | collective-permute-start | bytes 98312 | tf_op jit(solution)/shard_map/ppermute | solution.py:34
  42.4 5.7 %collective-permute-start.10 = (bf16[8,16,128]{2,1,0:T(8,128)(2,1)S(1)}, bf16[8,16,128]{2,1,0:T(8,128)(2,1)S(1)}, u32[]{:S(2)}, u32[]{:S(2)}) collective-permute-start(bf16[8,16,128]{2,1,0:T(8,128)(2,1)S(1)} %get-tuple-element.49), channel_id=1, source_target_pairs={{0,28},{4,0},{8,4},{12,8},{16,12},{20,16},{24,20},{28,24},{1,29},{... | collective-permute-start | bytes 98312 | tf_op jit(solution)/shard_map/ppermute | solution.py:34
  45.0 3.9 %collective-permute-start.11 = (bf16[8,16,128]{2,1,0:T(8,128)(2,1)S(1)}, bf16[8,16,128]{2,1,0:T(8,128)(2,1)S(1)}, u32[]{:S(2)}, u32[]{:S(2)}) collective-permute-start(bf16[8,16,128]{2,1,0:T(8,128)(2,1)S(1)} %get-tuple-element.50), channel_id=1, source_target_pairs={{0,24},{4,28},{8,0},{12,4},{16,8},{20,12},{24,16},{28,20},{1,25},{... | collective-permute-start | bytes 98312 | tf_op jit(solution)/shard_map/ppermute | solution.py:34

commit v4 on v3

--- a/solution.py
+++ b/solution.py
@@ -150,6 +150,31 @@
             msg_ref[pair] = jnp.where(low, even, odd)
 
 
+def product_kernel(diag_ref, coupling_hbm, m_hbm, coupling_ref, m_ref, in_sems, out_sems):
+    chunks = in_sems.shape[0]
+    size = diag_ref.shape[0] // chunks
+    spans = [pl.ds(chunk * size, size) for chunk in range(chunks)]
+    loads = [
+        pltpu.make_async_copy(coupling_hbm.at[span], coupling_ref.at[span], in_sems.at[chunk])
+        for chunk, span in enumerate(spans)
+    ]
+    stores = [
+        pltpu.make_async_copy(m_ref.at[span], m_hbm.at[span], out_sems.at[chunk])
+        for chunk, span in enumerate(spans)
+    ]
+    for load in loads:
+        load.start()
+    for chunk in range(chunks):
+        loads[chunk].wait()
+        for block in range(chunk * size, (chunk + 1) * size):
+            m_ref[block] = jnp.dot(
+                diag_ref[block], coupling_ref[block], preferred_element_type=F32
+            ).astype(BF16)
+        stores[chunk].start()
+    for store in stores:
+        store.wait()
+
+
 def patches_of_columns(columns_ref, ids):
     columns = jnp.concatenate([columns_ref[...], columns_ref[...]], axis=0)
     here = jnp.broadcast_to(ids[:, :LANES], columns.shape)
@@ -162,24 +187,19 @@
 
 
 def first_kernel(
-    cols_ref, send_ref, patch_ref, columns_ref, got_ref, w_hbm, diag_ref, coupling_hbm,
+    cols_ref, send_ref, patch_ref, columns_ref, got_ref, w_hbm, m_hbm,
     m_ref, v_ref, names_ref, t1_ref, t2_ref, o0, o1, o2, o3,
-    ext_ref, row_ref, w_ref, coupling_ref, w_sem, sems,
+    ext_ref, row_ref, w_ref, w_sem, sems,
 ):
     w_copy = pltpu.make_async_copy(w_hbm, w_ref, w_sem)
     w_copy.start()
     chunks = sems.shape[0]
-    size = diag_ref.shape[0] // chunks
-    copies = [
-        pltpu.make_async_copy(
-            coupling_hbm.at[chunk * size : (chunk + 1) * size],
-            coupling_ref.at[chunk * size : (chunk + 1) * size],
-            sems.at[chunk],
-        )
-        for chunk in range(chunks)
-    ]
-    for copy in copies:
-        copy.start()
+    size = m_ref.shape[0] // chunks
+    copies = []
+    for chunk in range(chunks):
+        span = pl.ds(chunk * size, size)
+        copies.append(pltpu.make_async_copy(m_hbm.at[span], m_ref.at[span], sems.at[chunk]))
+        copies[-1].start()
     pert = t1_ref.shape[1]
     capacity = send_ref.shape[2]
     blocks = cols_ref.shape[1]
@@ -245,13 +265,8 @@
             spread = jnp.broadcast_to(ghost_picked[:, place : place + 1], (pert, LANES))
             ext_ref[blocks + place] = (spread * row).astype(BF16)
 
-    for chunk, copy in enumerate(copies):
+    for copy in copies:
         copy.wait()
-        for block in range(chunk * size, (chunk + 1) * size):
-            m_ref[block] = jnp.dot(
-                diag_ref[block], coupling_ref[block], preferred_element_type=F32
-            ).astype(BF16)
-
     low8 = low_half((8, LANES))
     masks = [(sub % 4 == k) & (low8 if k % 2 == 0 else ~low8) for k in range(4)]
     nothing = jnp.zeros((8, LANES), F32)
@@ -542,12 +557,12 @@
     curve_ref[...] = (curve[0:1] + curve[1:2]) * scale
 
 
-def call(body, outs, spaces, scratch=(), name=None, flops=0, moved=1 << 20, limit=12):
+def call(body, outs, spaces, scratch=(), name=None, flops=0, moved=1 << 20, limit=12, out_specs=None):
     return pl.pallas_call(
         body,
         out_shape=outs,
         in_specs=[{"s": SMEM, "v": VMEM, "h": HBM}[s] for s in spaces],
-        out_specs=jax.tree.map(lambda _: VMEM, outs),
+        out_specs=out_specs or jax.tree.map(lambda _: VMEM, outs),
         scratch_shapes=list(scratch),
         compiler_params=pltpu.CompilerParams(vmem_limit_bytes=limit * MIB),
         name=name,
@@ -593,6 +608,17 @@
     )(send_list, melt, patch, probes, jnp.transpose(diag_inverse, (1, 2, 0)))
     got = lax.all_to_all(outgoing, "dom", 0, 0, tiled=True)
     wide = [shape((capacity // 2 + capacity // 4 + 1, pert, LANES), BF16)] * 4
+    m = call(
+        product_kernel,
+        shape(coupling.shape, BF16),
+        "vh",
+        [pltpu.VMEM(coupling.shape, BF16)] * 2 + [pltpu.SemaphoreType.DMA((8,))] * 2,
+        out_specs=HBM,
+        name="product",
+        flops=1 << 28,
+        moved=10 << 20,
+        limit=50,
+    )(diag_inverse, coupling)
     m, v, names, t1, state, *out = call(
         first_kernel,
         [
@@ -603,18 +629,17 @@
             block_array,
         ]
         + wide,
-        "ssvvvhvh",
+        "ssvvvhh",
         [
             ext,
             pltpu.VMEM((blocks + 4 * capacity, LANES), F32),
             pltpu.VMEM((pairs, LANES), F32),
-            pltpu.VMEM(coupling.shape, BF16),
             pltpu.SemaphoreType.DMA,
             pltpu.SemaphoreType.DMA((8,)),
         ],
         name="first",
-        limit=46,
-    )(columns, send_list, patch, columns, got, w, diag_inverse, coupling)
+        limit=47,
+    )(columns, send_list, patch, columns, got, w, m)
     carried = [rotated(x, o) for x, o in zip(out, OFFSET_LIST)]
     state, *out = call(
         sweep_kernel, [block_array] + msgs, "ssvvvvvvv", [ext], name="sweep"

time: 69 us -> 70.5 us (1.022)
  Pallas kernels: 21.2 us -> 23.9 us
  waiting for transfers between devices: 11.5 us -> 9.38 us
  starting transfers between devices: 15.1 us -> 17 us
  local copies, waits for them, and re-layouts: 4.7 us -> 3.96 us
    pallas_call x0 -> x1, Pallas kernels: none -> 4.19 us  [shards(): call(product_kernel, shape(coupling.shape, BF16), 'vh', [pltpu.VMEM(coupl...]
    all_to_all x1, waiting for transfers between devices: 1.94 us -> 0.01 us  [shards(): got = lax.all_to_all(outgoing, 'dom', 0, 0, tiled=True)]
    ppermute x12, starting transfers between devices: 9.88 us -> 11.8 us  [rotated(): lax.ppermute(value, 'dom', [(i, (i + by) % peers) for i in range(peers)])]
    pallas_call x1, Pallas kernels: 6.37 us -> 4.89 us  [shards(): call(first_kernel, [shape(coupling.shape, BF16), shape((pairs, 8, LANES),...]
    unnamed x11, local copies, waits for them, and re-layouts: 4.7 us -> 3.96 us
  transfers between devices with their start and end apart: 13 -> 13, of which waited for: 8 -> 8; matrix products, arithmetic and copies ran while one was open for 6% -> 6% of each run, Pallas kernels for 2% -> 8%
where the time goes in v4:
time: 70.5 us; the launch traced here: 70.2 us
  Pallas kernels  23.9 us (34%)
  starting transfers between devices  17 us (24%)
  blocking collectives  15.2 us (22%)
  waiting for transfers between devices  9.38 us (13%)
  local copies, waits for them, and re-layouts  3.96 us (6%)
  between operations  0.79 us (1%)
    all_to_all x1, blocking collectives, shards(): terms = lax.all_to_all(terms, ('dom', 'pert'), 0, 0, tiled=True)  15.2 us
    ppermute x12, starting transfers between devices, rotated(): lax.ppermute(value, 'dom', [(i, (i + by) % peers) for i in range(peers)])  11.8 us
    ppermute x12, waiting for transfers between devices, rotated(): lax.ppermute(value, 'dom', [(i, (i + by) % peers) for i in range(peers)])  9.38 us
    all_to_all x1, starting transfers between devices, shards(): got = lax.all_to_all(outgoing, 'dom', 0, 0, tiled=True)  5.19 us
    pallas_call x1, Pallas kernels, shards(): call(first_kernel, [shape(coupling.shape, BF16), shape((pairs, 8, LANES),...  4.89 us
    pallas_call x1, Pallas kernels, shards(): call(turn_kernel, [shape((pert, blocks * HALF), F32), pair_array, pair_ar...  4.53 us
    pallas_call x1, Pallas kernels, shards(): call(product_kernel, shape(coupling.shape, BF16), 'vh', [pltpu.VMEM(coupl...  4.19 us
    unnamed x11, local copies, waits for them, and re-layouts  3.96 us
  transfers between devices with their start and end apart: 13, of which 8 were waited for; matrix products, arithmetic and copies ran while one was open for 6% of the time, Pallas kernels for 8%

profile of v4, /device:TPU:0, one launch (start us, length us, event | category | flops | bytes accessed | tf_op | source)
XLA Modules:
  0.0 70.2 jit_solution(11667492574779357800)
XLA Ops:
  0.6 2.7 %melt.1 = (f32[64,128]{1,0:T(8,128)}, f32[8,40,128]{2,1,0:T(8,128)}) custom-call(s32[1,4,16]{2,1,0:T(4,128)} %send_ref.5, f32[64,128]{1,0:T(8,128)} %bitcast.16, s32[1,128]{1,0:T(1,128)} %bitcast.12, f32[16,128]{1,0:T(8,128)} %probe_hbm.1, bf16[64,64,128]{2,1,0:T(8,128)(2,1)} %bitcast.15), custom_call_target="tpu_custom_call" | custom-call | bytes 1048576 | tf_op jit(solution)/shard_map/melt/pallas_call | solution.py:594
  3.3 5.2 %all-to-all-start = ((f32[8,40,128]{2,1,0:T(8,128)}), f32[8,40,128]{2,1,0:T(8,128)S(1)}, u32[]{:S(2)}, u32[]{:S(2)}) async-start(f32[8,40,128]{2,1,0:T(8,128)} %get-tuple-element.30), calls=%async_computation | async-start | bytes 327680 | tf_op jit(solution)/shard_map/all_to_all | solution.py:609
  8.5 3.9 %copy.11.diag_ref = bf16[128,64,64]{2,1,0:T(8,128)(2,1)S(1)} copy(bf16[128,64,64]{0,2,1:T(8,128)(2,1)} %param.11) | data formatting | bytes 2097152 | tf_op args[3]
  12.4 0.0 copy-start
  12.5 0.0 copy-start.1
  12.5 0.0 copy-start.2
  12.5 0.0 copy-start.4
  12.5 4.2 %product.1.m_hbm = bf16[128,64,256]{2,1,0:T(8,128)(2,1)} custom-call(bf16[128,64,64]{2,1,0:T(8,128)(2,1)S(1)} %copy.11.diag_ref, bf16[128,64,256]{2,1,0:T(8,128)(2,1)} %coupling_hbm.1), custom_call_target="tpu_custom_call" | custom-call | flops 268435456 | bytes 10485760 | tf_op jit(solution)/shard_map/product/pallas_call | solution.py:611
  16.7 0.0 all-to-all-done.got_ref
  16.7 0.0 copy-done
  16.7 0.0 copy-done.1
  16.7 0.0 copy-done.2
  16.7 0.0 copy-done.4
  16.7 0.0 copy-start.3
  16.8 4.9 %first.1 = (bf16[128,64,256]{2,1,0:T(8,128)(2,1)S(1)}, f32[64,8,128]{2,1,0:T(8,128)S(1)}, f32[8,128]{1,0:T(8,128)S(1)}, f32[64,16,128]{2,1,0:T(8,128)S(1)}, bf16...) custom-call(s32[4,128]{1,0:T(4,128)S(1)} %bitcast.6, ...), custom_call_target="tpu_custom_call" | custom-call | bytes 1048576 | tf_op jit(solution)/shard_map/first/pallas_call | solution.py:622
  21.7 3.0 %collective-permute-start = (bf16[13,16,128]{2,1,0:T(8,128)(2,1)S(1)}, bf16[13,16,128]{2,1,0:T(8,128)(2,1)S(1)}, u32[]{:S(2)}, u32[]{:S(2)}) collective-permute-start(bf16[13,16,128]{2,1,0:T(8,128)(2,1)S(1)} %get-tuple-element.34), channel_id=1, source_target_pairs={{0,24},{4,28},{8,0},{12,4},{16,8},{20,12},{24,16},{28,20},{1,25},{... | collective-permute-start | bytes 159752 | tf_op jit(solution)/shard_map/ppermute | solution.py:34
  24.6 0.1 collective-permute-start.1
  24.7 0.5 collective-permute-start.2
  25.1 1.0 %collective-permute-start.3 = (bf16[13,16,128]{2,1,0:T(8,128)(2,1)S(1)}, bf16[13,16,128]{2,1,0:T(8,128)(2,1)S(1)}, u32[]{:S(2)}, u32[]{:S(2)}) collective-permute-start(bf16[13,16,128]{2,1,0:T(8,128)(2,1)S(1)} %get-tuple-element.37), channel_id=1, source_target_pairs={{0,8},{4,12},{8,16},{12,20},{16,24},{20,28},{24,0},{28,4},{1,9},{5... | collective-permute-start | bytes 159752 | tf_op jit(solution)/shard_map/ppermute | solution.py:34
  26.2 0.2 collective-permute-done.g0.v0
  26.4 0.6 collective-permute-done.1.g1.v1
  27.0 2.1 %collective-permute-done.2.g2.v2 = bf16[13,16,128]{2,1,0:T(8,128)(2,1)S(1)} collective-permute-done((bf16[13,16,128]{2,1,0:T(8,128)(2,1)S(1)}, bf16[13,16,128]{2,1,0:T(8,128)(2,1)S(1)}, u32[]{:S(2)}, u32[]{:S(2)}) %collective-permute-start.2) | collective-permute-done | bytes 53280 | tf_op jit(solution)/shard_map/ppermute | solution.py:34
  29.1 1.4 %collective-permute-done.3.g3.v3 = bf16[13,16,128]{2,1,0:T(8,128)(2,1)S(1)} collective-permute-done((bf16[13,16,128]{2,1,0:T(8,128)(2,1)S(1)}, bf16[13,16,128]{2,1,0:T(8,128)(2,1)S(1)}, u32[]{:S(2)}, u32[]{:S(2)}) %collective-permute-start.3) | collective-permute-done | bytes 53280 | tf_op jit(solution)/shard_map/ppermute | solution.py:34
  30.6 2.2 %sweep.1 = (bf16[128,16,128]{2,1,0:T(8,128)(2,1)S(1)}, bf16[8,16,128]{2,1,0:T(8,128)(2,1)S(1)}, bf16[8,16,128]{2,1,0:T(8,128)(2,1)S(1)}, bf16[8,16,128]{2,1,0:T(8,128)(2,1)S(1)}, bf16[8,16,128]{2,1,0:T(8,128)(2,1)S(1)}) custom-call(s32[4,128]{1,0:T(4,128)S(1)} %bitcast.8, s32[1,4,16]{2,1,0:T(4,128)S(1)} %copy-done.2, ...), custom_call_target="tpu_custom_call" | custom-call | bytes 1048576 | tf_op jit(solution)/shard_map/sweep/pallas_call | solution.py:644
  32.8 0.2 collective-permute-start.4
  33.0 1.4 %collective-permute-start.5 = (bf16[8,16,128]{2,1,0:T(8,128)(2,1)S(1)}, bf16[8,16,128]{2,1,0:T(8,128)(2,1)S(1)}, u32[]{:S(2)}, u32[]{:S(2)}) collective-permute-start(bf16[8,16,128]{2,1,0:T(8,128)(2,1)S(1)} %get-tuple-element.41), channel_id=1, source_target_pairs={{0,28},{4,0},{8,4},{12,8},{16,12},{20,16},{24,20},{28,24},{1,29},{... | collective-permute-start | bytes 98312 | tf_op jit(solution)/shard_map/ppermute | solution.py:34
  34.4 0.0 collective-permute-start.6
  34.4 1.0 %collective-permute-start.7 = (bf16[8,16,128]{2,1,0:T(8,128)(2,1)S(1)}, bf16[8,16,128]{2,1,0:T(8,128)(2,1)S(1)}, u32[]{:S(2)}, u32[]{:S(2)}) collective-permute-start(bf16[8,16,128]{2,1,0:T(8,128)(2,1)S(1)} %get-tuple-element.43), channel_id=1, source_target_pairs={{0,8},{4,12},{8,16},{12,20},{16,24},{20,28},{24,0},{28,4},{1,9},{5... | collective-permute-start | bytes 98312 | tf_op jit(solution)/shard_map/ppermute | solution.py:34
  35.4 1.4 %collective-permute-done.4.g0 = bf16[8,16,128]{2,1,0:T(8,128)(2,1)S(1)} collective-permute-done((bf16[8,16,128]{2,1,0:T(8,128)(2,1)S(1)}, bf16[8,16,128]{2,1,0:T(8,128)(2,1)S(1)}, u32[]{:S(2)}, u32[]{:S(2)}) %collective-permute-start.4) | collective-permute-done | bytes 32800 | tf_op jit(solution)/shard_map/ppermute | solution.py:34
  36.7 0.0 collective-permute-done.5.g1
  36.7 1.9 %collective-permute-done.6.g2 = bf16[8,16,128]{2,1,0:T(8,128)(2,1)S(1)} collective-permute-done((bf16[8,16,128]{2,1,0:T(8,128)(2,1)S(1)}, bf16[8,16,128]{2,1,0:T(8,128)(2,1)S(1)}, u32[]{:S(2)}, u32[]{:S(2)}) %collective-permute-start.6) | collective-permute-done | bytes 32800 | tf_op jit(solution)/shard_map/ppermute | solution.py:34
  38.6 0.7 collective-permute-done.7.g3
  39.3 0.0 copy-done.3
  39.3 4.5 %turn.1 = (f32[16,8192]{1,0:T(8,128)}, f32[64,16,128]{2,1,0:T(8,128)S(1)}, f32[64,16,128]{2,1,0:T(8,128)S(1)}, bf16[8,16,128]{2,1,0:T(8,128)(2,1)S(1)}, bf16[8,1...) custom-call(s32[4,128]{1,0:T(4,128)S(1)} %bitcast.9, ...), custom_call_target="tpu_custom_call" | custom-call | bytes 1048576 | tf_op jit(solution)/shard_map/turn/pallas_call | solution.py:648
  43.9 0.0 collective-permute-start.8
  43.9 0.5 collective-permute-start.9
  44.4 2.2 %collective-permute-start.10 = (bf16[8,16,128]{2,1,0:T(8,128)(2,1)S(1)}, bf16[8,16,128]{2,1,0:T(8,128)(2,1)S(1)}, u32[]{:S(2)}, u32[]{:S(2)}) collective-permute-start(bf16[8,16,128]{2,1,0:T(8,128)(2,1)S(1)} %get-tuple-element.49), channel_id=1, source_target_pairs={{0,28},{4,0},{8,4},{12,8},{16,12},{20,16},{24,20},{28,24},{1,29},{... | collective-permute-start | bytes 98312 | tf_op jit(solution)/shard_map/ppermute | solution.py:34
  46.5 2.0 %collective-permute-start.11 = (bf16[8,16,128]{2,1,0:T(8,128)(2,1)S(1)}, bf16[8,16,128]{2,1,0:T(8,128)(2,1)S(1)}, u32[]{:S(2)}, u32[]{:S(2)}) collective-permute-start(bf16[8,16,128]{2,1,0:T(8,128)(2,1)S(1)} %get-tuple-element.50), channel_id=1, source_target_pairs={{0,24},{4,28},{8,0},{12,4},{16,8},{20,12},{24,16},{28,20},{1,25},{... | collective-permute-start | bytes 98312 | tf_op jit(solution)/shard_map/ppermute | solution.py:34
  48.5 1.1 %prepare.1 = (bf16[1024,896]{1,0:T(8,128)(2,1)S(1)}, f32[16,128]{1,0:T(8,128)S(1)}) custom-call(s32[1,128]{1,0:T(1,128)S(1)} %bitcast.14, f32[8,128]{1,0:T(8,128)S(1)} %get-tuple-element.52.names_ref, bf16[13,16,128]{2,1,0:T(8,128)(2,1)S(1)} %collective-permute-done.g0.v0, bf16[13,16,128]{2,1,0:T(8,128)(2,1)S(1)} %collective-permute-done.1.g1.v1, ...), custom_call_target="tpu_custom_call" | custom-call | bytes 4194304 | tf_op jit(solution)/shard_map/prepare/pallas_call | solution.py:656
  49.6 0.0 collective-permute-done.8.g0
  49.7 0.0 collective-permute-done.9.g1
  49.7 0.0 collective-permute-done.10.g2
  49.7 1.0 %collective-permute-done.11.g3 = bf16[8,16,128]{2,1,0:T(8,128)(2,1)S(1)} collective-permute-done((bf16[8,16,128]{2,1,0:T(8,128)(2,1)S(1)}, bf16[8,16,128]{2,1,0:T(8,128)(2,1)S(1)}, u32[]{:S(2)}, u32[]{:S(2)}) %collective-permute-start.11) | collective-permute-done | bytes 32800 | tf_op jit(solution)/shard_map/ppermute | solution.py:34
  50.7 3.7 %last.1 = bf16[32,24,128]{2,1,0:T(8,128)(2,1)S(1)} custom-call(s32[4,128]{1,0:T(4,128)S(1)} %bitcast.10, s32[1,4,16]{2,1,0:T(4,128)S(1)} %copy-done.2, f32[64,16,128]{2,1,0:T(8,128)S(1)} %get-tuple-element.45.base_in_ref, f32[64,16,128]{2,1,0:T(8,128)S(1)} %get-tuple-element.46.target_ref, bf16[8,16,128]{2,1,0:T(8,128)(2,1)S(1)} %collective-permute-done.8.g0, ...), custom_call_target="tpu_custom_call" | custom-call | bytes 1048576 | tf_op jit(solution)/shard_map/last/pallas_call | solution.py:663
  54.4 15.2 %all_to_all.10.terms_ref = bf16[32,24,128]{2,1,0:T(8,128)(2,1)S(1)} all-to-all(bf16[32,24,128]{2,1,0:T(8,128)(2,1)S(1)} %last.1), channel_id=1, replica_groups=mesh['dom'=8,'pert'=4] {'dom','pert'}, dimensions={0} | all-to-all | bytes 393216 | tf_op jit(solution)/shard_map/all_to_all | solution.py:670
  69.6 0.6 owner.1
Async XLA Ops:
  3.3 13.4 %all-to-all-start = ((f32[8,40,128]{2,1,0:T(8,128)}), f32[8,40,128]{2,1,0:T(8,128)S(1)}, u32[]{:S(2)}, u32[]{:S(2)}) async-start(f32[8,40,128]{2,1,0:T(8,128)} %get-tuple-element.30), calls=%async_computation | async-start | bytes 327680 | tf_op jit(solution)/shard_map/all_to_all | solution.py:609
  12.4 4.3 %copy-start = (f32[64,128]{1,0:T(8,128)S(1)}, f32[64,128]{1,0:T(8,128)}, u32[]{:S(2)}) copy-start(f32[64,128]{1,0:T(8,128)} %get-tuple-element.31.w_hbm.w_ref) | copy-start | bytes 98308
  12.5 4.3 %copy-start.1 = (s32[128,4]{0,1:T(4,128)S(1)}, s32[128,4]{0,1:T(4,128)}, u32[]{:S(2)}) copy-start(s32[128,4]{0,1:T(4,128)} %param.13) | copy-start | bytes 6148
  12.5 4.3 %copy-start.2 = (s32[1,4,16]{2,1,0:T(4,128)S(1)}, s32[1,4,16]{2,1,0:T(4,128)}, u32[]{:S(2)}) copy-start(s32[1,4,16]{2,1,0:T(4,128)} %send_ref.5) | copy-start | bytes 772
  12.5 4.3 %copy-start.4 = (s32[128]{0:T(128)S(1)}, s32[128]{0:T(128)}, u32[]{:S(2)}) copy-start(s32[128]{0:T(128)} %param.15) | copy-start | bytes 1540
  16.7 22.6 %copy-start.3 = (f32[8192]{0:T(1024)S(1)}, f32[8192]{0:T(1024)}, u32[]{:S(2)}) copy-start(f32[8192]{0:T(1024)} %param.10) | copy-start | bytes 98308
  21.7 4.7 %collective-permute-start = (bf16[13,16,128]{2,1,0:T(8,128)(2,1)S(1)}, bf16[13,16,128]{2,1,0:T(8,128)(2,1)S(1)}, u32[]{:S(2)}, u32[]{:S(2)}) collective-permute-start(bf16[13,16,128]{2,1,0:T(8,128)(2,1)S(1)} %get-tuple-element.34), channel_id=1, source_target_pairs={{0,24},{4,28},{8,0},{12,4},{16,8},{20,12},{24,16},{28,20},{1,25},{... | collective-permute-start | bytes 159752 | tf_op jit(solution)/shard_map/ppermute | solution.py:34
  24.6 2.4 %collective-permute-start.1 = (bf16[13,16,128]{2,1,0:T(8,128)(2,1)S(1)}, bf16[13,16,128]{2,1,0:T(8,128)(2,1)S(1)}, u32[]{:S(2)}, u32[]{:S(2)}) collective-permute-start(bf16[13,16,128]{2,1,0:T(8,128)(2,1)S(1)} %get-tuple-element.35), channel_id=1, source_target_pairs={{0,28},{4,0},{8,4},{12,8},{16,12},{20,16},{24,20},{28,24},{1,29},{... | collective-permute-start | bytes 159752 | tf_op jit(solution)/shard_map/ppermute | solution.py:34
  24.7 4.5 %collective-permute-start.2 = (bf16[13,16,128]{2,1,0:T(8,128)(2,1)S(1)}, bf16[13,16,128]{2,1,0:T(8,128)(2,1)S(1)}, u32[]{:S(2)}, u32[]{:S(2)}) collective-permute-start(bf16[13,16,128]{2,1,0:T(8,128)(2,1)S(1)} %get-tuple-element.36), channel_id=1, source_target_pairs={{0,4},{4,8},{8,12},{12,16},{16,20},{20,24},{24,28},{28,0},{1,5},{5... | collective-permute-start | bytes 159752 | tf_op jit(solution)/shard_map/ppermute | solution.py:34
  25.1 5.4 %collective-permute-start.3 = (bf16[13,16,128]{2,1,0:T(8,128)(2,1)S(1)}, bf16[13,16,128]{2,1,0:T(8,128)(2,1)S(1)}, u32[]{:S(2)}, u32[]{:S(2)}) collective-permute-start(bf16[13,16,128]{2,1,0:T(8,128)(2,1)S(1)} %get-tuple-element.37), channel_id=1, source_target_pairs={{0,8},{4,12},{8,16},{12,20},{16,24},{20,28},{24,0},{28,4},{1,9},{5... | collective-permute-start | bytes 159752 | tf_op jit(solution)/shard_map/ppermute | solution.py:34
  32.8 4.0 %collective-permute-start.4 = (bf16[8,16,128]{2,1,0:T(8,128)(2,1)S(1)}, bf16[8,16,128]{2,1,0:T(8,128)(2,1)S(1)}, u32[]{:S(2)}, u32[]{:S(2)}) collective-permute-start(bf16[8,16,128]{2,1,0:T(8,128)(2,1)S(1)} %get-tuple-element.40), channel_id=1, source_target_pairs={{0,24},{4,28},{8,0},{12,4},{16,8},{20,12},{24,16},{28,20},{1,25},{... | collective-permute-start | bytes 98312 | tf_op jit(solution)/shard_map/ppermute | solution.py:34
  33.0 3.8 %collective-permute-start.5 = (bf16[8,16,128]{2,1,0:T(8,128)(2,1)S(1)}, bf16[8,16,128]{2,1,0:T(8,128)(2,1)S(1)}, u32[]{:S(2)}, u32[]{:S(2)}) collective-permute-start(bf16[8,16,128]{2,1,0:T(8,128)(2,1)S(1)} %get-tuple-element.41), channel_id=1, source_target_pairs={{0,28},{4,0},{8,4},{12,8},{16,12},{20,16},{24,20},{28,24},{1,29},{... | collective-permute-start | bytes 98312 | tf_op jit(solution)/shard_map/ppermute | solution.py:34
  34.4 4.2 %collective-permute-start.6 = (bf16[8,16,128]{2,1,0:T(8,128)(2,1)S(1)}, bf16[8,16,128]{2,1,0:T(8,128)(2,1)S(1)}, u32[]{:S(2)}, u32[]{:S(2)}) collective-permute-start(bf16[8,16,128]{2,1,0:T(8,128)(2,1)S(1)} %get-tuple-element.42), channel_id=1, source_target_pairs={{0,4},{4,8},{8,12},{12,16},{16,20},{20,24},{24,28},{28,0},{1,5},{5... | collective-permute-start | bytes 98312 | tf_op jit(solution)/shard_map/ppermute | solution.py:34
  34.4 4.9 %collective-permute-start.7 = (bf16[8,16,128]{2,1,0:T(8,128)(2,1)S(1)}, bf16[8,16,128]{2,1,0:T(8,128)(2,1)S(1)}, u32[]{:S(2)}, u32[]{:S(2)}) collective-permute-start(bf16[8,16,128]{2,1,0:T(8,128)(2,1)S(1)} %get-tuple-element.43), channel_id=1, source_target_pairs={{0,8},{4,12},{8,16},{12,20},{16,24},{20,28},{24,0},{28,4},{1,9},{5... | collective-permute-start | bytes 98312 | tf_op jit(solution)/shard_map/ppermute | solution.py:34
  43.9 5.8 %collective-permute-start.8 = (bf16[8,16,128]{2,1,0:T(8,128)(2,1)S(1)}, bf16[8,16,128]{2,1,0:T(8,128)(2,1)S(1)}, u32[]{:S(2)}, u32[]{:S(2)}) collective-permute-start(bf16[8,16,128]{2,1,0:T(8,128)(2,1)S(1)} %get-tuple-element.47), channel_id=1, source_target_pairs={{0,8},{4,12},{8,16},{12,20},{16,24},{20,28},{24,0},{28,4},{1,9},{5... | collective-permute-start | bytes 98312 | tf_op jit(solution)/shard_map/ppermute | solution.py:34
  43.9 5.8 %collective-permute-start.9 = (bf16[8,16,128]{2,1,0:T(8,128)(2,1)S(1)}, bf16[8,16,128]{2,1,0:T(8,128)(2,1)S(1)}, u32[]{:S(2)}, u32[]{:S(2)}) collective-permute-start(bf16[8,16,128]{2,1,0:T(8,128)(2,1)S(1)} %get-tuple-element.48), channel_id=1, source_target_pairs={{0,4},{4,8},{8,12},{12,16},{16,20},{20,24},{24,28},{28,0},{1,5},{5... | collective-permute-start | bytes 98312 | tf_op jit(solution)/shard_map/ppermute | solution.py:34
  44.4 5.3 %collective-permute-start.10 = (bf16[8,16,128]{2,1,0:T(8,128)(2,1)S(1)}, bf16[8,16,128]{2,1,0:T(8,128)(2,1)S(1)}, u32[]{:S(2)}, u32[]{:S(2)}) collective-permute-start(bf16[8,16,128]{2,1,0:T(8,128)(2,1)S(1)} %get-tuple-element.49), channel_id=1, source_target_pairs={{0,28},{4,0},{8,4},{12,8},{16,12},{20,16},{24,20},{28,24},{1,29},{... | collective-permute-start | bytes 98312 | tf_op jit(solution)/shard_map/ppermute | solution.py:34
  46.5 4.2 %collective-permute-start.11 = (bf16[8,16,128]{2,1,0:T(8,128)(2,1)S(1)}, bf16[8,16,128]{2,1,0:T(8,128)(2,1)S(1)}, u32[]{:S(2)}, u32[]{:S(2)}) collective-permute-start(bf16[8,16,128]{2,1,0:T(8,128)(2,1)S(1)} %get-tuple-element.50), channel_id=1, source_target_pairs={{0,24},{4,28},{8,0},{12,4},{16,8},{20,12},{24,16},{28,20},{1,25},{... | collective-permute-start | bytes 98312 | tf_op jit(solution)/shard_map/ppermute | solution.py:34

commit v5 on v3

--- a/solution.py
+++ b/solution.py
@@ -163,7 +163,7 @@
 
 def first_kernel(
     cols_ref, send_ref, patch_ref, columns_ref, got_ref, w_hbm, diag_ref, coupling_hbm,
-    m_ref, v_ref, names_ref, t1_ref, t2_ref, o0, o1, o2, o3,
+    m_ref, v_ref, names_ref, patches_ref, t1_ref, t2_ref, o0, o1, o2, o3,
     ext_ref, row_ref, w_ref, coupling_ref, w_sem, sems,
 ):
     w_copy = pltpu.make_async_copy(w_hbm, w_ref, w_sem)
@@ -209,6 +209,7 @@
     ghost_picked = picked[:, LANES:]
     full_low = low.astype(jnp.int32)
     column_patches = patches_of_columns(columns_ref, ids)
+    patches_ref[...] = column_patches
     sub = lax.broadcasted_iota(jnp.int32, (8, LANES), 0)
     lane8 = lax.broadcasted_iota(jnp.int32, (8, LANES), 1)
     wanted = sub == lane8 % 4
@@ -373,55 +374,54 @@
     return jnp.where(low, even, odd) + swap_halves(jnp.where(low, odd, even))
 
 
-def finish_round(base_ref, target_ref, acc_refs, msg_refs, blocks, low):
-    def local(pair, _):
-        base_ref[pair] = target_ref[pair] - pair_sum(acc_refs, pair, low)
-        return 0
-
-    lax.fori_loop(0, blocks // 2, local, 0, unroll=16)
-    for group, ref in enumerate(msg_refs):
-        count = ref.shape[0]
-        for pair in range(count):
-            ref[pair] = pair_sum(acc_refs, blocks // 2 + group * count + pair, low).astype(BF16)
-
-
 def turn_kernel(
-    cols_ref, t1_ref, prev_ref, g0, g1, g2, g3, m_ref, weight_ref,
-    tangent_ref, target_ref, base_ref, o0, o1, o2, o3, ext_ref, *acc_refs,
+    cols_ref, t1_ref, prev_ref, g0, g1, g2, g3, m_ref, weight_ref, w_ref,
+    tangent_ref, terms_ref, z_ref, y_ref, ext_ref, target_ref, u_ref, *acc_refs,
 ):
+    pert = prev_ref.shape[1]
     low = low_half(prev_ref.shape[1:])
+    lane = lax.broadcasted_iota(jnp.int32, (pert, LANES), 1)
     blocks = cols_ref.shape[1]
     extend(ext_ref, prev_ref, (g0, g1, g2, g3), low)
 
-    def sweep(quad, _):
+    def sweep(quad, terms):
         coupled = gather_multiply(quad, cols_ref, ext_ref, m_ref, low)
         for place in range(2):
             pair = 2 * quad + place
             value = t1_ref[pair] - coupled[place]
             start = pl.multiple_of(pair * LANES, LANES)
             tangent_ref[:, pl.ds(start, LANES)] = value
-            target_ref[pair] = value * weight_ref[pl.ds(pair, 1), :]
+            target = value * weight_ref[pl.ds(pair, 1), :]
+            target_ref[pair] = target
+            product = target * w_ref[pl.ds(pair, 1), :]
+            even = jnp.sum(jnp.where(low, product, 0.0), axis=1, keepdims=True)
+            odd = jnp.sum(jnp.where(low, 0.0, product), axis=1, keepdims=True)
+            terms = jnp.where(
+                lane == 2 * pair, even, jnp.where(lane == 2 * pair + 1, odd, terms)
+            )
+        return terms
+
+    terms_ref[...] = lax.fori_loop(
+        0, blocks // QUAD, sweep, jnp.zeros((pert, LANES), F32), unroll=32
+    )
+    scatter_all(cols_ref, target_ref, m_ref, acc_refs, low)
+
+    def own(pair, _):
+        u_ref[pair] = target_ref[pair] - pair_sum(acc_refs, pair, low)
         return 0
 
-    lax.fori_loop(0, blocks // QUAD, sweep, 0, unroll=32)
-    scatter_all(cols_ref, target_ref, m_ref, acc_refs, low)
-    finish_round(base_ref, target_ref, acc_refs, (o0, o1, o2, o3), blocks, low)
-
-
-def take_returned(send_ref, base_ref, u_ref, ghosts, low):
-    u_ref[...] = base_ref[...]
-    which = 1 - low.astype(jnp.int32)
-    for group, ref in enumerate(ghosts):
-        for pair in range(ref.shape[0]):
-            value = ref[pair].astype(F32)
-            other = swap_halves(value)
-            for half, both in enumerate(
-                (jnp.where(low, value, other), jnp.where(low, other, value))
-            ):
-                block = send_ref[0, group, 2 * pair + half]
-                place = jnp.maximum(block, 0) // 2
-                wanted = jnp.where(block < 0, 2, block % 2)
-                u_ref[place] = u_ref[place] - jnp.where(which == wanted, both, 0.0)
+    lax.fori_loop(0, blocks // 2, own, 0, unroll=16)
+    for pair in range(y_ref.shape[0]):
+        y_ref[pair] = (-pair_sum(acc_refs, blocks // 2 + pair, low)).astype(BF16)
+    scatter_all(cols_ref, u_ref, m_ref, acc_refs, low)
+
+    def second(pair, _):
+        z_ref[pair] = (pair_sum(acc_refs, pair, low) - target_ref[pair]).astype(BF16)
+        return 0
+
+    lax.fori_loop(0, blocks // 2, second, 0, unroll=16)
+    for pair in range(blocks // 2, z_ref.shape[0]):
+        z_ref[pair] = pair_sum(acc_refs, pair, low).astype(BF16)
 
 
 def scatter_all(cols_ref, u_ref, m_ref, acc_refs, low):
@@ -435,89 +435,202 @@
     lax.fori_loop(0, cols_ref.shape[1] // QUAD, sweep, 0, unroll=32)
 
 
-def prepare_kernel(
-    patch_ref, names_ref, g0, g1, g2, g3, target_ref, w_ref, hot_ref, terms_ref
+def write_hot(hot_ref, rows, part):
+    start = pl.multiple_of(part * LANES, LANES)
+    names = lax.broadcasted_iota(jnp.int32, (LANES, LANES), 0) + part * LANES
+    names = names.astype(F32)
+    for tile, row in enumerate(rows):
+        hot_ref[pl.ds(start, LANES), tile * LANES : (tile + 1) * LANES] = jnp.where(
+            names == row, 1.0, 0.0
+        ).astype(BF16)
+
+
+def window_kernel(
+    cols_ref, send_ref, columns_ref, patch_ref, names_ref, patches_ref, g0, g1, g2, g3,
+    v_ref, m_ref, hot_ref, o0, o1, o2, o3, vector_ref,
 ):
-    pairs, pert, _ = target_ref.shape
-    low8 = low_half((1, LANES))
+    ghosts = (g0, g1, g2, g3)
+    capacity = send_ref.shape[2]
+    half = capacity // 2
+    blocks = cols_ref.shape[1]
+    low8 = low_half((8, LANES))
+    sub = lax.broadcasted_iota(jnp.int32, (8, LANES), 0)
+    lane = lax.broadcasted_iota(jnp.int32, (8, LANES), 1)
+
+    listed = []
+    there = jnp.zeros((8, LANES), F32)
+    for group, ref in enumerate(ghosts):
+        digits = ref[ref.shape[0] - 1].astype(F32)
+        listed.append(digits[0:1] * RADIX + digits[8:9])
+        taken = jnp.take_along_axis(
+            jnp.broadcast_to(listed[-1], (8, LANES)), (lane % capacity) * 4 + sub % 4, axis=1
+        )
+        there = jnp.where(lane // capacity == group, taken, there)
+    here = patches_ref[...]
     rows = [patch_ref[...].astype(F32)] + [names_ref[tile : tile + 1] for tile in range(4)]
-    ghosts = []
-    for ref in (g0, g1, g2, g3):
-        digits = ref[ref.shape[0] - 1].astype(F32)
-        ghosts.append(digits[0:1] * RADIX + digits[8:9])
     for tile in range(2):
-        rows.append(jnp.where(low8, ghosts[2 * tile], swap_halves(ghosts[2 * tile + 1])))
-    low = low_half((pert, LANES))
-    lane = lax.broadcasted_iota(jnp.int32, (pert, LANES), 1)
-    first = lax.broadcasted_iota(jnp.int32, (LANES, LANES), 0).astype(F32)
+        rows.append(
+            jnp.where(low8[:1], listed[2 * tile], swap_halves(listed[2 * tile + 1]))
+        )
+
+    def spread(pair, value):
+        other = swap_halves(value)
+        vector_ref[2 * pair] = jnp.where(low8, value, other)
+        vector_ref[2 * pair + 1] = jnp.where(low8, other, value)
+
+    for pair in range(blocks // 2):
+        spread(pair, v_ref[pair])
+    for group, ref in enumerate(ghosts):
+        for tile in range(half // 2):
+            both = ref[half + tile].astype(F32)
+            for side in range(2):
+                pair = blocks // 2 + group * half + 2 * tile + side
+                spread(pair, both[8 * side : 8 * side + 8])
+
+    own = (sub < 4) == low8
+    nothing = jnp.zeros((8, LANES), F32)
+    low = low_half((16, LANES))
+    columns = jnp.concatenate([columns_ref[...], columns_ref[...]], axis=0)
+    sub16 = lax.broadcasted_iota(jnp.int32, (16, LANES), 0)
+    for group, ref in enumerate((o0, o1, o2, o3)):
+        slots = [jnp.maximum(send_ref[0, group, slot], 0) for slot in range(capacity)]
+        for four in range(capacity // QUAD):
+            lhs = []
+            rhs = []
+            for block in slots[four * QUAD : (four + 1) * QUAD]:
+                a0, a1, a2, a3 = (vector_ref[cols_ref[k, block]] for k in range(4))
+                left = jnp.where(own, jnp.where(sub < 4, a0, a1), nothing)
+                right = jnp.where(own, jnp.where(sub < 4, a2, a3), nothing)
+                lhs.append(
+                    jnp.concatenate(
+                        [
+                            jnp.concatenate([left, nothing], axis=0),
+                            jnp.concatenate([nothing, right], axis=0),
+                        ],
+                        axis=1,
+                    ).astype(BF16)
+                )
+                rhs.append(m_ref[block])
+            out = lax.dot_general(
+                jnp.concatenate(lhs, axis=0),
+                jnp.concatenate(rhs, axis=0),
+                (((1,), (1,)), ((), ())),
+                preferred_element_type=F32,
+            )
+            for side, value in enumerate(own_pairs(out, 16, low)):
+                ref[2 * four + side] = value.astype(BF16)
+        digits = jnp.zeros((16, LANES), F32)
+        for tile in range(2):
+            places = jnp.zeros((8, LANES), jnp.int32)
+            for slot in range(half):
+                places = jnp.where(lane // 16 == slot, slots[tile * half + slot], places)
+            taken = jnp.take_along_axis(columns, places, axis=1).astype(F32)
+            mine = jnp.sum(
+                jnp.where(sub == (lane % 16) // 4, taken, 0.0), axis=0, keepdims=True
+            )
+            mine = jnp.broadcast_to(mine, (8, LANES)).astype(jnp.int32)
+            taken = jnp.where(
+                mine < LANES,
+                jnp.take_along_axis(here, jnp.minimum(mine, LANES - 1), axis=1),
+                jnp.take_along_axis(there, jnp.maximum(mine - LANES, 0), axis=1),
+            )
+            patch = jnp.sum(jnp.where(sub == lane % 4, taken, 0.0), axis=0, keepdims=True)
+            patch = patch.astype(jnp.int32)
+            digits = jnp.where(
+                sub16 == 2 * tile,
+                (patch // RADIX).astype(F32),
+                jnp.where(sub16 == 2 * tile + 1, (patch % RADIX).astype(F32), digits),
+            )
+        ref[half] = digits.astype(BF16)
 
     def one(part, _):
-        start = pl.multiple_of(part * LANES, LANES)
-        base = (part * LANES).astype(F32)
-        for tile, row in enumerate(rows):
-            hot_ref[pl.ds(start, LANES), tile * LANES : (tile + 1) * LANES] = jnp.where(
-                first == row - base, 1.0, 0.0
-            ).astype(BF16)
+        write_hot(hot_ref, rows, part)
         return 0
 
     lax.fori_loop(0, hot_ref.shape[0] // LANES, one, 0, unroll=2)
 
-    def local(pair, terms):
-        value = target_ref[pair] * w_ref[pl.ds(pair, 1), :]
-        even = jnp.sum(jnp.where(low, value, 0.0), axis=1, keepdims=True)
-        odd = jnp.sum(jnp.where(low, 0.0, value), axis=1, keepdims=True)
-        return jnp.where(lane == 2 * pair, even, jnp.where(lane == 2 * pair + 1, odd, terms))
-
-    terms_ref[...] = lax.fori_loop(0, pairs, local, jnp.zeros((pert, LANES), F32), unroll=16)
-
 
 def last_kernel(
-    cols_ref, send_ref, base_in_ref, target_ref, g0, g1, g2, g3, m_ref, v_ref, v0, v1, v2, v3,
-    hot_ref, terms_ref, got_ref, out_ref, u_ref, *acc_refs,
+    z_ref, y_ref, v_ref, v0, v1, v2, v3, x0, x1, x2, x3,
+    hot_ref, terms_ref, got_ref, out_ref,
 ):
-    pert = u_ref.shape[1]
-    blocks = cols_ref.shape[1]
-    half = send_ref.shape[2] // 2
+    pert = z_ref.shape[1]
+    local_pairs = v_ref.shape[0]
+    half = (z_ref.shape[0] - local_pairs) // 4
     parts = got_ref.shape[0]
-    low = low_half(u_ref.shape[1:])
-    take_returned(send_ref, base_in_ref, u_ref, (g0, g1, g2, g3), low)
-    scatter_all(cols_ref, u_ref, m_ref, acc_refs, low)
+    low8 = low_half((8, LANES))
+    low = low_half((16, LANES))
     sub = lax.broadcasted_iota(jnp.int32, (8, LANES), 0)
-    own = (sub < 4) == low_half((8, LANES))
+    own = (sub < 4) == low8
     nothing = jnp.zeros((8, LANES), F32)
-
-    def products(pair, first_v, second_v, first_z, second_z):
-        rhs = jnp.concatenate(
+    zero = jnp.zeros((16, LANES), F32)
+
+    def wide(left, right):
+        return jnp.concatenate([left, right], axis=1)
+
+    def product(lhs, rhs):
+        return lax.dot_general(
+            lhs, rhs.astype(BF16), (((1,), (1,)), ((), ())), preferred_element_type=F32
+        )
+
+    def first_level(first, second):
+        return jnp.concatenate(
             [
-                jnp.concatenate([jnp.where(own, first_v, nothing), nothing], axis=1),
-                jnp.concatenate([nothing, jnp.where(own, second_v, nothing)], axis=1),
+                wide(jnp.where(own, first, nothing), nothing),
+                wide(nothing, jnp.where(own, second, nothing)),
             ],
             axis=0,
         )
-        lhs = jnp.concatenate([first_z, second_z], axis=1)
-        return lax.dot_general(
-            lhs.astype(BF16), rhs.astype(BF16), (((1,), (1,)), ((), ())),
-            preferred_element_type=F32,
-        )
-
-    pieces = []
-    for pair in range(0, blocks // 2, 2):
-        z = [pair_sum(acc_refs, pair + i, low) - target_ref[pair + i] for i in range(2)]
-        pieces.append(products(pair, v_ref[pair], v_ref[pair + 1], *z))
+
+    def second_level(first, second):
+        return jnp.concatenate(
+            [
+                wide(jnp.where(low, first, zero), zero),
+                wide(jnp.where(low, zero, first), zero),
+                wide(zero, jnp.where(low, second, zero)),
+                wide(zero, jnp.where(low, zero, second)),
+            ],
+            axis=0,
+        )
+
+    pieces = [terms_ref[...]]
+    for pair in range(0, local_pairs, 2):
+        lhs = wide(z_ref[pair], z_ref[pair + 1])
+        pieces.append(product(lhs, first_level(v_ref[pair], v_ref[pair + 1])))
     for group, ref in enumerate((v0, v1, v2, v3)):
         for tile in range(half // 2):
             both = ref[half + tile].astype(F32)
-            pair = blocks // 2 + group * half + 2 * tile
-            z = [pair_sum(acc_refs, pair + i, low) for i in range(2)]
-            pieces.append(products(pair, both[:8], both[8:], *z))
-    terms = jnp.concatenate([terms_ref[...]] + pieces, axis=1)
+            pair = local_pairs + group * half + 2 * tile
+            lhs = wide(z_ref[pair], z_ref[pair + 1])
+            pieces.append(product(lhs, first_level(both[:8], both[8:])))
+    rows = []
+    for group, ref in enumerate((x0, x1, x2, x3)):
+        for tile in range(half // 2):
+            pair = group * half + 2 * tile
+            lhs = wide(y_ref[pair], y_ref[pair + 1])
+            first, second = (ref[2 * tile + side].astype(F32) for side in range(2))
+            pieces.append(product(lhs, second_level(first, second)))
+        digits = ref[half].astype(F32)
+        for tile in range(2):
+            rows.append(
+                digits[2 * tile : 2 * tile + 1] * RADIX + digits[2 * tile + 1 : 2 * tile + 2]
+            )
+    terms = jnp.concatenate(pieces, axis=1)
     top = terms.astype(BF16)
     rest = (terms - top.astype(F32)).astype(BF16)
     both = jnp.concatenate([top, rest], axis=0)
+    near = hot_ref.shape[1]
     perts = out_ref.shape[0] // parts
-    sub = lax.broadcasted_iota(jnp.int32, (8, LANES), 0)
+    first_names = lax.broadcasted_iota(jnp.int32, (LANES, LANES), 0).astype(F32)
     for part in range(parts):
-        hot = hot_ref[part * LANES : (part + 1) * LANES, :]
+        hot = jnp.concatenate(
+            [hot_ref[part * LANES : (part + 1) * LANES, :]]
+            + [
+                jnp.where(first_names == row - part * LANES, 1.0, 0.0).astype(BF16)
+                for row in rows
+            ],
+            axis=1,
+        )
         out = lax.dot_general(both, hot, (((1,), (1,)), ((), ())), preferred_element_type=F32)
         value = out[:pert] + out[pert:]
         curve = jnp.sum(value * got_ref[part, :pert], axis=0, keepdims=True)
@@ -593,11 +706,12 @@
     )(send_list, melt, patch, probes, jnp.transpose(diag_inverse, (1, 2, 0)))
     got = lax.all_to_all(outgoing, "dom", 0, 0, tiled=True)
     wide = [shape((capacity // 2 + capacity // 4 + 1, pert, LANES), BF16)] * 4
-    m, v, names, t1, state, *out = call(
+    m, v, names, patches, t1, state, *out = call(
         first_kernel,
         [
             shape(coupling.shape, BF16),
             shape((pairs, 8, LANES), F32),
+            shape((8, LANES), F32),
             shape((8, LANES), F32),
             pair_array,
             block_array,
@@ -620,28 +734,32 @@
         sweep_kernel, [block_array] + msgs, "ssvvvvvvv", [ext], name="sweep"
     )(columns, send_list, t1, state, *carried, m)
     ghosts = [rotated(v, o) for v, o in zip(out, OFFSET_LIST)]
-    tangent, target, base, *out = call(
+    hot, *far = call(
+        window_kernel,
+        [shape((parts * LANES, 7 * LANES), BF16)]
+        + [shape((capacity // 2 + 1, pert, LANES), BF16)] * 4,
+        "ss" + "v" * 10,
+        [pltpu.VMEM((blocks + 4 * capacity, 8, LANES), F32)],
+        name="window",
+        moved=4 << 20,
+    )(columns, send_list, columns, patch, names, patches, *carried, v, m)
+    far = [rotated(x, o) for x, o in zip(far, OFFSET_LIST)]
+    tangent, terms, z, y = call(
         turn_kernel,
-        [shape((pert, blocks * HALF), F32), pair_array, pair_array] + msgs,
-        "svvvvvvvv",
-        [ext] + accs,
+        [
+            shape((pert, blocks * HALF), F32),
+            shape((pert, LANES), F32),
+            shape((pairs + 2 * capacity, pert, LANES), BF16),
+            shape((2 * capacity, pert, LANES), BF16),
+        ],
+        "s" + "v" * 9,
+        [ext, held, held] + accs,
         name="turn",
-    )(columns, t1, state, *ghosts, m, weight)
-    ghosts = [rotated(v, -o) for v, o in zip(out, OFFSET_LIST)]
-    hot, terms = call(
-        prepare_kernel,
-        [shape((parts * LANES, 7 * LANES), BF16), shape((pert, LANES), F32)],
-        "vvvvvvvv",
-        name="prepare",
-        moved=4 << 20,
-    )(patch, names, *carried, target, w)
+        moved=16 << 20,
+    )(columns, t1, state, *ghosts, m, weight, w)
     terms = call(
-        last_kernel,
-        shape((parts * perts, pert + 8, LANES), BF16),
-        "ss" + "v" * 15,
-        [held] + accs,
-        name="last",
-    )(columns, send_list, base, target, *ghosts, m, v, *carried, hot, terms, got)
+        last_kernel, shape((parts * perts, pert + 8, LANES), BF16), "v" * 14, name="last"
+    )(z, y, v, *carried, *far, hot, terms, got)
     terms = lax.all_to_all(terms, ("dom", "pert"), 0, 0, tiled=True)
     hessian_probe, curvature = call(
         functools.partial(owner_kernel, parts=parts, scale=1.0 / (pert * perts)),

time: 69 us -> 67 us (0.971)
  blocking collectives: 15.4 us -> 13.6 us
  waiting for transfers between devices: 11.5 us -> 10.4 us
  Pallas kernels: 21.2 us -> 22.2 us
    all_to_all x1, blocking collectives: 15.4 us -> 13.6 us  [shards(): terms = lax.all_to_all(terms, ('dom', 'pert'), 0, 0, tiled=True)]
    ppermute x12, waiting for transfers between devices: 9.57 us -> 8.45 us  [rotated(): lax.ppermute(value, 'dom', [(i, (i + by) % peers) for i in range(peers)])]
    pallas_call x3, Pallas kernels: 9.29 us -> 10.3 us  [the longest x1 6.5 us: shards(): call(turn_kernel, [shape((pert, blocks * HALF), F32), shape((pert, LANES)...]
  transfers between devices with their start and end apart: 13 -> 13, of which waited for: 8 -> 5; matrix products, arithmetic and copies ran while one was open for 6% -> 6% of each run, Pallas kernels for 2% -> 13%
where the time goes in v5:
time: 67 us; the launch traced here: 66.7 us
  Pallas kernels  22.2 us (33%)
  starting transfers between devices  15 us (22%)
  blocking collectives  13.6 us (20%)
  waiting for transfers between devices  10.4 us (16%)
  local copies, waits for them, and re-layouts  4.7 us (7%)
  between operations  0.74 us (1%)
    all_to_all x1, blocking collectives, shards(): terms = lax.all_to_all(terms, ('dom', 'pert'), 0, 0, tiled=True)  13.6 us
    ppermute x12, starting transfers between devices, rotated(): lax.ppermute(value, 'dom', [(i, (i + by) % peers) for i in range(peers)])  9.85 us
    ppermute x12, waiting for transfers between devices, rotated(): lax.ppermute(value, 'dom', [(i, (i + by) % peers) for i in range(peers)])  8.45 us
    pallas_call x1, Pallas kernels, shards(): call(turn_kernel, [shape((pert, blocks * HALF), F32), shape((pert, LANES)...  6.5 us
    pallas_call x1, Pallas kernels, shards(): call(first_kernel, [shape(coupling.shape, BF16), shape((pairs, 8, LANES),...  6.4 us
    all_to_all x1, starting transfers between devices, shards(): got = lax.all_to_all(outgoing, 'dom', 0, 0, tiled=True)  5.19 us
    unnamed x11, local copies, waits for them, and re-layouts  4.7 us
    pallas_call x1, Pallas kernels, shards(): call(functools.partial(melt_kernel, parts=parts), [shape((pairs, LANES),...  2.7 us
  transfers between devices with their start and end apart: 13, of which 5 were waited for; matrix products, arithmetic and copies ran while one was open for 6% of the time, Pallas kernels for 13%

profile of v5, /device:TPU:0, one launch (start us, length us, event | category | flops | bytes accessed | tf_op | source)
XLA Modules:
  0.0 66.7 jit_solution(5426256750630589765)
XLA Ops:
  0.6 0.0 copy-start.3
  0.6 0.0 copy-start.4
  0.7 0.0 copy-start.1
  0.7 2.7 %melt.1 = (f32[64,128]{1,0:T(8,128)}, f32[8,40,128]{2,1,0:T(8,128)}) custom-call(s32[1,4,16]{2,1,0:T(4,128)} %send_ref.5, f32[64,128]{1,0:T(8,128)} %bitcast.17, s32[1,128]{1,0:T(1,128)} %bitcast.13, f32[16,128]{1,0:T(8,128)} %probe_hbm.1, bf16[64,64,128]{2,1,0:T(8,128)(2,1)} %bitcast.16), custom_call_target="tpu_custom_call" | custom-call | bytes 1048576 | tf_op jit(solution)/shard_map/melt/pallas_call | solution.py:692
  3.4 5.2 %all-to-all-start = ((f32[8,40,128]{2,1,0:T(8,128)}), f32[8,40,128]{2,1,0:T(8,128)S(1)}, u32[]{:S(2)}, u32[]{:S(2)}) async-start(f32[8,40,128]{2,1,0:T(8,128)} %get-tuple-element.31), calls=%async_computation | async-start | bytes 327680 | tf_op jit(solution)/shard_map/all_to_all | solution.py:707
  8.6 3.9 %copy.11.diag_ref = bf16[128,64,64]{2,1,0:T(8,128)(2,1)S(1)} copy(bf16[128,64,64]{0,2,1:T(8,128)(2,1)} %param.11) | data formatting | bytes 2097152 | tf_op args[3]
  12.5 1.9 %all-to-all-done.got_ref = f32[8,40,128]{2,1,0:T(8,128)S(1)} async-done(((f32[8,40,128]{2,1,0:T(8,128)}), f32[8,40,128]{2,1,0:T(8,128)S(1)}, u32[]{:S(2)}, u32[]{:S(2)}) %all-to-all-start) | async-done | bytes 163872 | tf_op jit(solution)/shard_map/all_to_all | solution.py:707
  14.4 0.0 copy-done.3
  14.4 0.0 copy-done.4
  14.4 0.0 copy-done.1
  14.4 0.0 copy-start
  14.5 0.7 %copy-done = f32[64,128]{1,0:T(8,128)S(1)} copy-done((f32[64,128]{1,0:T(8,128)S(1)}, f32[64,128]{1,0:T(8,128)}, u32[]{:S(2)}) %copy-start) | copy-done | bytes 32792
  15.2 6.4 %first.1 = (bf16[128,64,256]{2,1,0:T(8,128)(2,1)S(1)}, f32[64,8,128]{2,1,0:T(8,128)S(1)}, f32[8,128]{1,0:T(8,128)S(1)}, f32[8,128]{1,0:T(8,128)S(1)}, f32[64,16,...) custom-call(s32[4,128]{1,0:T(4,128)S(1)} %bitcast.6, ...), custom_call_target="tpu_custom_call" | custom-call | bytes 1048576 | tf_op jit(solution)/shard_map/first/pallas_call | solution.py:709
  21.6 1.1 %collective-permute-start = (bf16[13,16,128]{2,1,0:T(8,128)(2,1)S(1)}, bf16[13,16,128]{2,1,0:T(8,128)(2,1)S(1)}, u32[]{:S(2)}, u32[]{:S(2)}) collective-permute-start(bf16[13,16,128]{2,1,0:T(8,128)(2,1)S(1)} %get-tuple-element.35), channel_id=1, source_target_pairs={{0,24},{4,28},{8,0},{12,4},{16,8},{20,12},{24,16},{28,20},{1,25},{... | collective-permute-start | bytes 159752 | tf_op jit(solution)/shard_map/ppermute | solution.py:34
  22.7 0.0 collective-permute-start.1
  22.7 0.5 collective-permute-start.2
  23.2 1.0 %collective-permute-start.3 = (bf16[13,16,128]{2,1,0:T(8,128)(2,1)S(1)}, bf16[13,16,128]{2,1,0:T(8,128)(2,1)S(1)}, u32[]{:S(2)}, u32[]{:S(2)}) collective-permute-start(bf16[13,16,128]{2,1,0:T(8,128)(2,1)S(1)} %get-tuple-element.38), channel_id=1, source_target_pairs={{0,8},{4,12},{8,16},{12,20},{16,24},{20,28},{24,0},{28,4},{1,9},{5... | collective-permute-start | bytes 159752 | tf_op jit(solution)/shard_map/ppermute | solution.py:34
  24.2 1.6 %collective-permute-done.g0.v0 = bf16[13,16,128]{2,1,0:T(8,128)(2,1)S(1)} collective-permute-done((bf16[13,16,128]{2,1,0:T(8,128)(2,1)S(1)}, bf16[13,16,128]{2,1,0:T(8,128)(2,1)S(1)}, u32[]{:S(2)}, u32[]{:S(2)}) %collective-permute-start) | collective-permute-done | bytes 53280 | tf_op jit(solution)/shard_map/ppermute | solution.py:34
  25.8 0.0 collective-permute-done.1.g1.v1
  25.8 1.4 %collective-permute-done.2.g2.v2 = bf16[13,16,128]{2,1,0:T(8,128)(2,1)S(1)} collective-permute-done((bf16[13,16,128]{2,1,0:T(8,128)(2,1)S(1)}, bf16[13,16,128]{2,1,0:T(8,128)(2,1)S(1)}, u32[]{:S(2)}, u32[]{:S(2)}) %collective-permute-start.2) | collective-permute-done | bytes 53280 | tf_op jit(solution)/shard_map/ppermute | solution.py:34
  27.2 1.5 %collective-permute-done.3.g3.v3 = bf16[13,16,128]{2,1,0:T(8,128)(2,1)S(1)} collective-permute-done((bf16[13,16,128]{2,1,0:T(8,128)(2,1)S(1)}, bf16[13,16,128]{2,1,0:T(8,128)(2,1)S(1)}, u32[]{:S(2)}, u32[]{:S(2)}) %collective-permute-start.3) | collective-permute-done | bytes 53280 | tf_op jit(solution)/shard_map/ppermute | solution.py:34
  28.7 0.0 copy-start.2
  28.7 2.2 %sweep.1 = (bf16[128,16,128]{2,1,0:T(8,128)(2,1)S(1)}, bf16[8,16,128]{2,1,0:T(8,128)(2,1)S(1)}, bf16[8,16,128]{2,1,0:T(8,128)(2,1)S(1)}, bf16[8,16,128]{2,1,0:T(8,128)(2,1)S(1)}, bf16[8,16,128]{2,1,0:T(8,128)(2,1)S(1)}) custom-call(s32[4,128]{1,0:T(4,128)S(1)} %bitcast.8, s32[1,4,16]{2,1,0:T(4,128)S(1)} %copy-done.3, ...), custom_call_target="tpu_custom_call" | custom-call | bytes 1048576 | tf_op jit(solution)/shard_map/sweep/pallas_call | solution.py:733
  30.9 0.9 %collective-permute-start.4 = (bf16[8,16,128]{2,1,0:T(8,128)(2,1)S(1)}, bf16[8,16,128]{2,1,0:T(8,128)(2,1)S(1)}, u32[]{:S(2)}, u32[]{:S(2)}) collective-permute-start(bf16[8,16,128]{2,1,0:T(8,128)(2,1)S(1)} %get-tuple-element.41), channel_id=1, source_target_pairs={{0,24},{4,28},{8,0},{12,4},{16,8},{20,12},{24,16},{28,20},{1,25},{... | collective-permute-start | bytes 98312 | tf_op jit(solution)/shard_map/ppermute | solution.py:34
  31.8 1.0 %collective-permute-start.5 = (bf16[8,16,128]{2,1,0:T(8,128)(2,1)S(1)}, bf16[8,16,128]{2,1,0:T(8,128)(2,1)S(1)}, u32[]{:S(2)}, u32[]{:S(2)}) collective-permute-start(bf16[8,16,128]{2,1,0:T(8,128)(2,1)S(1)} %get-tuple-element.42), channel_id=1, source_target_pairs={{0,28},{4,0},{8,4},{12,8},{16,12},{20,16},{24,20},{28,24},{1,29},{... | collective-permute-start | bytes 98312 | tf_op jit(solution)/shard_map/ppermute | solution.py:34
  32.8 0.0 collective-permute-start.6
  32.8 2.0 %window.1 = (bf16[1024,896]{1,0:T(8,128)(2,1)S(1)}, bf16[9,16,128]{2,1,0:T(8,128)(2,1)S(1)}, bf16[9,16,128]{2,1,0:T(8,128)(2,1)S(1)}, bf16[9,16,128]{2,1,0:T(8,128)(2,1)S(1)}, bf16[9,16,128]{2,1,0:T(8,128)(2,1)S(1)}) custom-call(s32[4,128]{1,0:T(4,128)S(1)} %bitcast.9, s32[1,4,16]{2,1,0:T(4,128)S(1)} %copy-done.3, s32[4,128]{1,0:T(4,128)S(1)} %bitcast.10, ...), custom_call_target="tpu_custom_call" | custom-call | bytes 4194304 | tf_op jit(solution)/shard_map/window/pallas_call | solution.py:737
  34.8 1.2 %collective-permute-start.8 = (bf16[9,16,128]{2,1,0:T(8,128)(2,1)S(1)}, bf16[9,16,128]{2,1,0:T(8,128)(2,1)S(1)}, u32[]{:S(2)}, u32[]{:S(2)}) collective-permute-start(bf16[9,16,128]{2,1,0:T(8,128)(2,1)S(1)} %get-tuple-element.51), channel_id=1, source_target_pairs={{0,24},{4,28},{8,0},{12,4},{16,8},{20,12},{24,16},{28,20},{1,25},{... | collective-permute-start | bytes 110600 | tf_op jit(solution)/shard_map/ppermute | solution.py:34
  36.0 1.6 %collective-permute-start.9 = (bf16[9,16,128]{2,1,0:T(8,128)(2,1)S(1)}, bf16[9,16,128]{2,1,0:T(8,128)(2,1)S(1)}, u32[]{:S(2)}, u32[]{:S(2)}) collective-permute-start(bf16[9,16,128]{2,1,0:T(8,128)(2,1)S(1)} %get-tuple-element.52), channel_id=1, source_target_pairs={{0,28},{4,0},{8,4},{12,8},{16,12},{20,16},{24,20},{28,24},{1,29},{... | collective-permute-start | bytes 110600 | tf_op jit(solution)/shard_map/ppermute | solution.py:34
  37.6 0.0 collective-permute-done.4.g0
  37.6 0.1 collective-permute-start.10
  37.6 0.0 collective-permute-done.5.g1
  37.6 1.7 %collective-permute-start.11 = (bf16[9,16,128]{2,1,0:T(8,128)(2,1)S(1)}, bf16[9,16,128]{2,1,0:T(8,128)(2,1)S(1)}, u32[]{:S(2)}, u32[]{:S(2)}) collective-permute-start(bf16[9,16,128]{2,1,0:T(8,128)(2,1)S(1)} %get-tuple-element.54), channel_id=1, source_target_pairs={{0,8},{4,12},{8,16},{12,20},{16,24},{20,28},{24,0},{28,4},{1,9},{5... | collective-permute-start | bytes 110600 | tf_op jit(solution)/shard_map/ppermute | solution.py:34
  39.3 0.0 collective-permute-done.6.g2
  39.3 0.8 %collective-permute-start.7 = (bf16[8,16,128]{2,1,0:T(8,128)(2,1)S(1)}, bf16[8,16,128]{2,1,0:T(8,128)(2,1)S(1)}, u32[]{:S(2)}, u32[]{:S(2)}) collective-permute-start(bf16[8,16,128]{2,1,0:T(8,128)(2,1)S(1)} %get-tuple-element.44), channel_id=1, source_target_pairs={{0,8},{4,12},{8,16},{12,20},{16,24},{20,28},{24,0},{28,4},{1,9},{5... | collective-permute-start | bytes 98312 | tf_op jit(solution)/shard_map/ppermute | solution.py:34
  40.2 4.0 %collective-permute-done.7.g3 = bf16[8,16,128]{2,1,0:T(8,128)(2,1)S(1)} collective-permute-done((bf16[8,16,128]{2,1,0:T(8,128)(2,1)S(1)}, bf16[8,16,128]{2,1,0:T(8,128)(2,1)S(1)}, u32[]{:S(2)}, u32[]{:S(2)}) %collective-permute-start.7) | collective-permute-done | bytes 32800 | tf_op jit(solution)/shard_map/ppermute | solution.py:34
  44.1 0.0 copy-done.2
  44.1 6.5 %turn.1 = (f32[16,8192]{1,0:T(8,128)}, f32[16,128]{1,0:T(8,128)S(1)}, bf16[96,16,128]{2,1,0:T(8,128)(2,1)S(1)}, bf16[32,16,128]{2,1,0:T(8,128)(2,1)S(1)}) custom-call(s32[4,128]{1,0:T(4,128)S(1)} %bitcast.11, f32[64,16,128]{2,1,0:T(8,128)S(1)} %get-tuple-element.33.t1_ref, bf16[128,16,128]{2,1,0:T(8,128)(2,1)S(1)} %get-tuple-element.40.prev_ref, ...), custom_call_target="tpu_custom_call" | custom-call | bytes 16777216 | tf_op jit(solution)/shard_map/turn/pallas_call | solution.py:747
  50.7 0.0 collective-permute-done.8.x0
  50.7 0.0 collective-permute-done.9.x1
  50.7 0.0 collective-permute-done.10.x2
  50.7 0.0 collective-permute-done.11.x3
  50.7 1.8 %last.1 = bf16[32,24,128]{2,1,0:T(8,128)(2,1)S(1)} custom-call(bf16[96,16,128]{2,1,0:T(8,128)(2,1)S(1)} %get-tuple-element.46.z_ref, bf16[32,16,128]{2,1,0:T(8,128)(2,1)S(1)} %get-tuple-element.47.y_ref, f32[64,8,128]{2,1,0:T(8,128)S(1)} %get-tuple-element.48.v_ref, bf16[13,16,128]{2,1,0:T(8,128)(2,1)S(1)} %collective-permute-done.g0.v0, ...), custom_call_target="tpu_custom_call" | custom-call | bytes 1048576 | tf_op jit(solution)/shard_map/last/pallas_call | solution.py:760
  52.5 13.6 %all_to_all.10.terms_ref = bf16[32,24,128]{2,1,0:T(8,128)(2,1)S(1)} all-to-all(bf16[32,24,128]{2,1,0:T(8,128)(2,1)S(1)} %last.1), channel_id=1, replica_groups=mesh['dom'=8,'pert'=4] {'dom','pert'}, dimensions={0} | all-to-all | bytes 393216 | tf_op jit(solution)/shard_map/all_to_all | solution.py:763
  66.1 0.6 owner.1
Async XLA Ops:
  0.6 13.8 %copy-start.3 = (s32[1,4,16]{2,1,0:T(4,128)S(1)}, s32[1,4,16]{2,1,0:T(4,128)}, u32[]{:S(2)}) copy-start(s32[1,4,16]{2,1,0:T(4,128)} %send_ref.5) | copy-start | bytes 772
  0.6 13.8 %copy-start.4 = (s32[128]{0:T(128)S(1)}, s32[128]{0:T(128)}, u32[]{:S(2)}) copy-start(s32[128]{0:T(128)} %param.15) | copy-start | bytes 1540
  0.7 13.8 %copy-start.1 = (s32[128,4]{0,1:T(4,128)S(1)}, s32[128,4]{0,1:T(4,128)}, u32[]{:S(2)}) copy-start(s32[128,4]{0,1:T(4,128)} %param.13) | copy-start | bytes 6148
  3.4 11.1 %all-to-all-start = ((f32[8,40,128]{2,1,0:T(8,128)}), f32[8,40,128]{2,1,0:T(8,128)S(1)}, u32[]{:S(2)}, u32[]{:S(2)}) async-start(f32[8,40,128]{2,1,0:T(8,128)} %get-tuple-element.31), calls=%async_computation | async-start | bytes 327680 | tf_op jit(solution)/shard_map/all_to_all | solution.py:707
  14.4 0.8 %copy-start = (f32[64,128]{1,0:T(8,128)S(1)}, f32[64,128]{1,0:T(8,128)}, u32[]{:S(2)}) copy-start(f32[64,128]{1,0:T(8,128)} %get-tuple-element.32.w_hbm.w_ref) | copy-start | bytes 98308
  21.6 4.2 %collective-permute-start = (bf16[13,16,128]{2,1,0:T(8,128)(2,1)S(1)}, bf16[13,16,128]{2,1,0:T(8,128)(2,1)S(1)}, u32[]{:S(2)}, u32[]{:S(2)}) collective-permute-start(bf16[13,16,128]{2,1,0:T(8,128)(2,1)S(1)} %get-tuple-element.35), channel_id=1, source_target_pairs={{0,24},{4,28},{8,0},{12,4},{16,8},{20,12},{24,16},{28,20},{1,25},{... | collective-permute-start | bytes 159752 | tf_op jit(solution)/shard_map/ppermute | solution.py:34
  22.7 3.1 %collective-permute-start.1 = (bf16[13,16,128]{2,1,0:T(8,128)(2,1)S(1)}, bf16[13,16,128]{2,1,0:T(8,128)(2,1)S(1)}, u32[]{:S(2)}, u32[]{:S(2)}) collective-permute-start(bf16[13,16,128]{2,1,0:T(8,128)(2,1)S(1)} %get-tuple-element.36), channel_id=1, source_target_pairs={{0,28},{4,0},{8,4},{12,8},{16,12},{20,16},{24,20},{28,24},{1,29},{... | collective-permute-start | bytes 159752 | tf_op jit(solution)/shard_map/ppermute | solution.py:34
  22.7 4.5 %collective-permute-start.2 = (bf16[13,16,128]{2,1,0:T(8,128)(2,1)S(1)}, bf16[13,16,128]{2,1,0:T(8,128)(2,1)S(1)}, u32[]{:S(2)}, u32[]{:S(2)}) collective-permute-start(bf16[13,16,128]{2,1,0:T(8,128)(2,1)S(1)} %get-tuple-element.37), channel_id=1, source_target_pairs={{0,4},{4,8},{8,12},{12,16},{16,20},{20,24},{24,28},{28,0},{1,5},{5... | collective-permute-start | bytes 159752 | tf_op jit(solution)/shard_map/ppermute | solution.py:34
  23.2 5.5 %collective-permute-start.3 = (bf16[13,16,128]{2,1,0:T(8,128)(2,1)S(1)}, bf16[13,16,128]{2,1,0:T(8,128)(2,1)S(1)}, u32[]{:S(2)}, u32[]{:S(2)}) collective-permute-start(bf16[13,16,128]{2,1,0:T(8,128)(2,1)S(1)} %get-tuple-element.38), channel_id=1, source_target_pairs={{0,8},{4,12},{8,16},{12,20},{16,24},{20,28},{24,0},{28,4},{1,9},{5... | collective-permute-start | bytes 159752 | tf_op jit(solution)/shard_map/ppermute | solution.py:34
  28.7 15.5 %copy-start.2 = (f32[8192]{0:T(1024)S(1)}, f32[8192]{0:T(1024)}, u32[]{:S(2)}) copy-start(f32[8192]{0:T(1024)} %param.10) | copy-start | bytes 98308
  30.9 6.7 %collective-permute-start.4 = (bf16[8,16,128]{2,1,0:T(8,128)(2,1)S(1)}, bf16[8,16,128]{2,1,0:T(8,128)(2,1)S(1)}, u32[]{:S(2)}, u32[]{:S(2)}) collective-permute-start(bf16[8,16,128]{2,1,0:T(8,128)(2,1)S(1)} %get-tuple-element.41), channel_id=1, source_target_pairs={{0,24},{4,28},{8,0},{12,4},{16,8},{20,12},{24,16},{28,20},{1,25},{... | collective-permute-start | bytes 98312 | tf_op jit(solution)/shard_map/ppermute | solution.py:34
  31.8 5.8 %collective-permute-start.5 = (bf16[8,16,128]{2,1,0:T(8,128)(2,1)S(1)}, bf16[8,16,128]{2,1,0:T(8,128)(2,1)S(1)}, u32[]{:S(2)}, u32[]{:S(2)}) collective-permute-start(bf16[8,16,128]{2,1,0:T(8,128)(2,1)S(1)} %get-tuple-element.42), channel_id=1, source_target_pairs={{0,28},{4,0},{8,4},{12,8},{16,12},{20,16},{24,20},{28,24},{1,29},{... | collective-permute-start | bytes 98312 | tf_op jit(solution)/shard_map/ppermute | solution.py:34
  32.8 6.5 %collective-permute-start.6 = (bf16[8,16,128]{2,1,0:T(8,128)(2,1)S(1)}, bf16[8,16,128]{2,1,0:T(8,128)(2,1)S(1)}, u32[]{:S(2)}, u32[]{:S(2)}) collective-permute-start(bf16[8,16,128]{2,1,0:T(8,128)(2,1)S(1)} %get-tuple-element.43), channel_id=1, source_target_pairs={{0,4},{4,8},{8,12},{12,16},{16,20},{20,24},{24,28},{28,0},{1,5},{5... | collective-permute-start | bytes 98312 | tf_op jit(solution)/shard_map/ppermute | solution.py:34
  34.8 15.8 %collective-permute-start.8 = (bf16[9,16,128]{2,1,0:T(8,128)(2,1)S(1)}, bf16[9,16,128]{2,1,0:T(8,128)(2,1)S(1)}, u32[]{:S(2)}, u32[]{:S(2)}) collective-permute-start(bf16[9,16,128]{2,1,0:T(8,128)(2,1)S(1)} %get-tuple-element.51), channel_id=1, source_target_pairs={{0,24},{4,28},{8,0},{12,4},{16,8},{20,12},{24,16},{28,20},{1,25},{... | collective-permute-start | bytes 110600 | tf_op jit(solution)/shard_map/ppermute | solution.py:34
  36.0 14.7 %collective-permute-start.9 = (bf16[9,16,128]{2,1,0:T(8,128)(2,1)S(1)}, bf16[9,16,128]{2,1,0:T(8,128)(2,1)S(1)}, u32[]{:S(2)}, u32[]{:S(2)}) collective-permute-start(bf16[9,16,128]{2,1,0:T(8,128)(2,1)S(1)} %get-tuple-element.52), channel_id=1, source_target_pairs={{0,28},{4,0},{8,4},{12,8},{16,12},{20,16},{24,20},{28,24},{1,29},{... | collective-permute-start | bytes 110600 | tf_op jit(solution)/shard_map/ppermute | solution.py:34
  37.6 13.1 %collective-permute-start.10 = (bf16[9,16,128]{2,1,0:T(8,128)(2,1)S(1)}, bf16[9,16,128]{2,1,0:T(8,128)(2,1)S(1)}, u32[]{:S(2)}, u32[]{:S(2)}) collective-permute-start(bf16[9,16,128]{2,1,0:T(8,128)(2,1)S(1)} %get-tuple-element.53), channel_id=1, source_target_pairs={{0,4},{4,8},{8,12},{12,16},{16,20},{20,24},{24,28},{28,0},{1,5},{5... | collective-permute-start | bytes 110600 | tf_op jit(solution)/shard_map/ppermute | solution.py:34
  37.6 13.0 %collective-permute-start.11 = (bf16[9,16,128]{2,1,0:T(8,128)(2,1)S(1)}, bf16[9,16,128]{2,1,0:T(8,128)(2,1)S(1)}, u32[]{:S(2)}, u32[]{:S(2)}) collective-permute-start(bf16[9,16,128]{2,1,0:T(8,128)(2,1)S(1)} %get-tuple-element.54), channel_id=1, source_target_pairs={{0,8},{4,12},{8,16},{12,20},{16,24},{20,28},{24,0},{28,4},{1,9},{5... | collective-permute-start | bytes 110600 | tf_op jit(solution)/shard_map/ppermute | solution.py:34
  39.3 4.8 %collective-permute-start.7 = (bf16[8,16,128]{2,1,0:T(8,128)(2,1)S(1)}, bf16[8,16,128]{2,1,0:T(8,128)(2,1)S(1)}, u32[]{:S(2)}, u32[]{:S(2)}) collective-permute-start(bf16[8,16,128]{2,1,0:T(8,128)(2,1)S(1)} %get-tuple-element.44), channel_id=1, source_target_pairs={{0,8},{4,12},{8,16},{12,20},{16,24},{20,28},{24,0},{28,4},{1,9},{5... | collective-permute-start | bytes 98312 | tf_op jit(solution)/shard_map/ppermute | solution.py:34

commit v6 on v5

--- a/solution.py
+++ b/solution.py
@@ -743,6 +743,7 @@
         name="window",
         moved=4 << 20,
     )(columns, send_list, columns, patch, names, patches, *carried, v, m)
+    far, ghosts = lax.optimization_barrier((far, ghosts))
     far = [rotated(x, o) for x, o in zip(far, OFFSET_LIST)]
     tangent, terms, z, y = call(
         turn_kernel,

time: 67 us -> 64.3 us (0.960)
  starting transfers between devices: 15 us -> 12.9 us
  waiting for transfers between devices: 10.4 us -> 8.73 us
  blocking collectives: 13.6 us -> 14.6 us
    ppermute x12, starting transfers between devices: 9.85 us -> 7.75 us  [rotated(): lax.ppermute(value, 'dom', [(i, (i + by) % peers) for i in range(peers)])]
    ppermute x12, waiting for transfers between devices: 8.45 us -> 6.79 us  [rotated(): lax.ppermute(value, 'dom', [(i, (i + by) % peers) for i in range(peers)])]
    all_to_all x1, blocking collectives: 13.6 us -> 14.6 us  [shards(): terms = lax.all_to_all(terms, ('dom', 'pert'), 0, 0, tiled=True)]
  transfers between devices with their start and end apart: 13 -> 13, of which waited for: 5 -> 6; matrix products, arithmetic and copies ran while one was open for 6% -> 6% of each run, Pallas kernels for 13% -> 13%
where the time goes in v6:
time: 64.3 us; the launch traced here: 64 us
  Pallas kernels  22.2 us (35%)
  blocking collectives  14.6 us (23%)
  starting transfers between devices  12.9 us (20%)
  waiting for transfers between devices  8.73 us (14%)
  local copies, waits for them, and re-layouts  4.7 us (7%)
  between operations  0.75 us (1%)
    all_to_all x1, blocking collectives, shards(): terms = lax.all_to_all(terms, ('dom', 'pert'), 0, 0, tiled=True)  14.6 us
    ppermute x12, starting transfers between devices, rotated(): lax.ppermute(value, 'dom', [(i, (i + by) % peers) for i in range(peers)])  7.75 us
    ppermute x12, waiting for transfers between devices, rotated(): lax.ppermute(value, 'dom', [(i, (i + by) % peers) for i in range(peers)])  6.79 us
    pallas_call x1, Pallas kernels, shards(): call(turn_kernel, [shape((pert, blocks * HALF), F32), shape((pert, LANES)...  6.51 us
    pallas_call x1, Pallas kernels, shards(): call(first_kernel, [shape(coupling.shape, BF16), shape((pairs, 8, LANES),...  6.37 us
    all_to_all x1, starting transfers between devices, shards(): got = lax.all_to_all(outgoing, 'dom', 0, 0, tiled=True)  5.19 us
    unnamed x11, local copies, waits for them, and re-layouts  4.7 us
    pallas_call x1, Pallas kernels, shards(): call(functools.partial(melt_kernel, parts=parts), [shape((pairs, LANES),...  2.7 us
  transfers between devices with their start and end apart: 13, of which 6 were waited for; matrix products, arithmetic and copies ran while one was open for 6% of the time, Pallas kernels for 13%

profile of v6, /device:TPU:0, one launch (start us, length us, event | category | flops | bytes accessed | tf_op | source)
XLA Modules:
  0.0 64.0 jit_solution(8601909276276735044)
XLA Ops:
  0.6 0.0 copy-start.3
  0.6 0.0 copy-start.4
  0.7 0.0 copy-start.1
  0.7 2.7 %melt.1 = (f32[64,128]{1,0:T(8,128)}, f32[8,40,128]{2,1,0:T(8,128)}) custom-call(s32[1,4,16]{2,1,0:T(4,128)} %send_ref.5, f32[64,128]{1,0:T(8,128)} %bitcast.17, s32[1,128]{1,0:T(1,128)} %bitcast.13, f32[16,128]{1,0:T(8,128)} %probe_hbm.1, bf16[64,64,128]{2,1,0:T(8,128)(2,1)} %bitcast.16), custom_call_target="tpu_custom_call" | custom-call | bytes 1048576 | tf_op jit(solution)/shard_map/melt/pallas_call | solution.py:692
  3.4 5.2 %all-to-all-start = ((f32[8,40,128]{2,1,0:T(8,128)}), f32[8,40,128]{2,1,0:T(8,128)S(1)}, u32[]{:S(2)}, u32[]{:S(2)}) async-start(f32[8,40,128]{2,1,0:T(8,128)} %get-tuple-element.39), calls=%async_computation | async-start | bytes 327680 | tf_op jit(solution)/shard_map/all_to_all | solution.py:707
  8.6 3.9 %copy.11.diag_ref = bf16[128,64,64]{2,1,0:T(8,128)(2,1)S(1)} copy(bf16[128,64,64]{0,2,1:T(8,128)(2,1)} %param.11) | data formatting | bytes 2097152 | tf_op args[3]
  12.5 1.9 %all-to-all-done.got_ref = f32[8,40,128]{2,1,0:T(8,128)S(1)} async-done(((f32[8,40,128]{2,1,0:T(8,128)}), f32[8,40,128]{2,1,0:T(8,128)S(1)}, u32[]{:S(2)}, u32[]{:S(2)}) %all-to-all-start) | async-done | bytes 163872 | tf_op jit(solution)/shard_map/all_to_all | solution.py:707
  14.4 0.0 copy-done.3
  14.4 0.0 copy-done.4
  14.4 0.0 copy-done.1
  14.4 0.0 copy-start
  14.5 0.7 %copy-done = f32[64,128]{1,0:T(8,128)S(1)} copy-done((f32[64,128]{1,0:T(8,128)S(1)}, f32[64,128]{1,0:T(8,128)}, u32[]{:S(2)}) %copy-start) | copy-done | bytes 32792
  15.2 6.4 %first.1 = (bf16[128,64,256]{2,1,0:T(8,128)(2,1)S(1)}, f32[64,8,128]{2,1,0:T(8,128)S(1)}, f32[8,128]{1,0:T(8,128)S(1)}, f32[8,128]{1,0:T(8,128)S(1)}, f32[64,16,...) custom-call(s32[4,128]{1,0:T(4,128)S(1)} %bitcast.6, ...), custom_call_target="tpu_custom_call" | custom-call | bytes 1048576 | tf_op jit(solution)/shard_map/first/pallas_call | solution.py:709
  21.6 1.1 %collective-permute-start = (bf16[13,16,128]{2,1,0:T(8,128)(2,1)S(1)}, bf16[13,16,128]{2,1,0:T(8,128)(2,1)S(1)}, u32[]{:S(2)}, u32[]{:S(2)}) collective-permute-start(bf16[13,16,128]{2,1,0:T(8,128)(2,1)S(1)} %get-tuple-element.43), channel_id=1, source_target_pairs={{0,24},{4,28},{8,0},{12,4},{16,8},{20,12},{24,16},{28,20},{1,25},{... | collective-permute-start | bytes 159752 | tf_op jit(solution)/shard_map/ppermute | solution.py:34
  22.7 0.1 collective-permute-start.1
  22.7 0.4 collective-permute-start.2
  23.2 1.1 %collective-permute-start.3 = (bf16[13,16,128]{2,1,0:T(8,128)(2,1)S(1)}, bf16[13,16,128]{2,1,0:T(8,128)(2,1)S(1)}, u32[]{:S(2)}, u32[]{:S(2)}) collective-permute-start(bf16[13,16,128]{2,1,0:T(8,128)(2,1)S(1)} %get-tuple-element.46), channel_id=1, source_target_pairs={{0,8},{4,12},{8,16},{12,20},{16,24},{20,28},{24,0},{28,4},{1,9},{5... | collective-permute-start | bytes 159752 | tf_op jit(solution)/shard_map/ppermute | solution.py:34
  24.2 1.6 %collective-permute-done.g0.v0 = bf16[13,16,128]{2,1,0:T(8,128)(2,1)S(1)} collective-permute-done((bf16[13,16,128]{2,1,0:T(8,128)(2,1)S(1)}, bf16[13,16,128]{2,1,0:T(8,128)(2,1)S(1)}, u32[]{:S(2)}, u32[]{:S(2)}) %collective-permute-start) | collective-permute-done | bytes 53280 | tf_op jit(solution)/shard_map/ppermute | solution.py:34
  25.8 0.0 collective-permute-done.1.g1.v1
  25.8 1.4 %collective-permute-done.2.g2.v2 = bf16[13,16,128]{2,1,0:T(8,128)(2,1)S(1)} collective-permute-done((bf16[13,16,128]{2,1,0:T(8,128)(2,1)S(1)}, bf16[13,16,128]{2,1,0:T(8,128)(2,1)S(1)}, u32[]{:S(2)}, u32[]{:S(2)}) %collective-permute-start.2) | collective-permute-done | bytes 53280 | tf_op jit(solution)/shard_map/ppermute | solution.py:34
  27.2 1.4 %collective-permute-done.3.g3.v3 = bf16[13,16,128]{2,1,0:T(8,128)(2,1)S(1)} collective-permute-done((bf16[13,16,128]{2,1,0:T(8,128)(2,1)S(1)}, bf16[13,16,128]{2,1,0:T(8,128)(2,1)S(1)}, u32[]{:S(2)}, u32[]{:S(2)}) %collective-permute-start.3) | collective-permute-done | bytes 53280 | tf_op jit(solution)/shard_map/ppermute | solution.py:34
  28.6 0.0 copy-start.2
  28.6 2.2 %sweep.1 = (bf16[128,16,128]{2,1,0:T(8,128)(2,1)S(1)}, bf16[8,16,128]{2,1,0:T(8,128)(2,1)S(1)}, bf16[8,16,128]{2,1,0:T(8,128)(2,1)S(1)}, bf16[8,16,128]{2,1,0:T(8,128)(2,1)S(1)}, bf16[8,16,128]{2,1,0:T(8,128)(2,1)S(1)}) custom-call(s32[4,128]{1,0:T(4,128)S(1)} %bitcast.8, s32[1,4,16]{2,1,0:T(4,128)S(1)} %copy-done.3, ...), custom_call_target="tpu_custom_call" | custom-call | bytes 1048576 | tf_op jit(solution)/shard_map/sweep/pallas_call | solution.py:733
  30.8 0.9 %collective-permute-start.4 = (bf16[8,16,128]{2,1,0:T(8,128)(2,1)S(1)}, bf16[8,16,128]{2,1,0:T(8,128)(2,1)S(1)}, u32[]{:S(2)}, u32[]{:S(2)}) collective-permute-start(bf16[8,16,128]{2,1,0:T(8,128)(2,1)S(1)} %get-tuple-element.56), channel_id=1, source_target_pairs={{0,24},{4,28},{8,0},{12,4},{16,8},{20,12},{24,16},{28,20},{1,25},{... | collective-permute-start | bytes 98312 | tf_op jit(solution)/shard_map/ppermute | solution.py:34
  31.7 1.1 %collective-permute-start.5 = (bf16[8,16,128]{2,1,0:T(8,128)(2,1)S(1)}, bf16[8,16,128]{2,1,0:T(8,128)(2,1)S(1)}, u32[]{:S(2)}, u32[]{:S(2)}) collective-permute-start(bf16[8,16,128]{2,1,0:T(8,128)(2,1)S(1)} %get-tuple-element.57), channel_id=1, source_target_pairs={{0,28},{4,0},{8,4},{12,8},{16,12},{20,16},{24,20},{28,24},{1,29},{... | collective-permute-start | bytes 98312 | tf_op jit(solution)/shard_map/ppermute | solution.py:34
  32.9 0.0 collective-permute-start.6
  32.9 0.5 collective-permute-start.7
  33.4 2.0 %window.1 = (bf16[1024,896]{1,0:T(8,128)(2,1)S(1)}, bf16[9,16,128]{2,1,0:T(8,128)(2,1)S(1)}, bf16[9,16,128]{2,1,0:T(8,128)(2,1)S(1)}, bf16[9,16,128]{2,1,0:T(8,128)(2,1)S(1)}, bf16[9,16,128]{2,1,0:T(8,128)(2,1)S(1)}) custom-call(s32[4,128]{1,0:T(4,128)S(1)} %bitcast.9, s32[1,4,16]{2,1,0:T(4,128)S(1)} %copy-done.3, s32[4,128]{1,0:T(4,128)S(1)} %bitcast.10, ...), custom_call_target="tpu_custom_call" | custom-call | bytes 4194304 | tf_op jit(solution)/shard_map/window/pallas_call | solution.py:737
  35.4 0.0 collective-permute-done.4.g0
  35.4 0.0 collective-permute-done.5.g1
  35.4 1.7 %collective-permute-done.6.g2 = bf16[8,16,128]{2,1,0:T(8,128)(2,1)S(1)} collective-permute-done((bf16[8,16,128]{2,1,0:T(8,128)(2,1)S(1)}, bf16[8,16,128]{2,1,0:T(8,128)(2,1)S(1)}, u32[]{:S(2)}, u32[]{:S(2)}) %collective-permute-start.6) | collective-permute-done | bytes 32800 | tf_op jit(solution)/shard_map/ppermute | solution.py:34
  37.1 0.7 %collective-permute-done.7.g3 = bf16[8,16,128]{2,1,0:T(8,128)(2,1)S(1)} collective-permute-done((bf16[8,16,128]{2,1,0:T(8,128)(2,1)S(1)}, bf16[8,16,128]{2,1,0:T(8,128)(2,1)S(1)}, u32[]{:S(2)}, u32[]{:S(2)}) %collective-permute-start.7) | collective-permute-done | bytes 32800 | tf_op jit(solution)/shard_map/ppermute | solution.py:34
  37.8 0.1 collective-permute-start.8
  37.9 1.5 %collective-permute-start.9 = (bf16[9,16,128]{2,1,0:T(8,128)(2,1)S(1)}, bf16[9,16,128]{2,1,0:T(8,128)(2,1)S(1)}, u32[]{:S(2)}, u32[]{:S(2)}) collective-permute-start(bf16[9,16,128]{2,1,0:T(8,128)(2,1)S(1)} %get-tuple-element.68), channel_id=1, source_target_pairs={{0,28},{4,0},{8,4},{12,8},{16,12},{20,16},{24,20},{28,24},{1,29},{... | collective-permute-start | bytes 110600 | tf_op jit(solution)/shard_map/ppermute | solution.py:34
  39.4 0.0 collective-permute-start.10
  39.4 0.9 %collective-permute-start.11 = (bf16[9,16,128]{2,1,0:T(8,128)(2,1)S(1)}, bf16[9,16,128]{2,1,0:T(8,128)(2,1)S(1)}, u32[]{:S(2)}, u32[]{:S(2)}) collective-permute-start(bf16[9,16,128]{2,1,0:T(8,128)(2,1)S(1)} %get-tuple-element.70), channel_id=1, source_target_pairs={{0,8},{4,12},{8,16},{12,20},{16,24},{20,28},{24,0},{28,4},{1,9},{5... | collective-permute-start | bytes 110600 | tf_op jit(solution)/shard_map/ppermute | solution.py:34
  40.4 0.0 copy-done.2
  40.4 6.5 %turn.1 = (f32[16,8192]{1,0:T(8,128)}, f32[16,128]{1,0:T(8,128)S(1)}, bf16[96,16,128]{2,1,0:T(8,128)(2,1)S(1)}, bf16[32,16,128]{2,1,0:T(8,128)(2,1)S(1)}) custom-call(s32[4,128]{1,0:T(4,128)S(1)} %bitcast.11, f32[64,16,128]{2,1,0:T(8,128)S(1)} %get-tuple-element.41.t1_ref, bf16[128,16,128]{2,1,0:T(8,128)(2,1)S(1)} %get-tuple-element.48.prev_ref, ...), custom_call_target="tpu_custom_call" | custom-call | bytes 16777216 | tf_op jit(solution)/shard_map/turn/pallas_call | solution.py:748
  46.9 0.0 collective-permute-done.8.x0
  46.9 0.0 collective-permute-done.9.x1
  46.9 0.0 collective-permute-done.10.x2
  46.9 0.0 collective-permute-done.11.x3
  46.9 1.8 %last.1 = bf16[32,24,128]{2,1,0:T(8,128)(2,1)S(1)} custom-call(bf16[96,16,128]{2,1,0:T(8,128)(2,1)S(1)} %get-tuple-element.65.z_ref, bf16[32,16,128]{2,1,0:T(8,128)(2,1)S(1)} %get-tuple-element.66.y_ref, f32[64,8,128]{2,1,0:T(8,128)S(1)} %get-tuple-element.51.v_ref, bf16[13,16,128]{2,1,0:T(8,128)(2,1)S(1)} %collective-permute-done.g0.v0, ...), custom_call_target="tpu_custom_call" | custom-call | bytes 1048576 | tf_op jit(solution)/shard_map/last/pallas_call | solution.py:761
  48.7 14.6 %all_to_all.10.terms_ref = bf16[32,24,128]{2,1,0:T(8,128)(2,1)S(1)} all-to-all(bf16[32,24,128]{2,1,0:T(8,128)(2,1)S(1)} %last.1), channel_id=1, replica_groups=mesh['dom'=8,'pert'=4] {'dom','pert'}, dimensions={0} | all-to-all | bytes 393216 | tf_op jit(solution)/shard_map/all_to_all | solution.py:764
  63.4 0.6 owner.1
Async XLA Ops:
  0.6 13.8 %copy-start.3 = (s32[1,4,16]{2,1,0:T(4,128)S(1)}, s32[1,4,16]{2,1,0:T(4,128)}, u32[]{:S(2)}) copy-start(s32[1,4,16]{2,1,0:T(4,128)} %send_ref.5) | copy-start | bytes 772
  0.6 13.8 %copy-start.4 = (s32[128]{0:T(128)S(1)}, s32[128]{0:T(128)}, u32[]{:S(2)}) copy-start(s32[128]{0:T(128)} %param.15) | copy-start | bytes 1540
  0.7 13.8 %copy-start.1 = (s32[128,4]{0,1:T(4,128)S(1)}, s32[128,4]{0,1:T(4,128)}, u32[]{:S(2)}) copy-start(s32[128,4]{0,1:T(4,128)} %param.13) | copy-start | bytes 6148
  3.4 11.1 %all-to-all-start = ((f32[8,40,128]{2,1,0:T(8,128)}), f32[8,40,128]{2,1,0:T(8,128)S(1)}, u32[]{:S(2)}, u32[]{:S(2)}) async-start(f32[8,40,128]{2,1,0:T(8,128)} %get-tuple-element.39), calls=%async_computation | async-start | bytes 327680 | tf_op jit(solution)/shard_map/all_to_all | solution.py:707
  14.4 0.8 %copy-start = (f32[64,128]{1,0:T(8,128)S(1)}, f32[64,128]{1,0:T(8,128)}, u32[]{:S(2)}) copy-start(f32[64,128]{1,0:T(8,128)} %get-tuple-element.40.w_hbm.w_ref) | copy-start | bytes 98308
  21.6 4.2 %collective-permute-start = (bf16[13,16,128]{2,1,0:T(8,128)(2,1)S(1)}, bf16[13,16,128]{2,1,0:T(8,128)(2,1)S(1)}, u32[]{:S(2)}, u32[]{:S(2)}) collective-permute-start(bf16[13,16,128]{2,1,0:T(8,128)(2,1)S(1)} %get-tuple-element.43), channel_id=1, source_target_pairs={{0,24},{4,28},{8,0},{12,4},{16,8},{20,12},{24,16},{28,20},{1,25},{... | collective-permute-start | bytes 159752 | tf_op jit(solution)/shard_map/ppermute | solution.py:34
  22.7 3.1 %collective-permute-start.1 = (bf16[13,16,128]{2,1,0:T(8,128)(2,1)S(1)}, bf16[13,16,128]{2,1,0:T(8,128)(2,1)S(1)}, u32[]{:S(2)}, u32[]{:S(2)}) collective-permute-start(bf16[13,16,128]{2,1,0:T(8,128)(2,1)S(1)} %get-tuple-element.44), channel_id=1, source_target_pairs={{0,28},{4,0},{8,4},{12,8},{16,12},{20,16},{24,20},{28,24},{1,29},{... | collective-permute-start | bytes 159752 | tf_op jit(solution)/shard_map/ppermute | solution.py:34
  22.7 4.5 %collective-permute-start.2 = (bf16[13,16,128]{2,1,0:T(8,128)(2,1)S(1)}, bf16[13,16,128]{2,1,0:T(8,128)(2,1)S(1)}, u32[]{:S(2)}, u32[]{:S(2)}) collective-permute-start(bf16[13,16,128]{2,1,0:T(8,128)(2,1)S(1)} %get-tuple-element.45), channel_id=1, source_target_pairs={{0,4},{4,8},{8,12},{12,16},{16,20},{20,24},{24,28},{28,0},{1,5},{5... | collective-permute-start | bytes 159752 | tf_op jit(solution)/shard_map/ppermute | solution.py:34
  23.2 5.4 %collective-permute-start.3 = (bf16[13,16,128]{2,1,0:T(8,128)(2,1)S(1)}, bf16[13,16,128]{2,1,0:T(8,128)(2,1)S(1)}, u32[]{:S(2)}, u32[]{:S(2)}) collective-permute-start(bf16[13,16,128]{2,1,0:T(8,128)(2,1)S(1)} %get-tuple-element.46), channel_id=1, source_target_pairs={{0,8},{4,12},{8,16},{12,20},{16,24},{20,28},{24,0},{28,4},{1,9},{5... | collective-permute-start | bytes 159752 | tf_op jit(solution)/shard_map/ppermute | solution.py:34
  28.6 11.8 %copy-start.2 = (f32[8192]{0:T(1024)S(1)}, f32[8192]{0:T(1024)}, u32[]{:S(2)}) copy-start(f32[8192]{0:T(1024)} %param.10) | copy-start | bytes 98308
  30.8 4.6 %collective-permute-start.4 = (bf16[8,16,128]{2,1,0:T(8,128)(2,1)S(1)}, bf16[8,16,128]{2,1,0:T(8,128)(2,1)S(1)}, u32[]{:S(2)}, u32[]{:S(2)}) collective-permute-start(bf16[8,16,128]{2,1,0:T(8,128)(2,1)S(1)} %get-tuple-element.56), channel_id=1, source_target_pairs={{0,24},{4,28},{8,0},{12,4},{16,8},{20,12},{24,16},{28,20},{1,25},{... | collective-permute-start | bytes 98312 | tf_op jit(solution)/shard_map/ppermute | solution.py:34
  31.7 3.7 %collective-permute-start.5 = (bf16[8,16,128]{2,1,0:T(8,128)(2,1)S(1)}, bf16[8,16,128]{2,1,0:T(8,128)(2,1)S(1)}, u32[]{:S(2)}, u32[]{:S(2)}) collective-permute-start(bf16[8,16,128]{2,1,0:T(8,128)(2,1)S(1)} %get-tuple-element.57), channel_id=1, source_target_pairs={{0,28},{4,0},{8,4},{12,8},{16,12},{20,16},{24,20},{28,24},{1,29},{... | collective-permute-start | bytes 98312 | tf_op jit(solution)/shard_map/ppermute | solution.py:34
  32.9 4.2 %collective-permute-start.6 = (bf16[8,16,128]{2,1,0:T(8,128)(2,1)S(1)}, bf16[8,16,128]{2,1,0:T(8,128)(2,1)S(1)}, u32[]{:S(2)}, u32[]{:S(2)}) collective-permute-start(bf16[8,16,128]{2,1,0:T(8,128)(2,1)S(1)} %get-tuple-element.58), channel_id=1, source_target_pairs={{0,4},{4,8},{8,12},{12,16},{16,20},{20,24},{24,28},{28,0},{1,5},{5... | collective-permute-start | bytes 98312 | tf_op jit(solution)/shard_map/ppermute | solution.py:34
  32.9 4.9 %collective-permute-start.7 = (bf16[8,16,128]{2,1,0:T(8,128)(2,1)S(1)}, bf16[8,16,128]{2,1,0:T(8,128)(2,1)S(1)}, u32[]{:S(2)}, u32[]{:S(2)}) collective-permute-start(bf16[8,16,128]{2,1,0:T(8,128)(2,1)S(1)} %get-tuple-element.59), channel_id=1, source_target_pairs={{0,8},{4,12},{8,16},{12,20},{16,24},{20,28},{24,0},{28,4},{1,9},{5... | collective-permute-start | bytes 98312 | tf_op jit(solution)/shard_map/ppermute | solution.py:34
  37.8 9.1 %collective-permute-start.8 = (bf16[9,16,128]{2,1,0:T(8,128)(2,1)S(1)}, bf16[9,16,128]{2,1,0:T(8,128)(2,1)S(1)}, u32[]{:S(2)}, u32[]{:S(2)}) collective-permute-start(bf16[9,16,128]{2,1,0:T(8,128)(2,1)S(1)} %get-tuple-element.67), channel_id=1, source_target_pairs={{0,24},{4,28},{8,0},{12,4},{16,8},{20,12},{24,16},{28,20},{1,25},{... | collective-permute-start | bytes 110600 | tf_op jit(solution)/shard_map/ppermute | solution.py:34
  37.9 8.9 %collective-permute-start.9 = (bf16[9,16,128]{2,1,0:T(8,128)(2,1)S(1)}, bf16[9,16,128]{2,1,0:T(8,128)(2,1)S(1)}, u32[]{:S(2)}, u32[]{:S(2)}) collective-permute-start(bf16[9,16,128]{2,1,0:T(8,128)(2,1)S(1)} %get-tuple-element.68), channel_id=1, source_target_pairs={{0,28},{4,0},{8,4},{12,8},{16,12},{20,16},{24,20},{28,24},{1,29},{... | collective-permute-start | bytes 110600 | tf_op jit(solution)/shard_map/ppermute | solution.py:34
  39.4 7.4 %collective-permute-start.10 = (bf16[9,16,128]{2,1,0:T(8,128)(2,1)S(1)}, bf16[9,16,128]{2,1,0:T(8,128)(2,1)S(1)}, u32[]{:S(2)}, u32[]{:S(2)}) collective-permute-start(bf16[9,16,128]{2,1,0:T(8,128)(2,1)S(1)} %get-tuple-element.69), channel_id=1, source_target_pairs={{0,4},{4,8},{8,12},{12,16},{16,20},{20,24},{24,28},{28,0},{1,5},{5... | collective-permute-start | bytes 110600 | tf_op jit(solution)/shard_map/ppermute | solution.py:34
  39.4 7.4 %collective-permute-start.11 = (bf16[9,16,128]{2,1,0:T(8,128)(2,1)S(1)}, bf16[9,16,128]{2,1,0:T(8,128)(2,1)S(1)}, u32[]{:S(2)}, u32[]{:S(2)}) collective-permute-start(bf16[9,16,128]{2,1,0:T(8,128)(2,1)S(1)} %get-tuple-element.70), channel_id=1, source_target_pairs={{0,8},{4,12},{8,16},{12,20},{16,24},{20,28},{24,0},{28,4},{1,9},{5... | collective-permute-start | bytes 110600 | tf_op jit(solution)/shard_map/ppermute | solution.py:34

commit v7 on v6

--- a/solution.py
+++ b/solution.py
@@ -333,13 +333,10 @@
     fill_messages(send_ref, next_ref, (o0, o1, o2, o3), low)
 
 
-def clear(acc_refs):
-    def one(place, _):
-        for ref in acc_refs:
+def zero_rows(acc_refs, places):
+    for ref in acc_refs:
+        for place in places:
             ref[place] = jnp.zeros(ref.shape[1:], F32)
-        return 0
-
-    lax.fori_loop(0, acc_refs[0].shape[0], one, 0, unroll=16)
 
 
 def multiply_scatter(quad, cols_ref, pairs, m_ref, acc_refs, low):
@@ -376,7 +373,8 @@
 
 def turn_kernel(
     cols_ref, t1_ref, prev_ref, g0, g1, g2, g3, m_ref, weight_ref, w_ref,
-    tangent_ref, terms_ref, z_ref, y_ref, ext_ref, target_ref, u_ref, *acc_refs,
+    tangent_hbm, terms_ref, z_ref, y_ref,
+    ext_ref, tangent_ref, target_ref, u_ref, sem, *acc_refs,
 ):
     pert = prev_ref.shape[1]
     low = low_half(prev_ref.shape[1:])
@@ -384,7 +382,10 @@
     blocks = cols_ref.shape[1]
     extend(ext_ref, prev_ref, (g0, g1, g2, g3), low)
 
+    share = acc_refs[0].shape[0] // (blocks // QUAD)
+
     def sweep(quad, terms):
+        zero_rows(acc_refs, [share * quad + i for i in range(share)])
         coupled = gather_multiply(quad, cols_ref, ext_ref, m_ref, low)
         for place in range(2):
             pair = 2 * quad + place
@@ -404,15 +405,19 @@
     terms_ref[...] = lax.fori_loop(
         0, blocks // QUAD, sweep, jnp.zeros((pert, LANES), F32), unroll=32
     )
+    tangent_copy = pltpu.make_async_copy(tangent_ref, tangent_hbm, sem)
+    tangent_copy.start()
     scatter_all(cols_ref, target_ref, m_ref, acc_refs, low)
 
     def own(pair, _):
         u_ref[pair] = target_ref[pair] - pair_sum(acc_refs, pair, low)
+        zero_rows(acc_refs, (2 * pair, 2 * pair + 1))
         return 0
 
     lax.fori_loop(0, blocks // 2, own, 0, unroll=16)
     for pair in range(y_ref.shape[0]):
         y_ref[pair] = (-pair_sum(acc_refs, blocks // 2 + pair, low)).astype(BF16)
+        zero_rows(acc_refs, (blocks + 2 * pair, blocks + 2 * pair + 1))
     scatter_all(cols_ref, u_ref, m_ref, acc_refs, low)
 
     def second(pair, _):
@@ -422,11 +427,10 @@
     lax.fori_loop(0, blocks // 2, second, 0, unroll=16)
     for pair in range(blocks // 2, z_ref.shape[0]):
         z_ref[pair] = pair_sum(acc_refs, pair, low).astype(BF16)
+    tangent_copy.wait()
 
 
 def scatter_all(cols_ref, u_ref, m_ref, acc_refs, low):
-    clear(acc_refs)
-
     def sweep(quad, _):
         pairs = [u_ref[2 * quad], u_ref[2 * quad + 1]]
         multiply_scatter(quad, cols_ref, pairs, m_ref, acc_refs, low)
@@ -619,7 +623,8 @@
     top = terms.astype(BF16)
     rest = (terms - top.astype(F32)).astype(BF16)
     both = jnp.concatenate([top, rest], axis=0)
-    near = hot_ref.shape[1]
+    mine = lax.axis_index("pert")
+    sub16 = lax.broadcasted_iota(jnp.int32, (pert, LANES), 0)
     perts = out_ref.shape[0] // parts
     first_names = lax.broadcasted_iota(jnp.int32, (LANES, LANES), 0).astype(F32)
     for part in range(parts):
@@ -635,32 +640,32 @@
         value = out[:pert] + out[pert:]
         curve = jnp.sum(value * got_ref[part, :pert], axis=0, keepdims=True)
         top = curve.astype(BF16).astype(F32)
-        extra = jnp.where(sub == 0, top, jnp.where(sub == 1, curve - top, 0.0))
+        extra = jnp.where(sub16 == 0, top, jnp.where(sub16 == 1, curve - top, 0.0))
         for place in range(perts):
-            out_ref[part * perts + place, :pert] = value.astype(BF16)
-            out_ref[part * perts + place, pert:] = extra.astype(BF16)
-
-
-def owner_kernel(terms_ref, hessian_ref, curve_ref, *, parts, scale):
-    pert = hessian_ref.shape[0]
+            out_ref[part * perts + place] = jnp.where(place == mine, value, extra).astype(BF16)
+
+
+def owner_kernel(terms_ref, probe_ref, hessian_ref, curve_ref, *, parts, scale):
     perts = terms_ref.shape[0] // parts
     mine = lax.axis_index("pert")
     total = jnp.zeros(hessian_ref.shape, F32)
+    every = jnp.zeros(hessian_ref.shape, F32)
     for part in range(parts):
-        total = total + terms_ref[part * perts + mine, :pert].astype(F32)
+        total = total + terms_ref[part * perts + mine].astype(F32)
+        for place in range(perts):
+            value = terms_ref[part * perts + place].astype(F32)
+            every = every + jnp.where(place == mine, 0.0, value)
     hessian_ref[...] = total
-    curve = jnp.zeros((8, LANES), F32)
-    for place in range(terms_ref.shape[0]):
-        curve = curve + terms_ref[place, pert:].astype(F32)
-    curve_ref[...] = (curve[0:1] + curve[1:2]) * scale
-
-
-def call(body, outs, spaces, scratch=(), name=None, flops=0, moved=1 << 20, limit=12):
+    own = jnp.sum(total * probe_ref[...], axis=0, keepdims=True)
+    curve_ref[...] = (own + every[0:1] + every[1:2]) * scale
+
+
+def call(body, outs, spaces, scratch=(), name=None, flops=0, moved=1 << 20, limit=12, out_specs=None):
     return pl.pallas_call(
         body,
         out_shape=outs,
         in_specs=[{"s": SMEM, "v": VMEM, "h": HBM}[s] for s in spaces],
-        out_specs=jax.tree.map(lambda _: VMEM, outs),
+        out_specs=out_specs or jax.tree.map(lambda _: VMEM, outs),
         scratch_shapes=list(scratch),
         compiler_params=pltpu.CompilerParams(vmem_limit_bytes=limit * MIB),
         name=name,
@@ -754,20 +759,28 @@
             shape((2 * capacity, pert, LANES), BF16),
         ],
         "s" + "v" * 9,
-        [ext, held, held] + accs,
+        [
+            ext,
+            pltpu.VMEM((pert, blocks * HALF), F32),
+            held,
+            held,
+            pltpu.SemaphoreType.DMA,
+        ]
+        + accs,
         name="turn",
         moved=16 << 20,
+        out_specs=[HBM, VMEM, VMEM, VMEM],
     )(columns, t1, state, *ghosts, m, weight, w)
     terms = call(
-        last_kernel, shape((parts * perts, pert + 8, LANES), BF16), "v" * 14, name="last"
+        last_kernel, shape((parts * perts, pert, LANES), BF16), "v" * 14, name="last"
     )(z, y, v, *carried, *far, hot, terms, got)
     terms = lax.all_to_all(terms, ("dom", "pert"), 0, 0, tiled=True)
     hessian_probe, curvature = call(
         functools.partial(owner_kernel, parts=parts, scale=1.0 / (pert * perts)),
         [shape(probes.shape, F32), shape((1, LANES), F32)],
-        "v",
+        "vv",
         name="owner",
-    )(terms)
+    )(terms, probes)
     return tangent, hessian_probe, curvature.reshape(-1)
 
 

time: 64.3 us -> 62.4 us (0.970)
  Pallas kernels: 22.2 us -> 21.2 us
  blocking collectives: 14.6 us -> 13.7 us
    pallas_call x1, Pallas kernels: 6.51 us -> 5.52 us  [shards(): call(turn_kernel, [shape((pert, blocks * HALF), F32), shape((pert, LANES)...]
    all_to_all x1, blocking collectives: 14.6 us -> 13.7 us  [shards(): terms = lax.all_to_all(terms, ('dom', 'pert'), 0, 0, tiled=True)]
    unnamed x11 -> x13, local copies, waits for them, and re-layouts: 4.7 us -> 4.71 us
  transfers between devices with their start and end apart: 13 -> 13, of which waited for: 6 -> 6; matrix products, arithmetic and copies ran while one was open for 6% -> 6% of each run, Pallas kernels for 13% -> 12%
where the time goes in v7:
time: 62.4 us; the launch traced here: 62.1 us
  Pallas kernels  21.2 us (34%)
  blocking collectives  13.7 us (22%)
  starting transfers between devices  12.9 us (21%)
  waiting for transfers between devices  8.72 us (14%)
  local copies, waits for them, and re-layouts  4.71 us (8%)
  between operations  0.78 us (1%)
    all_to_all x1, blocking collectives, shards(): terms = lax.all_to_all(terms, ('dom', 'pert'), 0, 0, tiled=True)  13.7 us
    ppermute x12, starting transfers between devices, rotated(): lax.ppermute(value, 'dom', [(i, (i + by) % peers) for i in range(peers)])  7.74 us
    ppermute x12, waiting for transfers between devices, rotated(): lax.ppermute(value, 'dom', [(i, (i + by) % peers) for i in range(peers)])  6.78 us
    pallas_call x1, Pallas kernels, shards(): call(first_kernel, [shape(coupling.shape, BF16), shape((pairs, 8, LANES),...  6.38 us
    pallas_call x1, Pallas kernels, shards(): call(turn_kernel, [shape((pert, blocks * HALF), F32), shape((pert, LANES)...  5.52 us
    all_to_all x1, starting transfers between devices, shards(): got = lax.all_to_all(outgoing, 'dom', 0, 0, tiled=True)  5.19 us
    unnamed x13, local copies, waits for them, and re-layouts  4.71 us
    pallas_call x1, Pallas kernels, shards(): call(functools.partial(melt_kernel, parts=parts), [shape((pairs, LANES),...  2.7 us
  transfers between devices with their start and end apart: 13, of which 6 were waited for; matrix products, arithmetic and copies ran while one was open for 6% of the time, Pallas kernels for 12%

profile of v7, /device:TPU:0, one launch (start us, length us, event | category | flops | bytes accessed | tf_op | source)
XLA Modules:
  0.0 62.1 jit_solution(1685468746195490182)
XLA Ops:
  0.6 0.0 copy-start.3
  0.6 0.0 copy-start.5
  0.7 0.0 copy-start.1
  0.7 2.7 %melt.1 = (f32[64,128]{1,0:T(8,128)}, f32[8,40,128]{2,1,0:T(8,128)}) custom-call(s32[1,4,16]{2,1,0:T(4,128)} %send_ref.5, f32[64,128]{1,0:T(8,128)} %bitcast.17, s32[1,128]{1,0:T(1,128)} %bitcast.13, f32[16,128]{1,0:T(8,128)} %probe_ref.1, bf16[64,64,128]{2,1,0:T(8,128)(2,1)} %bitcast.16), custom_call_target="tpu_custom_call" | custom-call | bytes 1048576 | tf_op jit(solution)/shard_map/melt/pallas_call | solution.py:697
  3.4 5.2 %all-to-all-start = ((f32[8,40,128]{2,1,0:T(8,128)}), f32[8,40,128]{2,1,0:T(8,128)S(1)}, u32[]{:S(2)}, u32[]{:S(2)}) async-start(f32[8,40,128]{2,1,0:T(8,128)} %get-tuple-element.39), calls=%async_computation | async-start | bytes 327680 | tf_op jit(solution)/shard_map/all_to_all | solution.py:712
  8.6 3.9 %copy.11.diag_ref = bf16[128,64,64]{2,1,0:T(8,128)(2,1)S(1)} copy(bf16[128,64,64]{0,2,1:T(8,128)(2,1)} %param.11) | data formatting | bytes 2097152 | tf_op args[3]
  12.5 1.9 %all-to-all-done.got_ref = f32[8,40,128]{2,1,0:T(8,128)S(1)} async-done(((f32[8,40,128]{2,1,0:T(8,128)}), f32[8,40,128]{2,1,0:T(8,128)S(1)}, u32[]{:S(2)}, u32[]{:S(2)}) %all-to-all-start) | async-done | bytes 163872 | tf_op jit(solution)/shard_map/all_to_all | solution.py:712
  14.4 0.0 copy-done.3
  14.4 0.0 copy-done.5
  14.4 0.0 copy-done.1
  14.4 0.0 copy-start
  14.5 0.7 %copy-done = f32[64,128]{1,0:T(8,128)S(1)} copy-done((f32[64,128]{1,0:T(8,128)S(1)}, f32[64,128]{1,0:T(8,128)}, u32[]{:S(2)}) %copy-start) | copy-done | bytes 32792
  15.2 6.4 %first.1 = (bf16[128,64,256]{2,1,0:T(8,128)(2,1)S(1)}, f32[64,8,128]{2,1,0:T(8,128)S(1)}, f32[8,128]{1,0:T(8,128)S(1)}, f32[8,128]{1,0:T(8,128)S(1)}, f32[64,16,...) custom-call(s32[4,128]{1,0:T(4,128)S(1)} %bitcast.6, ...), custom_call_target="tpu_custom_call" | custom-call | bytes 1048576 | tf_op jit(solution)/shard_map/first/pallas_call | solution.py:714
  21.6 1.1 %collective-permute-start = (bf16[13,16,128]{2,1,0:T(8,128)(2,1)S(1)}, bf16[13,16,128]{2,1,0:T(8,128)(2,1)S(1)}, u32[]{:S(2)}, u32[]{:S(2)}) collective-permute-start(bf16[13,16,128]{2,1,0:T(8,128)(2,1)S(1)} %get-tuple-element.43), channel_id=1, source_target_pairs={{0,24},{4,28},{8,0},{12,4},{16,8},{20,12},{24,16},{28,20},{1,25},{... | collective-permute-start | bytes 159752 | tf_op jit(solution)/shard_map/ppermute | solution.py:34
  22.6 0.1 collective-permute-start.1
  22.7 0.4 collective-permute-start.2
  23.2 1.1 %collective-permute-start.3 = (bf16[13,16,128]{2,1,0:T(8,128)(2,1)S(1)}, bf16[13,16,128]{2,1,0:T(8,128)(2,1)S(1)}, u32[]{:S(2)}, u32[]{:S(2)}) collective-permute-start(bf16[13,16,128]{2,1,0:T(8,128)(2,1)S(1)} %get-tuple-element.46), channel_id=1, source_target_pairs={{0,8},{4,12},{8,16},{12,20},{16,24},{20,28},{24,0},{28,4},{1,9},{5... | collective-permute-start | bytes 159752 | tf_op jit(solution)/shard_map/ppermute | solution.py:34
  24.2 1.6 %collective-permute-done.g0.v0 = bf16[13,16,128]{2,1,0:T(8,128)(2,1)S(1)} collective-permute-done((bf16[13,16,128]{2,1,0:T(8,128)(2,1)S(1)}, bf16[13,16,128]{2,1,0:T(8,128)(2,1)S(1)}, u32[]{:S(2)}, u32[]{:S(2)}) %collective-permute-start) | collective-permute-done | bytes 53280 | tf_op jit(solution)/shard_map/ppermute | solution.py:34
  25.8 0.0 collective-permute-done.1.g1.v1
  25.8 1.4 %collective-permute-done.2.g2.v2 = bf16[13,16,128]{2,1,0:T(8,128)(2,1)S(1)} collective-permute-done((bf16[13,16,128]{2,1,0:T(8,128)(2,1)S(1)}, bf16[13,16,128]{2,1,0:T(8,128)(2,1)S(1)}, u32[]{:S(2)}, u32[]{:S(2)}) %collective-permute-start.2) | collective-permute-done | bytes 53280 | tf_op jit(solution)/shard_map/ppermute | solution.py:34
  27.2 1.4 %collective-permute-done.3.g3.v3 = bf16[13,16,128]{2,1,0:T(8,128)(2,1)S(1)} collective-permute-done((bf16[13,16,128]{2,1,0:T(8,128)(2,1)S(1)}, bf16[13,16,128]{2,1,0:T(8,128)(2,1)S(1)}, u32[]{:S(2)}, u32[]{:S(2)}) %collective-permute-start.3) | collective-permute-done | bytes 53280 | tf_op jit(solution)/shard_map/ppermute | solution.py:34
  28.6 0.0 copy-start.2
  28.6 2.2 %sweep.1 = (bf16[128,16,128]{2,1,0:T(8,128)(2,1)S(1)}, bf16[8,16,128]{2,1,0:T(8,128)(2,1)S(1)}, bf16[8,16,128]{2,1,0:T(8,128)(2,1)S(1)}, bf16[8,16,128]{2,1,0:T(8,128)(2,1)S(1)}, bf16[8,16,128]{2,1,0:T(8,128)(2,1)S(1)}) custom-call(s32[4,128]{1,0:T(4,128)S(1)} %bitcast.8, s32[1,4,16]{2,1,0:T(4,128)S(1)} %copy-done.3, ...), custom_call_target="tpu_custom_call" | custom-call | bytes 1048576 | tf_op jit(solution)/shard_map/sweep/pallas_call | solution.py:738
  30.8 0.9 %collective-permute-start.4 = (bf16[8,16,128]{2,1,0:T(8,128)(2,1)S(1)}, bf16[8,16,128]{2,1,0:T(8,128)(2,1)S(1)}, u32[]{:S(2)}, u32[]{:S(2)}) collective-permute-start(bf16[8,16,128]{2,1,0:T(8,128)(2,1)S(1)} %get-tuple-element.56), channel_id=1, source_target_pairs={{0,24},{4,28},{8,0},{12,4},{16,8},{20,12},{24,16},{28,20},{1,25},{... | collective-permute-start | bytes 98312 | tf_op jit(solution)/shard_map/ppermute | solution.py:34
  31.7 1.1 %collective-permute-start.5 = (bf16[8,16,128]{2,1,0:T(8,128)(2,1)S(1)}, bf16[8,16,128]{2,1,0:T(8,128)(2,1)S(1)}, u32[]{:S(2)}, u32[]{:S(2)}) collective-permute-start(bf16[8,16,128]{2,1,0:T(8,128)(2,1)S(1)} %get-tuple-element.57), channel_id=1, source_target_pairs={{0,28},{4,0},{8,4},{12,8},{16,12},{20,16},{24,20},{28,24},{1,29},{... | collective-permute-start | bytes 98312 | tf_op jit(solution)/shard_map/ppermute | solution.py:34
  32.9 0.0 collective-permute-start.6
  32.9 0.5 collective-permute-start.7
  33.4 2.0 %window.1 = (bf16[1024,896]{1,0:T(8,128)(2,1)S(1)}, bf16[9,16,128]{2,1,0:T(8,128)(2,1)S(1)}, bf16[9,16,128]{2,1,0:T(8,128)(2,1)S(1)}, bf16[9,16,128]{2,1,0:T(8,128)(2,1)S(1)}, bf16[9,16,128]{2,1,0:T(8,128)(2,1)S(1)}) custom-call(s32[4,128]{1,0:T(4,128)S(1)} %bitcast.9, s32[1,4,16]{2,1,0:T(4,128)S(1)} %copy-done.3, s32[4,128]{1,0:T(4,128)S(1)} %bitcast.10, ...), custom_call_target="tpu_custom_call" | custom-call | bytes 4194304 | tf_op jit(solution)/shard_map/window/pallas_call | solution.py:742
  35.4 0.0 collective-permute-done.4.g0
  35.4 0.0 collective-permute-done.5.g1
  35.4 1.7 %collective-permute-done.6.g2 = bf16[8,16,128]{2,1,0:T(8,128)(2,1)S(1)} collective-permute-done((bf16[8,16,128]{2,1,0:T(8,128)(2,1)S(1)}, bf16[8,16,128]{2,1,0:T(8,128)(2,1)S(1)}, u32[]{:S(2)}, u32[]{:S(2)}) %collective-permute-start.6) | collective-permute-done | bytes 32800 | tf_op jit(solution)/shard_map/ppermute | solution.py:34
  37.1 0.7 %collective-permute-done.7.g3 = bf16[8,16,128]{2,1,0:T(8,128)(2,1)S(1)} collective-permute-done((bf16[8,16,128]{2,1,0:T(8,128)(2,1)S(1)}, bf16[8,16,128]{2,1,0:T(8,128)(2,1)S(1)}, u32[]{:S(2)}, u32[]{:S(2)}) %collective-permute-start.7) | collective-permute-done | bytes 32800 | tf_op jit(solution)/shard_map/ppermute | solution.py:34
  37.8 0.1 collective-permute-start.8
  37.9 1.5 %collective-permute-start.9 = (bf16[9,16,128]{2,1,0:T(8,128)(2,1)S(1)}, bf16[9,16,128]{2,1,0:T(8,128)(2,1)S(1)}, u32[]{:S(2)}, u32[]{:S(2)}) collective-permute-start(bf16[9,16,128]{2,1,0:T(8,128)(2,1)S(1)} %get-tuple-element.68), channel_id=1, source_target_pairs={{0,28},{4,0},{8,4},{12,8},{16,12},{20,16},{24,20},{28,24},{1,29},{... | collective-permute-start | bytes 110600 | tf_op jit(solution)/shard_map/ppermute | solution.py:34
  39.4 0.0 collective-permute-start.10
  39.4 0.9 %collective-permute-start.11 = (bf16[9,16,128]{2,1,0:T(8,128)(2,1)S(1)}, bf16[9,16,128]{2,1,0:T(8,128)(2,1)S(1)}, u32[]{:S(2)}, u32[]{:S(2)}) collective-permute-start(bf16[9,16,128]{2,1,0:T(8,128)(2,1)S(1)} %get-tuple-element.70), channel_id=1, source_target_pairs={{0,8},{4,12},{8,16},{12,20},{16,24},{20,28},{24,0},{28,4},{1,9},{5... | collective-permute-start | bytes 110600 | tf_op jit(solution)/shard_map/ppermute | solution.py:34
  40.3 0.0 copy-done.2
  40.3 0.0 copy-start.4
  40.4 5.5 %turn.1 = (f32[16,8192]{1,0:T(8,128)}, f32[16,128]{1,0:T(8,128)S(1)}, bf16[96,16,128]{2,1,0:T(8,128)(2,1)S(1)}, bf16[32,16,128]{2,1,0:T(8,128)(2,1)S(1)}) custom-call(s32[4,128]{1,0:T(4,128)S(1)} %bitcast.11, f32[64,16,128]{2,1,0:T(8,128)S(1)} %get-tuple-element.41.t1_ref, bf16[128,16,128]{2,1,0:T(8,128)(2,1)S(1)} %get-tuple-element.48.prev_ref, ...), custom_call_target="tpu_custom_call" | custom-call | bytes 16777216 | tf_op jit(solution)/shard_map/turn/pallas_call | solution.py:753
  45.9 0.0 collective-permute-done.8.x0
  45.9 0.0 collective-permute-done.9.x1
  45.9 0.0 collective-permute-done.10.x2
  45.9 0.0 collective-permute-done.11.x3
  45.9 1.8 %last.1 = bf16[32,16,128]{2,1,0:T(8,128)(2,1)S(1)} custom-call(bf16[96,16,128]{2,1,0:T(8,128)(2,1)S(1)} %get-tuple-element.65.z_ref, bf16[32,16,128]{2,1,0:T(8,128)(2,1)S(1)} %get-tuple-element.66.y_ref, f32[64,8,128]{2,1,0:T(8,128)S(1)} %get-tuple-element.51.v_ref, bf16[13,16,128]{2,1,0:T(8,128)(2,1)S(1)} %collective-permute-done.g0.v0, ...), custom_call_target="tpu_custom_call" | custom-call | bytes 1048576 | tf_op jit(solution)/shard_map/last/pallas_call | solution.py:774
  47.8 13.7 %all_to_all.10.terms_ref = bf16[32,16,128]{2,1,0:T(8,128)(2,1)S(1)} all-to-all(bf16[32,16,128]{2,1,0:T(8,128)(2,1)S(1)} %last.1), channel_id=1, replica_groups=mesh['dom'=8,'pert'=4] {'dom','pert'}, dimensions={0} | all-to-all | bytes 262144 | tf_op jit(solution)/shard_map/all_to_all | solution.py:777
  61.5 0.0 copy-done.4
  61.5 0.6 owner.1
Async XLA Ops:
  0.6 13.8 %copy-start.3 = (s32[1,4,16]{2,1,0:T(4,128)S(1)}, s32[1,4,16]{2,1,0:T(4,128)}, u32[]{:S(2)}) copy-start(s32[1,4,16]{2,1,0:T(4,128)} %send_ref.5) | copy-start | bytes 772
  0.6 13.8 %copy-start.5 = (s32[128]{0:T(128)S(1)}, s32[128]{0:T(128)}, u32[]{:S(2)}) copy-start(s32[128]{0:T(128)} %param.15) | copy-start | bytes 1540
  0.7 13.8 %copy-start.1 = (s32[128,4]{0,1:T(4,128)S(1)}, s32[128,4]{0,1:T(4,128)}, u32[]{:S(2)}) copy-start(s32[128,4]{0,1:T(4,128)} %param.13) | copy-start | bytes 6148
  3.4 11.1 %all-to-all-start = ((f32[8,40,128]{2,1,0:T(8,128)}), f32[8,40,128]{2,1,0:T(8,128)S(1)}, u32[]{:S(2)}, u32[]{:S(2)}) async-start(f32[8,40,128]{2,1,0:T(8,128)} %get-tuple-element.39), calls=%async_computation | async-start | bytes 327680 | tf_op jit(solution)/shard_map/all_to_all | solution.py:712
  14.4 0.8 %copy-start = (f32[64,128]{1,0:T(8,128)S(1)}, f32[64,128]{1,0:T(8,128)}, u32[]{:S(2)}) copy-start(f32[64,128]{1,0:T(8,128)} %get-tuple-element.40.w_hbm.w_ref) | copy-start | bytes 98308
  21.6 4.2 %collective-permute-start = (bf16[13,16,128]{2,1,0:T(8,128)(2,1)S(1)}, bf16[13,16,128]{2,1,0:T(8,128)(2,1)S(1)}, u32[]{:S(2)}, u32[]{:S(2)}) collective-permute-start(bf16[13,16,128]{2,1,0:T(8,128)(2,1)S(1)} %get-tuple-element.43), channel_id=1, source_target_pairs={{0,24},{4,28},{8,0},{12,4},{16,8},{20,12},{24,16},{28,20},{1,25},{... | collective-permute-start | bytes 159752 | tf_op jit(solution)/shard_map/ppermute | solution.py:34
  22.6 3.1 %collective-permute-start.1 = (bf16[13,16,128]{2,1,0:T(8,128)(2,1)S(1)}, bf16[13,16,128]{2,1,0:T(8,128)(2,1)S(1)}, u32[]{:S(2)}, u32[]{:S(2)}) collective-permute-start(bf16[13,16,128]{2,1,0:T(8,128)(2,1)S(1)} %get-tuple-element.44), channel_id=1, source_target_pairs={{0,28},{4,0},{8,4},{12,8},{16,12},{20,16},{24,20},{28,24},{1,29},{... | collective-permute-start | bytes 159752 | tf_op jit(solution)/shard_map/ppermute | solution.py:34
  22.7 4.5 %collective-permute-start.2 = (bf16[13,16,128]{2,1,0:T(8,128)(2,1)S(1)}, bf16[13,16,128]{2,1,0:T(8,128)(2,1)S(1)}, u32[]{:S(2)}, u32[]{:S(2)}) collective-permute-start(bf16[13,16,128]{2,1,0:T(8,128)(2,1)S(1)} %get-tuple-element.45), channel_id=1, source_target_pairs={{0,4},{4,8},{8,12},{12,16},{16,20},{20,24},{24,28},{28,0},{1,5},{5... | collective-permute-start | bytes 159752 | tf_op jit(solution)/shard_map/ppermute | solution.py:34
  23.2 5.4 %collective-permute-start.3 = (bf16[13,16,128]{2,1,0:T(8,128)(2,1)S(1)}, bf16[13,16,128]{2,1,0:T(8,128)(2,1)S(1)}, u32[]{:S(2)}, u32[]{:S(2)}) collective-permute-start(bf16[13,16,128]{2,1,0:T(8,128)(2,1)S(1)} %get-tuple-element.46), channel_id=1, source_target_pairs={{0,8},{4,12},{8,16},{12,20},{16,24},{20,28},{24,0},{28,4},{1,9},{5... | collective-permute-start | bytes 159752 | tf_op jit(solution)/shard_map/ppermute | solution.py:34
  28.6 11.8 %copy-start.2 = (f32[8192]{0:T(1024)S(1)}, f32[8192]{0:T(1024)}, u32[]{:S(2)}) copy-start(f32[8192]{0:T(1024)} %param.10) | copy-start | bytes 98308
  30.8 4.6 %collective-permute-start.4 = (bf16[8,16,128]{2,1,0:T(8,128)(2,1)S(1)}, bf16[8,16,128]{2,1,0:T(8,128)(2,1)S(1)}, u32[]{:S(2)}, u32[]{:S(2)}) collective-permute-start(bf16[8,16,128]{2,1,0:T(8,128)(2,1)S(1)} %get-tuple-element.56), channel_id=1, source_target_pairs={{0,24},{4,28},{8,0},{12,4},{16,8},{20,12},{24,16},{28,20},{1,25},{... | collective-permute-start | bytes 98312 | tf_op jit(solution)/shard_map/ppermute | solution.py:34
  31.7 3.7 %collective-permute-start.5 = (bf16[8,16,128]{2,1,0:T(8,128)(2,1)S(1)}, bf16[8,16,128]{2,1,0:T(8,128)(2,1)S(1)}, u32[]{:S(2)}, u32[]{:S(2)}) collective-permute-start(bf16[8,16,128]{2,1,0:T(8,128)(2,1)S(1)} %get-tuple-element.57), channel_id=1, source_target_pairs={{0,28},{4,0},{8,4},{12,8},{16,12},{20,16},{24,20},{28,24},{1,29},{... | collective-permute-start | bytes 98312 | tf_op jit(solution)/shard_map/ppermute | solution.py:34
  32.9 4.2 %collective-permute-start.6 = (bf16[8,16,128]{2,1,0:T(8,128)(2,1)S(1)}, bf16[8,16,128]{2,1,0:T(8,128)(2,1)S(1)}, u32[]{:S(2)}, u32[]{:S(2)}) collective-permute-start(bf16[8,16,128]{2,1,0:T(8,128)(2,1)S(1)} %get-tuple-element.58), channel_id=1, source_target_pairs={{0,4},{4,8},{8,12},{12,16},{16,20},{20,24},{24,28},{28,0},{1,5},{5... | collective-permute-start | bytes 98312 | tf_op jit(solution)/shard_map/ppermute | solution.py:34
  32.9 4.9 %collective-permute-start.7 = (bf16[8,16,128]{2,1,0:T(8,128)(2,1)S(1)}, bf16[8,16,128]{2,1,0:T(8,128)(2,1)S(1)}, u32[]{:S(2)}, u32[]{:S(2)}) collective-permute-start(bf16[8,16,128]{2,1,0:T(8,128)(2,1)S(1)} %get-tuple-element.59), channel_id=1, source_target_pairs={{0,8},{4,12},{8,16},{12,20},{16,24},{20,28},{24,0},{28,4},{1,9},{5... | collective-permute-start | bytes 98312 | tf_op jit(solution)/shard_map/ppermute | solution.py:34
  37.8 8.1 %collective-permute-start.8 = (bf16[9,16,128]{2,1,0:T(8,128)(2,1)S(1)}, bf16[9,16,128]{2,1,0:T(8,128)(2,1)S(1)}, u32[]{:S(2)}, u32[]{:S(2)}) collective-permute-start(bf16[9,16,128]{2,1,0:T(8,128)(2,1)S(1)} %get-tuple-element.67), channel_id=1, source_target_pairs={{0,24},{4,28},{8,0},{12,4},{16,8},{20,12},{24,16},{28,20},{1,25},{... | collective-permute-start | bytes 110600 | tf_op jit(solution)/shard_map/ppermute | solution.py:34
  37.9 8.0 %collective-permute-start.9 = (bf16[9,16,128]{2,1,0:T(8,128)(2,1)S(1)}, bf16[9,16,128]{2,1,0:T(8,128)(2,1)S(1)}, u32[]{:S(2)}, u32[]{:S(2)}) collective-permute-start(bf16[9,16,128]{2,1,0:T(8,128)(2,1)S(1)} %get-tuple-element.68), channel_id=1, source_target_pairs={{0,28},{4,0},{8,4},{12,8},{16,12},{20,16},{24,20},{28,24},{1,29},{... | collective-permute-start | bytes 110600 | tf_op jit(solution)/shard_map/ppermute | solution.py:34
  39.4 6.5 %collective-permute-start.10 = (bf16[9,16,128]{2,1,0:T(8,128)(2,1)S(1)}, bf16[9,16,128]{2,1,0:T(8,128)(2,1)S(1)}, u32[]{:S(2)}, u32[]{:S(2)}) collective-permute-start(bf16[9,16,128]{2,1,0:T(8,128)(2,1)S(1)} %get-tuple-element.69), channel_id=1, source_target_pairs={{0,4},{4,8},{8,12},{12,16},{16,20},{20,24},{24,28},{28,0},{1,5},{5... | collective-permute-start | bytes 110600 | tf_op jit(solution)/shard_map/ppermute | solution.py:34
  39.4 6.5 %collective-permute-start.11 = (bf16[9,16,128]{2,1,0:T(8,128)(2,1)S(1)}, bf16[9,16,128]{2,1,0:T(8,128)(2,1)S(1)}, u32[]{:S(2)}, u32[]{:S(2)}) collective-permute-start(bf16[9,16,128]{2,1,0:T(8,128)(2,1)S(1)} %get-tuple-element.70), channel_id=1, source_target_pairs={{0,8},{4,12},{8,16},{12,20},{16,24},{20,28},{24,0},{28,4},{1,9},{5... | collective-permute-start | bytes 110600 | tf_op jit(solution)/shard_map/ppermute | solution.py:34
  40.3 21.1 %copy-start.4 = (f32[16,128]{1,0:T(8,128)S(1)}, f32[16,128]{1,0:T(8,128)}, u32[]{:S(2)}) copy-start(f32[16,128]{1,0:T(8,128)} %probe_ref.1) | copy-start | bytes 24580

commit v8 on v7

--- a/solution.py
+++ b/solution.py
@@ -14,6 +14,7 @@
 HALF = 64
 QUAD = 4
 RADIX = 64
+EARLY = 32
 
 VMEM = pl.BlockSpec(memory_space=pltpu.VMEM)
 SMEM = pl.BlockSpec(memory_space=pltpu.SMEM)
@@ -150,6 +151,39 @@
             msg_ref[pair] = jnp.where(low, even, odd)
 
 
+def start_streams(coupling_hbm, coupling_ref, sems, first):
+    size = coupling_ref.shape[0] // sems.shape[0]
+    copies = [
+        pltpu.make_async_copy(
+            coupling_hbm.at[pl.ds(first + chunk * size, size)],
+            coupling_ref.at[pl.ds(chunk * size, size)],
+            sems.at[chunk],
+        )
+        for chunk in range(sems.shape[0])
+    ]
+    for copy in copies:
+        copy.start()
+    return copies
+
+
+def multiply_streams(copies, diag_ref, coupling_ref, m_ref, first):
+    size = coupling_ref.shape[0] // len(copies)
+    for chunk, copy in enumerate(copies):
+        copy.wait()
+        for block in range(chunk * size, (chunk + 1) * size):
+            m_ref[first + block] = jnp.dot(
+                diag_ref[first + block], coupling_ref[block], preferred_element_type=F32
+            ).astype(BF16)
+
+
+def settle_kernel(w_hbm, diag_ref, coupling_hbm, w_ref, m_ref, coupling_ref, w_sem, sems):
+    w_copy = pltpu.make_async_copy(w_hbm, w_ref, w_sem)
+    w_copy.start()
+    copies = start_streams(coupling_hbm, coupling_ref, sems, 0)
+    multiply_streams(copies, diag_ref, coupling_ref, m_ref, 0)
+    w_copy.wait()
+
+
 def patches_of_columns(columns_ref, ids):
     columns = jnp.concatenate([columns_ref[...], columns_ref[...]], axis=0)
     here = jnp.broadcast_to(ids[:, :LANES], columns.shape)
@@ -162,24 +196,11 @@
 
 
 def first_kernel(
-    cols_ref, send_ref, patch_ref, columns_ref, got_ref, w_hbm, diag_ref, coupling_hbm,
+    cols_ref, send_ref, patch_ref, columns_ref, got_ref, w_ref, diag_ref, coupling_hbm, early_ref,
     m_ref, v_ref, names_ref, patches_ref, t1_ref, t2_ref, o0, o1, o2, o3,
-    ext_ref, row_ref, w_ref, coupling_ref, w_sem, sems,
+    ext_ref, row_ref, coupling_ref, sems,
 ):
-    w_copy = pltpu.make_async_copy(w_hbm, w_ref, w_sem)
-    w_copy.start()
-    chunks = sems.shape[0]
-    size = diag_ref.shape[0] // chunks
-    copies = [
-        pltpu.make_async_copy(
-            coupling_hbm.at[chunk * size : (chunk + 1) * size],
-            coupling_ref.at[chunk * size : (chunk + 1) * size],
-            sems.at[chunk],
-        )
-        for chunk in range(chunks)
-    ]
-    for copy in copies:
-        copy.start()
+    copies = start_streams(coupling_hbm, coupling_ref, sems, EARLY)
     pert = t1_ref.shape[1]
     capacity = send_ref.shape[2]
     blocks = cols_ref.shape[1]
@@ -220,7 +241,6 @@
 
     for tile in range(4 * blocks // LANES):
         names_ref[tile : tile + 1, :] = listed(tile * (LANES // 4) + lane8 // 4)
-    w_copy.wait()
     w = w_ref[...]
     w_other = swap_halves(w)
     low_w = low_half(w.shape)
@@ -246,13 +266,8 @@
             spread = jnp.broadcast_to(ghost_picked[:, place : place + 1], (pert, LANES))
             ext_ref[blocks + place] = (spread * row).astype(BF16)
 
-    for chunk, copy in enumerate(copies):
-        copy.wait()
-        for block in range(chunk * size, (chunk + 1) * size):
-            m_ref[block] = jnp.dot(
-                diag_ref[block], coupling_ref[block], preferred_element_type=F32
-            ).astype(BF16)
-
+    multiply_streams(copies, diag_ref, coupling_ref, m_ref, EARLY)
+    m_ref[:EARLY] = early_ref[...]
     low8 = low_half((8, LANES))
     masks = [(sub % 4 == k) & (low8 if k % 2 == 0 else ~low8) for k in range(4)]
     nothing = jnp.zeros((8, LANES), F32)
@@ -711,6 +726,19 @@
     )(send_list, melt, patch, probes, jnp.transpose(diag_inverse, (1, 2, 0)))
     got = lax.all_to_all(outgoing, "dom", 0, 0, tiled=True)
     wide = [shape((capacity // 2 + capacity // 4 + 1, pert, LANES), BF16)] * 4
+    w, early = call(
+        settle_kernel,
+        [shape(w.shape, F32), shape((EARLY,) + coupling.shape[1:], BF16)],
+        "hvh",
+        [
+            pltpu.VMEM((EARLY,) + coupling.shape[1:], BF16),
+            pltpu.SemaphoreType.DMA,
+            pltpu.SemaphoreType.DMA((2,)),
+        ],
+        name="settle",
+        moved=4 << 20,
+        limit=49,
+    )(w, diag_inverse, coupling)
     m, v, names, patches, t1, state, *out = call(
         first_kernel,
         [
@@ -722,18 +750,16 @@
             block_array,
         ]
         + wide,
-        "ssvvvhvh",
+        "ssvvvvvhv",
         [
             ext,
             pltpu.VMEM((blocks + 4 * capacity, LANES), F32),
-            pltpu.VMEM((pairs, LANES), F32),
-            pltpu.VMEM(coupling.shape, BF16),
-            pltpu.SemaphoreType.DMA,
-            pltpu.SemaphoreType.DMA((8,)),
+            pltpu.VMEM((blocks - EARLY,) + coupling.shape[1:], BF16),
+            pltpu.SemaphoreType.DMA((6,)),
         ],
         name="first",
-        limit=46,
-    )(columns, send_list, patch, columns, got, w, diag_inverse, coupling)
+        limit=44,
+    )(columns, send_list, patch, columns, got, w, diag_inverse, coupling, early)
     carried = [rotated(x, o) for x, o in zip(out, OFFSET_LIST)]
     state, *out = call(
         sweep_kernel, [block_array] + msgs, "ssvvvvvvv", [ext], name="sweep"

time: 62.4 us -> 63.4 us (1.016)
  waiting for transfers between devices: 8.72 us -> 6.39 us
  starting transfers between devices: 12.9 us -> 14.8 us
  Pallas kernels: 21.2 us -> 22.2 us
    all_to_all x1, waiting for transfers between devices: 1.94 us -> 0.01 us  [shards(): got = lax.all_to_all(outgoing, 'dom', 0, 0, tiled=True)]
    ppermute x12, starting transfers between devices: 7.74 us -> 9.62 us  [rotated(): lax.ppermute(value, 'dom', [(i, (i + by) % peers) for i in range(peers)])]
    pallas_call x0 -> x1, Pallas kernels: none -> 1.62 us  [shards(): call(settle_kernel, [shape(w.shape, F32), shape((EARLY,) + coupling.shape...]
    pallas_call x1, Pallas kernels: 6.38 us -> 5.72 us  [shards(): call(first_kernel, [shape(coupling.shape, BF16), shape((pairs, 8, LANES),...]
  transfers between devices with their start and end apart: 13 -> 13, of which waited for: 6 -> 6; matrix products, arithmetic and copies ran while one was open for 6% -> 6% of each run, Pallas kernels for 12% -> 14%
where the time goes in v8:
time: 63.4 us; the launch traced here: 63.1 us
  Pallas kernels  22.2 us (35%)
  starting transfers between devices  14.8 us (23%)
  blocking collectives  14.1 us (22%)
  waiting for transfers between devices  6.39 us (10%)
  local copies, waits for them, and re-layouts  4.73 us (7%)
  between operations  0.82 us (1%)
    all_to_all x1, blocking collectives, shards(): terms = lax.all_to_all(terms, ('dom', 'pert'), 0, 0, tiled=True)  14.1 us
    ppermute x12, starting transfers between devices, rotated(): lax.ppermute(value, 'dom', [(i, (i + by) % peers) for i in range(peers)])  9.62 us
    ppermute x12, waiting for transfers between devices, rotated(): lax.ppermute(value, 'dom', [(i, (i + by) % peers) for i in range(peers)])  6.39 us
    pallas_call x1, Pallas kernels, shards(): call(first_kernel, [shape(coupling.shape, BF16), shape((pairs, 8, LANES),...  5.72 us
    pallas_call x1, Pallas kernels, shards(): call(turn_kernel, [shape((pert, blocks * HALF), F32), shape((pert, LANES)...  5.53 us
    all_to_all x1, starting transfers between devices, shards(): got = lax.all_to_all(outgoing, 'dom', 0, 0, tiled=True)  5.18 us
    unnamed x13, local copies, waits for them, and re-layouts  4.73 us
    pallas_call x1, Pallas kernels, shards(): call(functools.partial(melt_kernel, parts=parts), [shape((pairs, LANES),...  2.69 us
  transfers between devices with their start and end apart: 13, of which 6 were waited for; matrix products, arithmetic and copies ran while one was open for 6% of the time, Pallas kernels for 14%

profile of v8, /device:TPU:0, one launch (start us, length us, event | category | flops | bytes accessed | tf_op | source)
XLA Modules:
  0.0 63.1 jit_solution(16691372183220266103)
XLA Ops:
  0.6 2.7 %melt.1 = (f32[64,128]{1,0:T(8,128)}, f32[8,40,128]{2,1,0:T(8,128)}) custom-call(s32[1,4,16]{2,1,0:T(4,128)} %send_ref.5, f32[64,128]{1,0:T(8,128)} %bitcast.17, s32[1,128]{1,0:T(1,128)} %bitcast.13, f32[16,128]{1,0:T(8,128)} %probe_ref.1, bf16[64,64,128]{2,1,0:T(8,128)(2,1)} %bitcast.16), custom_call_target="tpu_custom_call" | custom-call | bytes 1048576 | tf_op jit(solution)/shard_map/melt/pallas_call | solution.py:712
  3.3 5.2 %all-to-all-start = ((f32[8,40,128]{2,1,0:T(8,128)}), f32[8,40,128]{2,1,0:T(8,128)S(1)}, u32[]{:S(2)}, u32[]{:S(2)}) async-start(f32[8,40,128]{2,1,0:T(8,128)} %get-tuple-element.41), calls=%async_computation | async-start | bytes 327680 | tf_op jit(solution)/shard_map/all_to_all | solution.py:727
  8.5 0.0 copy-start
  8.5 0.0 copy-start.4
  8.5 0.0 copy-start.5
  8.5 4.0 %copy.11.diag_ref = bf16[128,64,64]{2,1,0:T(8,128)(2,1)S(1)} copy(bf16[128,64,64]{0,2,1:T(8,128)(2,1)} %param.11) | data formatting | bytes 2097152 | tf_op args[3]
  12.5 0.0 copy-start.2
  12.5 0.7 %copy-done.2 = f32[64,128]{1,0:T(8,128)S(1)} copy-done((f32[64,128]{1,0:T(8,128)S(1)}, f32[64,128]{1,0:T(8,128)}, u32[]{:S(2)}) %copy-start.2) | copy-done | bytes 32792
  13.3 1.6 %settle.1 = (f32[64,128]{1,0:T(8,128)S(1)}, bf16[32,64,256]{2,1,0:T(8,128)(2,1)S(1)}) custom-call(f32[64,128]{1,0:T(8,128)S(1)} %copy-done.2, bf16[128,64,64]{2,1,0:T(8,128)(2,1)S(1)} %copy.11.diag_ref, bf16[128,64,256]{2,1,0:T(8,128)(2,1)} %coupling_hbm.3), custom_call_target="tpu_custom_call" | custom-call | bytes 4194304 | tf_op jit(solution)/shard_map/settle/pallas_call | solution.py:729
  14.9 0.0 all-to-all-done.got_ref
  14.9 0.0 copy-done
  14.9 0.0 copy-done.4
  14.9 0.0 copy-done.5
  14.9 5.7 %first.1 = (bf16[128,64,256]{2,1,0:T(8,128)(2,1)S(1)}, f32[64,8,128]{2,1,0:T(8,128)S(1)}, f32[8,128]{1,0:T(8,128)S(1)}, f32[8,128]{1,0:T(8,128)S(1)}, f32[64,16,...) custom-call(s32[4,128]{1,0:T(4,128)S(1)} %bitcast.6, ...), custom_call_target="tpu_custom_call" | custom-call | bytes 1048576 | tf_op jit(solution)/shard_map/first/pallas_call | solution.py:742
  20.7 3.0 %collective-permute-start = (bf16[13,16,128]{2,1,0:T(8,128)(2,1)S(1)}, bf16[13,16,128]{2,1,0:T(8,128)(2,1)S(1)}, u32[]{:S(2)}, u32[]{:S(2)}) collective-permute-start(bf16[13,16,128]{2,1,0:T(8,128)(2,1)S(1)} %get-tuple-element.47), channel_id=1, source_target_pairs={{0,24},{4,28},{8,0},{12,4},{16,8},{20,12},{24,16},{28,20},{1,25},{... | collective-permute-start | bytes 159752 | tf_op jit(solution)/shard_map/ppermute | solution.py:35
  23.7 0.0 collective-permute-start.1
  23.7 0.5 collective-permute-start.2
  24.2 1.0 %collective-permute-start.3 = (bf16[13,16,128]{2,1,0:T(8,128)(2,1)S(1)}, bf16[13,16,128]{2,1,0:T(8,128)(2,1)S(1)}, u32[]{:S(2)}, u32[]{:S(2)}) collective-permute-start(bf16[13,16,128]{2,1,0:T(8,128)(2,1)S(1)} %get-tuple-element.50), channel_id=1, source_target_pairs={{0,8},{4,12},{8,16},{12,20},{16,24},{20,28},{24,0},{28,4},{1,9},{5... | collective-permute-start | bytes 159752 | tf_op jit(solution)/shard_map/ppermute | solution.py:35
  25.2 0.3 collective-permute-done.g0.v0
  25.5 0.7 %collective-permute-done.1.g1.v1 = bf16[13,16,128]{2,1,0:T(8,128)(2,1)S(1)} collective-permute-done((bf16[13,16,128]{2,1,0:T(8,128)(2,1)S(1)}, bf16[13,16,128]{2,1,0:T(8,128)(2,1)S(1)}, u32[]{:S(2)}, u32[]{:S(2)}) %collective-permute-start.1) | collective-permute-done | bytes 53280 | tf_op jit(solution)/shard_map/ppermute | solution.py:35
  26.1 2.0 %collective-permute-done.2.g2.v2 = bf16[13,16,128]{2,1,0:T(8,128)(2,1)S(1)} collective-permute-done((bf16[13,16,128]{2,1,0:T(8,128)(2,1)S(1)}, bf16[13,16,128]{2,1,0:T(8,128)(2,1)S(1)}, u32[]{:S(2)}, u32[]{:S(2)}) %collective-permute-start.2) | collective-permute-done | bytes 53280 | tf_op jit(solution)/shard_map/ppermute | solution.py:35
  28.2 1.5 %collective-permute-done.3.g3.v3 = bf16[13,16,128]{2,1,0:T(8,128)(2,1)S(1)} collective-permute-done((bf16[13,16,128]{2,1,0:T(8,128)(2,1)S(1)}, bf16[13,16,128]{2,1,0:T(8,128)(2,1)S(1)}, u32[]{:S(2)}, u32[]{:S(2)}) %collective-permute-start.3) | collective-permute-done | bytes 53280 | tf_op jit(solution)/shard_map/ppermute | solution.py:35
  29.7 0.0 copy-start.1
  29.7 2.2 %sweep.1 = (bf16[128,16,128]{2,1,0:T(8,128)(2,1)S(1)}, bf16[8,16,128]{2,1,0:T(8,128)(2,1)S(1)}, bf16[8,16,128]{2,1,0:T(8,128)(2,1)S(1)}, bf16[8,16,128]{2,1,0:T(8,128)(2,1)S(1)}, bf16[8,16,128]{2,1,0:T(8,128)(2,1)S(1)}) custom-call(s32[4,128]{1,0:T(4,128)S(1)} %bitcast.8, s32[1,4,16]{2,1,0:T(4,128)S(1)} %copy-done.4, ...), custom_call_target="tpu_custom_call" | custom-call | bytes 1048576 | tf_op jit(solution)/shard_map/sweep/pallas_call | solution.py:764
  31.9 0.1 collective-permute-start.4
  32.0 1.5 %collective-permute-start.5 = (bf16[8,16,128]{2,1,0:T(8,128)(2,1)S(1)}, bf16[8,16,128]{2,1,0:T(8,128)(2,1)S(1)}, u32[]{:S(2)}, u32[]{:S(2)}) collective-permute-start(bf16[8,16,128]{2,1,0:T(8,128)(2,1)S(1)} %get-tuple-element.61), channel_id=1, source_target_pairs={{0,28},{4,0},{8,4},{12,8},{16,12},{20,16},{24,20},{28,24},{1,29},{... | collective-permute-start | bytes 98312 | tf_op jit(solution)/shard_map/ppermute | solution.py:35
  33.4 0.0 collective-permute-start.6
  33.4 1.1 %collective-permute-start.7 = (bf16[8,16,128]{2,1,0:T(8,128)(2,1)S(1)}, bf16[8,16,128]{2,1,0:T(8,128)(2,1)S(1)}, u32[]{:S(2)}, u32[]{:S(2)}) collective-permute-start(bf16[8,16,128]{2,1,0:T(8,128)(2,1)S(1)} %get-tuple-element.63), channel_id=1, source_target_pairs={{0,8},{4,12},{8,16},{12,20},{16,24},{20,28},{24,0},{28,4},{1,9},{5... | collective-permute-start | bytes 98312 | tf_op jit(solution)/shard_map/ppermute | solution.py:35
  34.5 2.0 %window.1 = (bf16[1024,896]{1,0:T(8,128)(2,1)S(1)}, bf16[9,16,128]{2,1,0:T(8,128)(2,1)S(1)}, bf16[9,16,128]{2,1,0:T(8,128)(2,1)S(1)}, bf16[9,16,128]{2,1,0:T(8,128)(2,1)S(1)}, bf16[9,16,128]{2,1,0:T(8,128)(2,1)S(1)}) custom-call(s32[4,128]{1,0:T(4,128)S(1)} %bitcast.9, s32[1,4,16]{2,1,0:T(4,128)S(1)} %copy-done.4, s32[4,128]{1,0:T(4,128)S(1)} %bitcast.10, ...), custom_call_target="tpu_custom_call" | custom-call | bytes 4194304 | tf_op jit(solution)/shard_map/window/pallas_call | solution.py:768
  36.5 0.0 collective-permute-done.4.g0
  36.5 0.0 collective-permute-done.5.g1
  36.5 1.2 %collective-permute-done.6.g2 = bf16[8,16,128]{2,1,0:T(8,128)(2,1)S(1)} collective-permute-done((bf16[8,16,128]{2,1,0:T(8,128)(2,1)S(1)}, bf16[8,16,128]{2,1,0:T(8,128)(2,1)S(1)}, u32[]{:S(2)}, u32[]{:S(2)}) %collective-permute-start.6) | collective-permute-done | bytes 32800 | tf_op jit(solution)/shard_map/ppermute | solution.py:35
  37.7 0.7 %collective-permute-done.7.g3 = bf16[8,16,128]{2,1,0:T(8,128)(2,1)S(1)} collective-permute-done((bf16[8,16,128]{2,1,0:T(8,128)(2,1)S(1)}, bf16[8,16,128]{2,1,0:T(8,128)(2,1)S(1)}, u32[]{:S(2)}, u32[]{:S(2)}) %collective-permute-start.7) | collective-permute-done | bytes 32800 | tf_op jit(solution)/shard_map/ppermute | solution.py:35
  38.4 0.2 collective-permute-start.8
  38.6 1.9 %collective-permute-start.9 = (bf16[9,16,128]{2,1,0:T(8,128)(2,1)S(1)}, bf16[9,16,128]{2,1,0:T(8,128)(2,1)S(1)}, u32[]{:S(2)}, u32[]{:S(2)}) collective-permute-start(bf16[9,16,128]{2,1,0:T(8,128)(2,1)S(1)} %get-tuple-element.72), channel_id=1, source_target_pairs={{0,28},{4,0},{8,4},{12,8},{16,12},{20,16},{24,20},{28,24},{1,29},{... | collective-permute-start | bytes 110600 | tf_op jit(solution)/shard_map/ppermute | solution.py:35
  40.5 0.0 collective-permute-start.10
  40.5 0.4 collective-permute-start.11
  40.9 0.0 copy-done.1
  40.9 0.0 copy-start.3
  40.9 5.5 %turn.1 = (f32[16,8192]{1,0:T(8,128)}, f32[16,128]{1,0:T(8,128)S(1)}, bf16[96,16,128]{2,1,0:T(8,128)(2,1)S(1)}, bf16[32,16,128]{2,1,0:T(8,128)(2,1)S(1)}) custom-call(s32[4,128]{1,0:T(4,128)S(1)} %bitcast.11, f32[64,16,128]{2,1,0:T(8,128)S(1)} %get-tuple-element.45.t1_ref, bf16[128,16,128]{2,1,0:T(8,128)(2,1)S(1)} %get-tuple-element.52.prev_ref, ...), custom_call_target="tpu_custom_call" | custom-call | bytes 16777216 | tf_op jit(solution)/shard_map/turn/pallas_call | solution.py:779
  46.4 0.0 collective-permute-done.8.x0
  46.5 0.0 collective-permute-done.9.x1
  46.5 0.0 collective-permute-done.10.x2
  46.5 0.0 collective-permute-done.11.x3
  46.5 1.8 %last.1 = bf16[32,16,128]{2,1,0:T(8,128)(2,1)S(1)} custom-call(bf16[96,16,128]{2,1,0:T(8,128)(2,1)S(1)} %get-tuple-element.69.z_ref, bf16[32,16,128]{2,1,0:T(8,128)(2,1)S(1)} %get-tuple-element.70.y_ref, f32[64,8,128]{2,1,0:T(8,128)S(1)} %get-tuple-element.55.v_ref, bf16[13,16,128]{2,1,0:T(8,128)(2,1)S(1)} %collective-permute-done.g0.v0, ...), custom_call_target="tpu_custom_call" | custom-call | bytes 1048576 | tf_op jit(solution)/shard_map/last/pallas_call | solution.py:800
  48.3 14.1 %all_to_all.10.terms_ref = bf16[32,16,128]{2,1,0:T(8,128)(2,1)S(1)} all-to-all(bf16[32,16,128]{2,1,0:T(8,128)(2,1)S(1)} %last.1), channel_id=1, replica_groups=mesh['dom'=8,'pert'=4] {'dom','pert'}, dimensions={0} | all-to-all | bytes 262144 | tf_op jit(solution)/shard_map/all_to_all | solution.py:803
  62.5 0.0 copy-done.3
  62.5 0.6 owner.1
Async XLA Ops:
  3.3 11.6 %all-to-all-start = ((f32[8,40,128]{2,1,0:T(8,128)}), f32[8,40,128]{2,1,0:T(8,128)S(1)}, u32[]{:S(2)}, u32[]{:S(2)}) async-start(f32[8,40,128]{2,1,0:T(8,128)} %get-tuple-element.41), calls=%async_computation | async-start | bytes 327680 | tf_op jit(solution)/shard_map/all_to_all | solution.py:727
  8.5 6.4 %copy-start = (s32[128,4]{0,1:T(4,128)S(1)}, s32[128,4]{0,1:T(4,128)}, u32[]{:S(2)}) copy-start(s32[128,4]{0,1:T(4,128)} %param.13) | copy-start | bytes 6148
  8.5 6.4 %copy-start.4 = (s32[1,4,16]{2,1,0:T(4,128)S(1)}, s32[1,4,16]{2,1,0:T(4,128)}, u32[]{:S(2)}) copy-start(s32[1,4,16]{2,1,0:T(4,128)} %send_ref.5) | copy-start | bytes 772
  8.5 6.4 %copy-start.5 = (s32[128]{0:T(128)S(1)}, s32[128]{0:T(128)}, u32[]{:S(2)}) copy-start(s32[128]{0:T(128)} %param.15) | copy-start | bytes 1540
  12.5 0.8 %copy-start.2 = (f32[64,128]{1,0:T(8,128)S(1)}, f32[64,128]{1,0:T(8,128)}, u32[]{:S(2)}) copy-start(f32[64,128]{1,0:T(8,128)} %get-tuple-element.42.w_hbm) | copy-start | bytes 98308
  20.7 4.8 %collective-permute-start = (bf16[13,16,128]{2,1,0:T(8,128)(2,1)S(1)}, bf16[13,16,128]{2,1,0:T(8,128)(2,1)S(1)}, u32[]{:S(2)}, u32[]{:S(2)}) collective-permute-start(bf16[13,16,128]{2,1,0:T(8,128)(2,1)S(1)} %get-tuple-element.47), channel_id=1, source_target_pairs={{0,24},{4,28},{8,0},{12,4},{16,8},{20,12},{24,16},{28,20},{1,25},{... | collective-permute-start | bytes 159752 | tf_op jit(solution)/shard_map/ppermute | solution.py:35
  23.7 2.5 %collective-permute-start.1 = (bf16[13,16,128]{2,1,0:T(8,128)(2,1)S(1)}, bf16[13,16,128]{2,1,0:T(8,128)(2,1)S(1)}, u32[]{:S(2)}, u32[]{:S(2)}) collective-permute-start(bf16[13,16,128]{2,1,0:T(8,128)(2,1)S(1)} %get-tuple-element.48), channel_id=1, source_target_pairs={{0,28},{4,0},{8,4},{12,8},{16,12},{20,16},{24,20},{28,24},{1,29},{... | collective-permute-start | bytes 159752 | tf_op jit(solution)/shard_map/ppermute | solution.py:35
  23.7 4.5 %collective-permute-start.2 = (bf16[13,16,128]{2,1,0:T(8,128)(2,1)S(1)}, bf16[13,16,128]{2,1,0:T(8,128)(2,1)S(1)}, u32[]{:S(2)}, u32[]{:S(2)}) collective-permute-start(bf16[13,16,128]{2,1,0:T(8,128)(2,1)S(1)} %get-tuple-element.49), channel_id=1, source_target_pairs={{0,4},{4,8},{8,12},{12,16},{16,20},{20,24},{24,28},{28,0},{1,5},{5... | collective-permute-start | bytes 159752 | tf_op jit(solution)/shard_map/ppermute | solution.py:35
  24.2 5.5 %collective-permute-start.3 = (bf16[13,16,128]{2,1,0:T(8,128)(2,1)S(1)}, bf16[13,16,128]{2,1,0:T(8,128)(2,1)S(1)}, u32[]{:S(2)}, u32[]{:S(2)}) collective-permute-start(bf16[13,16,128]{2,1,0:T(8,128)(2,1)S(1)} %get-tuple-element.50), channel_id=1, source_target_pairs={{0,8},{4,12},{8,16},{12,20},{16,24},{20,28},{24,0},{28,4},{1,9},{5... | collective-permute-start | bytes 159752 | tf_op jit(solution)/shard_map/ppermute | solution.py:35
  29.7 11.2 %copy-start.1 = (f32[8192]{0:T(1024)S(1)}, f32[8192]{0:T(1024)}, u32[]{:S(2)}) copy-start(f32[8192]{0:T(1024)} %param.10) | copy-start | bytes 98308
  31.9 4.6 %collective-permute-start.4 = (bf16[8,16,128]{2,1,0:T(8,128)(2,1)S(1)}, bf16[8,16,128]{2,1,0:T(8,128)(2,1)S(1)}, u32[]{:S(2)}, u32[]{:S(2)}) collective-permute-start(bf16[8,16,128]{2,1,0:T(8,128)(2,1)S(1)} %get-tuple-element.60), channel_id=1, source_target_pairs={{0,24},{4,28},{8,0},{12,4},{16,8},{20,12},{24,16},{28,20},{1,25},{... | collective-permute-start | bytes 98312 | tf_op jit(solution)/shard_map/ppermute | solution.py:35
  32.0 4.5 %collective-permute-start.5 = (bf16[8,16,128]{2,1,0:T(8,128)(2,1)S(1)}, bf16[8,16,128]{2,1,0:T(8,128)(2,1)S(1)}, u32[]{:S(2)}, u32[]{:S(2)}) collective-permute-start(bf16[8,16,128]{2,1,0:T(8,128)(2,1)S(1)} %get-tuple-element.61), channel_id=1, source_target_pairs={{0,28},{4,0},{8,4},{12,8},{16,12},{20,16},{24,20},{28,24},{1,29},{... | collective-permute-start | bytes 98312 | tf_op jit(solution)/shard_map/ppermute | solution.py:35
  33.4 4.2 %collective-permute-start.6 = (bf16[8,16,128]{2,1,0:T(8,128)(2,1)S(1)}, bf16[8,16,128]{2,1,0:T(8,128)(2,1)S(1)}, u32[]{:S(2)}, u32[]{:S(2)}) collective-permute-start(bf16[8,16,128]{2,1,0:T(8,128)(2,1)S(1)} %get-tuple-element.62), channel_id=1, source_target_pairs={{0,4},{4,8},{8,12},{12,16},{16,20},{20,24},{24,28},{28,0},{1,5},{5... | collective-permute-start | bytes 98312 | tf_op jit(solution)/shard_map/ppermute | solution.py:35
  33.4 4.9 %collective-permute-start.7 = (bf16[8,16,128]{2,1,0:T(8,128)(2,1)S(1)}, bf16[8,16,128]{2,1,0:T(8,128)(2,1)S(1)}, u32[]{:S(2)}, u32[]{:S(2)}) collective-permute-start(bf16[8,16,128]{2,1,0:T(8,128)(2,1)S(1)} %get-tuple-element.63), channel_id=1, source_target_pairs={{0,8},{4,12},{8,16},{12,20},{16,24},{20,28},{24,0},{28,4},{1,9},{5... | collective-permute-start | bytes 98312 | tf_op jit(solution)/shard_map/ppermute | solution.py:35
  38.4 8.1 %collective-permute-start.8 = (bf16[9,16,128]{2,1,0:T(8,128)(2,1)S(1)}, bf16[9,16,128]{2,1,0:T(8,128)(2,1)S(1)}, u32[]{:S(2)}, u32[]{:S(2)}) collective-permute-start(bf16[9,16,128]{2,1,0:T(8,128)(2,1)S(1)} %get-tuple-element.71), channel_id=1, source_target_pairs={{0,24},{4,28},{8,0},{12,4},{16,8},{20,12},{24,16},{28,20},{1,25},{... | collective-permute-start | bytes 110600 | tf_op jit(solution)/shard_map/ppermute | solution.py:35
  38.6 7.9 %collective-permute-start.9 = (bf16[9,16,128]{2,1,0:T(8,128)(2,1)S(1)}, bf16[9,16,128]{2,1,0:T(8,128)(2,1)S(1)}, u32[]{:S(2)}, u32[]{:S(2)}) collective-permute-start(bf16[9,16,128]{2,1,0:T(8,128)(2,1)S(1)} %get-tuple-element.72), channel_id=1, source_target_pairs={{0,28},{4,0},{8,4},{12,8},{16,12},{20,16},{24,20},{28,24},{1,29},{... | collective-permute-start | bytes 110600 | tf_op jit(solution)/shard_map/ppermute | solution.py:35
  40.5 6.0 %collective-permute-start.10 = (bf16[9,16,128]{2,1,0:T(8,128)(2,1)S(1)}, bf16[9,16,128]{2,1,0:T(8,128)(2,1)S(1)}, u32[]{:S(2)}, u32[]{:S(2)}) collective-permute-start(bf16[9,16,128]{2,1,0:T(8,128)(2,1)S(1)} %get-tuple-element.73), channel_id=1, source_target_pairs={{0,4},{4,8},{8,12},{12,16},{16,20},{20,24},{24,28},{28,0},{1,5},{5... | collective-permute-start | bytes 110600 | tf_op jit(solution)/shard_map/ppermute | solution.py:35
  40.5 6.0 %collective-permute-start.11 = (bf16[9,16,128]{2,1,0:T(8,128)(2,1)S(1)}, bf16[9,16,128]{2,1,0:T(8,128)(2,1)S(1)}, u32[]{:S(2)}, u32[]{:S(2)}) collective-permute-start(bf16[9,16,128]{2,1,0:T(8,128)(2,1)S(1)} %get-tuple-element.74), channel_id=1, source_target_pairs={{0,8},{4,12},{8,16},{12,20},{16,24},{20,28},{24,0},{28,4},{1,9},{5... | collective-permute-start | bytes 110600 | tf_op jit(solution)/shard_map/ppermute | solution.py:35
  40.9 21.6 %copy-start.3 = (f32[16,128]{1,0:T(8,128)S(1)}, f32[16,128]{1,0:T(8,128)}, u32[]{:S(2)}) copy-start(f32[16,128]{1,0:T(8,128)} %probe_ref.1) | copy-start | bytes 24580

commit v9 on v7

--- a/solution.py
+++ b/solution.py
@@ -14,6 +14,7 @@
 HALF = 64
 QUAD = 4
 RADIX = 64
+PITCH = 136
 
 VMEM = pl.BlockSpec(memory_space=pltpu.VMEM)
 SMEM = pl.BlockSpec(memory_space=pltpu.SMEM)
@@ -162,14 +163,16 @@
 
 
 def first_kernel(
-    cols_ref, send_ref, patch_ref, columns_ref, got_ref, w_hbm, diag_ref, coupling_hbm,
+    cols_ref, send_ref, patch_ref, columns_ref, got_ref, w_hbm, diag_hbm, coupling_hbm,
     m_ref, v_ref, names_ref, patches_ref, t1_ref, t2_ref, o0, o1, o2, o3,
-    ext_ref, row_ref, w_ref, coupling_ref, w_sem, sems,
+    ext_ref, row_ref, w_ref, coupling_ref, diag_ref, turned_ref, w_sem, diag_sem, sems,
 ):
     w_copy = pltpu.make_async_copy(w_hbm, w_ref, w_sem)
     w_copy.start()
+    diag_copy = pltpu.make_async_copy(diag_hbm, diag_ref, diag_sem)
+    diag_copy.start()
     chunks = sems.shape[0]
-    size = diag_ref.shape[0] // chunks
+    size = m_ref.shape[0] // chunks
     copies = [
         pltpu.make_async_copy(
             coupling_hbm.at[chunk * size : (chunk + 1) * size],
@@ -246,11 +249,19 @@
             spread = jnp.broadcast_to(ghost_picked[:, place : place + 1], (pert, LANES))
             ext_ref[blocks + place] = (spread * row).astype(BF16)
 
+    diag_copy.wait()
+    for i in range(HALF // 2):
+        both = jnp.concatenate(
+            [diag_ref[i].astype(F32), diag_ref[i + HALF // 2].astype(F32)], axis=0
+        )
+        turned_ref[i * PITCH : i * PITCH + LANES, :] = jnp.transpose(both)
     for chunk, copy in enumerate(copies):
         copy.wait()
         for block in range(chunk * size, (chunk + 1) * size):
+            rows = turned_ref[pl.ds(block, HALF // 2, stride=PITCH), :]
+            diag = jnp.concatenate([rows, swap_halves(rows)], axis=0)[:, :HALF]
             m_ref[block] = jnp.dot(
-                diag_ref[block], coupling_ref[block], preferred_element_type=F32
+                diag.astype(BF16), coupling_ref[block], preferred_element_type=F32
             ).astype(BF16)
 
     low8 = low_half((8, LANES))
@@ -694,6 +705,7 @@
 
     perts = lax.axis_size("pert")
     columns = columns.T
+    diag_turned = jnp.transpose(diag_inverse, (1, 2, 0))
     w, outgoing = call(
         functools.partial(melt_kernel, parts=parts),
         [shape((pairs, LANES), F32), shape((parts, pert + capacity + 8, LANES), F32)],
@@ -708,7 +720,7 @@
         ],
         name="melt",
         limit=60,
-    )(send_list, melt, patch, probes, jnp.transpose(diag_inverse, (1, 2, 0)))
+    )(send_list, melt, patch, probes, diag_turned)
     got = lax.all_to_all(outgoing, "dom", 0, 0, tiled=True)
     wide = [shape((capacity // 2 + capacity // 4 + 1, pert, LANES), BF16)] * 4
     m, v, names, patches, t1, state, *out = call(
@@ -722,18 +734,21 @@
             block_array,
         ]
         + wide,
-        "ssvvvhvh",
+        "ssvvvhhh",
         [
             ext,
             pltpu.VMEM((blocks + 4 * capacity, LANES), F32),
             pltpu.VMEM((pairs, LANES), F32),
             pltpu.VMEM(coupling.shape, BF16),
+            pltpu.VMEM((HALF, HALF, blocks), BF16),
+            pltpu.VMEM((HALF // 2 * PITCH, LANES), F32),
+            pltpu.SemaphoreType.DMA,
             pltpu.SemaphoreType.DMA,
             pltpu.SemaphoreType.DMA((8,)),
         ],
         name="first",
         limit=46,
-    )(columns, send_list, patch, columns, got, w, diag_inverse, coupling)
+    )(columns, send_list, patch, columns, got, w, diag_turned, coupling)
     carried = [rotated(x, o) for x, o in zip(out, OFFSET_LIST)]
     state, *out = call(
         sweep_kernel, [block_array] + msgs, "ssvvvvvvv", [ext], name="sweep"

time: 62.4 us -> 66.5 us (1.066)
  blocking collectives: 13.7 us -> 24.7 us
  starting transfers between devices: 12.9 us -> 7.94 us
  waiting for transfers between devices: 8.72 us -> 6.52 us
  Pallas kernels: 21.2 us -> 22.1 us
  local copies, waits for them, and re-layouts: 4.71 us -> 4.01 us
    all_to_all x0 -> x1, blocking collectives: none -> 11.1 us  [shards(): got = lax.all_to_all(outgoing, 'dom', 0, 0, tiled=True)]
    all_to_all x1 -> x0, starting transfers between devices: 5.19 us -> none  [shards(): got = lax.all_to_all(outgoing, 'dom', 0, 0, tiled=True)]
    all_to_all x1 -> x0, waiting for transfers between devices: 1.94 us -> none  [shards(): got = lax.all_to_all(outgoing, 'dom', 0, 0, tiled=True)]
    pallas_call x1, Pallas kernels: 6.38 us -> 7.27 us  [shards(): call(first_kernel, [shape(coupling.shape, BF16), shape((pairs, 8, LANES),...]
    unnamed x13 -> x14, local copies, waits for them, and re-layouts: 4.71 us -> 4.01 us
  transfers between devices with their start and end apart: 13 -> 12, of which waited for: 6 -> 5; matrix products, arithmetic and copies ran while one was open for 6% -> 0% of each run, Pallas kernels for 12% -> 11%
where the time goes in v9:
time: 66.5 us; the launch traced here: 66 us
  blocking collectives  24.7 us (37%)
  Pallas kernels  22.1 us (33%)
  starting transfers between devices  7.94 us (12%)
  waiting for transfers between devices  6.52 us (10%)
  local copies, waits for them, and re-layouts  4.01 us (6%)
  between operations  0.74 us (1%)
    all_to_all x1, blocking collectives, shards(): terms = lax.all_to_all(terms, ('dom', 'pert'), 0, 0, tiled=True)  13.7 us
    all_to_all x1, blocking collectives, shards(): got = lax.all_to_all(outgoing, 'dom', 0, 0, tiled=True)  11.1 us
    ppermute x12, starting transfers between devices, rotated(): lax.ppermute(value, 'dom', [(i, (i + by) % peers) for i in range(peers)])  7.94 us
    pallas_call x1, Pallas kernels, shards(): call(first_kernel, [shape(coupling.shape, BF16), shape((pairs, 8, LANES),...  7.27 us
    ppermute x12, waiting for transfers between devices, rotated(): lax.ppermute(value, 'dom', [(i, (i + by) % peers) for i in range(peers)])  6.52 us
    pallas_call x1, Pallas kernels, shards(): call(turn_kernel, [shape((pert, blocks * HALF), F32), shape((pert, LANES)...  5.52 us
    unnamed x14, local copies, waits for them, and re-layouts  4.01 us
    pallas_call x1, Pallas kernels, shards(): call(functools.partial(melt_kernel, parts=parts), [shape((pairs, LANES),...  2.68 us
  transfers between devices with their start and end apart: 12, of which 5 were waited for; matrix products, arithmetic and copies ran while one was open for 0% of the time, Pallas kernels for 11%

profile of v9, /device:TPU:0, one launch (start us, length us, event | category | flops | bytes accessed | tf_op | source)
XLA Modules:
  0.0 66.0 jit_solution(14637767720045836045)
XLA Ops:
  0.6 2.7 %melt.1 = (f32[64,128]{1,0:T(8,128)}, f32[8,40,128]{2,1,0:T(8,128)}) custom-call(s32[1,4,16]{2,1,0:T(4,128)} %send_ref.5, f32[64,128]{1,0:T(8,128)} %bitcast.18, s32[1,128]{1,0:T(1,128)} %bitcast.15, f32[16,128]{1,0:T(8,128)} %probe_ref.1, bf16[64,64,128]{2,1,0:T(8,128)(2,1)} %bitcast.6), custom_call_target="tpu_custom_call" | custom-call | bytes 1048576 | tf_op jit(solution)/shard_map/melt/pallas_call | solution.py:709
  3.3 11.1 %all_to_all.10.got_ref = f32[8,40,128]{2,1,0:T(8,128)S(1)} all-to-all(f32[8,40,128]{2,1,0:T(8,128)} %get-tuple-element.39), channel_id=1, replica_groups=mesh['dom'=8,'pert'=4] {'dom'}, dimensions={0} | all-to-all | bytes 327680 | tf_op jit(solution)/shard_map/all_to_all | solution.py:724
  14.4 0.0 copy-start
  14.4 1.2 %copy-done = bf16[128,64,64]{0,2,1:T(8,128)(2,1)S(1)} copy-done((bf16[128,64,64]{0,2,1:T(8,128)(2,1)S(1)}, bf16[128,64,64]{0,2,1:T(8,128)(2,1)}, u32[]{:S(2)}) %copy-start) | copy-done | bytes 1048600
  15.6 0.0 copy-start.1
  15.6 0.8 %copy-done.1 = f32[64,128]{1,0:T(8,128)S(1)} copy-done((f32[64,128]{1,0:T(8,128)S(1)}, f32[64,128]{1,0:T(8,128)}, u32[]{:S(2)}) %copy-start.1) | copy-done | bytes 32792
  16.4 0.0 copy-start.2
  16.4 0.7 %copy-done.2 = s32[128,4]{0,1:T(4,128)S(1)} copy-done((s32[128,4]{0,1:T(4,128)S(1)}, s32[128,4]{0,1:T(4,128)}, u32[]{:S(2)}) %copy-start.2) | copy-done | bytes 2072
  17.0 0.0 copy-start.4
  17.1 0.7 %copy-done.4 = s32[1,4,16]{2,1,0:T(4,128)S(1)} copy-done((s32[1,4,16]{2,1,0:T(4,128)S(1)}, s32[1,4,16]{2,1,0:T(4,128)}, u32[]{:S(2)}) %copy-start.4) | copy-done | bytes 280
  17.7 0.0 copy-start.6
  17.7 0.7 copy-done.6
  18.4 7.3 %first.1 = (bf16[128,64,256]{2,1,0:T(8,128)(2,1)S(1)}, f32[64,8,128]{2,1,0:T(8,128)S(1)}, f32[8,128]{1,0:T(8,128)S(1)}, f32[8,128]{1,0:T(8,128)S(1)}, f32[64,16,...) custom-call(s32[4,128]{1,0:T(4,128)S(1)} %bitcast.8, ...), custom_call_target="tpu_custom_call" | custom-call | bytes 1048576 | tf_op jit(solution)/shard_map/first/pallas_call | solution.py:726
  25.7 0.6 collective-permute-start
  26.3 0.4 collective-permute-start.1
  26.7 0.1 collective-permute-start.2
  26.8 1.5 %collective-permute-start.3 = (bf16[13,16,128]{2,1,0:T(8,128)(2,1)S(1)}, bf16[13,16,128]{2,1,0:T(8,128)(2,1)S(1)}, u32[]{:S(2)}, u32[]{:S(2)}) collective-permute-start(bf16[13,16,128]{2,1,0:T(8,128)(2,1)S(1)} %get-tuple-element.46), channel_id=1, source_target_pairs={{0,8},{4,12},{8,16},{12,20},{16,24},{20,28},{24,0},{28,4},{1,9},{5... | collective-permute-start | bytes 159752 | tf_op jit(solution)/shard_map/ppermute | solution.py:35
  28.3 1.6 %collective-permute-done.g0.v0 = bf16[13,16,128]{2,1,0:T(8,128)(2,1)S(1)} collective-permute-done((bf16[13,16,128]{2,1,0:T(8,128)(2,1)S(1)}, bf16[13,16,128]{2,1,0:T(8,128)(2,1)S(1)}, u32[]{:S(2)}, u32[]{:S(2)}) %collective-permute-start) | collective-permute-done | bytes 53280 | tf_op jit(solution)/shard_map/ppermute | solution.py:35
  29.8 0.0 collective-permute-done.1.g1.v1
  29.9 1.3 %collective-permute-done.2.g2.v2 = bf16[13,16,128]{2,1,0:T(8,128)(2,1)S(1)} collective-permute-done((bf16[13,16,128]{2,1,0:T(8,128)(2,1)S(1)}, bf16[13,16,128]{2,1,0:T(8,128)(2,1)S(1)}, u32[]{:S(2)}, u32[]{:S(2)}) %collective-permute-start.2) | collective-permute-done | bytes 53280 | tf_op jit(solution)/shard_map/ppermute | solution.py:35
  31.2 1.1 %collective-permute-done.3.g3.v3 = bf16[13,16,128]{2,1,0:T(8,128)(2,1)S(1)} collective-permute-done((bf16[13,16,128]{2,1,0:T(8,128)(2,1)S(1)}, bf16[13,16,128]{2,1,0:T(8,128)(2,1)S(1)}, u32[]{:S(2)}, u32[]{:S(2)}) %collective-permute-start.3) | collective-permute-done | bytes 53280 | tf_op jit(solution)/shard_map/ppermute | solution.py:35
  32.3 0.0 copy-start.3
  32.3 2.2 %sweep.1 = (bf16[128,16,128]{2,1,0:T(8,128)(2,1)S(1)}, bf16[8,16,128]{2,1,0:T(8,128)(2,1)S(1)}, bf16[8,16,128]{2,1,0:T(8,128)(2,1)S(1)}, bf16[8,16,128]{2,1,0:T(8,128)(2,1)S(1)}, bf16[8,16,128]{2,1,0:T(8,128)(2,1)S(1)}) custom-call(s32[4,128]{1,0:T(4,128)S(1)} %bitcast.10, s32[1,4,16]{2,1,0:T(4,128)S(1)} %copy-done.4, ...), custom_call_target="tpu_custom_call" | custom-call | bytes 1048576 | tf_op jit(solution)/shard_map/sweep/pallas_call | solution.py:753
  34.5 1.4 %collective-permute-start.4 = (bf16[8,16,128]{2,1,0:T(8,128)(2,1)S(1)}, bf16[8,16,128]{2,1,0:T(8,128)(2,1)S(1)}, u32[]{:S(2)}, u32[]{:S(2)}) collective-permute-start(bf16[8,16,128]{2,1,0:T(8,128)(2,1)S(1)} %get-tuple-element.56), channel_id=1, source_target_pairs={{0,24},{4,28},{8,0},{12,4},{16,8},{20,12},{24,16},{28,20},{1,25},{... | collective-permute-start | bytes 98312 | tf_op jit(solution)/shard_map/ppermute | solution.py:35
  35.9 1.0 %collective-permute-start.5 = (bf16[8,16,128]{2,1,0:T(8,128)(2,1)S(1)}, bf16[8,16,128]{2,1,0:T(8,128)(2,1)S(1)}, u32[]{:S(2)}, u32[]{:S(2)}) collective-permute-start(bf16[8,16,128]{2,1,0:T(8,128)(2,1)S(1)} %get-tuple-element.57), channel_id=1, source_target_pairs={{0,28},{4,0},{8,4},{12,8},{16,12},{20,16},{24,20},{28,24},{1,29},{... | collective-permute-start | bytes 98312 | tf_op jit(solution)/shard_map/ppermute | solution.py:35
  36.9 0.0 collective-permute-start.6
  36.9 0.4 collective-permute-start.7
  37.3 2.0 %window.1 = (bf16[1024,896]{1,0:T(8,128)(2,1)S(1)}, bf16[9,16,128]{2,1,0:T(8,128)(2,1)S(1)}, bf16[9,16,128]{2,1,0:T(8,128)(2,1)S(1)}, bf16[9,16,128]{2,1,0:T(8,128)(2,1)S(1)}, bf16[9,16,128]{2,1,0:T(8,128)(2,1)S(1)}) custom-call(s32[4,128]{1,0:T(4,128)S(1)} %bitcast.11, s32[1,4,16]{2,1,0:T(4,128)S(1)} %copy-done.4, s32[4,128]{1,0:T(4,128)S(1)} %bitcast.12, ...), custom_call_target="tpu_custom_call" | custom-call | bytes 4194304 | tf_op jit(solution)/shard_map/window/pallas_call | solution.py:757
  39.3 0.0 collective-permute-done.4.g0
  39.3 0.0 collective-permute-done.5.g1
  39.3 1.8 %collective-permute-done.6.g2 = bf16[8,16,128]{2,1,0:T(8,128)(2,1)S(1)} collective-permute-done((bf16[8,16,128]{2,1,0:T(8,128)(2,1)S(1)}, bf16[8,16,128]{2,1,0:T(8,128)(2,1)S(1)}, u32[]{:S(2)}, u32[]{:S(2)}) %collective-permute-start.6) | collective-permute-done | bytes 32800 | tf_op jit(solution)/shard_map/ppermute | solution.py:35
  41.1 0.7 %collective-permute-done.7.g3 = bf16[8,16,128]{2,1,0:T(8,128)(2,1)S(1)} collective-permute-done((bf16[8,16,128]{2,1,0:T(8,128)(2,1)S(1)}, bf16[8,16,128]{2,1,0:T(8,128)(2,1)S(1)}, u32[]{:S(2)}, u32[]{:S(2)}) %collective-permute-start.7) | collective-permute-done | bytes 32800 | tf_op jit(solution)/shard_map/ppermute | solution.py:35
  41.8 0.1 collective-permute-start.8
  41.9 1.2 %collective-permute-start.9 = (bf16[9,16,128]{2,1,0:T(8,128)(2,1)S(1)}, bf16[9,16,128]{2,1,0:T(8,128)(2,1)S(1)}, u32[]{:S(2)}, u32[]{:S(2)}) collective-permute-start(bf16[9,16,128]{2,1,0:T(8,128)(2,1)S(1)} %get-tuple-element.68), channel_id=1, source_target_pairs={{0,28},{4,0},{8,4},{12,8},{16,12},{20,16},{24,20},{28,24},{1,29},{... | collective-permute-start | bytes 110600 | tf_op jit(solution)/shard_map/ppermute | solution.py:35
  43.1 0.0 collective-permute-start.10
  43.1 1.3 %collective-permute-start.11 = (bf16[9,16,128]{2,1,0:T(8,128)(2,1)S(1)}, bf16[9,16,128]{2,1,0:T(8,128)(2,1)S(1)}, u32[]{:S(2)}, u32[]{:S(2)}) collective-permute-start(bf16[9,16,128]{2,1,0:T(8,128)(2,1)S(1)} %get-tuple-element.70), channel_id=1, source_target_pairs={{0,8},{4,12},{8,16},{12,20},{16,24},{20,28},{24,0},{28,4},{1,9},{5... | collective-permute-start | bytes 110600 | tf_op jit(solution)/shard_map/ppermute | solution.py:35
  44.4 0.0 copy-done.3
  44.4 0.0 copy-start.5
  44.4 5.5 %turn.1 = (f32[16,8192]{1,0:T(8,128)}, f32[16,128]{1,0:T(8,128)S(1)}, bf16[96,16,128]{2,1,0:T(8,128)(2,1)S(1)}, bf16[32,16,128]{2,1,0:T(8,128)(2,1)S(1)}) custom-call(s32[4,128]{1,0:T(4,128)S(1)} %bitcast.13, f32[64,16,128]{2,1,0:T(8,128)S(1)} %get-tuple-element.41.t1_ref, bf16[128,16,128]{2,1,0:T(8,128)(2,1)S(1)} %get-tuple-element.48.prev_ref, ...), custom_call_target="tpu_custom_call" | custom-call | bytes 16777216 | tf_op jit(solution)/shard_map/turn/pallas_call | solution.py:768
  49.9 0.0 collective-permute-done.8.x0
  49.9 0.0 collective-permute-done.9.x1
  49.9 0.0 collective-permute-done.10.x2
  49.9 0.0 collective-permute-done.11.x3
  49.9 1.8 %last.1 = bf16[32,16,128]{2,1,0:T(8,128)(2,1)S(1)} custom-call(bf16[96,16,128]{2,1,0:T(8,128)(2,1)S(1)} %get-tuple-element.65.z_ref, bf16[32,16,128]{2,1,0:T(8,128)(2,1)S(1)} %get-tuple-element.66.y_ref, f32[64,8,128]{2,1,0:T(8,128)S(1)} %get-tuple-element.51.v_ref, bf16[13,16,128]{2,1,0:T(8,128)(2,1)S(1)} %collective-permute-done.g0.v0, ...), custom_call_target="tpu_custom_call" | custom-call | bytes 1048576 | tf_op jit(solution)/shard_map/last/pallas_call | solution.py:789
  51.8 13.7 %all_to_all.11.terms_ref = bf16[32,16,128]{2,1,0:T(8,128)(2,1)S(1)} all-to-all(bf16[32,16,128]{2,1,0:T(8,128)(2,1)S(1)} %last.1), channel_id=1, replica_groups=mesh['dom'=8,'pert'=4] {'dom','pert'}, dimensions={0} | all-to-all | bytes 262144 | tf_op jit(solution)/shard_map/all_to_all | solution.py:792
  65.4 0.0 copy-done.5
  65.4 0.6 owner.1
Async XLA Ops:
  14.4 1.2 %copy-start = (bf16[128,64,64]{0,2,1:T(8,128)(2,1)S(1)}, bf16[128,64,64]{0,2,1:T(8,128)(2,1)}, u32[]{:S(2)}) copy-start(bf16[128,64,64]{0,2,1:T(8,128)(2,1)} %param.11) | copy-start | bytes 3145732
  15.6 0.8 %copy-start.1 = (f32[64,128]{1,0:T(8,128)S(1)}, f32[64,128]{1,0:T(8,128)}, u32[]{:S(2)}) copy-start(f32[64,128]{1,0:T(8,128)} %get-tuple-element.40.w_hbm.w_ref) | copy-start | bytes 98308
  16.4 0.7 %copy-start.2 = (s32[128,4]{0,1:T(4,128)S(1)}, s32[128,4]{0,1:T(4,128)}, u32[]{:S(2)}) copy-start(s32[128,4]{0,1:T(4,128)} %param.13) | copy-start | bytes 6148
  17.0 0.7 %copy-start.4 = (s32[1,4,16]{2,1,0:T(4,128)S(1)}, s32[1,4,16]{2,1,0:T(4,128)}, u32[]{:S(2)}) copy-start(s32[1,4,16]{2,1,0:T(4,128)} %send_ref.5) | copy-start | bytes 772
  17.7 0.7 copy-start.6
  25.7 4.2 %collective-permute-start = (bf16[13,16,128]{2,1,0:T(8,128)(2,1)S(1)}, bf16[13,16,128]{2,1,0:T(8,128)(2,1)S(1)}, u32[]{:S(2)}, u32[]{:S(2)}) collective-permute-start(bf16[13,16,128]{2,1,0:T(8,128)(2,1)S(1)} %get-tuple-element.43), channel_id=1, source_target_pairs={{0,24},{4,28},{8,0},{12,4},{16,8},{20,12},{24,16},{28,20},{1,25},{... | collective-permute-start | bytes 159752 | tf_op jit(solution)/shard_map/ppermute | solution.py:35
  26.3 3.6 %collective-permute-start.1 = (bf16[13,16,128]{2,1,0:T(8,128)(2,1)S(1)}, bf16[13,16,128]{2,1,0:T(8,128)(2,1)S(1)}, u32[]{:S(2)}, u32[]{:S(2)}) collective-permute-start(bf16[13,16,128]{2,1,0:T(8,128)(2,1)S(1)} %get-tuple-element.44), channel_id=1, source_target_pairs={{0,28},{4,0},{8,4},{12,8},{16,12},{20,16},{24,20},{28,24},{1,29},{... | collective-permute-start | bytes 159752 | tf_op jit(solution)/shard_map/ppermute | solution.py:35
  26.7 4.5 %collective-permute-start.2 = (bf16[13,16,128]{2,1,0:T(8,128)(2,1)S(1)}, bf16[13,16,128]{2,1,0:T(8,128)(2,1)S(1)}, u32[]{:S(2)}, u32[]{:S(2)}) collective-permute-start(bf16[13,16,128]{2,1,0:T(8,128)(2,1)S(1)} %get-tuple-element.45), channel_id=1, source_target_pairs={{0,4},{4,8},{8,12},{12,16},{16,20},{20,24},{24,28},{28,0},{1,5},{5... | collective-permute-start | bytes 159752 | tf_op jit(solution)/shard_map/ppermute | solution.py:35
  26.8 5.5 %collective-permute-start.3 = (bf16[13,16,128]{2,1,0:T(8,128)(2,1)S(1)}, bf16[13,16,128]{2,1,0:T(8,128)(2,1)S(1)}, u32[]{:S(2)}, u32[]{:S(2)}) collective-permute-start(bf16[13,16,128]{2,1,0:T(8,128)(2,1)S(1)} %get-tuple-element.46), channel_id=1, source_target_pairs={{0,8},{4,12},{8,16},{12,20},{16,24},{20,28},{24,0},{28,4},{1,9},{5... | collective-permute-start | bytes 159752 | tf_op jit(solution)/shard_map/ppermute | solution.py:35
  32.3 12.1 %copy-start.3 = (f32[8192]{0:T(1024)S(1)}, f32[8192]{0:T(1024)}, u32[]{:S(2)}) copy-start(f32[8192]{0:T(1024)} %param.10) | copy-start | bytes 98308
  34.5 4.8 %collective-permute-start.4 = (bf16[8,16,128]{2,1,0:T(8,128)(2,1)S(1)}, bf16[8,16,128]{2,1,0:T(8,128)(2,1)S(1)}, u32[]{:S(2)}, u32[]{:S(2)}) collective-permute-start(bf16[8,16,128]{2,1,0:T(8,128)(2,1)S(1)} %get-tuple-element.56), channel_id=1, source_target_pairs={{0,24},{4,28},{8,0},{12,4},{16,8},{20,12},{24,16},{28,20},{1,25},{... | collective-permute-start | bytes 98312 | tf_op jit(solution)/shard_map/ppermute | solution.py:35
  35.9 3.5 %collective-permute-start.5 = (bf16[8,16,128]{2,1,0:T(8,128)(2,1)S(1)}, bf16[8,16,128]{2,1,0:T(8,128)(2,1)S(1)}, u32[]{:S(2)}, u32[]{:S(2)}) collective-permute-start(bf16[8,16,128]{2,1,0:T(8,128)(2,1)S(1)} %get-tuple-element.57), channel_id=1, source_target_pairs={{0,28},{4,0},{8,4},{12,8},{16,12},{20,16},{24,20},{28,24},{1,29},{... | collective-permute-start | bytes 98312 | tf_op jit(solution)/shard_map/ppermute | solution.py:35
  36.9 4.2 %collective-permute-start.6 = (bf16[8,16,128]{2,1,0:T(8,128)(2,1)S(1)}, bf16[8,16,128]{2,1,0:T(8,128)(2,1)S(1)}, u32[]{:S(2)}, u32[]{:S(2)}) collective-permute-start(bf16[8,16,128]{2,1,0:T(8,128)(2,1)S(1)} %get-tuple-element.58), channel_id=1, source_target_pairs={{0,4},{4,8},{8,12},{12,16},{16,20},{20,24},{24,28},{28,0},{1,5},{5... | collective-permute-start | bytes 98312 | tf_op jit(solution)/shard_map/ppermute | solution.py:35
  36.9 4.9 %collective-permute-start.7 = (bf16[8,16,128]{2,1,0:T(8,128)(2,1)S(1)}, bf16[8,16,128]{2,1,0:T(8,128)(2,1)S(1)}, u32[]{:S(2)}, u32[]{:S(2)}) collective-permute-start(bf16[8,16,128]{2,1,0:T(8,128)(2,1)S(1)} %get-tuple-element.59), channel_id=1, source_target_pairs={{0,8},{4,12},{8,16},{12,20},{16,24},{20,28},{24,0},{28,4},{1,9},{5... | collective-permute-start | bytes 98312 | tf_op jit(solution)/shard_map/ppermute | solution.py:35
  41.8 8.1 %collective-permute-start.8 = (bf16[9,16,128]{2,1,0:T(8,128)(2,1)S(1)}, bf16[9,16,128]{2,1,0:T(8,128)(2,1)S(1)}, u32[]{:S(2)}, u32[]{:S(2)}) collective-permute-start(bf16[9,16,128]{2,1,0:T(8,128)(2,1)S(1)} %get-tuple-element.67), channel_id=1, source_target_pairs={{0,24},{4,28},{8,0},{12,4},{16,8},{20,12},{24,16},{28,20},{1,25},{... | collective-permute-start | bytes 110600 | tf_op jit(solution)/shard_map/ppermute | solution.py:35
  41.9 8.0 %collective-permute-start.9 = (bf16[9,16,128]{2,1,0:T(8,128)(2,1)S(1)}, bf16[9,16,128]{2,1,0:T(8,128)(2,1)S(1)}, u32[]{:S(2)}, u32[]{:S(2)}) collective-permute-start(bf16[9,16,128]{2,1,0:T(8,128)(2,1)S(1)} %get-tuple-element.68), channel_id=1, source_target_pairs={{0,28},{4,0},{8,4},{12,8},{16,12},{20,16},{24,20},{28,24},{1,29},{... | collective-permute-start | bytes 110600 | tf_op jit(solution)/shard_map/ppermute | solution.py:35
  43.1 6.8 %collective-permute-start.10 = (bf16[9,16,128]{2,1,0:T(8,128)(2,1)S(1)}, bf16[9,16,128]{2,1,0:T(8,128)(2,1)S(1)}, u32[]{:S(2)}, u32[]{:S(2)}) collective-permute-start(bf16[9,16,128]{2,1,0:T(8,128)(2,1)S(1)} %get-tuple-element.69), channel_id=1, source_target_pairs={{0,4},{4,8},{8,12},{12,16},{16,20},{20,24},{24,28},{28,0},{1,5},{5... | collective-permute-start | bytes 110600 | tf_op jit(solution)/shard_map/ppermute | solution.py:35
  43.1 6.8 %collective-permute-start.11 = (bf16[9,16,128]{2,1,0:T(8,128)(2,1)S(1)}, bf16[9,16,128]{2,1,0:T(8,128)(2,1)S(1)}, u32[]{:S(2)}, u32[]{:S(2)}) collective-permute-start(bf16[9,16,128]{2,1,0:T(8,128)(2,1)S(1)} %get-tuple-element.70), channel_id=1, source_target_pairs={{0,8},{4,12},{8,16},{12,20},{16,24},{20,28},{24,0},{28,4},{1,9},{5... | collective-permute-start | bytes 110600 | tf_op jit(solution)/shard_map/ppermute | solution.py:35
  44.4 21.1 %copy-start.5 = (f32[16,128]{1,0:T(8,128)S(1)}, f32[16,128]{1,0:T(8,128)}, u32[]{:S(2)}) copy-start(f32[16,128]{1,0:T(8,128)} %probe_ref.1) | copy-start | bytes 24580

commit v10 on v7

--- a/solution.py
+++ b/solution.py
@@ -14,6 +14,7 @@
 HALF = 64
 QUAD = 4
 RADIX = 64
+W_ROWS = 24576
 
 VMEM = pl.BlockSpec(memory_space=pltpu.VMEM)
 SMEM = pl.BlockSpec(memory_space=pltpu.SMEM)
@@ -40,8 +41,8 @@
 
 
 def melt_kernel(
-    send_hbm, melt_hbm, patch_hbm, probe_hbm, diag_hbm, w_ref, out_ref,
-    send_ref, melt_ref, patch_ref, probe_ref, diag_ref, sems, *, parts,
+    send_hbm, melt_hbm, patch_hbm, probe_hbm, diag_hbm, w_hbm, out_ref,
+    send_ref, melt_ref, patch_ref, probe_ref, diag_ref, w_ref, sems, w_sem, *, parts,
 ):
     copies = [
         pltpu.make_async_copy(source, target, sems.at[number])
@@ -82,6 +83,8 @@
         axis=0,
     )
     w_ref[...] = jnp.transpose(both)[:pairs]
+    w_copy = pltpu.make_async_copy(w_ref, w_hbm.at[pl.ds(0, pairs)], w_sem)
+    w_copy.start()
     patch_row = jnp.broadcast_to(patch_ref[...].astype(F32), (8, LANES))
     lane = lax.broadcasted_iota(jnp.int32, (8, LANES), 1)
     for part in range(parts):
@@ -101,6 +104,7 @@
         out_ref[to, pert + capacity :, :] = jnp.where(
             mine, jnp.take_along_axis(patch_row, ids, axis=1), 0.0
         )
+    w_copy.wait()
 
 
 def gather_rows(quad, cols_ref, ext_ref, low):
@@ -163,10 +167,10 @@
 
 def first_kernel(
     cols_ref, send_ref, patch_ref, columns_ref, got_ref, w_hbm, diag_ref, coupling_hbm,
-    m_ref, v_ref, names_ref, patches_ref, t1_ref, t2_ref, o0, o1, o2, o3,
-    ext_ref, row_ref, w_ref, coupling_ref, w_sem, sems,
+    m_ref, w_ref, v_ref, names_ref, patches_ref, t1_ref, t2_ref, o0, o1, o2, o3,
+    ext_ref, row_ref, coupling_ref, w_sem, sems,
 ):
-    w_copy = pltpu.make_async_copy(w_hbm, w_ref, w_sem)
+    w_copy = pltpu.make_async_copy(w_hbm.at[pl.ds(0, w_ref.shape[0])], w_ref, w_sem)
     w_copy.start()
     chunks = sems.shape[0]
     size = diag_ref.shape[0] // chunks
@@ -694,9 +698,9 @@
 
     perts = lax.axis_size("pert")
     columns = columns.T
-    w, outgoing = call(
+    w_far, outgoing = call(
         functools.partial(melt_kernel, parts=parts),
-        [shape((pairs, LANES), F32), shape((parts, pert + capacity + 8, LANES), F32)],
+        [shape((W_ROWS, LANES), F32), shape((parts, pert + capacity + 8, LANES), F32)],
         "hhhhh",
         [
             pltpu.SMEM(send_list.shape, jnp.int32),
@@ -704,17 +708,21 @@
             pltpu.VMEM((1, blocks), jnp.int32),
             pltpu.VMEM(probes.shape, F32),
             pltpu.VMEM((HALF, HALF, blocks), BF16),
+            pltpu.VMEM((pairs, LANES), F32),
             pltpu.SemaphoreType.DMA((5,)),
+            pltpu.SemaphoreType.DMA,
         ],
         name="melt",
+        out_specs=[HBM, VMEM],
         limit=60,
     )(send_list, melt, patch, probes, jnp.transpose(diag_inverse, (1, 2, 0)))
     got = lax.all_to_all(outgoing, "dom", 0, 0, tiled=True)
     wide = [shape((capacity // 2 + capacity // 4 + 1, pert, LANES), BF16)] * 4
-    m, v, names, patches, t1, state, *out = call(
+    m, w, v, names, patches, t1, state, *out = call(
         first_kernel,
         [
             shape(coupling.shape, BF16),
+            shape((pairs, LANES), F32),
             shape((pairs, 8, LANES), F32),
             shape((8, LANES), F32),
             shape((8, LANES), F32),
@@ -726,14 +734,13 @@
         [
             ext,
             pltpu.VMEM((blocks + 4 * capacity, LANES), F32),
-            pltpu.VMEM((pairs, LANES), F32),
             pltpu.VMEM(coupling.shape, BF16),
             pltpu.SemaphoreType.DMA,
             pltpu.SemaphoreType.DMA((8,)),
         ],
         name="first",
         limit=46,
-    )(columns, send_list, patch, columns, got, w, diag_inverse, coupling)
+    )(columns, send_list, patch, columns, got, w_far, diag_inverse, coupling)
     carried = [rotated(x, o) for x, o in zip(out, OFFSET_LIST)]
     state, *out = call(
         sweep_kernel, [block_array] + msgs, "ssvvvvvvv", [ext], name="sweep"

time: 62.4 us -> 63 us (level)
  Pallas kernels: 21.2 us -> 22.6 us
  local copies, waits for them, and re-layouts: 4.71 us -> 3.95 us
    pallas_call x2, Pallas kernels: 9.08 us -> 10.5 us  [the longest x1 7.14 us: shards(): call(first_kernel, [shape(coupling.shape, BF16), shape((pairs, LANES), F3...]
    unnamed x13 -> x11, local copies, waits for them, and re-layouts: 4.71 us -> 3.95 us
where the time goes in v10:
time: 63 us; the launch traced here: 62.7 us
  Pallas kernels  22.6 us (36%)
  blocking collectives  13.8 us (22%)
  starting transfers between devices  12.9 us (20%)
  waiting for transfers between devices  8.65 us (14%)
  local copies, waits for them, and re-layouts  3.95 us (6%)
  between operations  0.77 us (1%)
    all_to_all x1, blocking collectives, shards(): terms = lax.all_to_all(terms, ('dom', 'pert'), 0, 0, tiled=True)  13.8 us
    ppermute x12, starting transfers between devices, rotated(): lax.ppermute(value, 'dom', [(i, (i + by) % peers) for i in range(peers)])  7.73 us
    pallas_call x1, Pallas kernels, shards(): call(first_kernel, [shape(coupling.shape, BF16), shape((pairs, LANES), F3...  7.14 us
    ppermute x12, waiting for transfers between devices, rotated(): lax.ppermute(value, 'dom', [(i, (i + by) % peers) for i in range(peers)])  6.71 us
    pallas_call x1, Pallas kernels, shards(): call(turn_kernel, [shape((pert, blocks * HALF), F32), shape((pert, LANES)...  5.52 us
    all_to_all x1, starting transfers between devices, shards(): got = lax.all_to_all(outgoing, 'dom', 0, 0, tiled=True)  5.19 us
    unnamed x11, local copies, waits for them, and re-layouts  3.95 us
    pallas_call x1, Pallas kernels, shards(): call(functools.partial(melt_kernel, parts=parts), [shape((W_ROWS, LANES),...  3.31 us
  transfers between devices with their start and end apart: 13, of which 6 were waited for; matrix products, arithmetic and copies ran while one was open for 6% of the time, Pallas kernels for 12%

profile of v10, /device:TPU:0, one launch (start us, length us, event | category | flops | bytes accessed | tf_op | source)
XLA Modules:
  0.0 62.7 jit_solution(14158514959517696157)
XLA Ops:
  0.6 0.0 copy-start.2
  0.6 0.0 copy-start.4
  0.7 0.0 copy-start
  0.7 3.3 %melt.1 = (f32[24576,128]{1,0:T(8,128)}, f32[8,40,128]{2,1,0:T(8,128)}) custom-call(s32[1,4,16]{2,1,0:T(4,128)} %send_ref.5, f32[64,128]{1,0:T(8,128)} %bitcast.17, s32[1,128]{1,0:T(1,128)} %bitcast.13, f32[16,128]{1,0:T(8,128)} %probe_ref.1, bf16[64,64,128]{2,1,0:T(8,128)(2,1)} %bitcast.16), custom_call_target="tpu_custom_call" | custom-call | bytes 1048576 | tf_op jit(solution)/shard_map/melt/pallas_call | solution.py:701
  4.0 5.2 %all-to-all-start = ((f32[8,40,128]{2,1,0:T(8,128)}), f32[8,40,128]{2,1,0:T(8,128)S(1)}, u32[]{:S(2)}, u32[]{:S(2)}) async-start(f32[8,40,128]{2,1,0:T(8,128)} %get-tuple-element.40), calls=%async_computation | async-start | bytes 327680 | tf_op jit(solution)/shard_map/all_to_all | solution.py:719
  9.2 3.9 %copy.11.diag_ref = bf16[128,64,64]{2,1,0:T(8,128)(2,1)S(1)} copy(bf16[128,64,64]{0,2,1:T(8,128)(2,1)} %param.11) | data formatting | bytes 2097152 | tf_op args[3]
  13.1 1.9 %all-to-all-done.got_ref = f32[8,40,128]{2,1,0:T(8,128)S(1)} async-done(((f32[8,40,128]{2,1,0:T(8,128)}), f32[8,40,128]{2,1,0:T(8,128)S(1)}, u32[]{:S(2)}, u32[]{:S(2)}) %all-to-all-start) | async-done | bytes 163872 | tf_op jit(solution)/shard_map/all_to_all | solution.py:719
  15.0 0.0 copy-done.2
  15.1 0.0 copy-done.4
  15.1 0.0 copy-done
  15.1 7.1 %first.1 = (bf16[128,64,256]{2,1,0:T(8,128)(2,1)S(1)}, f32[64,128]{1,0:T(8,128)S(1)}, f32[64,8,128]{2,1,0:T(8,128)S(1)}, f32[8,128]{1,0:T(8,128)S(1)}, f32[8,128...) custom-call(s32[4,128]{1,0:T(4,128)S(1)} %bitcast.6, ...), custom_call_target="tpu_custom_call" | custom-call | bytes 1048576 | tf_op jit(solution)/shard_map/first/pallas_call | solution.py:721
  22.2 1.1 %collective-permute-start = (bf16[13,16,128]{2,1,0:T(8,128)(2,1)S(1)}, bf16[13,16,128]{2,1,0:T(8,128)(2,1)S(1)}, u32[]{:S(2)}, u32[]{:S(2)}) collective-permute-start(bf16[13,16,128]{2,1,0:T(8,128)(2,1)S(1)} %get-tuple-element.44), channel_id=1, source_target_pairs={{0,24},{4,28},{8,0},{12,4},{16,8},{20,12},{24,16},{28,20},{1,25},{... | collective-permute-start | bytes 159752 | tf_op jit(solution)/shard_map/ppermute | solution.py:35
  23.3 0.0 collective-permute-start.1
  23.3 0.5 collective-permute-start.2
  23.8 1.0 %collective-permute-start.3 = (bf16[13,16,128]{2,1,0:T(8,128)(2,1)S(1)}, bf16[13,16,128]{2,1,0:T(8,128)(2,1)S(1)}, u32[]{:S(2)}, u32[]{:S(2)}) collective-permute-start(bf16[13,16,128]{2,1,0:T(8,128)(2,1)S(1)} %get-tuple-element.47), channel_id=1, source_target_pairs={{0,8},{4,12},{8,16},{12,20},{16,24},{20,28},{24,0},{28,4},{1,9},{5... | collective-permute-start | bytes 159752 | tf_op jit(solution)/shard_map/ppermute | solution.py:35
  24.8 1.6 %collective-permute-done.g0.v0 = bf16[13,16,128]{2,1,0:T(8,128)(2,1)S(1)} collective-permute-done((bf16[13,16,128]{2,1,0:T(8,128)(2,1)S(1)}, bf16[13,16,128]{2,1,0:T(8,128)(2,1)S(1)}, u32[]{:S(2)}, u32[]{:S(2)}) %collective-permute-start) | collective-permute-done | bytes 53280 | tf_op jit(solution)/shard_map/ppermute | solution.py:35
  26.4 0.0 collective-permute-done.1.g1.v1
  26.4 1.4 %collective-permute-done.2.g2.v2 = bf16[13,16,128]{2,1,0:T(8,128)(2,1)S(1)} collective-permute-done((bf16[13,16,128]{2,1,0:T(8,128)(2,1)S(1)}, bf16[13,16,128]{2,1,0:T(8,128)(2,1)S(1)}, u32[]{:S(2)}, u32[]{:S(2)}) %collective-permute-start.2) | collective-permute-done | bytes 53280 | tf_op jit(solution)/shard_map/ppermute | solution.py:35
  27.8 1.5 %collective-permute-done.3.g3.v3 = bf16[13,16,128]{2,1,0:T(8,128)(2,1)S(1)} collective-permute-done((bf16[13,16,128]{2,1,0:T(8,128)(2,1)S(1)}, bf16[13,16,128]{2,1,0:T(8,128)(2,1)S(1)}, u32[]{:S(2)}, u32[]{:S(2)}) %collective-permute-start.3) | collective-permute-done | bytes 53280 | tf_op jit(solution)/shard_map/ppermute | solution.py:35
  29.3 0.0 copy-start.1
  29.3 2.2 %sweep.1 = (bf16[128,16,128]{2,1,0:T(8,128)(2,1)S(1)}, bf16[8,16,128]{2,1,0:T(8,128)(2,1)S(1)}, bf16[8,16,128]{2,1,0:T(8,128)(2,1)S(1)}, bf16[8,16,128]{2,1,0:T(8,128)(2,1)S(1)}, bf16[8,16,128]{2,1,0:T(8,128)(2,1)S(1)}) custom-call(s32[4,128]{1,0:T(4,128)S(1)} %bitcast.8, s32[1,4,16]{2,1,0:T(4,128)S(1)} %copy-done.2, ...), custom_call_target="tpu_custom_call" | custom-call | bytes 1048576 | tf_op jit(solution)/shard_map/sweep/pallas_call | solution.py:745
  31.5 0.9 %collective-permute-start.4 = (bf16[8,16,128]{2,1,0:T(8,128)(2,1)S(1)}, bf16[8,16,128]{2,1,0:T(8,128)(2,1)S(1)}, u32[]{:S(2)}, u32[]{:S(2)}) collective-permute-start(bf16[8,16,128]{2,1,0:T(8,128)(2,1)S(1)} %get-tuple-element.57), channel_id=1, source_target_pairs={{0,24},{4,28},{8,0},{12,4},{16,8},{20,12},{24,16},{28,20},{1,25},{... | collective-permute-start | bytes 98312 | tf_op jit(solution)/shard_map/ppermute | solution.py:35
  32.4 1.0 %collective-permute-start.5 = (bf16[8,16,128]{2,1,0:T(8,128)(2,1)S(1)}, bf16[8,16,128]{2,1,0:T(8,128)(2,1)S(1)}, u32[]{:S(2)}, u32[]{:S(2)}) collective-permute-start(bf16[8,16,128]{2,1,0:T(8,128)(2,1)S(1)} %get-tuple-element.58), channel_id=1, source_target_pairs={{0,28},{4,0},{8,4},{12,8},{16,12},{20,16},{24,20},{28,24},{1,29},{... | collective-permute-start | bytes 98312 | tf_op jit(solution)/shard_map/ppermute | solution.py:35
  33.4 0.0 collective-permute-start.6
  33.4 0.7 %collective-permute-start.7 = (bf16[8,16,128]{2,1,0:T(8,128)(2,1)S(1)}, bf16[8,16,128]{2,1,0:T(8,128)(2,1)S(1)}, u32[]{:S(2)}, u32[]{:S(2)}) collective-permute-start(bf16[8,16,128]{2,1,0:T(8,128)(2,1)S(1)} %get-tuple-element.60), channel_id=1, source_target_pairs={{0,8},{4,12},{8,16},{12,20},{16,24},{20,28},{24,0},{28,4},{1,9},{5... | collective-permute-start | bytes 98312 | tf_op jit(solution)/shard_map/ppermute | solution.py:35
  34.1 2.0 %window.1 = (bf16[1024,896]{1,0:T(8,128)(2,1)S(1)}, bf16[9,16,128]{2,1,0:T(8,128)(2,1)S(1)}, bf16[9,16,128]{2,1,0:T(8,128)(2,1)S(1)}, bf16[9,16,128]{2,1,0:T(8,128)(2,1)S(1)}, bf16[9,16,128]{2,1,0:T(8,128)(2,1)S(1)}) custom-call(s32[4,128]{1,0:T(4,128)S(1)} %bitcast.9, s32[1,4,16]{2,1,0:T(4,128)S(1)} %copy-done.2, s32[4,128]{1,0:T(4,128)S(1)} %bitcast.10, ...), custom_call_target="tpu_custom_call" | custom-call | bytes 4194304 | tf_op jit(solution)/shard_map/window/pallas_call | solution.py:749
  36.1 0.0 collective-permute-done.4.g0
  36.1 0.0 collective-permute-done.5.g1
  36.1 1.6 %collective-permute-done.6.g2 = bf16[8,16,128]{2,1,0:T(8,128)(2,1)S(1)} collective-permute-done((bf16[8,16,128]{2,1,0:T(8,128)(2,1)S(1)}, bf16[8,16,128]{2,1,0:T(8,128)(2,1)S(1)}, u32[]{:S(2)}, u32[]{:S(2)}) %collective-permute-start.6) | collective-permute-done | bytes 32800 | tf_op jit(solution)/shard_map/ppermute | solution.py:35
  37.6 0.7 %collective-permute-done.7.g3 = bf16[8,16,128]{2,1,0:T(8,128)(2,1)S(1)} collective-permute-done((bf16[8,16,128]{2,1,0:T(8,128)(2,1)S(1)}, bf16[8,16,128]{2,1,0:T(8,128)(2,1)S(1)}, u32[]{:S(2)}, u32[]{:S(2)}) %collective-permute-start.7) | collective-permute-done | bytes 32800 | tf_op jit(solution)/shard_map/ppermute | solution.py:35
  38.3 0.1 collective-permute-start.8
  38.5 1.6 %collective-permute-start.9 = (bf16[9,16,128]{2,1,0:T(8,128)(2,1)S(1)}, bf16[9,16,128]{2,1,0:T(8,128)(2,1)S(1)}, u32[]{:S(2)}, u32[]{:S(2)}) collective-permute-start(bf16[9,16,128]{2,1,0:T(8,128)(2,1)S(1)} %get-tuple-element.70), channel_id=1, source_target_pairs={{0,28},{4,0},{8,4},{12,8},{16,12},{20,16},{24,20},{28,24},{1,29},{... | collective-permute-start | bytes 110600 | tf_op jit(solution)/shard_map/ppermute | solution.py:35
  40.1 0.0 collective-permute-start.10
  40.1 0.8 %collective-permute-start.11 = (bf16[9,16,128]{2,1,0:T(8,128)(2,1)S(1)}, bf16[9,16,128]{2,1,0:T(8,128)(2,1)S(1)}, u32[]{:S(2)}, u32[]{:S(2)}) collective-permute-start(bf16[9,16,128]{2,1,0:T(8,128)(2,1)S(1)} %get-tuple-element.72), channel_id=1, source_target_pairs={{0,8},{4,12},{8,16},{12,20},{16,24},{20,28},{24,0},{28,4},{1,9},{5... | collective-permute-start | bytes 110600 | tf_op jit(solution)/shard_map/ppermute | solution.py:35
  40.9 0.0 copy-done.1
  40.9 0.0 copy-start.3
  40.9 5.5 %turn.1 = (f32[16,8192]{1,0:T(8,128)}, f32[16,128]{1,0:T(8,128)S(1)}, bf16[96,16,128]{2,1,0:T(8,128)(2,1)S(1)}, bf16[32,16,128]{2,1,0:T(8,128)(2,1)S(1)}) custom-call(s32[4,128]{1,0:T(4,128)S(1)} %bitcast.11, f32[64,16,128]{2,1,0:T(8,128)S(1)} %get-tuple-element.42.t1_ref, bf16[128,16,128]{2,1,0:T(8,128)(2,1)S(1)} %get-tuple-element.49.prev_ref, ...), custom_call_target="tpu_custom_call" | custom-call | bytes 16777216 | tf_op jit(solution)/shard_map/turn/pallas_call | solution.py:760
  46.4 0.0 collective-permute-done.8.x0
  46.4 0.0 collective-permute-done.9.x1
  46.4 0.0 collective-permute-done.10.x2
  46.4 0.0 collective-permute-done.11.x3
  46.5 1.8 %last.1 = bf16[32,16,128]{2,1,0:T(8,128)(2,1)S(1)} custom-call(bf16[96,16,128]{2,1,0:T(8,128)(2,1)S(1)} %get-tuple-element.67.z_ref, bf16[32,16,128]{2,1,0:T(8,128)(2,1)S(1)} %get-tuple-element.68.y_ref, f32[64,8,128]{2,1,0:T(8,128)S(1)} %get-tuple-element.52.v_ref, bf16[13,16,128]{2,1,0:T(8,128)(2,1)S(1)} %collective-permute-done.g0.v0, ...), custom_call_target="tpu_custom_call" | custom-call | bytes 1048576 | tf_op jit(solution)/shard_map/last/pallas_call | solution.py:781
  48.3 13.8 %all_to_all.10.terms_ref = bf16[32,16,128]{2,1,0:T(8,128)(2,1)S(1)} all-to-all(bf16[32,16,128]{2,1,0:T(8,128)(2,1)S(1)} %last.1), channel_id=1, replica_groups=mesh['dom'=8,'pert'=4] {'dom','pert'}, dimensions={0} | all-to-all | bytes 262144 | tf_op jit(solution)/shard_map/all_to_all | solution.py:784
  62.0 0.0 copy-done.3
  62.1 0.6 owner.1
Async XLA Ops:
  0.6 14.4 %copy-start.2 = (s32[1,4,16]{2,1,0:T(4,128)S(1)}, s32[1,4,16]{2,1,0:T(4,128)}, u32[]{:S(2)}) copy-start(s32[1,4,16]{2,1,0:T(4,128)} %send_ref.5) | copy-start | bytes 772
  0.6 14.4 %copy-start.4 = (s32[128]{0:T(128)S(1)}, s32[128]{0:T(128)}, u32[]{:S(2)}) copy-start(s32[128]{0:T(128)} %param.15) | copy-start | bytes 1540
  0.7 14.4 %copy-start = (s32[128,4]{0,1:T(4,128)S(1)}, s32[128,4]{0,1:T(4,128)}, u32[]{:S(2)}) copy-start(s32[128,4]{0,1:T(4,128)} %param.13) | copy-start | bytes 6148
  4.0 11.1 %all-to-all-start = ((f32[8,40,128]{2,1,0:T(8,128)}), f32[8,40,128]{2,1,0:T(8,128)S(1)}, u32[]{:S(2)}, u32[]{:S(2)}) async-start(f32[8,40,128]{2,1,0:T(8,128)} %get-tuple-element.40), calls=%async_computation | async-start | bytes 327680 | tf_op jit(solution)/shard_map/all_to_all | solution.py:719
  22.2 4.2 %collective-permute-start = (bf16[13,16,128]{2,1,0:T(8,128)(2,1)S(1)}, bf16[13,16,128]{2,1,0:T(8,128)(2,1)S(1)}, u32[]{:S(2)}, u32[]{:S(2)}) collective-permute-start(bf16[13,16,128]{2,1,0:T(8,128)(2,1)S(1)} %get-tuple-element.44), channel_id=1, source_target_pairs={{0,24},{4,28},{8,0},{12,4},{16,8},{20,12},{24,16},{28,20},{1,25},{... | collective-permute-start | bytes 159752 | tf_op jit(solution)/shard_map/ppermute | solution.py:35
  23.3 3.1 %collective-permute-start.1 = (bf16[13,16,128]{2,1,0:T(8,128)(2,1)S(1)}, bf16[13,16,128]{2,1,0:T(8,128)(2,1)S(1)}, u32[]{:S(2)}, u32[]{:S(2)}) collective-permute-start(bf16[13,16,128]{2,1,0:T(8,128)(2,1)S(1)} %get-tuple-element.45), channel_id=1, source_target_pairs={{0,28},{4,0},{8,4},{12,8},{16,12},{20,16},{24,20},{28,24},{1,29},{... | collective-permute-start | bytes 159752 | tf_op jit(solution)/shard_map/ppermute | solution.py:35
  23.3 4.5 %collective-permute-start.2 = (bf16[13,16,128]{2,1,0:T(8,128)(2,1)S(1)}, bf16[13,16,128]{2,1,0:T(8,128)(2,1)S(1)}, u32[]{:S(2)}, u32[]{:S(2)}) collective-permute-start(bf16[13,16,128]{2,1,0:T(8,128)(2,1)S(1)} %get-tuple-element.46), channel_id=1, source_target_pairs={{0,4},{4,8},{8,12},{12,16},{16,20},{20,24},{24,28},{28,0},{1,5},{5... | collective-permute-start | bytes 159752 | tf_op jit(solution)/shard_map/ppermute | solution.py:35
  23.8 5.5 %collective-permute-start.3 = (bf16[13,16,128]{2,1,0:T(8,128)(2,1)S(1)}, bf16[13,16,128]{2,1,0:T(8,128)(2,1)S(1)}, u32[]{:S(2)}, u32[]{:S(2)}) collective-permute-start(bf16[13,16,128]{2,1,0:T(8,128)(2,1)S(1)} %get-tuple-element.47), channel_id=1, source_target_pairs={{0,8},{4,12},{8,16},{12,20},{16,24},{20,28},{24,0},{28,4},{1,9},{5... | collective-permute-start | bytes 159752 | tf_op jit(solution)/shard_map/ppermute | solution.py:35
  29.3 11.6 %copy-start.1 = (f32[8192]{0:T(1024)S(1)}, f32[8192]{0:T(1024)}, u32[]{:S(2)}) copy-start(f32[8192]{0:T(1024)} %param.10) | copy-start | bytes 98308
  31.5 4.6 %collective-permute-start.4 = (bf16[8,16,128]{2,1,0:T(8,128)(2,1)S(1)}, bf16[8,16,128]{2,1,0:T(8,128)(2,1)S(1)}, u32[]{:S(2)}, u32[]{:S(2)}) collective-permute-start(bf16[8,16,128]{2,1,0:T(8,128)(2,1)S(1)} %get-tuple-element.57), channel_id=1, source_target_pairs={{0,24},{4,28},{8,0},{12,4},{16,8},{20,12},{24,16},{28,20},{1,25},{... | collective-permute-start | bytes 98312 | tf_op jit(solution)/shard_map/ppermute | solution.py:35
  32.4 3.7 %collective-permute-start.5 = (bf16[8,16,128]{2,1,0:T(8,128)(2,1)S(1)}, bf16[8,16,128]{2,1,0:T(8,128)(2,1)S(1)}, u32[]{:S(2)}, u32[]{:S(2)}) collective-permute-start(bf16[8,16,128]{2,1,0:T(8,128)(2,1)S(1)} %get-tuple-element.58), channel_id=1, source_target_pairs={{0,28},{4,0},{8,4},{12,8},{16,12},{20,16},{24,20},{28,24},{1,29},{... | collective-permute-start | bytes 98312 | tf_op jit(solution)/shard_map/ppermute | solution.py:35
  33.4 4.2 %collective-permute-start.6 = (bf16[8,16,128]{2,1,0:T(8,128)(2,1)S(1)}, bf16[8,16,128]{2,1,0:T(8,128)(2,1)S(1)}, u32[]{:S(2)}, u32[]{:S(2)}) collective-permute-start(bf16[8,16,128]{2,1,0:T(8,128)(2,1)S(1)} %get-tuple-element.59), channel_id=1, source_target_pairs={{0,4},{4,8},{8,12},{12,16},{16,20},{20,24},{24,28},{28,0},{1,5},{5... | collective-permute-start | bytes 98312 | tf_op jit(solution)/shard_map/ppermute | solution.py:35
  33.4 4.9 %collective-permute-start.7 = (bf16[8,16,128]{2,1,0:T(8,128)(2,1)S(1)}, bf16[8,16,128]{2,1,0:T(8,128)(2,1)S(1)}, u32[]{:S(2)}, u32[]{:S(2)}) collective-permute-start(bf16[8,16,128]{2,1,0:T(8,128)(2,1)S(1)} %get-tuple-element.60), channel_id=1, source_target_pairs={{0,8},{4,12},{8,16},{12,20},{16,24},{20,28},{24,0},{28,4},{1,9},{5... | collective-permute-start | bytes 98312 | tf_op jit(solution)/shard_map/ppermute | solution.py:35
  38.3 8.1 %collective-permute-start.8 = (bf16[9,16,128]{2,1,0:T(8,128)(2,1)S(1)}, bf16[9,16,128]{2,1,0:T(8,128)(2,1)S(1)}, u32[]{:S(2)}, u32[]{:S(2)}) collective-permute-start(bf16[9,16,128]{2,1,0:T(8,128)(2,1)S(1)} %get-tuple-element.69), channel_id=1, source_target_pairs={{0,24},{4,28},{8,0},{12,4},{16,8},{20,12},{24,16},{28,20},{1,25},{... | collective-permute-start | bytes 110600 | tf_op jit(solution)/shard_map/ppermute | solution.py:35
  38.5 7.9 %collective-permute-start.9 = (bf16[9,16,128]{2,1,0:T(8,128)(2,1)S(1)}, bf16[9,16,128]{2,1,0:T(8,128)(2,1)S(1)}, u32[]{:S(2)}, u32[]{:S(2)}) collective-permute-start(bf16[9,16,128]{2,1,0:T(8,128)(2,1)S(1)} %get-tuple-element.70), channel_id=1, source_target_pairs={{0,28},{4,0},{8,4},{12,8},{16,12},{20,16},{24,20},{28,24},{1,29},{... | collective-permute-start | bytes 110600 | tf_op jit(solution)/shard_map/ppermute | solution.py:35
  40.1 6.3 %collective-permute-start.10 = (bf16[9,16,128]{2,1,0:T(8,128)(2,1)S(1)}, bf16[9,16,128]{2,1,0:T(8,128)(2,1)S(1)}, u32[]{:S(2)}, u32[]{:S(2)}) collective-permute-start(bf16[9,16,128]{2,1,0:T(8,128)(2,1)S(1)} %get-tuple-element.71), channel_id=1, source_target_pairs={{0,4},{4,8},{8,12},{12,16},{16,20},{20,24},{24,28},{28,0},{1,5},{5... | collective-permute-start | bytes 110600 | tf_op jit(solution)/shard_map/ppermute | solution.py:35
  40.1 6.4 %collective-permute-start.11 = (bf16[9,16,128]{2,1,0:T(8,128)(2,1)S(1)}, bf16[9,16,128]{2,1,0:T(8,128)(2,1)S(1)}, u32[]{:S(2)}, u32[]{:S(2)}) collective-permute-start(bf16[9,16,128]{2,1,0:T(8,128)(2,1)S(1)} %get-tuple-element.72), channel_id=1, source_target_pairs={{0,8},{4,12},{8,16},{12,20},{16,24},{20,28},{24,0},{28,4},{1,9},{5... | collective-permute-start | bytes 110600 | tf_op jit(solution)/shard_map/ppermute | solution.py:35
  40.9 21.2 %copy-start.3 = (f32[16,128]{1,0:T(8,128)S(1)}, f32[16,128]{1,0:T(8,128)}, u32[]{:S(2)}) copy-start(f32[16,128]{1,0:T(8,128)} %probe_ref.1) | copy-start | bytes 24580

commit v11 on v7

--- a/solution.py
+++ b/solution.py
@@ -93,12 +93,15 @@
         for slot in range(capacity):
             block = jnp.maximum(send_ref[0, group, slot], 0)
             row = w_ref[pl.ds(block // 2, 1), :]
-            out_ref[to, pert + slot : pert + slot + 1, :] = jnp.where(
-                low == (block % 2 == 0), row, swap_halves(row)
-            )
+            row = jnp.where(low == (block % 2 == 0), row, swap_halves(row))
+            if slot % 2 == 0:
+                left = row
+            else:
+                place = pert + slot // 2
+                out_ref[to, place : place + 1, :] = jnp.where(low, left, row)
             ids = jnp.where(lane == group * capacity + slot, block, ids)
         mine = (lane >= group * capacity) & (lane < (group + 1) * capacity)
-        out_ref[to, pert + capacity :, :] = jnp.where(
+        out_ref[to, pert + capacity // 2 :, :] = jnp.where(
             mine, jnp.take_along_axis(patch_row, ids, axis=1), 0.0
         )
 
@@ -187,7 +190,8 @@
     sources = neighbours(parts)
     low = low_half((pert, LANES))
     lane = lax.broadcasted_iota(jnp.int32, (1, LANES), 1)
-    ghost_ids = sum(got_ref[source, pert + capacity : pert + capacity + 1, :] for source in sources)
+    names = pert + capacity // 2
+    ghost_ids = sum(got_ref[source, names : names + 1, :] for source in sources)
     ghost_ids = jnp.where(lane < 4 * capacity, ghost_ids, -1.0)
     ids = jnp.concatenate([patch_ref[...].astype(F32), ghost_ids], axis=1)
     total = jnp.zeros((3 * pert, 2 * LANES), F32)
@@ -228,7 +232,11 @@
     row_ref[pl.ds(1, blocks // 2, stride=2), :] = jnp.where(low_w, w_other, w)
     for group, source in enumerate(sources):
         start = blocks + group * capacity
-        row_ref[start : start + capacity, :] = got_ref[source, pert : pert + capacity, :]
+        both = got_ref[source, pert : pert + capacity // 2, :]
+        other = swap_halves(both)
+        low_both = low_half(both.shape)
+        row_ref[pl.ds(start, capacity // 2, stride=2), :] = jnp.where(low_both, both, other)
+        row_ref[pl.ds(start + 1, capacity // 2, stride=2), :] = jnp.where(low_both, other, both)
 
     def seed(pair, _):
         index = 2 * pair + 1 - full_low
@@ -242,7 +250,7 @@
     for group, source in enumerate(sources):
         for slot in range(capacity):
             place = group * capacity + slot
-            row = got_ref[source, pert + slot : pert + slot + 1, :]
+            row = row_ref[blocks + place : blocks + place + 1, :]
             spread = jnp.broadcast_to(ghost_picked[:, place : place + 1], (pert, LANES))
             ext_ref[blocks + place] = (spread * row).astype(BF16)
 
@@ -696,7 +704,7 @@
     columns = columns.T
     w, outgoing = call(
         functools.partial(melt_kernel, parts=parts),
-        [shape((pairs, LANES), F32), shape((parts, pert + capacity + 8, LANES), F32)],
+        [shape((pairs, LANES), F32), shape((parts, pert + capacity // 2 + 8, LANES), F32)],
         "hhhhh",
         [
             pltpu.SMEM(send_list.shape, jnp.int32),

time: 62.4 us -> 62.4 us (level)
  no operation moved by 1% of the time
where the time goes in v11:
time: 62.4 us; the launch traced here: 62.1 us
  Pallas kernels  21.2 us (34%)
  blocking collectives  14 us (22%)
  starting transfers between devices  13.3 us (21%)
  waiting for transfers between devices  8.1 us (13%)
  local copies, waits for them, and re-layouts  4.71 us (8%)
  between operations  0.78 us (1%)
    all_to_all x1, blocking collectives, shards(): terms = lax.all_to_all(terms, ('dom', 'pert'), 0, 0, tiled=True)  14 us
    ppermute x12, starting transfers between devices, rotated(): lax.ppermute(value, 'dom', [(i, (i + by) % peers) for i in range(peers)])  8.07 us
    ppermute x12, waiting for transfers between devices, rotated(): lax.ppermute(value, 'dom', [(i, (i + by) % peers) for i in range(peers)])  6.51 us
    pallas_call x1, Pallas kernels, shards(): call(first_kernel, [shape(coupling.shape, BF16), shape((pairs, 8, LANES),...  6.37 us
    pallas_call x1, Pallas kernels, shards(): call(turn_kernel, [shape((pert, blocks * HALF), F32), shape((pert, LANES)...  5.52 us
    all_to_all x1, starting transfers between devices, shards(): got = lax.all_to_all(outgoing, 'dom', 0, 0, tiled=True)  5.18 us
    unnamed x13, local copies, waits for them, and re-layouts  4.71 us
    pallas_call x1, Pallas kernels, shards(): call(functools.partial(melt_kernel, parts=parts), [shape((pairs, LANES),...  2.71 us
  transfers between devices with their start and end apart: 13, of which 6 were waited for; matrix products, arithmetic and copies ran while one was open for 6% of the time, Pallas kernels for 12%

profile of v11, /device:TPU:0, one launch (start us, length us, event | category | flops | bytes accessed | tf_op | source)
XLA Modules:
  0.0 62.1 jit_solution(3833943287557468701)
XLA Ops:
  0.6 0.0 copy-start.3
  0.6 0.0 copy-start.5
  0.7 0.0 copy-start.1
  0.7 2.7 %melt.1 = (f32[64,128]{1,0:T(8,128)}, f32[8,32,128]{2,1,0:T(8,128)}) custom-call(s32[1,4,16]{2,1,0:T(4,128)} %send_ref.5, f32[64,128]{1,0:T(8,128)} %bitcast.17, s32[1,128]{1,0:T(1,128)} %bitcast.13, f32[16,128]{1,0:T(8,128)} %probe_ref.1, bf16[64,64,128]{2,1,0:T(8,128)(2,1)} %bitcast.16), custom_call_target="tpu_custom_call" | custom-call | bytes 1048576 | tf_op jit(solution)/shard_map/melt/pallas_call | solution.py:705
  3.4 5.2 %all-to-all-start = ((f32[8,32,128]{2,1,0:T(8,128)}), f32[8,32,128]{2,1,0:T(8,128)S(1)}, u32[]{:S(2)}, u32[]{:S(2)}) async-start(f32[8,32,128]{2,1,0:T(8,128)} %get-tuple-element.39), calls=%async_computation | async-start | bytes 262144 | tf_op jit(solution)/shard_map/all_to_all | solution.py:720
  8.6 3.9 %copy.11.diag_ref = bf16[128,64,64]{2,1,0:T(8,128)(2,1)S(1)} copy(bf16[128,64,64]{0,2,1:T(8,128)(2,1)} %param.11) | data formatting | bytes 2097152 | tf_op args[3]
  12.5 1.6 %all-to-all-done.got_ref = f32[8,32,128]{2,1,0:T(8,128)S(1)} async-done(((f32[8,32,128]{2,1,0:T(8,128)}), f32[8,32,128]{2,1,0:T(8,128)S(1)}, u32[]{:S(2)}, u32[]{:S(2)}) %all-to-all-start) | async-done | bytes 131104 | tf_op jit(solution)/shard_map/all_to_all | solution.py:720
  14.1 0.0 copy-done.3
  14.1 0.0 copy-done.5
  14.1 0.0 copy-done.1
  14.1 0.0 copy-start
  14.1 0.7 %copy-done = f32[64,128]{1,0:T(8,128)S(1)} copy-done((f32[64,128]{1,0:T(8,128)S(1)}, f32[64,128]{1,0:T(8,128)}, u32[]{:S(2)}) %copy-start) | copy-done | bytes 32792
  14.9 6.4 %first.1 = (bf16[128,64,256]{2,1,0:T(8,128)(2,1)S(1)}, f32[64,8,128]{2,1,0:T(8,128)S(1)}, f32[8,128]{1,0:T(8,128)S(1)}, f32[8,128]{1,0:T(8,128)S(1)}, f32[64,16,...) custom-call(s32[4,128]{1,0:T(4,128)S(1)} %bitcast.6, ...), custom_call_target="tpu_custom_call" | custom-call | bytes 1048576 | tf_op jit(solution)/shard_map/first/pallas_call | solution.py:722
  21.2 1.4 %collective-permute-start = (bf16[13,16,128]{2,1,0:T(8,128)(2,1)S(1)}, bf16[13,16,128]{2,1,0:T(8,128)(2,1)S(1)}, u32[]{:S(2)}, u32[]{:S(2)}) collective-permute-start(bf16[13,16,128]{2,1,0:T(8,128)(2,1)S(1)} %get-tuple-element.43), channel_id=1, source_target_pairs={{0,24},{4,28},{8,0},{12,4},{16,8},{20,12},{24,16},{28,20},{1,25},{... | collective-permute-start | bytes 159752 | tf_op jit(solution)/shard_map/ppermute | solution.py:34
  22.7 0.0 collective-permute-start.1
  22.7 0.5 collective-permute-start.2
  23.2 1.0 %collective-permute-start.3 = (bf16[13,16,128]{2,1,0:T(8,128)(2,1)S(1)}, bf16[13,16,128]{2,1,0:T(8,128)(2,1)S(1)}, u32[]{:S(2)}, u32[]{:S(2)}) collective-permute-start(bf16[13,16,128]{2,1,0:T(8,128)(2,1)S(1)} %get-tuple-element.46), channel_id=1, source_target_pairs={{0,8},{4,12},{8,16},{12,20},{16,24},{20,28},{24,0},{28,4},{1,9},{5... | collective-permute-start | bytes 159752 | tf_op jit(solution)/shard_map/ppermute | solution.py:34
  24.2 1.2 %collective-permute-done.g0.v0 = bf16[13,16,128]{2,1,0:T(8,128)(2,1)S(1)} collective-permute-done((bf16[13,16,128]{2,1,0:T(8,128)(2,1)S(1)}, bf16[13,16,128]{2,1,0:T(8,128)(2,1)S(1)}, u32[]{:S(2)}, u32[]{:S(2)}) %collective-permute-start) | collective-permute-done | bytes 53280 | tf_op jit(solution)/shard_map/ppermute | solution.py:34
  25.4 0.0 collective-permute-done.1.g1.v1
  25.4 1.7 %collective-permute-done.2.g2.v2 = bf16[13,16,128]{2,1,0:T(8,128)(2,1)S(1)} collective-permute-done((bf16[13,16,128]{2,1,0:T(8,128)(2,1)S(1)}, bf16[13,16,128]{2,1,0:T(8,128)(2,1)S(1)}, u32[]{:S(2)}, u32[]{:S(2)}) %collective-permute-start.2) | collective-permute-done | bytes 53280 | tf_op jit(solution)/shard_map/ppermute | solution.py:34
  27.2 1.5 %collective-permute-done.3.g3.v3 = bf16[13,16,128]{2,1,0:T(8,128)(2,1)S(1)} collective-permute-done((bf16[13,16,128]{2,1,0:T(8,128)(2,1)S(1)}, bf16[13,16,128]{2,1,0:T(8,128)(2,1)S(1)}, u32[]{:S(2)}, u32[]{:S(2)}) %collective-permute-start.3) | collective-permute-done | bytes 53280 | tf_op jit(solution)/shard_map/ppermute | solution.py:34
  28.7 0.0 copy-start.2
  28.7 2.2 %sweep.1 = (bf16[128,16,128]{2,1,0:T(8,128)(2,1)S(1)}, bf16[8,16,128]{2,1,0:T(8,128)(2,1)S(1)}, bf16[8,16,128]{2,1,0:T(8,128)(2,1)S(1)}, bf16[8,16,128]{2,1,0:T(8,128)(2,1)S(1)}, bf16[8,16,128]{2,1,0:T(8,128)(2,1)S(1)}) custom-call(s32[4,128]{1,0:T(4,128)S(1)} %bitcast.8, s32[1,4,16]{2,1,0:T(4,128)S(1)} %copy-done.3, ...), custom_call_target="tpu_custom_call" | custom-call | bytes 1048576 | tf_op jit(solution)/shard_map/sweep/pallas_call | solution.py:746
  30.9 0.2 collective-permute-start.4
  31.1 1.5 %collective-permute-start.5 = (bf16[8,16,128]{2,1,0:T(8,128)(2,1)S(1)}, bf16[8,16,128]{2,1,0:T(8,128)(2,1)S(1)}, u32[]{:S(2)}, u32[]{:S(2)}) collective-permute-start(bf16[8,16,128]{2,1,0:T(8,128)(2,1)S(1)} %get-tuple-element.57), channel_id=1, source_target_pairs={{0,28},{4,0},{8,4},{12,8},{16,12},{20,16},{24,20},{28,24},{1,29},{... | collective-permute-start | bytes 98312 | tf_op jit(solution)/shard_map/ppermute | solution.py:34
  32.6 0.0 collective-permute-start.6
  32.6 0.9 %collective-permute-start.7 = (bf16[8,16,128]{2,1,0:T(8,128)(2,1)S(1)}, bf16[8,16,128]{2,1,0:T(8,128)(2,1)S(1)}, u32[]{:S(2)}, u32[]{:S(2)}) collective-permute-start(bf16[8,16,128]{2,1,0:T(8,128)(2,1)S(1)} %get-tuple-element.59), channel_id=1, source_target_pairs={{0,8},{4,12},{8,16},{12,20},{16,24},{20,28},{24,0},{28,4},{1,9},{5... | collective-permute-start | bytes 98312 | tf_op jit(solution)/shard_map/ppermute | solution.py:34
  33.5 2.0 %window.1 = (bf16[1024,896]{1,0:T(8,128)(2,1)S(1)}, bf16[9,16,128]{2,1,0:T(8,128)(2,1)S(1)}, bf16[9,16,128]{2,1,0:T(8,128)(2,1)S(1)}, bf16[9,16,128]{2,1,0:T(8,128)(2,1)S(1)}, bf16[9,16,128]{2,1,0:T(8,128)(2,1)S(1)}) custom-call(s32[4,128]{1,0:T(4,128)S(1)} %bitcast.9, s32[1,4,16]{2,1,0:T(4,128)S(1)} %copy-done.3, s32[4,128]{1,0:T(4,128)S(1)} %bitcast.10, ...), custom_call_target="tpu_custom_call" | custom-call | bytes 4194304 | tf_op jit(solution)/shard_map/window/pallas_call | solution.py:750
  35.5 0.0 collective-permute-done.4.g0
  35.5 0.0 collective-permute-done.5.g1
  35.5 1.3 %collective-permute-done.6.g2 = bf16[8,16,128]{2,1,0:T(8,128)(2,1)S(1)} collective-permute-done((bf16[8,16,128]{2,1,0:T(8,128)(2,1)S(1)}, bf16[8,16,128]{2,1,0:T(8,128)(2,1)S(1)}, u32[]{:S(2)}, u32[]{:S(2)}) %collective-permute-start.6) | collective-permute-done | bytes 32800 | tf_op jit(solution)/shard_map/ppermute | solution.py:34
  36.8 0.7 %collective-permute-done.7.g3 = bf16[8,16,128]{2,1,0:T(8,128)(2,1)S(1)} collective-permute-done((bf16[8,16,128]{2,1,0:T(8,128)(2,1)S(1)}, bf16[8,16,128]{2,1,0:T(8,128)(2,1)S(1)}, u32[]{:S(2)}, u32[]{:S(2)}) %collective-permute-start.7) | collective-permute-done | bytes 32800 | tf_op jit(solution)/shard_map/ppermute | solution.py:34
  37.5 0.1 collective-permute-start.8
  37.6 1.9 %collective-permute-start.9 = (bf16[9,16,128]{2,1,0:T(8,128)(2,1)S(1)}, bf16[9,16,128]{2,1,0:T(8,128)(2,1)S(1)}, u32[]{:S(2)}, u32[]{:S(2)}) collective-permute-start(bf16[9,16,128]{2,1,0:T(8,128)(2,1)S(1)} %get-tuple-element.68), channel_id=1, source_target_pairs={{0,28},{4,0},{8,4},{12,8},{16,12},{20,16},{24,20},{28,24},{1,29},{... | collective-permute-start | bytes 110600 | tf_op jit(solution)/shard_map/ppermute | solution.py:34
  39.5 0.0 collective-permute-start.10
  39.5 0.5 collective-permute-start.11
  40.1 0.0 copy-done.2
  40.1 0.0 copy-start.4
  40.1 5.5 %turn.1 = (f32[16,8192]{1,0:T(8,128)}, f32[16,128]{1,0:T(8,128)S(1)}, bf16[96,16,128]{2,1,0:T(8,128)(2,1)S(1)}, bf16[32,16,128]{2,1,0:T(8,128)(2,1)S(1)}) custom-call(s32[4,128]{1,0:T(4,128)S(1)} %bitcast.11, f32[64,16,128]{2,1,0:T(8,128)S(1)} %get-tuple-element.41.t1_ref, bf16[128,16,128]{2,1,0:T(8,128)(2,1)S(1)} %get-tuple-element.48.prev_ref, ...), custom_call_target="tpu_custom_call" | custom-call | bytes 16777216 | tf_op jit(solution)/shard_map/turn/pallas_call | solution.py:761
  45.6 0.0 collective-permute-done.8.x0
  45.6 0.0 collective-permute-done.9.x1
  45.6 0.0 collective-permute-done.10.x2
  45.6 0.0 collective-permute-done.11.x3
  45.6 1.8 %last.1 = bf16[32,16,128]{2,1,0:T(8,128)(2,1)S(1)} custom-call(bf16[96,16,128]{2,1,0:T(8,128)(2,1)S(1)} %get-tuple-element.65.z_ref, bf16[32,16,128]{2,1,0:T(8,128)(2,1)S(1)} %get-tuple-element.66.y_ref, f32[64,8,128]{2,1,0:T(8,128)S(1)} %get-tuple-element.51.v_ref, bf16[13,16,128]{2,1,0:T(8,128)(2,1)S(1)} %collective-permute-done.g0.v0, ...), custom_call_target="tpu_custom_call" | custom-call | bytes 1048576 | tf_op jit(solution)/shard_map/last/pallas_call | solution.py:782
  47.5 14.0 %all_to_all.10.terms_ref = bf16[32,16,128]{2,1,0:T(8,128)(2,1)S(1)} all-to-all(bf16[32,16,128]{2,1,0:T(8,128)(2,1)S(1)} %last.1), channel_id=1, replica_groups=mesh['dom'=8,'pert'=4] {'dom','pert'}, dimensions={0} | all-to-all | bytes 262144 | tf_op jit(solution)/shard_map/all_to_all | solution.py:785
  61.5 0.0 copy-done.4
  61.5 0.6 owner.1
Async XLA Ops:
  0.6 13.5 %copy-start.3 = (s32[1,4,16]{2,1,0:T(4,128)S(1)}, s32[1,4,16]{2,1,0:T(4,128)}, u32[]{:S(2)}) copy-start(s32[1,4,16]{2,1,0:T(4,128)} %send_ref.5) | copy-start | bytes 772
  0.6 13.5 %copy-start.5 = (s32[128]{0:T(128)S(1)}, s32[128]{0:T(128)}, u32[]{:S(2)}) copy-start(s32[128]{0:T(128)} %param.15) | copy-start | bytes 1540
  0.7 13.4 %copy-start.1 = (s32[128,4]{0,1:T(4,128)S(1)}, s32[128,4]{0,1:T(4,128)}, u32[]{:S(2)}) copy-start(s32[128,4]{0,1:T(4,128)} %param.13) | copy-start | bytes 6148
  3.4 10.7 %all-to-all-start = ((f32[8,32,128]{2,1,0:T(8,128)}), f32[8,32,128]{2,1,0:T(8,128)S(1)}, u32[]{:S(2)}, u32[]{:S(2)}) async-start(f32[8,32,128]{2,1,0:T(8,128)} %get-tuple-element.39), calls=%async_computation | async-start | bytes 262144 | tf_op jit(solution)/shard_map/all_to_all | solution.py:720
  14.1 0.8 %copy-start = (f32[64,128]{1,0:T(8,128)S(1)}, f32[64,128]{1,0:T(8,128)}, u32[]{:S(2)}) copy-start(f32[64,128]{1,0:T(8,128)} %get-tuple-element.40.w_hbm.w_ref) | copy-start | bytes 98308
  21.2 4.2 %collective-permute-start = (bf16[13,16,128]{2,1,0:T(8,128)(2,1)S(1)}, bf16[13,16,128]{2,1,0:T(8,128)(2,1)S(1)}, u32[]{:S(2)}, u32[]{:S(2)}) collective-permute-start(bf16[13,16,128]{2,1,0:T(8,128)(2,1)S(1)} %get-tuple-element.43), channel_id=1, source_target_pairs={{0,24},{4,28},{8,0},{12,4},{16,8},{20,12},{24,16},{28,20},{1,25},{... | collective-permute-start | bytes 159752 | tf_op jit(solution)/shard_map/ppermute | solution.py:34
  22.7 2.8 %collective-permute-start.1 = (bf16[13,16,128]{2,1,0:T(8,128)(2,1)S(1)}, bf16[13,16,128]{2,1,0:T(8,128)(2,1)S(1)}, u32[]{:S(2)}, u32[]{:S(2)}) collective-permute-start(bf16[13,16,128]{2,1,0:T(8,128)(2,1)S(1)} %get-tuple-element.44), channel_id=1, source_target_pairs={{0,28},{4,0},{8,4},{12,8},{16,12},{20,16},{24,20},{28,24},{1,29},{... | collective-permute-start | bytes 159752 | tf_op jit(solution)/shard_map/ppermute | solution.py:34
  22.7 4.5 %collective-permute-start.2 = (bf16[13,16,128]{2,1,0:T(8,128)(2,1)S(1)}, bf16[13,16,128]{2,1,0:T(8,128)(2,1)S(1)}, u32[]{:S(2)}, u32[]{:S(2)}) collective-permute-start(bf16[13,16,128]{2,1,0:T(8,128)(2,1)S(1)} %get-tuple-element.45), channel_id=1, source_target_pairs={{0,4},{4,8},{8,12},{12,16},{16,20},{20,24},{24,28},{28,0},{1,5},{5... | collective-permute-start | bytes 159752 | tf_op jit(solution)/shard_map/ppermute | solution.py:34
  23.2 5.5 %collective-permute-start.3 = (bf16[13,16,128]{2,1,0:T(8,128)(2,1)S(1)}, bf16[13,16,128]{2,1,0:T(8,128)(2,1)S(1)}, u32[]{:S(2)}, u32[]{:S(2)}) collective-permute-start(bf16[13,16,128]{2,1,0:T(8,128)(2,1)S(1)} %get-tuple-element.46), channel_id=1, source_target_pairs={{0,8},{4,12},{8,16},{12,20},{16,24},{20,28},{24,0},{28,4},{1,9},{5... | collective-permute-start | bytes 159752 | tf_op jit(solution)/shard_map/ppermute | solution.py:34
  28.7 11.4 %copy-start.2 = (f32[8192]{0:T(1024)S(1)}, f32[8192]{0:T(1024)}, u32[]{:S(2)}) copy-start(f32[8192]{0:T(1024)} %param.10) | copy-start | bytes 98308
  30.9 4.6 %collective-permute-start.4 = (bf16[8,16,128]{2,1,0:T(8,128)(2,1)S(1)}, bf16[8,16,128]{2,1,0:T(8,128)(2,1)S(1)}, u32[]{:S(2)}, u32[]{:S(2)}) collective-permute-start(bf16[8,16,128]{2,1,0:T(8,128)(2,1)S(1)} %get-tuple-element.56), channel_id=1, source_target_pairs={{0,24},{4,28},{8,0},{12,4},{16,8},{20,12},{24,16},{28,20},{1,25},{... | collective-permute-start | bytes 98312 | tf_op jit(solution)/shard_map/ppermute | solution.py:34
  31.1 4.4 %collective-permute-start.5 = (bf16[8,16,128]{2,1,0:T(8,128)(2,1)S(1)}, bf16[8,16,128]{2,1,0:T(8,128)(2,1)S(1)}, u32[]{:S(2)}, u32[]{:S(2)}) collective-permute-start(bf16[8,16,128]{2,1,0:T(8,128)(2,1)S(1)} %get-tuple-element.57), channel_id=1, source_target_pairs={{0,28},{4,0},{8,4},{12,8},{16,12},{20,16},{24,20},{28,24},{1,29},{... | collective-permute-start | bytes 98312 | tf_op jit(solution)/shard_map/ppermute | solution.py:34
  32.6 4.2 %collective-permute-start.6 = (bf16[8,16,128]{2,1,0:T(8,128)(2,1)S(1)}, bf16[8,16,128]{2,1,0:T(8,128)(2,1)S(1)}, u32[]{:S(2)}, u32[]{:S(2)}) collective-permute-start(bf16[8,16,128]{2,1,0:T(8,128)(2,1)S(1)} %get-tuple-element.58), channel_id=1, source_target_pairs={{0,4},{4,8},{8,12},{12,16},{16,20},{20,24},{24,28},{28,0},{1,5},{5... | collective-permute-start | bytes 98312 | tf_op jit(solution)/shard_map/ppermute | solution.py:34
  32.6 4.9 %collective-permute-start.7 = (bf16[8,16,128]{2,1,0:T(8,128)(2,1)S(1)}, bf16[8,16,128]{2,1,0:T(8,128)(2,1)S(1)}, u32[]{:S(2)}, u32[]{:S(2)}) collective-permute-start(bf16[8,16,128]{2,1,0:T(8,128)(2,1)S(1)} %get-tuple-element.59), channel_id=1, source_target_pairs={{0,8},{4,12},{8,16},{12,20},{16,24},{20,28},{24,0},{28,4},{1,9},{5... | collective-permute-start | bytes 98312 | tf_op jit(solution)/shard_map/ppermute | solution.py:34
  37.5 8.1 %collective-permute-start.8 = (bf16[9,16,128]{2,1,0:T(8,128)(2,1)S(1)}, bf16[9,16,128]{2,1,0:T(8,128)(2,1)S(1)}, u32[]{:S(2)}, u32[]{:S(2)}) collective-permute-start(bf16[9,16,128]{2,1,0:T(8,128)(2,1)S(1)} %get-tuple-element.67), channel_id=1, source_target_pairs={{0,24},{4,28},{8,0},{12,4},{16,8},{20,12},{24,16},{28,20},{1,25},{... | collective-permute-start | bytes 110600 | tf_op jit(solution)/shard_map/ppermute | solution.py:34
  37.6 8.0 %collective-permute-start.9 = (bf16[9,16,128]{2,1,0:T(8,128)(2,1)S(1)}, bf16[9,16,128]{2,1,0:T(8,128)(2,1)S(1)}, u32[]{:S(2)}, u32[]{:S(2)}) collective-permute-start(bf16[9,16,128]{2,1,0:T(8,128)(2,1)S(1)} %get-tuple-element.68), channel_id=1, source_target_pairs={{0,28},{4,0},{8,4},{12,8},{16,12},{20,16},{24,20},{28,24},{1,29},{... | collective-permute-start | bytes 110600 | tf_op jit(solution)/shard_map/ppermute | solution.py:34
  39.5 6.1 %collective-permute-start.10 = (bf16[9,16,128]{2,1,0:T(8,128)(2,1)S(1)}, bf16[9,16,128]{2,1,0:T(8,128)(2,1)S(1)}, u32[]{:S(2)}, u32[]{:S(2)}) collective-permute-start(bf16[9,16,128]{2,1,0:T(8,128)(2,1)S(1)} %get-tuple-element.69), channel_id=1, source_target_pairs={{0,4},{4,8},{8,12},{12,16},{16,20},{20,24},{24,28},{28,0},{1,5},{5... | collective-permute-start | bytes 110600 | tf_op jit(solution)/shard_map/ppermute | solution.py:34
  39.5 6.1 %collective-permute-start.11 = (bf16[9,16,128]{2,1,0:T(8,128)(2,1)S(1)}, bf16[9,16,128]{2,1,0:T(8,128)(2,1)S(1)}, u32[]{:S(2)}, u32[]{:S(2)}) collective-permute-start(bf16[9,16,128]{2,1,0:T(8,128)(2,1)S(1)} %get-tuple-element.70), channel_id=1, source_target_pairs={{0,8},{4,12},{8,16},{12,20},{16,24},{20,28},{24,0},{28,4},{1,9},{5... | collective-permute-start | bytes 110600 | tf_op jit(solution)/shard_map/ppermute | solution.py:34
  40.1 21.4 %copy-start.4 = (f32[16,128]{1,0:T(8,128)S(1)}, f32[16,128]{1,0:T(8,128)}, u32[]{:S(2)}) copy-start(f32[16,128]{1,0:T(8,128)} %probe_ref.1) | copy-start | bytes 24580
